TPU v7x, 32 devices: a whole 2x2x4 slice. The times are simulated.
32 devices in a mesh: groups: 2 (over y), coef: 4 (over x, core), slab: 4 (over z).
Axes of the slice: x: 2, y: 2, z: 4, core: 2. Of those that a mesh axis runs over, the one named last changes fastest.
Arguments:
- coefficients: float32 [896, 32768], P('coef', ('groups', 'slab')), parts along dimension 1, may hold values from -6 to 6
- measured: float32 [16, 4, 64, 256], P('groups', 'slab'), parts along dimension 0, may hold values from -6 to 6
- ray_voxels: int32 [8, 64, 128], replicated, may hold values from 0 to 4095
- ray_weights: int32 [8, 64, 128], replicated, may hold values from 1 to 63
- angle_ids: int32 [8], replicated, may hold values from 0 to 15
- angle_table: bfloat16 [16, 896, 256], P(None, 'coef'), may hold values from -0.1875 to 0.1875
- harmonics: bfloat16 [896, 2048], P('coef'), may hold values from -0.1875 to 0.1875
Outputs:
- updated: float32 [896, 32768], P('coef', ('groups', 'slab')), parts along dimension 1
- residual: float32 [16, 4, 64, 256], P('groups', 'slab', None, 'coef'), parts along dimension 0
There are 2 independent parts, one for each index of `groups`. A program takes and returns all parts, laid end to end along the dimension named above; an argument that names none is the same for every part. Nothing has to cross between parts.
All inputs are finite; a program needn't handle non-finite values.
Results may differ from a plain program's by a relative error of at most 0.0034.
Values may be sent and summed in bfloat16 or wider, within the bound.
No kernel may reach another device: no remote copies, remote signals or barrier semaphores. Data moves between devices by JAX's collectives and lax.ppermute only.
A program may use at most 64 MiB of HBM per device.

v0:
```python
import jax
import jax.numpy as jnp
from jax import lax
from jax.sharding import PartitionSpec as P

NG = 64


def build_matrix(ray_voxels, ray_weights):
    shape_all = ray_voxels.shape
    side_count = NG
    high_part = ray_voxels // side_count
    low_part = ray_voxels % side_count
    positions = jnp.arange(side_count, dtype=jnp.int32)
    values = (ray_weights.astype(jnp.float32) / 256.0).astype(jnp.bfloat16)
    high_table = jnp.where(
        high_part[..., None] == positions, values[..., None], jnp.zeros((), jnp.bfloat16)
    )
    low_table = (low_part[..., None] == positions).astype(jnp.bfloat16)
    high_flat = high_table.reshape(shape_all[0] * shape_all[1], shape_all[2], side_count)
    low_flat = low_table.reshape(shape_all[0] * shape_all[1], shape_all[2], side_count)
    product = lax.dot_general(
        high_flat, low_flat, (((1,), (1,)), ((0,), (0,))), preferred_element_type=jnp.float32
    )
    return product.astype(jnp.bfloat16).reshape(shape_all[0], shape_all[1], side_count * side_count)


def select_angles(angle_ids, angle_table):
    entries = angle_table.shape[0]
    onehot = (angle_ids[:, None] == jnp.arange(entries)[None, :]).astype(jnp.bfloat16)
    flat_table = angle_table.reshape(entries, -1)
    picked = jnp.dot(onehot, flat_table, preferred_element_type=jnp.float32)
    return picked.astype(jnp.bfloat16).reshape((angle_ids.shape[0],) + angle_table.shape[1:])


def body(coefficients, measured, ray_voxels, ray_weights, angle_ids, angle_table, harmonics):
    coef_local = coefficients.shape[0]
    layers = coefficients.shape[1] // (NG * NG)
    system_matrix = build_matrix(ray_voxels, ray_weights)
    chosen = select_angles(angle_ids, angle_table)
    coef_half = coefficients.astype(jnp.bfloat16)
    stacked_rows = coef_half.reshape(coef_local, layers, NG * NG)
    ray_totals = jnp.einsum(
        "dmj,hqj->dqmh", system_matrix, stacked_rows, preferred_element_type=jnp.float32
    ).astype(jnp.bfloat16)
    partial_value = jnp.einsum(
        "azrk,akc->azrc", ray_totals, chosen, preferred_element_type=jnp.float32
    )
    chan_width = measured.shape[3] // lax.axis_size("coef")
    chan_start = lax.axis_index("coef") * chan_width
    predicted = lax.psum_scatter(partial_value, "coef", scatter_dimension=3, tiled=True)
    residual = predicted - lax.dynamic_slice_in_dim(measured, chan_start, chan_width, 3)
    resid_half = residual.astype(jnp.bfloat16)
    backward_projection = jnp.einsum(
        "azrc,akc->azrk",
        lax.all_gather(resid_half, "coef", axis=3, tiled=True),
        chosen,
        preferred_element_type=jnp.float32,
    )
    backward_half = backward_projection.astype(jnp.bfloat16)
    misfit_gradient = jnp.einsum(
        "qci,qbcy->ybi", system_matrix, backward_half, preferred_element_type=jnp.float32
    )
    misfit_gradient = misfit_gradient.reshape(coef_local, layers * NG * NG)
    grid_rows = coef_half.reshape(coef_local, layers * NG, NG)
    blocks = lax.all_to_all(grid_rows, "coef", split_axis=1, concat_axis=0, tiled=True)
    width_all, row_span, item_count = blocks.shape
    flat_cols = blocks.reshape(width_all, row_span * item_count)
    orient_field = lax.dot_general(
        flat_cols,
        lax.all_gather(harmonics, "coef", axis=0, tiled=True),
        (((0,), (0,)), ((), ())),
        preferred_element_type=jnp.float32,
    )
    slope_half = (-jax.nn.sigmoid(-orient_field)).astype(jnp.bfloat16)
    reg_grad = lax.dot_general(
        lax.all_gather(harmonics, "coef", axis=0, tiled=True),
        slope_half,
        (((1,), (1,)), ((), ())),
        preferred_element_type=jnp.float32,
    )
    reg_grad = reg_grad.reshape(width_all, row_span, item_count)
    reg_grad = lax.all_to_all(reg_grad, "coef", split_axis=0, concat_axis=1, tiled=True)
    reg_grad = reg_grad.reshape(coef_local, layers * NG * NG)
    updated = coefficients - 0.5 * misfit_gradient - 0.5 * reg_grad
    return (updated, residual)


def solution(mesh):
    in_specs = (
        P("coef", ("groups", "slab")),
        P("groups", "slab", None, None),
        P(),
        P(),
        P(),
        P(None, "coef", None),
        P("coef", None),
    )
    out_specs = (P("coef", ("groups", "slab")), P("groups", "slab", None, "coef"))
    return jax.shard_map(body, mesh=mesh, in_specs=in_specs, out_specs=out_specs, check_vma=False)
```

profile of v0, /device:TPU:0, one launch (start us, length us, event | category | flops | bytes accessed | tf_op | source)
XLA Modules:
  0.0 229.0 jit_solution(1820628051874065335)
XLA Ops:
  7.2 0.0 all-gather.2.cloned.1.call-start
  7.2 0.7 all-gather.2.cloned.1.call-update
  7.9 2.3 convert_element_type.36
  10.2 0.0 copy-start
  10.2 0.0 copy-start.3
  10.2 0.0 copy-start.2
  10.2 2.5 %copy.37 = bf16[224,4096]{0,1:T(8,128)(2,1)} copy(bf16[224,4096]{1,0:T(8,128)(2,1)S(1)} %convert_element_type.36) | data formatting | bytes 3670016 | tf_op jit(solution)/shard_map/convert_element_type | solution.py:41
  12.7 0.0 copy-done
  12.7 4.2 %all-to-all-start = ((bf16[224,64,64]{0,2,1:T(8,128)(2,1)}), bf16[224,64,64]{0,2,1:T(8,128)(2,1)S(1)}, u32[]{:S(2)}, u32[]{:S(2)}) async-start(bf16[224,64,64]{0,2,1:T(8,128)(2,1)} %bitcast.58), calls=%async_computation | async-start | bytes 4194304 | tf_op jit(solution)/shard_map/all_to_all | solution.py:66
  16.9 0.0 copy-done.3
  17.0 0.0 copy-done.2
  17.0 0.2 add_select_fusion.1
  17.2 45.1 %all-to-all-done = bf16[224,64,64]{0,2,1:T(8,128)(2,1)S(1)} async-done(((bf16[224,64,64]{0,2,1:T(8,128)(2,1)}), bf16[224,64,64]{0,2,1:T(8,128)(2,1)S(1)}, u32[]{:S(2)}, u32[]{:S(2)}) %all-to-all-start) | async-done | bytes 1835040 | tf_op jit(solution)/shard_map/all_to_all | solution.py:66
  62.3 3.1 %copy.53 = bf16[224,4,16,64]{0,1,3,2:T(4,128)(2,1)} copy(bf16[224,4,16,64]{0,3,2,1:T(8,128)(2,1)S(1)} %bitcast.57) | data formatting | bytes 3670016 | tf_op jit(solution)/shard_map/all_to_all | solution.py:66
  65.3 3.9 %reshape.62 = bf16[896,1024]{0,1:T(8,128)(2,1)S(1)} reshape(bf16[4,224,16,64]{1,0,3,2:T(4,128)(2,1)} %bitcast.59) | data formatting | bytes 3670016 | tf_op jit(solution)/shard_map/reshape | solution.py:68
  69.3 0.0 all-gather.2.cloned.1.call-done
  69.3 13.8 %fusion.13 = f32[1024,896]{1,0:T(8,128)} fusion(bf16[896,2048]{1,0:T(8,128)(2,1)} %all-gather.2.cloned.1.call-done, bf16[896,1024]{0,1:T(8,128)(2,1)S(1)} %reshape.62), kind=kOutput, calls=%fused_computation.15 | convolution fusion | flops 7524581376 | bytes 9175040 | tf_op jit(solution)/shard_map/dot_general | solution.py:76
  83.1 7.7 %copy.39 = f32[896,16,64]{2,1,0:T(8,128)} copy(f32[896,16,64]{0,2,1:T(8,128)} %bitcast.64) | data formatting | bytes 7340032 | tf_op jit(solution)/shard_map/reshape | solution.py:82
  90.8 7.8 %reshape.68 = f32[4,1,229376]{2,1,0:T(1,128)} reshape(f32[896,16,64]{2,1,0:T(8,128)} %copy.39) | data formatting | bytes 7340032
  98.6 4.8 %all-to-all-start.1 = ((f32[4,1,229376]{2,1,0:T(1,128)}), f32[4,1,229376]{2,1,0:T(1,128)}, u32[]{:S(2)}, u32[]{:S(2)}) async-start(f32[4,1,229376]{2,1,0:T(1,128)} %reshape.68), calls=%async_computation.1 | async-start | bytes 7340032 | tf_op jit(solution)/shard_map/all_to_all | solution.py:83
  103.4 0.2 reduce-scatter.4.cloned.1.call-start
  103.6 6.6 %fusion.5 = bf16[512,64,64]{2,1,0:T(8,128)(2,1)} fusion(s32[512,128]{1,0:T(8,128)S(1)} %bitcast.68, s32[512,128]{1,0:T(8,128)S(1)} %bitcast.67, bf16[512,128]{1,0:T(8,128)(2,1)S(1)} %bitcast.70), kind=kOutput, calls=%fused_computation.8 | convolution fusion | flops 551550976 | bytes 4849664 | tf_op jit(solution)/shard_map/dot_general | solution.py:22
  110.3 12.0 %reshape.57 = bf16[8,64,4096]{2,1,0:T(8,128)(2,1)} reshape(bf16[512,64,64]{2,1,0:T(8,128)(2,1)} %fusion.5) | data formatting | bytes 8388608 | tf_op jit(solution)/shard_map/reshape | solution.py:25
  122.3 2.7 %copy.46 = bf16[2,8,224,256]{3,1,2,0:T(8,128)(2,1)S(1)} copy(bf16[2,8,224,256]{3,2,1,0:T(8,128)(2,1)} %bitcast.65) | data formatting | bytes 3670016
  125.0 0.5 convolution_convert_fusion
  125.4 0.0 copy-done.1
  125.5 3.8 %convolution_bitcast_fusion.1 = f32[8,1,64,256]{3,2,0,1:T(8,128)S(1)} fusion(bf16[8,224,256]{2,0,1:T(8,128)(2,1)S(1)} %bitcast.62, bf16[8,64,4096]{2,1,0:T(8,128)(2,1)} %reshape.57, bf16[224,4096]{1,0:T(8,128)(2,1)S(1)} %copy-done.1), kind=kOutput, calls=%fused_computation.20 | convolution fusion | flops 998359040 | bytes 7471104 | tf_op jit(solution)/shard_map/azrk,akc->azrc/dot_general | solution.py:46
  129.3 0.0 copy-start.4
  129.3 0.4 copy.44
  129.7 1.1 reshape.66
  130.8 0.0 reduce-scatter.4.cloned.1.call-update
  130.8 24.1 %reduce-scatter.4.cloned.1.call-done = f32[64,512]{1,0:T(8,128)} async-done(((f32[256,512]{1,0:T(8,128)}), f32[64,512]{1,0:T(8,128)}) %reduce-scatter.4.cloned.1.call-update) | async-done | bytes 131088
  155.0 1.0 reshape.67
  156.0 0.1 copy.45
  156.1 0.8 fusion.28
  157.0 0.1 copy.34
  157.1 6.8 %all_gather.7 = bf16[8,1,64,256]{2,0,1,3:T(8,128)(2,1)S(1)} all-gather(bf16[8,1,64,64]{2,0,1,3:T(8,128)(2,1)S(1)} %copy.34), channel_id=1, replica_groups=mesh['groups'=2,'coef'=4,'slab'=4] {'coef'}, dimensions={3}, use_global_device_ids=true | all-gather | bytes 327680 | tf_op jit(solution)/shard_map/all_gather | solution.py:56
  163.9 0.3 copy.35
  164.2 0.0 all-to-all-done.1
  164.3 0.5 broadcast.44
  164.8 13.6 %reduce = f32[4,229376]{1,0:T(4,128)} reduce(f32[4,1,229376]{2,1,0:T(1,128)} %all-to-all-done.1, f32[]{:T(128)} %broadcast.44), dimensions={1}, to_apply=%all_to_all.21.reduce_sub_computation | reduce | bytes 7340036 | tf_op jit(solution)/shard_map/all_to_all | solution.py:83
  178.4 8.4 %reshape.69 = f32[896,16,64]{2,1,0:T(8,128)} reshape(f32[4,229376]{1,0:T(4,128)} %reduce) | data formatting | bytes 7340032
  186.8 6.5 %copy.40 = f32[896,16,64]{0,2,1:T(8,128)} copy(f32[896,16,64]{2,1,0:T(8,128)} %reshape.69) | data formatting | bytes 7340032 | tf_op jit(solution)/shard_map/all_to_all | solution.py:83
  193.3 4.2 %broadcast_multiply_fusion = f32[896,16,64]{0,2,1:T(8,128)} fusion(f32[896,16,64]{0,2,1:T(8,128)} %copy.40), kind=kLoop, calls=%fused_computation.19 | loop fusion | flops 917504 | bytes 7340032 | tf_op jit(solution)/shard_map/mul | solution.py:85
  197.6 6.4 %mul.21 = f32[4,224,16,64]{1,0,3,2:T(4,128)} reshape(f32[896,16,64]{0,2,1:T(8,128)} %broadcast_multiply_fusion) | data formatting | bytes 7340032 | tf_op jit(solution)/shard_map/mul | solution.py:85
  204.0 5.0 %copy.41 = f32[224,4,16,64]{0,3,2,1:T(8,128)} copy(f32[224,4,16,64]{0,1,3,2:T(4,128)} %bitcast.55) | data formatting | bytes 7340032 | tf_op jit(solution)/shard_map/mul | solution.py:85
  209.0 5.5 %copy.42 = f32[224,4096]{1,0:T(8,128)} copy(f32[224,4096]{0,1:T(8,128)} %bitcast.56) | data formatting | bytes 7340032 | tf_op jit(solution)/shard_map/mul | solution.py:85
  214.4 7.8 %fusion.10 = f32[224,4096]{1,0:T(8,128)} fusion(f32[224,4096]{1,0:T(8,128)} %copy.42, f32[224,4096]{1,0:T(8,128)} %param.7, bf16[8,64,4096]{2,1,0:T(8,128)(2,1)} %reshape.57, bf16[8,224,256]{2,0,1:T(8,128)(2,1)S(1)} %bitcast.63, bf16[8,1,64,256]{3,2,0,1:T(8,128)(2,1)S(1)} %copy.35), kind=kOutput, calls=%fused_computation.12 | convolution fusion | flops 1001111552 | bytes 16384000 | tf_op jit(solution)/shard_map/qci,qbcy->ybi/dot_general | solution.py:61
  (5 shorter events, 0.0 us)
Async XLA Ops:
  7.2 62.1 %all-gather.2.cloned.1.call-start = ((), (), s32[]{:S(2)}) async-start(), calls=%async_computation.3 | async-start | bytes 4587520 | tf_op jit(solution)/shard_map/all_gather | solution.py:77
  10.2 2.5 %copy-start = (bf16[224,4096]{1,0:T(8,128)(2,1)}, bf16[224,4096]{1,0:T(8,128)(2,1)S(1)}, u32[]{:S(2)}) copy-start(bf16[224,4096]{1,0:T(8,128)(2,1)S(1)} %convert_element_type.36) | copy-start | bytes 5505028
  10.2 6.7 %copy-start.3 = (s32[8,64,128]{2,1,0:T(8,128)S(1)}, s32[8,64,128]{2,1,0:T(8,128)}, u32[]{:S(2)}) copy-start(s32[8,64,128]{2,1,0:T(8,128)} %param.10) | copy-start | bytes 786436
  10.2 6.8 %copy-start.2 = (s32[8,64,128]{2,1,0:T(8,128)S(1)}, s32[8,64,128]{2,1,0:T(8,128)}, u32[]{:S(2)}) copy-start(s32[8,64,128]{2,1,0:T(8,128)} %param.9) | copy-start | bytes 786436
  12.7 49.6 %all-to-all-start = ((bf16[224,64,64]{0,2,1:T(8,128)(2,1)}), bf16[224,64,64]{0,2,1:T(8,128)(2,1)S(1)}, u32[]{:S(2)}, u32[]{:S(2)}) async-start(bf16[224,64,64]{0,2,1:T(8,128)(2,1)} %bitcast.58), calls=%async_computation | async-start | bytes 4194304 | tf_op jit(solution)/shard_map/all_to_all | solution.py:66
  98.6 65.7 %all-to-all-start.1 = ((f32[4,1,229376]{2,1,0:T(1,128)}), f32[4,1,229376]{2,1,0:T(1,128)}, u32[]{:S(2)}, u32[]{:S(2)}) async-start(f32[4,1,229376]{2,1,0:T(1,128)} %reshape.68), calls=%async_computation.1 | async-start | bytes 7340032 | tf_op jit(solution)/shard_map/all_to_all | solution.py:83
  103.4 51.6 %reduce-scatter.4.cloned.1.call-start = ((), (), s32[]{:S(2)}) async-start(), calls=%async_computation.4 | async-start | bytes 655360
  122.3 2.7 %copy-start.5 = (s32[8]{0:T(128)S(1)}, s32[8]{0:T(128)}, u32[]{:S(2)}) copy-start(s32[8]{0:T(128)} %param.11) | copy-start | bytes 100
  122.3 3.1 %copy-start.1 = (bf16[224,4096]{1,0:T(8,128)(2,1)S(1)}, bf16[224,4096]{1,0:T(8,128)(2,1)}, u32[]{:S(2)}) copy-start(bf16[224,4096]{1,0:T(8,128)(2,1)} %copy-done) | copy-start | bytes 5505028
  129.3 26.8 %copy-start.4 = (f32[8,1,64,256]{3,2,1,0:T(8,128)S(1)}, f32[8,1,64,256]{3,2,1,0:T(8,128)}, u32[]{:S(2)}) copy-start(f32[8,1,64,256]{3,2,1,0:T(8,128)} %param.8) | copy-start | bytes 1572868
Sparse Core Ops, SparseCore 0:
  9.5 53.6 all-gather.1
  130.9 23.9 reduce-scatter.3
where the time goes:
time: 230 us; the launch traced here: 229 us
  local copies, waits for them, and re-layouts  75 us (33%)
  waiting for transfers between devices  69.9 us (30%)
  matrix products  32.5 us (14%)
  other arithmetic  21.3 us (9%)
  between operations  14.2 us (6%)
  starting transfers between devices  9.3 us (4%)
  blocking collectives  6.81 us (3%)
    all_to_all x1, waiting for transfers between devices, body(): lax.all_to_all(grid_rows, 'coef', split_axis=1, concat_axis=0, tiled=True)  45.1 us
    unnamed x3, waiting for transfers between devices  24.8 us
    unnamed x19, local copies, waits for them, and re-layouts  21.5 us
    mul x3, local copies, waits for them, and re-layouts, body(): updated = coefficients - 0.5 * misfit_gradient - 0.5 * reg_grad  16.9 us
    dot_general x1, matrix products, body(): lax.dot_general(lax.all_gather(harmonics, 'coef', axis=0, tiled=True), sl...  13.8 us
    all_to_all x1, other arithmetic, body(): lax.all_to_all(reg_grad, 'coef', split_axis=0, concat_axis=1, tiled=True)  13.6 us
    reshape x1, local copies, waits for them, and re-layouts, build_matrix(): product.astype(jnp.bfloat16)  12 us
    dot_general x1, matrix products, body(): jnp.einsum('qci,qbcy->ybi', system_matrix, backward_half, preferred_eleme...  7.78 us
  transfers between devices with their start and end apart: 4, of which 2 were waited for; matrix products, arithmetic and copies ran while one was open for 18% of the time, Pallas kernels for 0%

commit v1 on v0

v1 whole, which is shorter than its diff:
```python
import jax
import jax.numpy as jnp
from jax import lax
from jax.experimental import pallas as pl
from jax.experimental.pallas import tpu as pltpu
from jax.sharding import PartitionSpec as P


LANES = 128
CHUNKS = 2
GROUP = 16
NT = (((1,), (1,)), ((), ()))
NN = (((1,), (0,)), ((), ()))
VMEM = pl.BlockSpec(memory_space=pltpu.VMEM)
SMEM = pl.BlockSpec(memory_space=pltpu.SMEM)
HBM = pl.BlockSpec(memory_space=pltpu.HBM)


def dot(a, b, dims):
    return lax.dot_general(a, b, dims, preferred_element_type=jnp.float32)


def swap(value, axis, mask):
    count = lax.axis_size(axis)
    return lax.ppermute(value, axis, [(i, i ^ mask) for i in range(count)])


def aligned(index, width):
    return pl.ds(pl.multiple_of(index * width, width), width)


def prepare_kernel(count, info, ids, coef, harm, vox, wgt, table, *refs):
    blocks, (piece, vox_out, wgt_out, chosen, stage, sems) = refs[:count], refs[count:]
    me, side, place = info[0], info[1], info[2]
    block, width = blocks[0].shape[1], piece.shape[1]
    half_rows, projections = vox_out.shape[0], chosen.shape[0]
    half = projections // 2
    order = list(range(2, count)) + [1, 0]
    copies = {}
    for m in order:
        copies[m] = pltpu.make_async_copy(coef.at[:, aligned(me ^ m, block)], stage.at[m], sems.at[m])
    rest = [
        pltpu.make_async_copy(harm.at[:, aligned(place, width)], piece, sems.at[count]),
        pltpu.make_async_copy(vox.at[aligned(side, half_rows)], vox_out, sems.at[count + 1]),
        pltpu.make_async_copy(wgt.at[aligned(side, half_rows)], wgt_out, sems.at[count + 2]),
    ]
    for i in range(projections):
        a = jnp.where(i < half, side, 1 - side) * half + i % half
        rest.append(pltpu.make_async_copy(table.at[ids[a]], chosen.at[i], sems.at[count + 3 + i]))
    for m in order:
        copies[m].start()
    for c in rest:
        c.start()
    for m in order:
        copies[m].wait()
        blocks[m][...] = stage[m].astype(jnp.bfloat16)
    for c in rest:
        c.wait()


def build_kernel(vox_ref, wgt_ref, matrix_ref, tile_ref):
    rows, samples = vox_ref.shape
    cols = matrix_ref.shape[1]
    high_count = cols // LANES
    low_pos = lax.broadcasted_iota(jnp.int32, (LANES, samples), 0)
    high_pos = lax.broadcasted_iota(jnp.int32, (high_count, samples), 0)

    def build(step, carry):
        first = pl.multiple_of(step * GROUP, GROUP)
        vox = vox_ref[pl.ds(first, GROUP), :]
        wgt = wgt_ref[pl.ds(first, GROUP), :].astype(jnp.float32) * (1.0 / 256.0)
        low = vox & (LANES - 1)
        high = lax.shift_right_logical(vox, LANES.bit_length() - 1)
        for i in range(GROUP):
            low_hot = (low_pos == low[i:i + 1]).astype(jnp.float32).astype(jnp.bfloat16)
            high_hot = jnp.where(high_pos == high[i:i + 1], wgt[i:i + 1], 0.0).astype(jnp.bfloat16)
            tile_ref[i * high_count:(i + 1) * high_count, :] = dot(high_hot, low_hot, NT)
        for h in range(high_count):
            part = tile_ref[pl.ds(h, GROUP, stride=high_count), :]
            matrix_ref[pl.ds(first, GROUP), h * LANES:(h + 1) * LANES] = part.astype(jnp.bfloat16)
        return carry

    lax.fori_loop(0, rows // GROUP, build, 0)


def sums_kernel(count, info, top_ref, low_ref, *refs):
    blocks = refs[:count]
    chosen, measured, mine_ref, other_ref, target, sem = refs[count:]
    half, rays = mine_ref.shape[:2]
    block = blocks[0].shape[1]
    me, side = info[0], info[1]
    fetch = pltpu.make_async_copy(measured.at[pl.ds(side * half, half)], target, sem)
    fetch.start()
    for out_ref, ref, start in ((other_ref, low_ref, half), (mine_ref, top_ref, 0)):
        sums = jnp.zeros((ref.shape[0], blocks[0].shape[0]), jnp.float32)
        for j in range(count):
            sums += dot(ref[:, aligned(me ^ j, block)], blocks[j][...], NT)
        sums = sums.astype(jnp.bfloat16)
        for i in range(half):
            out_ref[i] = dot(sums[i * rays:(i + 1) * rays], chosen[start + i], NN)
    fetch.wait()
    mine_ref[...] = mine_ref[...] - (2.0 / count) * target[...]


def gather_kernel(count, pieces, info, own, near, *refs):
    far, (out, sems) = refs[:-2], refs[-2:]
    place = info[2]
    height = own.shape[0]
    width = own.shape[1] // pieces
    copies = []
    for r in range(pieces):
        spot = out.at[0:height, r * width:(r + 1) * width]
        copies.append(pltpu.make_async_copy(own.at[:, aligned(place ^ r, width)], spot, sems.at[r]))
    for c in copies:
        c.start()
    for r in range(pieces):
        out[height:2 * height, r * width:(r + 1) * width] = near[:, aligned(place ^ r, width)]
        for j in range(count - 2):
            out[(j + 2) * height:(j + 3) * height, r * width:(r + 1) * width] = far[j * pieces + r][...]
    for c in copies:
        c.wait()


def penalty_kernel(count, pieces, t, waves, *refs):
    blocks, outs = refs[:count], refs[count:2 * count]
    stack, turned, acc = refs[2 * count:]
    height, chunk = outs[0].shape
    width = waves.shape[1] // pieces
    for j in range(count):
        stack[j * height:(j + 1) * height, :] = blocks[j][:, t * chunk:(t + 1) * chunk]
    turned[...] = jnp.swapaxes(stack[...], 0, 1)
    for r in range(pieces):
        wave = waves[:, r * width:(r + 1) * width]
        field = dot(turned[...], wave, NN)
        slope = (0.5 * jnp.tanh(0.5 * field) - 0.5).astype(jnp.bfloat16)
        part = dot(wave, slope, NT)
        if r > 0:
            part += acc[...]
        if r < pieces - 1:
            acc[...] = part
        else:
            for j in range(count):
                outs[j][...] = part[j * height:(j + 1) * height].astype(outs[j].dtype)


def data_kernel(count, info, mine_ref, other_ref, chosen, top_ref, low_ref, coef, *refs):
    grads = refs[:count]
    updated, residual_ref, later, back_a, back_b, buf, sems, out_sems = refs[count:]
    me, side = info[0], info[1]
    half, rays = mine_ref.shape[:2]
    chunk = grads[0].shape[1]
    own_width = residual_ref.shape[2]

    def columns(j, t):
        return aligned((me ^ j) * CHUNKS + t, chunk)

    order = [(t, j) for t in range(CHUNKS) for j in range(count)]
    copies = {}
    for n, (t, j) in enumerate(order):
        spot = buf.at[j] if t == 0 else later.at[(t - 1) * count + j]
        copies[t, j] = pltpu.make_async_copy(coef.at[:, columns(j, t)], spot, sems.at[n])
        copies[t, j].start()
    for back, ref, start in ((back_a, mine_ref, 0), (back_b, other_ref, half)):
        for i in range(half):
            part = dot(chosen[start + i], ref[i].astype(jnp.bfloat16), NT)
            back[:, i * rays:(i + 1) * rays] = part.astype(jnp.bfloat16)
    writes = []
    for t, j in order:
        at = columns(j, t)
        grad = dot(back_a[...], top_ref[:, at], NN) + dot(back_b[...], low_ref[:, at], NN)
        copies[t, j].wait()
        if t == 0:
            buf[j] = buf[j] - 0.5 * grad - 0.5 * grads[j][...].astype(jnp.float32)
            writes.append(pltpu.make_async_copy(buf.at[j], updated.at[:, at], out_sems.at[j]))
            writes[-1].start()
        else:
            later[(t - 1) * count + j] = later[(t - 1) * count + j] - 0.5 * grad
    for q in range(count):
        @pl.when(me == q)
        def _():
            for i in range(half):
                residual_ref[side * half + i] = mine_ref[i, :, q * own_width:(q + 1) * own_width]
                residual_ref[(1 - side) * half + i] = other_ref[i, :, q * own_width:(q + 1) * own_width]
    for w in writes:
        w.wait()


def finish_kernel(count, t, info, later, *refs):
    grads = refs[:count]
    _, updated, buf, sems = refs[count:]
    chunk = grads[0].shape[1]
    writes = []
    for j in range(count):
        buf[j] = later[(t - 1) * count + j] - 0.5 * grads[j][...].astype(jnp.float32)
        at = aligned((info[0] ^ j) * CHUNKS + t, chunk)
        writes.append(pltpu.make_async_copy(buf.at[j], updated.at[:, at], sems.at[j]))
        writes[-1].start()
    for w in writes:
        w.wait()


def step_of(coefficients, measured, ray_voxels, ray_weights, angle_ids, angle_table, harmonics):
    coef_local, cols = coefficients.shape
    projections, _, rays, channels = measured.shape
    rows = projections * rays
    samples = ray_voxels.shape[2]
    count = lax.axis_size("coef")
    me = lax.axis_index("coef")
    half = projections // 2
    block = cols // count
    chunk = block // CHUNKS
    bf16, f32 = jnp.bfloat16, jnp.float32
    shape = jax.ShapeDtypeStruct

    def kernel(body_of, ins, outs, out_shape, scratch=(), grant=12, aliases={}):
        return pl.pallas_call(
            body_of,
            in_specs=ins,
            out_specs=outs,
            out_shape=out_shape,
            scratch_shapes=list(scratch),
            input_output_aliases=aliases,
            compiler_params=pltpu.CompilerParams(vmem_limit_bytes=grant << 20),
        )

    group_bits = 1 if lax.axis_size("groups") % 2 == 0 else 0
    slab_count = lax.axis_size("slab")
    slab_bits = 1 if slab_count % 2 == 0 else 0
    pieces = 1 << (group_bits + slab_bits)
    place = jnp.zeros((), jnp.int32)
    if slab_bits:
        place = place + (lax.axis_index("slab") & 1)
    if group_bits:
        place = place + ((lax.axis_index("groups") & 1) << slab_bits)
    width = harmonics.shape[1] // pieces
    info = jnp.stack([me, me & 1, place]).astype(jnp.int32)
    rows_shape = (rows, samples)
    coef_far, measured_far, vox_far, wgt_far, table_far, harm_far = [
        pltpu.with_memory_space_constraint(v, pltpu.HBM)
        for v in (
            coefficients,
            measured.reshape(projections, rays, channels),
            ray_voxels.reshape(rows_shape),
            ray_weights.reshape(rows_shape),
            angle_table,
            harmonics,
        )
    ]

    *blocks, piece, vox, wgt, chosen = kernel(
        lambda *refs: prepare_kernel(count, *refs),
        [SMEM, SMEM] + [HBM] * 5,
        [VMEM] * (count + 4),
        [shape((coef_local, block), bf16)] * count
        + [
            shape((coef_local, width), bf16),
            shape((rows // 2, samples), jnp.int32),
            shape((rows // 2, samples), jnp.int32),
            shape((projections,) + angle_table.shape[1:], bf16),
        ],
        [pltpu.VMEM((count, coef_local, block), f32), pltpu.SemaphoreType.DMA((count + 3 + projections,))],
    )(info, angle_ids, coef_far, harm_far, vox_far, wgt_far, table_far)

    fetched = {m: [swap(piece, "coef", m)] for m in range(2, count, 2)}
    received = {m: swap(blocks[m], "coef", m) for m in range(2, count)}
    received[0] = blocks[0]
    received[1] = swap(blocks[1], "coef", 1)
    near = swap(harmonics, "coef", 1)
    moves = [(0, 1)] * slab_bits + [(1, 0)] * group_bits + [(1, 1)] * (slab_bits * group_bits)
    for m in fetched:
        for up, along in moves:
            total = lax.axis_size("groups") * slab_count
            pairs = [(i, (((i // slab_count) ^ up) * slab_count) + ((i % slab_count) ^ along)) for i in range(total)]
            fetched[m].append(lax.ppermute(fetched[m][0], ("groups", "slab"), pairs))

    top = kernel(
        build_kernel,
        [VMEM, VMEM],
        VMEM,
        shape((rows // 2, cols), bf16),
        [pltpu.VMEM((GROUP * cols // LANES, LANES), f32)],
    )(vox, wgt)
    low = swap(top, "coef", 1)
    for m in list(fetched):
        fetched[m ^ 1] = [swap(v, "coef", 1) for v in fetched[m]]
    far = [v for m in range(2, count) for v in fetched[m]]

    mine, other = kernel(
        lambda *refs: sums_kernel(count, *refs),
        [SMEM] + [VMEM] * (count + 3) + [HBM],
        [VMEM, VMEM],
        [shape((half, rays, channels), f32)] * 2,
        [pltpu.VMEM((half, rays, channels), f32), pltpu.SemaphoreType.DMA(())],
    )(info, top, low, *blocks, chosen, measured_far)
    total = mine + swap(other, "coef", 1)
    mask = 2
    while mask < count:
        total = total + swap(total, "coef", mask)
        mask *= 2
    waves = kernel(
        lambda *refs: gather_kernel(count, pieces, *refs),
        [SMEM, HBM] + [VMEM] * (1 + len(far)),
        VMEM,
        shape((count * coef_local, harmonics.shape[1]), bf16),
        [pltpu.SemaphoreType.DMA((pieces,))],
    )(info, harm_far, near, *far)

    returned = []
    for t in range(CHUNKS):
        outs = kernel(
            lambda *refs: penalty_kernel(count, pieces, t, *refs),
            [VMEM] * (count + 1),
            [VMEM] * count,
            [shape((coef_local, chunk), bf16)] * count,
            [
                pltpu.VMEM((count * coef_local, chunk), bf16),
                pltpu.VMEM((chunk, count * coef_local), bf16),
                pltpu.VMEM((count * coef_local, chunk), f32),
            ],
        )(waves, *[received[m] for m in range(count)])
        returned.append([outs[0]] + [swap(outs[m], "coef", m) for m in range(1, count)])

    resid_other = swap(total, "coef", 1)
    updated, residual, later = kernel(
        lambda *refs: data_kernel(count, *refs),
        [SMEM] + [VMEM] * 5 + [HBM] + [VMEM] * count,
        [HBM, VMEM, VMEM],
        [
            shape((coef_local, cols), f32),
            shape((projections, rays, channels // count), f32),
            shape(((CHUNKS - 1) * count, coef_local, chunk), f32),
        ],
        [
            pltpu.VMEM((coef_local, rows // 2), bf16),
            pltpu.VMEM((coef_local, rows // 2), bf16),
            pltpu.VMEM((count, coef_local, chunk), f32),
            pltpu.SemaphoreType.DMA((CHUNKS * count,)),
            pltpu.SemaphoreType.DMA((count,)),
        ],
    )(info, total, resid_other, chosen, top, low, coef_far, *returned[0])
    for t in range(1, CHUNKS):
        updated = kernel(
            lambda *refs: finish_kernel(count, t, *refs),
            [SMEM] + [VMEM] * (count + 1) + [HBM],
            HBM,
            shape((coef_local, cols), f32),
            [pltpu.VMEM((count, coef_local, chunk), f32), pltpu.SemaphoreType.DMA((count,))],
            aliases={count + 2: 0},
        )(info, later, *returned[t], updated)
    return (updated, residual[:, None])


def solution(mesh):
    in_specs = (
        P("coef", ("groups", "slab")),
        P("groups", "slab", None, None),
        P(),
        P(),
        P(),
        P(None, "coef", None),
        P("coef", None),
    )
    out_specs = (P("coef", ("groups", "slab")), P("groups", "slab", None, "coef"))
    return jax.shard_map(step_of, mesh=mesh, in_specs=in_specs, out_specs=out_specs, check_vma=False)
```

time: 230 us -> 92.4 us (0.40)
  local copies, waits for them, and re-layouts: 75 us -> 0.66 us
  matrix products: 32.5 us -> 0 us
  Pallas kernels: 0 us -> 31.4 us
  waiting for transfers between devices: 69.9 us -> 41.4 us
  other arithmetic: 21.3 us -> 0.15 us
  between operations: 14.2 us -> 0.75 us
  starting transfers between devices: 9.3 us -> 17.9 us
  blocking collectives: 6.81 us -> 0 us
    all_to_all x2 -> x0, waiting for transfers between devices: 45.1 us -> none  [the longest x1 45.1 us: body(): lax.all_to_all(grid_rows, 'coef', split_axis=1, concat_axis=0, tiled=True)]
    ppermute x0 -> x22, waiting for transfers between devices: none -> 41.4 us  [the longest x19 33.2 us: swap(): return lax.ppermute(value, axis, [(i, i ^ mask) for i in range(count)])]
    dot_general x5 -> x0, matrix products: 32.5 us -> none  [the longest x1 13.8 us: body(): lax.dot_general(lax.all_gather(harmonics, 'coef', axis=0, tiled=True), sl...]
    pallas_call x0 -> x8, Pallas kernels: none -> 31.4 us  [the longest x2 9.23 us: step_of(): kernel(lambda *refs: penalty_kernel(count, pieces, t, *refs), [VMEM] * (c...]
    unnamed x3 -> x0, waiting for transfers between devices: 24.8 us -> none
    reshape x3 -> x0, local copies, waits for them, and re-layouts: 23.6 us -> none  [the longest x1 12 us: build_matrix(): product.astype(jnp.bfloat16)]
    unnamed x19 -> x4, local copies, waits for them, and re-layouts: 21.5 us -> 0.66 us
    ppermute x0 -> x22, starting transfers between devices: none -> 17.9 us  [the longest x19 13.1 us: swap(): return lax.ppermute(value, axis, [(i, i ^ mask) for i in range(count)])]
  transfers between devices with their start and end apart: 4 -> 22, of which waited for: 2 -> 9; matrix products, arithmetic and copies ran while one was open for 18% -> 0% of each run, Pallas kernels for 0% -> 21%
where the time goes in v1:
time: 92.4 us; the launch traced here: 92.2 us
  waiting for transfers between devices  41.4 us (45%)
  Pallas kernels  31.4 us (34%)
  starting transfers between devices  17.9 us (19%)
    ppermute x19, waiting for transfers between devices, swap(): return lax.ppermute(value, axis, [(i, i ^ mask) for i in range(count)])  33.2 us
    ppermute x19, starting transfers between devices, swap(): return lax.ppermute(value, axis, [(i, i ^ mask) for i in range(count)])  13.1 us
    pallas_call x2, Pallas kernels, step_of(): kernel(lambda *refs: penalty_kernel(count, pieces, t, *refs), [VMEM] * (c...  9.23 us
    ppermute x3, waiting for transfers between devices, step_of(): fetched[m].append(lax.ppermute(fetched[m][0], ('groups', 'slab'), pairs))  8.1 us
    pallas_call x1, Pallas kernels, step_of(): kernel(build_kernel, [VMEM, VMEM], VMEM, shape((rows // 2, cols), bf16),...  7.07 us
    pallas_call x1, Pallas kernels, step_of(): kernel(lambda *refs: data_kernel(count, *refs), [SMEM] + [VMEM] * 5 + [HB...  5.06 us
    ppermute x3, starting transfers between devices, step_of(): fetched[m].append(lax.ppermute(fetched[m][0], ('groups', 'slab'), pairs))  4.84 us
    pallas_call x1, Pallas kernels, step_of(): kernel(lambda *refs: sums_kernel(count, *refs), [SMEM] + [VMEM] * (count...  3.29 us
  transfers between devices with their start and end apart: 22, of which 9 were waited for; matrix products, arithmetic and copies ran while one was open for 0% of the time, Pallas kernels for 21%

profile of v1, /device:TPU:0, one launch (start us, length us, event | category | flops | bytes accessed | tf_op | source)
XLA Modules:
  0.0 92.2 jit_solution(18341374729979434506)
XLA Ops:
  0.6 0.1 pad_add_fusion.refs_0_
  0.7 0.7 copy-done
  1.4 3.1 %shard_map.86 = (bf16[224,1024]{1,0:T(8,128)(2,1)S(1)}, bf16[224,1024]{1,0:T(8,128)(2,1)S(1)}, bf16[224,1024]{1,0:T(8,128)(2,1)S(1)}, bf16[224,1024]{1,0:T(8,128...) custom-call(s32[3]{0:T(128)S(1)} %pad_add_fusion.refs_0_, ...), custom_call_target="tpu_custom_call" | custom-call | tf_op jit(solution)/shard_map/pallas_call | solution.py:250
  4.5 7.1 %shard_map.87.refs_1_.refs_4_ = bf16[256,4096]{1,0:T(8,128)(2,1)S(1)} custom-call(s32[256,128]{1,0:T(8,128)S(1)} %get-tuple-element.23.vox_ref, s32[256,128]{1,0:T(8,128)S(1)} %get-tuple-element.24.wgt_ref), custom_call_target="tpu_custom_call" | custom-call | tf_op jit(solution)/shard_map/pallas_call | solution.py:276
  11.5 0.6 collective-permute-start
  12.1 2.6 %collective-permute-start.5 = (bf16[224,512]{1,0:T(8,128)(2,1)S(1)}, bf16[224,512]{1,0:T(8,128)(2,1)S(1)}, u32[]{:S(2)}, u32[]{:S(2)}) collective-permute-start(bf16[224,512]{1,0:T(8,128)(2,1)S(1)} %get-tuple-element.32), channel_id=1, source_target_pairs={{0,8},{4,12},{8,0},{12,4},{1,9},{5,13},{9,1},{13,5},{2,10},{6,14},... | collective-permute-start | bytes 688136 | tf_op jit(solution)/shard_map/ppermute | solution.py:25
  14.6 6.2 %collective-permute-done.5.refs_3_ = bf16[224,512]{1,0:T(8,128)(2,1)S(1)} collective-permute-done((bf16[224,512]{1,0:T(8,128)(2,1)S(1)}, bf16[224,512]{1,0:T(8,128)(2,1)S(1)}, u32[]{:S(2)}, u32[]{:S(2)}) %collective-permute-start.5) | collective-permute-done | bytes 229408 | tf_op jit(solution)/shard_map/ppermute | solution.py:25
  20.8 2.8 %collective-permute-start.8 = (bf16[224,512]{1,0:T(8,128)(2,1)S(1)}, bf16[224,512]{1,0:T(8,128)(2,1)S(1)}, u32[]{:S(2)}, u32[]{:S(2)}) collective-permute-start(bf16[224,512]{1,0:T(8,128)(2,1)S(1)} %collective-permute-done.5.refs_3_), channel_id=1, source_target_pairs={{0,17},{1,16},{2,19},{3,18},{16,1},{17,0},{18,3},{19,2},{4,21},{5,... | collective-permute-start | bytes 688136 | tf_op jit(solution)/shard_map/ppermute | solution.py:274
  23.6 0.0 collective-permute-start.4
  23.6 0.5 collective-permute-start.7
  24.1 0.2 collective-permute-start.9
  24.4 4.8 %collective-permute-done.8.refs_6_ = bf16[224,512]{1,0:T(8,128)(2,1)S(1)} collective-permute-done((bf16[224,512]{1,0:T(8,128)(2,1)S(1)}, bf16[224,512]{1,0:T(8,128)(2,1)S(1)}, u32[]{:S(2)}, u32[]{:S(2)}) %collective-permute-start.8) | collective-permute-done | bytes 229408 | tf_op jit(solution)/shard_map/ppermute | solution.py:274
  29.2 1.5 %collective-permute-start.6 = (bf16[224,512]{1,0:T(8,128)(2,1)S(1)}, bf16[224,512]{1,0:T(8,128)(2,1)S(1)}, u32[]{:S(2)}, u32[]{:S(2)}) collective-permute-start(bf16[224,512]{1,0:T(8,128)(2,1)S(1)} %collective-permute-done.5.refs_3_), channel_id=1, source_target_pairs={{0,1},{1,0},{2,3},{3,2},{16,17},{17,16},{18,19},{19,18},{4,5},{5,4... | collective-permute-start | bytes 688136 | tf_op jit(solution)/shard_map/ppermute | solution.py:274
  30.8 3.3 %collective-permute-done.7.refs_5_ = bf16[224,512]{1,0:T(8,128)(2,1)S(1)} collective-permute-done((bf16[224,512]{1,0:T(8,128)(2,1)S(1)}, bf16[224,512]{1,0:T(8,128)(2,1)S(1)}, u32[]{:S(2)}, u32[]{:S(2)}) %collective-permute-start.7) | collective-permute-done | bytes 229408 | tf_op jit(solution)/shard_map/ppermute | solution.py:274
  34.0 0.1 collective-permute-start.12
  34.1 0.0 collective-permute-done.refs_2_.refs_5_
  34.1 0.4 collective-permute-start.11
  34.5 3.3 %shard_map.88 = (f32[4,64,256]{2,1,0:T(8,128)S(1)}, f32[4,64,256]{2,1,0:T(8,128)S(1)}) custom-call(s32[3]{0:T(128)S(1)} %pad_add_fusion.refs_0_, bf16[256,4096]{1,0:T(8,128)(2,1)S(1)} %shard_map.87.refs_1_.refs_4_, bf16[256,4096]{1,0:T(8,128)(2,1)S(1)} %collective-permute-done.refs_2_.refs_5_, bf16[224,1024]{1,0:T(8,128)(2,1)S(1)} %get-tuple-element.25.refs_3_.refs_1_, ...), custom_call_target="tpu_custom_call" | custom-call | tf_op jit(solution)/shard_map/pallas_call | solution.py:288
  37.8 0.0 collective-permute-done.9.refs_7_
  37.8 0.1 collective-permute-start.1
  38.0 0.4 collective-permute-start.13
  38.4 0.0 collective-permute-done.12.refs_10_
  38.4 1.5 %collective-permute-start.14 = (bf16[224,1024]{1,0:T(8,128)(2,1)S(1)}, bf16[224,1024]{1,0:T(8,128)(2,1)S(1)}, u32[]{:S(2)}, u32[]{:S(2)}) collective-permute-start(bf16[224,1024]{1,0:T(8,128)(2,1)S(1)} %get-tuple-element.27.refs_5_), channel_id=1, source_target_pairs={{0,8},{4,12},{8,0},{12,4},{1,9},{5,13},{9,1},{13,5},{2,10},{6,14},... | collective-permute-start | bytes 1376264 | tf_op jit(solution)/shard_map/ppermute | solution.py:25
  39.9 0.7 collective-permute-start.10
  40.6 1.1 %collective-permute-done.10.refs_8_ = bf16[224,512]{1,0:T(8,128)(2,1)S(1)} collective-permute-done((bf16[224,512]{1,0:T(8,128)(2,1)S(1)}, bf16[224,512]{1,0:T(8,128)(2,1)S(1)}, u32[]{:S(2)}, u32[]{:S(2)}) %collective-permute-start.10) | collective-permute-done | bytes 229408 | tf_op jit(solution)/shard_map/ppermute | solution.py:25
  41.7 1.5 %collective-permute-start.2 = (f32[4,64,256]{2,1,0:T(8,128)S(1)}, f32[4,64,256]{2,1,0:T(8,128)S(1)}, u32[]{:S(2)}, u32[]{:S(2)}) collective-permute-start(f32[4,64,256]{2,1,0:T(8,128)S(1)} %add.10), channel_id=1, source_target_pairs={{0,8},{4,12},{8,0},{12,4},{1,9},{5,13},{9,1},{13,5},{2,10},{6,14},... | collective-permute-start | bytes 786440 | tf_op jit(solution)/shard_map/ppermute | solution.py:25
  43.2 0.0 collective-permute-done.4.refs_2_
  43.2 1.9 %shard_map.89.refs_0_ = bf16[896,2048]{1,0:T(8,128)(2,1)S(1)} custom-call(s32[3]{0:T(128)S(1)} %pad_add_fusion.refs_0_, bf16[224,2048]{1,0:T(8,128)(2,1)} %refs_1_.3, bf16[224,2048]{1,0:T(8,128)(2,1)S(1)} %collective-permute-done.4.refs_2_, bf16[224,512]{1,0:T(8,128)(2,1)S(1)} %collective-permute-done.5.refs_3_, ...), custom_call_target="tpu_custom_call" | custom-call | tf_op jit(solution)/shard_map/pallas_call | solution.py:300
  45.0 0.0 collective-permute-done.13.refs_2_
  45.0 6.8 %collective-permute-done.14.refs_3_ = bf16[224,1024]{1,0:T(8,128)(2,1)S(1)} collective-permute-done((bf16[224,1024]{1,0:T(8,128)(2,1)S(1)}, bf16[224,1024]{1,0:T(8,128)(2,1)S(1)}, u32[]{:S(2)}, u32[]{:S(2)}) %collective-permute-start.14) | collective-permute-done | bytes 458784 | tf_op jit(solution)/shard_map/ppermute | solution.py:25
  51.8 8.8 %collective-permute-done.15.refs_4_ = bf16[224,1024]{1,0:T(8,128)(2,1)S(1)} collective-permute-done((bf16[224,1024]{1,0:T(8,128)(2,1)S(1)}, bf16[224,1024]{1,0:T(8,128)(2,1)S(1)}, u32[]{:S(2)}, u32[]{:S(2)}) %collective-permute-start.15) | collective-permute-done | bytes 458784 | tf_op jit(solution)/shard_map/ppermute | solution.py:25
  60.6 4.6 %shard_map.90 = (bf16[224,512]{1,0:T(8,128)(2,1)S(1)}, bf16[224,512]{1,0:T(8,128)(2,1)S(1)}, bf16[224,512]{1,0:T(8,128)(2,1)S(1)}, bf16[224,512]{1,0:T(8,128)(2,1)S(1)}) custom-call(bf16[896,2048]{1,0:T(8,128)(2,1)S(1)} %shard_map.89.refs_0_, bf16[224,1024]{1,0:T(8,128)(2,1)S(1)} %get-tuple-element.25.refs_3_.refs_1_, ...), custom_call_target="tpu_custom_call" | custom-call | tf_op jit(solution)/shard_map/pallas_call | solution.py:310
  65.2 0.9 collective-permute-start.16
  66.2 1.5 %collective-permute-start.17 = (bf16[224,512]{1,0:T(8,128)(2,1)S(1)}, bf16[224,512]{1,0:T(8,128)(2,1)S(1)}, u32[]{:S(2)}, u32[]{:S(2)}) collective-permute-start(bf16[224,512]{1,0:T(8,128)(2,1)S(1)} %get-tuple-element.35), channel_id=1, source_target_pairs={{0,8},{4,12},{8,0},{12,4},{1,9},{5,13},{9,1},{13,5},{2,10},{6,14},... | collective-permute-start | bytes 688136 | tf_op jit(solution)/shard_map/ppermute | solution.py:25
  67.6 0.0 collective-permute-done.2
  67.7 0.1 collective-permute-start.3
  67.7 4.6 %shard_map.92 = (bf16[224,512]{1,0:T(8,128)(2,1)S(1)}, bf16[224,512]{1,0:T(8,128)(2,1)S(1)}, bf16[224,512]{1,0:T(8,128)(2,1)S(1)}, bf16[224,512]{1,0:T(8,128)(2,1)S(1)}) custom-call(bf16[896,2048]{1,0:T(8,128)(2,1)S(1)} %shard_map.89.refs_0_, bf16[224,1024]{1,0:T(8,128)(2,1)S(1)} %get-tuple-element.25.refs_3_.refs_1_, ...), custom_call_target="tpu_custom_call" | custom-call | tf_op jit(solution)/shard_map/pallas_call | solution.py:310
  72.4 0.6 collective-permute-start.19
  72.9 0.2 collective-permute-start.18
  73.2 0.0 collective-permute-done.16.refs_8_
  73.2 1.5 %collective-permute-start.20 = (bf16[224,512]{1,0:T(8,128)(2,1)S(1)}, bf16[224,512]{1,0:T(8,128)(2,1)S(1)}, u32[]{:S(2)}, u32[]{:S(2)}) collective-permute-start(bf16[224,512]{1,0:T(8,128)(2,1)S(1)} %get-tuple-element.40), channel_id=1, source_target_pairs={{0,8},{4,12},{8,0},{12,4},{1,9},{5,13},{9,1},{13,5},{2,10},{6,14},... | collective-permute-start | bytes 688136 | tf_op jit(solution)/shard_map/ppermute | solution.py:25
  74.6 0.0 collective-permute-done.17.refs_9_
  74.6 0.3 collective-permute-start.21
  75.0 5.6 %collective-permute-done.18.refs_10_ = bf16[224,512]{1,0:T(8,128)(2,1)S(1)} collective-permute-done((bf16[224,512]{1,0:T(8,128)(2,1)S(1)}, bf16[224,512]{1,0:T(8,128)(2,1)S(1)}, u32[]{:S(2)}, u32[]{:S(2)}) %collective-permute-start.18) | collective-permute-done | bytes 229408 | tf_op jit(solution)/shard_map/ppermute | solution.py:25
  80.6 5.1 %shard_map.91 = (f32[224,4096]{1,0:T(8,128)}, f32[8,64,64]{2,1,0:T(8,128)}, f32[4,224,512]{2,1,0:T(8,128)S(1)}) custom-call(s32[3]{0:T(128)S(1)} %pad_add_fusion.refs_0_, f32[4,64,256]{2,1,0:T(8,128)S(1)} %add.11.refs_1_, f32[4,64,256]{2,1,0:T(8,128)S(1)} %collective-permute-done.3.refs_2_, bf16[8,224,256]{2,1,0:T(8,128)(2,1)S(1)} %get-tuple-element.29.refs_7_.refs_3_, ...), custom_call_target="tpu_custom_call" | custom-call | tf_op jit(solution)/shard_map/pallas_call | solution.py:324
  85.6 0.4 collective-permute-done.20.refs_4_
  86.0 4.4 %collective-permute-done.21.refs_5_ = bf16[224,512]{1,0:T(8,128)(2,1)S(1)} collective-permute-done((bf16[224,512]{1,0:T(8,128)(2,1)S(1)}, bf16[224,512]{1,0:T(8,128)(2,1)S(1)}, u32[]{:S(2)}, u32[]{:S(2)}) %collective-permute-start.21) | collective-permute-done | bytes 229408 | tf_op jit(solution)/shard_map/ppermute | solution.py:25
  90.4 1.8 %shard_map.93 = f32[224,4096]{1,0:T(8,128)} custom-call(s32[3]{0:T(128)S(1)} %pad_add_fusion.refs_0_, f32[4,224,512]{2,1,0:T(8,128)S(1)} %get-tuple-element.37.refs_1_, bf16[224,512]{1,0:T(8,128)(2,1)S(1)} %get-tuple-element.38.refs_2_, bf16[224,512]{1,0:T(8,128)(2,1)S(1)} %collective-permute-done.19.refs_3_, ...), custom_call_target="tpu_custom_call", output_to_operand_aliasing={{}: (6, {})} | custom-call | tf_op jit(solution)/shard_map/pallas_call | solution.py:342
  (11 shorter events, 0.1 us)
Async XLA Ops:
  0.7 0.7 copy-start
  1.4 22.3 %copy-start.1 = (bf16[224,2048]{1,0:T(8,128)(2,1)S(1)}, bf16[224,2048]{1,0:T(8,128)(2,1)}, u32[]{:S(2)}) copy-start(bf16[224,2048]{1,0:T(8,128)(2,1)} %refs_1_.3) | copy-start | bytes 2752516
  11.5 22.6 %collective-permute-start = (bf16[256,4096]{1,0:T(8,128)(2,1)S(1)}, bf16[256,4096]{1,0:T(8,128)(2,1)S(1)}, u32[]{:S(2)}, u32[]{:S(2)}) collective-permute-start(bf16[256,4096]{1,0:T(8,128)(2,1)S(1)} %shard_map.87.refs_1_.refs_4_), channel_id=1, source_target_pairs={{0,4},{4,0},{8,12},{12,8},{1,5},{5,1},{9,13},{13,9},{2,6},{6,2},{1... | collective-permute-start | bytes 6291464 | tf_op jit(solution)/shard_map/ppermute | solution.py:25
  12.1 8.8 %collective-permute-start.5 = (bf16[224,512]{1,0:T(8,128)(2,1)S(1)}, bf16[224,512]{1,0:T(8,128)(2,1)S(1)}, u32[]{:S(2)}, u32[]{:S(2)}) collective-permute-start(bf16[224,512]{1,0:T(8,128)(2,1)S(1)} %get-tuple-element.32), channel_id=1, source_target_pairs={{0,8},{4,12},{8,0},{12,4},{1,9},{5,13},{9,1},{13,5},{2,10},{6,14},... | collective-permute-start | bytes 688136 | tf_op jit(solution)/shard_map/ppermute | solution.py:25
  20.8 8.4 %collective-permute-start.8 = (bf16[224,512]{1,0:T(8,128)(2,1)S(1)}, bf16[224,512]{1,0:T(8,128)(2,1)S(1)}, u32[]{:S(2)}, u32[]{:S(2)}) collective-permute-start(bf16[224,512]{1,0:T(8,128)(2,1)S(1)} %collective-permute-done.5.refs_3_), channel_id=1, source_target_pairs={{0,17},{1,16},{2,19},{3,18},{16,1},{17,0},{18,3},{19,2},{4,21},{5,... | collective-permute-start | bytes 688136 | tf_op jit(solution)/shard_map/ppermute | solution.py:274
  23.6 19.5 %collective-permute-start.4 = (bf16[224,2048]{1,0:T(8,128)(2,1)S(1)}, bf16[224,2048]{1,0:T(8,128)(2,1)S(1)}, u32[]{:S(2)}, u32[]{:S(2)}) collective-permute-start(bf16[224,2048]{1,0:T(8,128)(2,1)S(1)} %copy-done.1), channel_id=1, source_target_pairs={{0,4},{4,0},{8,12},{12,8},{1,5},{5,1},{9,13},{13,9},{2,6},{6,2},{1... | collective-permute-start | bytes 2752520 | tf_op jit(solution)/shard_map/ppermute | solution.py:25
  23.6 10.4 %collective-permute-start.7 = (bf16[224,512]{1,0:T(8,128)(2,1)S(1)}, bf16[224,512]{1,0:T(8,128)(2,1)S(1)}, u32[]{:S(2)}, u32[]{:S(2)}) collective-permute-start(bf16[224,512]{1,0:T(8,128)(2,1)S(1)} %collective-permute-done.5.refs_3_), channel_id=1, source_target_pairs={{0,16},{1,17},{2,18},{3,19},{16,0},{17,1},{18,2},{19,3},{4,20},{5,... | collective-permute-start | bytes 688136 | tf_op jit(solution)/shard_map/ppermute | solution.py:274
  24.1 13.7 %collective-permute-start.9 = (bf16[224,512]{1,0:T(8,128)(2,1)S(1)}, bf16[224,512]{1,0:T(8,128)(2,1)S(1)}, u32[]{:S(2)}, u32[]{:S(2)}) collective-permute-start(bf16[224,512]{1,0:T(8,128)(2,1)S(1)} %collective-permute-done.5.refs_3_), channel_id=1, source_target_pairs={{0,4},{4,0},{8,12},{12,8},{1,5},{5,1},{9,13},{13,9},{2,6},{6,2},{1... | collective-permute-start | bytes 688136 | tf_op jit(solution)/shard_map/ppermute | solution.py:25
  29.2 8.8 %collective-permute-start.6 = (bf16[224,512]{1,0:T(8,128)(2,1)S(1)}, bf16[224,512]{1,0:T(8,128)(2,1)S(1)}, u32[]{:S(2)}, u32[]{:S(2)}) collective-permute-start(bf16[224,512]{1,0:T(8,128)(2,1)S(1)} %collective-permute-done.5.refs_3_), channel_id=1, source_target_pairs={{0,1},{1,0},{2,3},{3,2},{16,17},{17,16},{18,19},{19,18},{4,5},{5,4... | collective-permute-start | bytes 688136 | tf_op jit(solution)/shard_map/ppermute | solution.py:274
  34.0 4.4 %collective-permute-start.12 = (bf16[224,512]{1,0:T(8,128)(2,1)S(1)}, bf16[224,512]{1,0:T(8,128)(2,1)S(1)}, u32[]{:S(2)}, u32[]{:S(2)}) collective-permute-start(bf16[224,512]{1,0:T(8,128)(2,1)S(1)} %collective-permute-done.8.refs_6_), channel_id=1, source_target_pairs={{0,4},{4,0},{8,12},{12,8},{1,5},{5,1},{9,13},{13,9},{2,6},{6,2},{1... | collective-permute-start | bytes 688136 | tf_op jit(solution)/shard_map/ppermute | solution.py:25
  34.1 5.8 %collective-permute-start.11 = (bf16[224,512]{1,0:T(8,128)(2,1)S(1)}, bf16[224,512]{1,0:T(8,128)(2,1)S(1)}, u32[]{:S(2)}, u32[]{:S(2)}) collective-permute-start(bf16[224,512]{1,0:T(8,128)(2,1)S(1)} %collective-permute-done.7.refs_5_), channel_id=1, source_target_pairs={{0,4},{4,0},{8,12},{12,8},{1,5},{5,1},{9,13},{13,9},{2,6},{6,2},{1... | collective-permute-start | bytes 688136 | tf_op jit(solution)/shard_map/ppermute | solution.py:25
  37.8 2.1 %collective-permute-start.1 = (f32[4,64,256]{2,1,0:T(8,128)S(1)}, f32[4,64,256]{2,1,0:T(8,128)S(1)}, u32[]{:S(2)}, u32[]{:S(2)}) collective-permute-start(f32[4,64,256]{2,1,0:T(8,128)S(1)} %get-tuple-element.31), channel_id=1, source_target_pairs={{0,4},{4,0},{8,12},{12,8},{1,5},{5,1},{9,13},{13,9},{2,6},{6,2},{1... | collective-permute-start | bytes 786440 | tf_op jit(solution)/shard_map/ppermute | solution.py:25
  38.0 7.1 %collective-permute-start.13 = (bf16[224,1024]{1,0:T(8,128)(2,1)S(1)}, bf16[224,1024]{1,0:T(8,128)(2,1)S(1)}, u32[]{:S(2)}, u32[]{:S(2)}) collective-permute-start(bf16[224,1024]{1,0:T(8,128)(2,1)S(1)} %get-tuple-element.26.refs_4_), channel_id=1, source_target_pairs={{0,4},{4,0},{8,12},{12,8},{1,5},{5,1},{9,13},{13,9},{2,6},{6,2},{1... | collective-permute-start | bytes 1376264 | tf_op jit(solution)/shard_map/ppermute | solution.py:25
  38.4 13.4 %collective-permute-start.14 = (bf16[224,1024]{1,0:T(8,128)(2,1)S(1)}, bf16[224,1024]{1,0:T(8,128)(2,1)S(1)}, u32[]{:S(2)}, u32[]{:S(2)}) collective-permute-start(bf16[224,1024]{1,0:T(8,128)(2,1)S(1)} %get-tuple-element.27.refs_5_), channel_id=1, source_target_pairs={{0,8},{4,12},{8,0},{12,4},{1,9},{5,13},{9,1},{13,5},{2,10},{6,14},... | collective-permute-start | bytes 1376264 | tf_op jit(solution)/shard_map/ppermute | solution.py:25
  39.9 20.7 %collective-permute-start.15 = (bf16[224,1024]{1,0:T(8,128)(2,1)S(1)}, bf16[224,1024]{1,0:T(8,128)(2,1)S(1)}, u32[]{:S(2)}, u32[]{:S(2)}) collective-permute-start(bf16[224,1024]{1,0:T(8,128)(2,1)S(1)} %get-tuple-element.28.refs_6_), channel_id=1, source_target_pairs={{0,12},{4,8},{8,4},{12,0},{1,13},{5,9},{9,5},{13,1},{2,14},{6,10},... | collective-permute-start | bytes 1376264 | tf_op jit(solution)/shard_map/ppermute | solution.py:25
  39.9 1.8 %collective-permute-start.10 = (bf16[224,512]{1,0:T(8,128)(2,1)S(1)}, bf16[224,512]{1,0:T(8,128)(2,1)S(1)}, u32[]{:S(2)}, u32[]{:S(2)}) collective-permute-start(bf16[224,512]{1,0:T(8,128)(2,1)S(1)} %collective-permute-done.6.refs_4_), channel_id=1, source_target_pairs={{0,4},{4,0},{8,12},{12,8},{1,5},{5,1},{9,13},{13,9},{2,6},{6,2},{1... | collective-permute-start | bytes 688136 | tf_op jit(solution)/shard_map/ppermute | solution.py:25
  41.7 25.9 %collective-permute-start.2 = (f32[4,64,256]{2,1,0:T(8,128)S(1)}, f32[4,64,256]{2,1,0:T(8,128)S(1)}, u32[]{:S(2)}, u32[]{:S(2)}) collective-permute-start(f32[4,64,256]{2,1,0:T(8,128)S(1)} %add.10), channel_id=1, source_target_pairs={{0,8},{4,12},{8,0},{12,4},{1,9},{5,13},{9,1},{13,5},{2,10},{6,14},... | collective-permute-start | bytes 786440 | tf_op jit(solution)/shard_map/ppermute | solution.py:25
  65.2 7.9 %collective-permute-start.16 = (bf16[224,512]{1,0:T(8,128)(2,1)S(1)}, bf16[224,512]{1,0:T(8,128)(2,1)S(1)}, u32[]{:S(2)}, u32[]{:S(2)}) collective-permute-start(bf16[224,512]{1,0:T(8,128)(2,1)S(1)} %get-tuple-element.34), channel_id=1, source_target_pairs={{0,4},{4,0},{8,12},{12,8},{1,5},{5,1},{9,13},{13,9},{2,6},{6,2},{1... | collective-permute-start | bytes 688136 | tf_op jit(solution)/shard_map/ppermute | solution.py:25
  66.2 8.5 %collective-permute-start.17 = (bf16[224,512]{1,0:T(8,128)(2,1)S(1)}, bf16[224,512]{1,0:T(8,128)(2,1)S(1)}, u32[]{:S(2)}, u32[]{:S(2)}) collective-permute-start(bf16[224,512]{1,0:T(8,128)(2,1)S(1)} %get-tuple-element.35), channel_id=1, source_target_pairs={{0,8},{4,12},{8,0},{12,4},{1,9},{5,13},{9,1},{13,5},{2,10},{6,14},... | collective-permute-start | bytes 688136 | tf_op jit(solution)/shard_map/ppermute | solution.py:25
  67.7 12.9 %collective-permute-start.3 = (f32[4,64,256]{2,1,0:T(8,128)S(1)}, f32[4,64,256]{2,1,0:T(8,128)S(1)}, u32[]{:S(2)}, u32[]{:S(2)}) collective-permute-start(f32[4,64,256]{2,1,0:T(8,128)S(1)} %add.11.refs_1_), channel_id=1, source_target_pairs={{0,4},{4,0},{8,12},{12,8},{1,5},{5,1},{9,13},{13,9},{2,6},{6,2},{1... | collective-permute-start | bytes 786440 | tf_op jit(solution)/shard_map/ppermute | solution.py:25
  72.4 13.3 %collective-permute-start.19 = (bf16[224,512]{1,0:T(8,128)(2,1)S(1)}, bf16[224,512]{1,0:T(8,128)(2,1)S(1)}, u32[]{:S(2)}, u32[]{:S(2)}) collective-permute-start(bf16[224,512]{1,0:T(8,128)(2,1)S(1)} %get-tuple-element.39), channel_id=1, source_target_pairs={{0,4},{4,0},{8,12},{12,8},{1,5},{5,1},{9,13},{13,9},{2,6},{6,2},{1... | collective-permute-start | bytes 688136 | tf_op jit(solution)/shard_map/ppermute | solution.py:25
  72.9 7.6 %collective-permute-start.18 = (bf16[224,512]{1,0:T(8,128)(2,1)S(1)}, bf16[224,512]{1,0:T(8,128)(2,1)S(1)}, u32[]{:S(2)}, u32[]{:S(2)}) collective-permute-start(bf16[224,512]{1,0:T(8,128)(2,1)S(1)} %get-tuple-element.36), channel_id=1, source_target_pairs={{0,12},{4,8},{8,4},{12,0},{1,13},{5,9},{9,5},{13,1},{2,14},{6,10},... | collective-permute-start | bytes 688136 | tf_op jit(solution)/shard_map/ppermute | solution.py:25
  73.2 12.8 %collective-permute-start.20 = (bf16[224,512]{1,0:T(8,128)(2,1)S(1)}, bf16[224,512]{1,0:T(8,128)(2,1)S(1)}, u32[]{:S(2)}, u32[]{:S(2)}) collective-permute-start(bf16[224,512]{1,0:T(8,128)(2,1)S(1)} %get-tuple-element.40), channel_id=1, source_target_pairs={{0,8},{4,12},{8,0},{12,4},{1,9},{5,13},{9,1},{13,5},{2,10},{6,14},... | collective-permute-start | bytes 688136 | tf_op jit(solution)/shard_map/ppermute | solution.py:25
  74.6 15.8 %collective-permute-start.21 = (bf16[224,512]{1,0:T(8,128)(2,1)S(1)}, bf16[224,512]{1,0:T(8,128)(2,1)S(1)}, u32[]{:S(2)}, u32[]{:S(2)}) collective-permute-start(bf16[224,512]{1,0:T(8,128)(2,1)S(1)} %get-tuple-element.41), channel_id=1, source_target_pairs={{0,12},{4,8},{8,4},{12,0},{1,13},{5,9},{9,5},{13,1},{2,14},{6,10},... | collective-permute-start | bytes 688136 | tf_op jit(solution)/shard_map/ppermute | solution.py:25

commit v2 on v1

--- a/solution.py
+++ b/solution.py
@@ -7,7 +7,7 @@
 
 
 LANES = 128
-CHUNKS = 2
+QUARTERS = (1, 2, 1)
 GROUP = 16
 NT = (((1,), (1,)), ((), ()))
 NN = (((1,), (0,)), ((), ()))
@@ -29,10 +29,22 @@
     return pl.ds(pl.multiple_of(index * width, width), width)
 
 
-def prepare_kernel(count, info, ids, coef, harm, vox, wgt, table, *refs):
-    blocks, (piece, vox_out, wgt_out, chosen, stage, sems) = refs[:count], refs[count:]
-    me, side, place = info[0], info[1], info[2]
-    block, width = blocks[0].shape[1], piece.shape[1]
+def cuts_of(block):
+    if block % (4 * LANES):
+        return [(0, block)]
+    unit = block // 4
+    starts = [unit * sum(QUARTERS[:t]) for t in range(len(QUARTERS))]
+    return [(start, unit * size) for start, size in zip(starts, QUARTERS)]
+
+
+def columns(index, block, cut):
+    return pl.ds(pl.multiple_of(index * block + cut[0], LANES), cut[1])
+
+
+def prepare_kernel(count, info, ids, coef, vox, wgt, table, *refs):
+    blocks, (vox_out, wgt_out, chosen, stage, sems) = refs[:count], refs[count:]
+    me, side = info[0], info[1]
+    block = blocks[0].shape[1]
     half_rows, projections = vox_out.shape[0], chosen.shape[0]
     half = projections // 2
     order = list(range(2, count)) + [1, 0]
@@ -40,13 +52,12 @@
     for m in order:
         copies[m] = pltpu.make_async_copy(coef.at[:, aligned(me ^ m, block)], stage.at[m], sems.at[m])
     rest = [
-        pltpu.make_async_copy(harm.at[:, aligned(place, width)], piece, sems.at[count]),
-        pltpu.make_async_copy(vox.at[aligned(side, half_rows)], vox_out, sems.at[count + 1]),
-        pltpu.make_async_copy(wgt.at[aligned(side, half_rows)], wgt_out, sems.at[count + 2]),
+        pltpu.make_async_copy(vox.at[aligned(side, half_rows)], vox_out, sems.at[count]),
+        pltpu.make_async_copy(wgt.at[aligned(side, half_rows)], wgt_out, sems.at[count + 1]),
     ]
     for i in range(projections):
         a = jnp.where(i < half, side, 1 - side) * half + i % half
-        rest.append(pltpu.make_async_copy(table.at[ids[a]], chosen.at[i], sems.at[count + 3 + i]))
+        rest.append(pltpu.make_async_copy(table.at[ids[a]], chosen.at[i], sems.at[count + 2 + i]))
     for m in order:
         copies[m].start()
     for c in rest:
@@ -121,13 +132,13 @@
         c.wait()
 
 
-def penalty_kernel(count, pieces, t, waves, *refs):
+def penalty_kernel(count, pieces, cut, waves, *refs):
     blocks, outs = refs[:count], refs[count:2 * count]
     stack, turned, acc = refs[2 * count:]
-    height, chunk = outs[0].shape
+    height = outs[0].shape[0]
     width = waves.shape[1] // pieces
     for j in range(count):
-        stack[j * height:(j + 1) * height, :] = blocks[j][:, t * chunk:(t + 1) * chunk]
+        stack[j * height:(j + 1) * height, :] = blocks[j][:, cut[0]:cut[0] + cut[1]]
     turned[...] = jnp.swapaxes(stack[...], 0, 1)
     for r in range(pieces):
         wave = waves[:, r * width:(r + 1) * width]
@@ -143,22 +154,19 @@
                 outs[j][...] = part[j * height:(j + 1) * height].astype(outs[j].dtype)
 
 
-def data_kernel(count, info, mine_ref, other_ref, chosen, top_ref, low_ref, coef, *refs):
-    grads = refs[:count]
-    updated, residual_ref, later, back_a, back_b, buf, sems, out_sems = refs[count:]
+def data_kernel(count, cuts, info, mine_ref, other_ref, chosen, top_ref, low_ref, coef, *refs):
+    grads, later = refs[:count], refs[count + 2:count + 1 + len(cuts)]
+    updated, residual_ref = refs[count:count + 2]
+    back_a, back_b, buf, sems, out_sems = refs[count + 1 + len(cuts):]
     me, side = info[0], info[1]
     half, rays = mine_ref.shape[:2]
-    chunk = grads[0].shape[1]
+    block = coef.shape[1] // count
     own_width = residual_ref.shape[2]
-
-    def columns(j, t):
-        return aligned((me ^ j) * CHUNKS + t, chunk)
-
-    order = [(t, j) for t in range(CHUNKS) for j in range(count)]
+    order = [(t, j) for t in range(len(cuts)) for j in range(count)]
     copies = {}
     for n, (t, j) in enumerate(order):
-        spot = buf.at[j] if t == 0 else later.at[(t - 1) * count + j]
-        copies[t, j] = pltpu.make_async_copy(coef.at[:, columns(j, t)], spot, sems.at[n])
+        spot = (buf if t == 0 else later[t - 1]).at[j]
+        copies[t, j] = pltpu.make_async_copy(coef.at[:, columns(me ^ j, block, cuts[t])], spot, sems.at[n])
         copies[t, j].start()
     for back, ref, start in ((back_a, mine_ref, 0), (back_b, other_ref, half)):
         for i in range(half):
@@ -166,7 +174,7 @@
             back[:, i * rays:(i + 1) * rays] = part.astype(jnp.bfloat16)
     writes = []
     for t, j in order:
-        at = columns(j, t)
+        at = columns(me ^ j, block, cuts[t])
         grad = dot(back_a[...], top_ref[:, at], NN) + dot(back_b[...], low_ref[:, at], NN)
         copies[t, j].wait()
         if t == 0:
@@ -174,7 +182,7 @@
             writes.append(pltpu.make_async_copy(buf.at[j], updated.at[:, at], out_sems.at[j]))
             writes[-1].start()
         else:
-            later[(t - 1) * count + j] = later[(t - 1) * count + j] - 0.5 * grad
+            later[t - 1][j] = later[t - 1][j] - 0.5 * grad
     for q in range(count):
         @pl.when(me == q)
         def _():
@@ -185,14 +193,14 @@
         w.wait()
 
 
-def finish_kernel(count, t, info, later, *refs):
+def finish_kernel(count, cut, info, later, *refs):
     grads = refs[:count]
     _, updated, buf, sems = refs[count:]
-    chunk = grads[0].shape[1]
+    block = updated.shape[1] // count
     writes = []
     for j in range(count):
-        buf[j] = later[(t - 1) * count + j] - 0.5 * grads[j][...].astype(jnp.float32)
-        at = aligned((info[0] ^ j) * CHUNKS + t, chunk)
+        buf[j] = later[j] - 0.5 * grads[j][...].astype(jnp.float32)
+        at = columns(info[0] ^ j, block, cut)
         writes.append(pltpu.make_async_copy(buf.at[j], updated.at[:, at], sems.at[j]))
         writes[-1].start()
     for w in writes:
@@ -208,7 +216,7 @@
     me = lax.axis_index("coef")
     half = projections // 2
     block = cols // count
-    chunk = block // CHUNKS
+    cuts = cuts_of(block)
     bf16, f32 = jnp.bfloat16, jnp.float32
     shape = jax.ShapeDtypeStruct
 
@@ -235,33 +243,34 @@
     width = harmonics.shape[1] // pieces
     info = jnp.stack([me, me & 1, place]).astype(jnp.int32)
     rows_shape = (rows, samples)
-    coef_far, measured_far, vox_far, wgt_far, table_far, harm_far = [
+    coef_far, measured_far, vox_far, wgt_far, ids_far, table_far, harm_far = [
         pltpu.with_memory_space_constraint(v, pltpu.HBM)
         for v in (
             coefficients,
             measured.reshape(projections, rays, channels),
             ray_voxels.reshape(rows_shape),
             ray_weights.reshape(rows_shape),
+            angle_ids,
             angle_table,
             harmonics,
         )
     ]
 
-    *blocks, piece, vox, wgt, chosen = kernel(
+    piece = lax.dynamic_slice_in_dim(harmonics, place * width, width, 1)
+    fetched = {m: [swap(piece, "coef", m)] for m in range(2, count, 2)}
+    *blocks, vox, wgt, chosen = kernel(
         lambda *refs: prepare_kernel(count, *refs),
-        [SMEM, SMEM] + [HBM] * 5,
-        [VMEM] * (count + 4),
+        [SMEM, SMEM] + [HBM] * 4,
+        [VMEM] * (count + 3),
         [shape((coef_local, block), bf16)] * count
         + [
-            shape((coef_local, width), bf16),
             shape((rows // 2, samples), jnp.int32),
             shape((rows // 2, samples), jnp.int32),
             shape((projections,) + angle_table.shape[1:], bf16),
         ],
-        [pltpu.VMEM((count, coef_local, block), f32), pltpu.SemaphoreType.DMA((count + 3 + projections,))],
-    )(info, angle_ids, coef_far, harm_far, vox_far, wgt_far, table_far)
-
-    fetched = {m: [swap(piece, "coef", m)] for m in range(2, count, 2)}
+        [pltpu.VMEM((count, coef_local, block), f32), pltpu.SemaphoreType.DMA((count + 2 + projections,))],
+    )(info, ids_far, coef_far, vox_far, wgt_far, table_far)
+
     received = {m: swap(blocks[m], "coef", m) for m in range(2, count)}
     received[0] = blocks[0]
     received[1] = swap(blocks[1], "coef", 1)
@@ -306,9 +315,10 @@
     )(info, harm_far, near, *far)
 
     returned = []
-    for t in range(CHUNKS):
+    for cut in cuts:
+        chunk = cut[1]
         outs = kernel(
-            lambda *refs: penalty_kernel(count, pieces, t, *refs),
+            lambda *refs: penalty_kernel(count, pieces, cut, *refs),
             [VMEM] * (count + 1),
             [VMEM] * count,
             [shape((coef_local, chunk), bf16)] * count,
@@ -321,32 +331,29 @@
         returned.append([outs[0]] + [swap(outs[m], "coef", m) for m in range(1, count)])
 
     resid_other = swap(total, "coef", 1)
-    updated, residual, later = kernel(
-        lambda *refs: data_kernel(count, *refs),
+    updated, residual, *later = kernel(
+        lambda *refs: data_kernel(count, cuts, *refs),
         [SMEM] + [VMEM] * 5 + [HBM] + [VMEM] * count,
-        [HBM, VMEM, VMEM],
-        [
-            shape((coef_local, cols), f32),
-            shape((projections, rays, channels // count), f32),
-            shape(((CHUNKS - 1) * count, coef_local, chunk), f32),
-        ],
+        [HBM] + [VMEM] * len(cuts),
+        [shape((coef_local, cols), f32), shape((projections, rays, channels // count), f32)]
+        + [shape((count, coef_local, cut[1]), f32) for cut in cuts[1:]],
         [
             pltpu.VMEM((coef_local, rows // 2), bf16),
             pltpu.VMEM((coef_local, rows // 2), bf16),
-            pltpu.VMEM((count, coef_local, chunk), f32),
-            pltpu.SemaphoreType.DMA((CHUNKS * count,)),
+            pltpu.VMEM((count, coef_local, cuts[0][1]), f32),
+            pltpu.SemaphoreType.DMA((len(cuts) * count,)),
             pltpu.SemaphoreType.DMA((count,)),
         ],
     )(info, total, resid_other, chosen, top, low, coef_far, *returned[0])
-    for t in range(1, CHUNKS):
+    for t, cut in list(enumerate(cuts))[1:]:
         updated = kernel(
-            lambda *refs: finish_kernel(count, t, *refs),
+            lambda *refs: finish_kernel(count, cut, *refs),
             [SMEM] + [VMEM] * (count + 1) + [HBM],
             HBM,
             shape((coef_local, cols), f32),
-            [pltpu.VMEM((count, coef_local, chunk), f32), pltpu.SemaphoreType.DMA((count,))],
+            [pltpu.VMEM((count, coef_local, cut[1]), f32), pltpu.SemaphoreType.DMA((count,))],
             aliases={count + 2: 0},
-        )(info, later, *returned[t], updated)
+        )(info, later[t - 1], *returned[t], updated)
     return (updated, residual[:, None])
 
 

time: 92.4 us -> 98.4 us (1.065)
  waiting for transfers between devices: 41.4 us -> 33.5 us
  Pallas kernels: 31.4 us -> 38.1 us
  local copies, waits for them, and re-layouts: 0.66 us -> 4.54 us
  starting transfers between devices: 17.9 us -> 21.1 us
    ppermute x19 -> x22, waiting for transfers between devices: 33.2 us -> 25 us  [swap(): return lax.ppermute(value, axis, [(i, i ^ mask) for i in range(count)])]
    pallas_call x4 -> x6, Pallas kernels: 16.1 us -> 20.8 us  [the longest x3 10.2 us: step_of(): kernel(lambda *refs: penalty_kernel(count, pieces, cut, *refs), [VMEM] *...]
    unnamed x4 -> x10, local copies, waits for them, and re-layouts: 0.66 us -> 3.58 us
    ppermute x19 -> x22, starting transfers between devices: 13.1 us -> 15.2 us  [swap(): return lax.ppermute(value, axis, [(i, i ^ mask) for i in range(count)])]
    pallas_call x1, Pallas kernels: 3.29 us -> 4.5 us  [step_of(): kernel(lambda *refs: sums_kernel(count, *refs), [SMEM] + [VMEM] * (count...]
    ppermute x3, starting transfers between devices: 4.84 us -> 5.86 us  [step_of(): fetched[m].append(lax.ppermute(fetched[m][0], ('groups', 'slab'), pairs))]
  transfers between devices with their start and end apart: 22 -> 25, of which waited for: 9 -> 11; matrix products, arithmetic and copies ran while one was open for 0% -> 1% of each run, Pallas kernels for 21% -> 26%
where the time goes in v2:
time: 98.4 us; the launch traced here: 98.1 us
  Pallas kernels  38.1 us (39%)
  waiting for transfers between devices  33.5 us (34%)
  starting transfers between devices  21.1 us (21%)
  local copies, waits for them, and re-layouts  4.54 us (5%)
    ppermute x22, waiting for transfers between devices, swap(): return lax.ppermute(value, axis, [(i, i ^ mask) for i in range(count)])  25 us
    ppermute x22, starting transfers between devices, swap(): return lax.ppermute(value, axis, [(i, i ^ mask) for i in range(count)])  15.2 us
    pallas_call x3, Pallas kernels, step_of(): kernel(lambda *refs: penalty_kernel(count, pieces, cut, *refs), [VMEM] *...  10.2 us
    ppermute x3, waiting for transfers between devices, step_of(): fetched[m].append(lax.ppermute(fetched[m][0], ('groups', 'slab'), pairs))  8.52 us
    pallas_call x1, Pallas kernels, step_of(): kernel(lambda *refs: data_kernel(count, cuts, *refs), [SMEM] + [VMEM] * 5...  7.22 us
    pallas_call x1, Pallas kernels, step_of(): kernel(build_kernel, [VMEM, VMEM], VMEM, shape((rows // 2, cols), bf16),...  7.07 us
    ppermute x3, starting transfers between devices, step_of(): fetched[m].append(lax.ppermute(fetched[m][0], ('groups', 'slab'), pairs))  5.86 us
    pallas_call x1, Pallas kernels, step_of(): kernel(lambda *refs: sums_kernel(count, *refs), [SMEM] + [VMEM] * (count...  4.5 us
  transfers between devices with their start and end apart: 25, of which 11 were waited for; matrix products, arithmetic and copies ran while one was open for 1% of the time, Pallas kernels for 26%

profile of v2, /device:TPU:0, one launch (start us, length us, event | category | flops | bytes accessed | tf_op | source)
XLA Modules:
  0.0 98.1 jit_solution(5657022209759651657)
XLA Ops:
  0.6 0.1 pad_add_fusion.refs_0_
  0.7 3.9 %shard_map.86 = (bf16[224,1024]{1,0:T(8,128)(2,1)S(1)}, bf16[224,1024]{1,0:T(8,128)(2,1)S(1)}, bf16[224,1024]{1,0:T(8,128)(2,1)}, bf16[224,1024]{1,0:T(8,128)(2,...) custom-call(s32[3]{0:T(128)S(1)} %pad_add_fusion.refs_0_, s32[8]{0:T(128)} %refs_1_.2, ...), custom_call_target="tpu_custom_call" | custom-call | tf_op jit(solution)/shard_map/pallas_call | solution.py:261
  4.6 0.8 copy-done
  5.4 0.8 copy-done.2
  6.2 7.1 %shard_map.87.refs_1_.refs_4_ = bf16[256,4096]{1,0:T(8,128)(2,1)S(1)} custom-call(s32[256,128]{1,0:T(8,128)S(1)} %get-tuple-element.27.vox_ref, s32[256,128]{1,0:T(8,128)S(1)} %get-tuple-element.28.wgt_ref), custom_call_target="tpu_custom_call" | custom-call | tf_op jit(solution)/shard_map/pallas_call | solution.py:285
  13.2 0.6 collective-permute-start
  13.8 1.0 constant_dynamic-slice_fusion
  14.8 2.6 %collective-permute-start.5 = (bf16[224,512]{1,0:T(8,128)(2,1)S(1)}, bf16[224,512]{1,0:T(8,128)(2,1)S(1)}, u32[]{:S(2)}, u32[]{:S(2)}) collective-permute-start(bf16[224,512]{1,0:T(8,128)(2,1)S(1)} %constant_dynamic-slice_fusion), channel_id=1, source_target_pairs={{0,8},{4,12},{8,0},{12,4},{1,9},{5,13},{9,1},{13,5},{2,10},{6,14},... | collective-permute-start | bytes 688136 | tf_op jit(solution)/shard_map/ppermute | solution.py:25
  17.3 0.4 collective-permute-done.refs_2_.refs_5_
  17.7 1.0 %copy-done.1 = bf16[224,1024]{1,0:T(8,128)(2,1)S(1)} copy-done((bf16[224,1024]{1,0:T(8,128)(2,1)S(1)}, bf16[224,1024]{1,0:T(8,128)(2,1)}, u32[]{:S(2)}) %copy-start.1) | copy-done | bytes 458776
  18.7 1.0 %copy-done.3 = bf16[224,1024]{1,0:T(8,128)(2,1)S(1)} copy-done((bf16[224,1024]{1,0:T(8,128)(2,1)S(1)}, bf16[224,1024]{1,0:T(8,128)(2,1)}, u32[]{:S(2)}) %copy-start.3) | copy-done | bytes 458776
  19.8 4.5 %shard_map.88 = (f32[4,64,256]{2,1,0:T(8,128)S(1)}, f32[4,64,256]{2,1,0:T(8,128)S(1)}) custom-call(s32[3]{0:T(128)S(1)} %pad_add_fusion.refs_0_, bf16[256,4096]{1,0:T(8,128)(2,1)S(1)} %shard_map.87.refs_1_.refs_4_, bf16[256,4096]{1,0:T(8,128)(2,1)} %collective-permute-done.refs_2_.refs_5_, bf16[224,1024]{1,0:T(8,128)(2,1)S(1)} %get-tuple-element.29.refs_3_.refs_1_, ...), custom_call_target="tpu_custom_call" | custom-call | tf_op jit(solution)/shard_map/pallas_call | solution.py:297
  24.3 0.4 collective-permute-start.1
  24.7 3.7 %collective-permute-start.8 = (bf16[224,512]{1,0:T(8,128)(2,1)S(1)}, bf16[224,512]{1,0:T(8,128)(2,1)S(1)}, u32[]{:S(2)}, u32[]{:S(2)}) collective-permute-start(bf16[224,512]{1,0:T(8,128)(2,1)S(1)} %collective-permute-done.5.refs_3_), channel_id=1, source_target_pairs={{0,17},{1,16},{2,19},{3,18},{16,1},{17,0},{18,3},{19,2},{4,21},{5,... | collective-permute-start | bytes 688136 | tf_op jit(solution)/shard_map/ppermute | solution.py:283
  28.4 0.5 collective-permute-start.7
  28.9 0.5 collective-permute-start.9
  29.4 5.2 %collective-permute-done.8.refs_6_ = bf16[224,512]{1,0:T(8,128)(2,1)S(1)} collective-permute-done((bf16[224,512]{1,0:T(8,128)(2,1)S(1)}, bf16[224,512]{1,0:T(8,128)(2,1)S(1)}, u32[]{:S(2)}, u32[]{:S(2)}) %collective-permute-start.8) | collective-permute-done | bytes 229408 | tf_op jit(solution)/shard_map/ppermute | solution.py:283
  34.6 1.7 %collective-permute-start.6 = (bf16[224,512]{1,0:T(8,128)(2,1)S(1)}, bf16[224,512]{1,0:T(8,128)(2,1)S(1)}, u32[]{:S(2)}, u32[]{:S(2)}) collective-permute-start(bf16[224,512]{1,0:T(8,128)(2,1)S(1)} %collective-permute-done.5.refs_3_), channel_id=1, source_target_pairs={{0,1},{1,0},{2,3},{3,2},{16,17},{17,16},{18,19},{19,18},{4,5},{5,4... | collective-permute-start | bytes 688136 | tf_op jit(solution)/shard_map/ppermute | solution.py:283
  36.3 3.1 %collective-permute-done.7.refs_5_ = bf16[224,512]{1,0:T(8,128)(2,1)S(1)} collective-permute-done((bf16[224,512]{1,0:T(8,128)(2,1)S(1)}, bf16[224,512]{1,0:T(8,128)(2,1)S(1)}, u32[]{:S(2)}, u32[]{:S(2)}) %collective-permute-start.7) | collective-permute-done | bytes 229408 | tf_op jit(solution)/shard_map/ppermute | solution.py:283
  39.4 0.0 collective-permute-start.12
  39.4 0.5 collective-permute-start.11
  40.0 1.7 %collective-permute-start.2 = (f32[4,64,256]{2,1,0:T(8,128)S(1)}, f32[4,64,256]{2,1,0:T(8,128)S(1)}, u32[]{:S(2)}, u32[]{:S(2)}) collective-permute-start(f32[4,64,256]{2,1,0:T(8,128)S(1)} %add.13), channel_id=1, source_target_pairs={{0,8},{4,12},{8,0},{12,4},{1,9},{5,13},{9,1},{13,5},{2,10},{6,14},... | collective-permute-start | bytes 786440 | tf_op jit(solution)/shard_map/ppermute | solution.py:25
  41.7 0.2 collective-permute-done.6.refs_4_
  41.8 1.4 %collective-permute-start.14 = (bf16[224,1024]{1,0:T(8,128)(2,1)}, bf16[224,1024]{1,0:T(8,128)(2,1)S(1)}, u32[]{:S(2)}, u32[]{:S(2)}) collective-permute-start(bf16[224,1024]{1,0:T(8,128)(2,1)} %get-tuple-element.31.refs_5_), channel_id=1, source_target_pairs={{0,8},{4,12},{8,0},{12,4},{1,9},{5,13},{9,1},{13,5},{2,10},{6,14},... | collective-permute-start | bytes 1376264 | tf_op jit(solution)/shard_map/ppermute | solution.py:25
  43.2 0.5 collective-permute-start.15
  43.7 5.5 %collective-permute-done.2 = f32[4,64,256]{2,1,0:T(8,128)S(1)} collective-permute-done((f32[4,64,256]{2,1,0:T(8,128)S(1)}, f32[4,64,256]{2,1,0:T(8,128)S(1)}, u32[]{:S(2)}, u32[]{:S(2)}) %collective-permute-start.2) | collective-permute-done | bytes 262176 | tf_op jit(solution)/shard_map/ppermute | solution.py:25
  49.3 1.4 %collective-permute-done.10.refs_8_ = bf16[224,512]{1,0:T(8,128)(2,1)S(1)} collective-permute-done((bf16[224,512]{1,0:T(8,128)(2,1)S(1)}, bf16[224,512]{1,0:T(8,128)(2,1)S(1)}, u32[]{:S(2)}, u32[]{:S(2)}) %collective-permute-start.10) | collective-permute-done | bytes 229408 | tf_op jit(solution)/shard_map/ppermute | solution.py:25
  50.7 0.1 collective-permute-start.3
  50.8 1.9 %shard_map.89.refs_0_ = bf16[896,2048]{1,0:T(8,128)(2,1)S(1)} custom-call(s32[3]{0:T(128)S(1)} %pad_add_fusion.refs_0_, bf16[224,2048]{1,0:T(8,128)(2,1)} %refs_1_.3, bf16[224,2048]{1,0:T(8,128)(2,1)S(1)} %collective-permute-done.4.refs_2_, bf16[224,512]{1,0:T(8,128)(2,1)S(1)} %collective-permute-done.5.refs_3_, ...), custom_call_target="tpu_custom_call" | custom-call | tf_op jit(solution)/shard_map/pallas_call | solution.py:309
  52.7 6.3 %collective-permute-done.14.refs_3_ = bf16[224,1024]{1,0:T(8,128)(2,1)S(1)} collective-permute-done((bf16[224,1024]{1,0:T(8,128)(2,1)}, bf16[224,1024]{1,0:T(8,128)(2,1)S(1)}, u32[]{:S(2)}, u32[]{:S(2)}) %collective-permute-start.14) | collective-permute-done | bytes 458784 | tf_op jit(solution)/shard_map/ppermute | solution.py:25
  59.0 8.0 %collective-permute-done.15.refs_4_ = bf16[224,1024]{1,0:T(8,128)(2,1)S(1)} collective-permute-done((bf16[224,1024]{1,0:T(8,128)(2,1)S(1)}, bf16[224,1024]{1,0:T(8,128)(2,1)S(1)}, u32[]{:S(2)}, u32[]{:S(2)}) %collective-permute-start.15) | collective-permute-done | bytes 458784 | tf_op jit(solution)/shard_map/ppermute | solution.py:25
  67.1 2.8 %shard_map.90 = (bf16[224,256]{1,0:T(8,128)(2,1)S(1)}, bf16[224,256]{1,0:T(8,128)(2,1)S(1)}, bf16[224,256]{1,0:T(8,128)(2,1)S(1)}, bf16[224,256]{1,0:T(8,128)(2,1)S(1)}) custom-call(bf16[896,2048]{1,0:T(8,128)(2,1)S(1)} %shard_map.89.refs_0_, bf16[224,1024]{1,0:T(8,128)(2,1)S(1)} %get-tuple-element.29.refs_3_.refs_1_, ...), custom_call_target="tpu_custom_call" | custom-call | tf_op jit(solution)/shard_map/pallas_call | solution.py:320
  69.9 0.8 collective-permute-start.16
  70.6 1.6 %collective-permute-start.17 = (bf16[224,256]{1,0:T(8,128)(2,1)S(1)}, bf16[224,256]{1,0:T(8,128)(2,1)S(1)}, u32[]{:S(2)}, u32[]{:S(2)}) collective-permute-start(bf16[224,256]{1,0:T(8,128)(2,1)S(1)} %get-tuple-element.38), channel_id=1, source_target_pairs={{0,8},{4,12},{8,0},{12,4},{1,9},{5,13},{9,1},{13,5},{2,10},{6,14},... | collective-permute-start | bytes 344072 | tf_op jit(solution)/shard_map/ppermute | solution.py:25
  72.2 4.6 %shard_map.93 = (bf16[224,512]{1,0:T(8,128)(2,1)S(1)}, bf16[224,512]{1,0:T(8,128)(2,1)S(1)}, bf16[224,512]{1,0:T(8,128)(2,1)S(1)}, bf16[224,512]{1,0:T(8,128)(2,1)S(1)}) custom-call(bf16[896,2048]{1,0:T(8,128)(2,1)S(1)} %shard_map.89.refs_0_, bf16[224,1024]{1,0:T(8,128)(2,1)S(1)} %get-tuple-element.29.refs_3_.refs_1_, ...), custom_call_target="tpu_custom_call" | custom-call | tf_op jit(solution)/shard_map/pallas_call | solution.py:320
  76.9 0.1 collective-permute-start.22
  77.0 0.5 collective-permute-start.18
  77.5 1.6 %collective-permute-start.23 = (bf16[224,512]{1,0:T(8,128)(2,1)S(1)}, bf16[224,512]{1,0:T(8,128)(2,1)S(1)}, u32[]{:S(2)}, u32[]{:S(2)}) collective-permute-start(bf16[224,512]{1,0:T(8,128)(2,1)S(1)} %get-tuple-element.48), channel_id=1, source_target_pairs={{0,8},{4,12},{8,0},{12,4},{1,9},{5,13},{9,1},{13,5},{2,10},{6,14},... | collective-permute-start | bytes 688136 | tf_op jit(solution)/shard_map/ppermute | solution.py:25
  79.1 2.8 %shard_map.92 = (bf16[224,256]{1,0:T(8,128)(2,1)S(1)}, bf16[224,256]{1,0:T(8,128)(2,1)S(1)}, bf16[224,256]{1,0:T(8,128)(2,1)S(1)}, bf16[224,256]{1,0:T(8,128)(2,1)S(1)}) custom-call(bf16[896,2048]{1,0:T(8,128)(2,1)S(1)} %shard_map.89.refs_0_, bf16[224,1024]{1,0:T(8,128)(2,1)S(1)} %get-tuple-element.29.refs_3_.refs_1_, ...), custom_call_target="tpu_custom_call" | custom-call | tf_op jit(solution)/shard_map/pallas_call | solution.py:320
  81.9 1.0 %collective-permute-start.19 = (bf16[224,256]{1,0:T(8,128)(2,1)S(1)}, bf16[224,256]{1,0:T(8,128)(2,1)S(1)}, u32[]{:S(2)}, u32[]{:S(2)}) collective-permute-start(bf16[224,256]{1,0:T(8,128)(2,1)S(1)} %get-tuple-element.42), channel_id=1, source_target_pairs={{0,4},{4,0},{8,12},{12,8},{1,5},{5,1},{9,13},{13,9},{2,6},{6,2},{1... | collective-permute-start | bytes 344072 | tf_op jit(solution)/shard_map/ppermute | solution.py:25
  82.9 1.2 %collective-permute-start.20 = (bf16[224,256]{1,0:T(8,128)(2,1)S(1)}, bf16[224,256]{1,0:T(8,128)(2,1)S(1)}, u32[]{:S(2)}, u32[]{:S(2)}) collective-permute-start(bf16[224,256]{1,0:T(8,128)(2,1)S(1)} %get-tuple-element.43), channel_id=1, source_target_pairs={{0,8},{4,12},{8,0},{12,4},{1,9},{5,13},{9,1},{13,5},{2,10},{6,14},... | collective-permute-start | bytes 344072 | tf_op jit(solution)/shard_map/ppermute | solution.py:25
  84.1 0.2 collective-permute-start.21
  84.3 7.2 %shard_map.91 = (f32[224,4096]{1,0:T(8,128)}, f32[8,64,64]{2,1,0:T(8,128)}, f32[4,224,512]{2,1,0:T(8,128)S(1)}, f32[4,224,256]{2,1,0:T(8,128)S(1)}) custom-call(s32[3]{0:T(128)S(1)} %pad_add_fusion.refs_0_, f32[4,64,256]{2,1,0:T(8,128)S(1)} %add.14.refs_1_, f32[4,64,256]{2,1,0:T(8,128)S(1)} %collective-permute-done.3.refs_2_, ...), custom_call_target="tpu_custom_call" | custom-call | tf_op jit(solution)/shard_map/pallas_call | solution.py:334
  91.5 0.2 collective-permute-done.24.refs_5_
  91.7 1.8 %shard_map.94.refs_6_ = f32[224,4096]{1,0:T(8,128)} custom-call(s32[3]{0:T(128)S(1)} %pad_add_fusion.refs_0_, f32[4,224,512]{2,1,0:T(8,128)S(1)} %get-tuple-element.45.refs_1_, bf16[224,512]{1,0:T(8,128)(2,1)S(1)} %get-tuple-element.46.refs_2_, bf16[224,512]{1,0:T(8,128)(2,1)S(1)} %collective-permute-done.22.refs_3_, ...), custom_call_target="tpu_custom_call", output_to_operand_aliasing={{}: (6, {})} | custom-call | tf_op jit(solution)/shard_map/pallas_call | solution.py:349
  93.5 1.8 %collective-permute-done.20.refs_4_ = bf16[224,256]{1,0:T(8,128)(2,1)S(1)} collective-permute-done((bf16[224,256]{1,0:T(8,128)(2,1)S(1)}, bf16[224,256]{1,0:T(8,128)(2,1)S(1)}, u32[]{:S(2)}, u32[]{:S(2)}) %collective-permute-start.20) | collective-permute-done | bytes 114720 | tf_op jit(solution)/shard_map/ppermute | solution.py:25
  95.4 1.2 %collective-permute-done.21.refs_5_ = bf16[224,256]{1,0:T(8,128)(2,1)S(1)} collective-permute-done((bf16[224,256]{1,0:T(8,128)(2,1)S(1)}, bf16[224,256]{1,0:T(8,128)(2,1)S(1)}, u32[]{:S(2)}, u32[]{:S(2)}) %collective-permute-start.21) | collective-permute-done | bytes 114720 | tf_op jit(solution)/shard_map/ppermute | solution.py:25
  96.6 1.5 %shard_map.95 = f32[224,4096]{1,0:T(8,128)} custom-call(s32[3]{0:T(128)S(1)} %pad_add_fusion.refs_0_, f32[4,224,256]{2,1,0:T(8,128)S(1)} %get-tuple-element.40.refs_1_, bf16[224,256]{1,0:T(8,128)(2,1)S(1)} %get-tuple-element.41.refs_2_, bf16[224,256]{1,0:T(8,128)(2,1)S(1)} %collective-permute-done.19.refs_3_, ...), custom_call_target="tpu_custom_call", output_to_operand_aliasing={{}: (6, {})} | custom-call | tf_op jit(solution)/shard_map/pallas_call | solution.py:349
  (26 shorter events, 0.1 us)
Async XLA Ops:
  4.6 0.8 copy-start
  5.4 0.8 copy-start.2
  13.2 4.5 %collective-permute-start = (bf16[256,4096]{1,0:T(8,128)(2,1)S(1)}, bf16[256,4096]{1,0:T(8,128)(2,1)}, u32[]{:S(2)}, u32[]{:S(2)}) collective-permute-start(bf16[256,4096]{1,0:T(8,128)(2,1)S(1)} %shard_map.87.refs_1_.refs_4_), channel_id=1, source_target_pairs={{0,4},{4,0},{8,12},{12,8},{1,5},{5,1},{9,13},{13,9},{2,6},{6,2},{1... | collective-permute-start | bytes 6291464 | tf_op jit(solution)/shard_map/ppermute | solution.py:25
  14.8 9.9 %collective-permute-start.5 = (bf16[224,512]{1,0:T(8,128)(2,1)S(1)}, bf16[224,512]{1,0:T(8,128)(2,1)S(1)}, u32[]{:S(2)}, u32[]{:S(2)}) collective-permute-start(bf16[224,512]{1,0:T(8,128)(2,1)S(1)} %constant_dynamic-slice_fusion), channel_id=1, source_target_pairs={{0,8},{4,12},{8,0},{12,4},{1,9},{5,13},{9,1},{13,5},{2,10},{6,14},... | collective-permute-start | bytes 688136 | tf_op jit(solution)/shard_map/ppermute | solution.py:25
  17.7 1.0 %copy-start.1 = (bf16[224,1024]{1,0:T(8,128)(2,1)S(1)}, bf16[224,1024]{1,0:T(8,128)(2,1)}, u32[]{:S(2)}) copy-start(bf16[224,1024]{1,0:T(8,128)(2,1)} %copy-done) | copy-start | bytes 1376260
  18.7 1.0 %copy-start.3 = (bf16[224,1024]{1,0:T(8,128)(2,1)S(1)}, bf16[224,1024]{1,0:T(8,128)(2,1)}, u32[]{:S(2)}) copy-start(bf16[224,1024]{1,0:T(8,128)(2,1)} %copy-done.2) | copy-start | bytes 1376260
  19.8 9.1 %copy-start.4 = (bf16[224,2048]{1,0:T(8,128)(2,1)S(1)}, bf16[224,2048]{1,0:T(8,128)(2,1)}, u32[]{:S(2)}) copy-start(bf16[224,2048]{1,0:T(8,128)(2,1)} %refs_1_.3) | copy-start | bytes 2752516
  24.3 15.2 %collective-permute-start.1 = (f32[4,64,256]{2,1,0:T(8,128)S(1)}, f32[4,64,256]{2,1,0:T(8,128)S(1)}, u32[]{:S(2)}, u32[]{:S(2)}) collective-permute-start(f32[4,64,256]{2,1,0:T(8,128)S(1)} %get-tuple-element.35), channel_id=1, source_target_pairs={{0,4},{4,0},{8,12},{12,8},{1,5},{5,1},{9,13},{13,9},{2,6},{6,2},{1... | collective-permute-start | bytes 786440 | tf_op jit(solution)/shard_map/ppermute | solution.py:25
  24.7 9.9 %collective-permute-start.8 = (bf16[224,512]{1,0:T(8,128)(2,1)S(1)}, bf16[224,512]{1,0:T(8,128)(2,1)S(1)}, u32[]{:S(2)}, u32[]{:S(2)}) collective-permute-start(bf16[224,512]{1,0:T(8,128)(2,1)S(1)} %collective-permute-done.5.refs_3_), channel_id=1, source_target_pairs={{0,17},{1,16},{2,19},{3,18},{16,1},{17,0},{18,3},{19,2},{4,21},{5,... | collective-permute-start | bytes 688136 | tf_op jit(solution)/shard_map/ppermute | solution.py:283
  28.4 11.1 %collective-permute-start.7 = (bf16[224,512]{1,0:T(8,128)(2,1)S(1)}, bf16[224,512]{1,0:T(8,128)(2,1)S(1)}, u32[]{:S(2)}, u32[]{:S(2)}) collective-permute-start(bf16[224,512]{1,0:T(8,128)(2,1)S(1)} %collective-permute-done.5.refs_3_), channel_id=1, source_target_pairs={{0,16},{1,17},{2,18},{3,19},{16,0},{17,1},{18,2},{19,3},{4,20},{5,... | collective-permute-start | bytes 688136 | tf_op jit(solution)/shard_map/ppermute | solution.py:283
  28.9 22.0 %collective-permute-start.4 = (bf16[224,2048]{1,0:T(8,128)(2,1)S(1)}, bf16[224,2048]{1,0:T(8,128)(2,1)S(1)}, u32[]{:S(2)}, u32[]{:S(2)}) collective-permute-start(bf16[224,2048]{1,0:T(8,128)(2,1)S(1)} %copy-done.4), channel_id=1, source_target_pairs={{0,4},{4,0},{8,12},{12,8},{1,5},{5,1},{9,13},{13,9},{2,6},{6,2},{1... | collective-permute-start | bytes 2752520 | tf_op jit(solution)/shard_map/ppermute | solution.py:25
  28.9 11.1 %collective-permute-start.9 = (bf16[224,512]{1,0:T(8,128)(2,1)S(1)}, bf16[224,512]{1,0:T(8,128)(2,1)S(1)}, u32[]{:S(2)}, u32[]{:S(2)}) collective-permute-start(bf16[224,512]{1,0:T(8,128)(2,1)S(1)} %collective-permute-done.5.refs_3_), channel_id=1, source_target_pairs={{0,4},{4,0},{8,12},{12,8},{1,5},{5,1},{9,13},{13,9},{2,6},{6,2},{1... | collective-permute-start | bytes 688136 | tf_op jit(solution)/shard_map/ppermute | solution.py:25
  34.6 7.2 %collective-permute-start.6 = (bf16[224,512]{1,0:T(8,128)(2,1)S(1)}, bf16[224,512]{1,0:T(8,128)(2,1)S(1)}, u32[]{:S(2)}, u32[]{:S(2)}) collective-permute-start(bf16[224,512]{1,0:T(8,128)(2,1)S(1)} %collective-permute-done.5.refs_3_), channel_id=1, source_target_pairs={{0,1},{1,0},{2,3},{3,2},{16,17},{17,16},{18,19},{19,18},{4,5},{5,4... | collective-permute-start | bytes 688136 | tf_op jit(solution)/shard_map/ppermute | solution.py:283
  39.4 2.4 %collective-permute-start.12 = (bf16[224,512]{1,0:T(8,128)(2,1)S(1)}, bf16[224,512]{1,0:T(8,128)(2,1)S(1)}, u32[]{:S(2)}, u32[]{:S(2)}) collective-permute-start(bf16[224,512]{1,0:T(8,128)(2,1)S(1)} %collective-permute-done.8.refs_6_), channel_id=1, source_target_pairs={{0,4},{4,0},{8,12},{12,8},{1,5},{5,1},{9,13},{13,9},{2,6},{6,2},{1... | collective-permute-start | bytes 688136 | tf_op jit(solution)/shard_map/ppermute | solution.py:25
  39.4 3.8 %collective-permute-start.11 = (bf16[224,512]{1,0:T(8,128)(2,1)S(1)}, bf16[224,512]{1,0:T(8,128)(2,1)S(1)}, u32[]{:S(2)}, u32[]{:S(2)}) collective-permute-start(bf16[224,512]{1,0:T(8,128)(2,1)S(1)} %collective-permute-done.7.refs_5_), channel_id=1, source_target_pairs={{0,4},{4,0},{8,12},{12,8},{1,5},{5,1},{9,13},{13,9},{2,6},{6,2},{1... | collective-permute-start | bytes 688136 | tf_op jit(solution)/shard_map/ppermute | solution.py:25
  40.0 9.2 %collective-permute-start.2 = (f32[4,64,256]{2,1,0:T(8,128)S(1)}, f32[4,64,256]{2,1,0:T(8,128)S(1)}, u32[]{:S(2)}, u32[]{:S(2)}) collective-permute-start(f32[4,64,256]{2,1,0:T(8,128)S(1)} %add.13), channel_id=1, source_target_pairs={{0,8},{4,12},{8,0},{12,4},{1,9},{5,13},{9,1},{13,5},{2,10},{6,14},... | collective-permute-start | bytes 786440 | tf_op jit(solution)/shard_map/ppermute | solution.py:25
  41.8 10.9 %collective-permute-start.13 = (bf16[224,1024]{1,0:T(8,128)(2,1)S(1)}, bf16[224,1024]{1,0:T(8,128)(2,1)S(1)}, u32[]{:S(2)}, u32[]{:S(2)}) collective-permute-start(bf16[224,1024]{1,0:T(8,128)(2,1)S(1)} %copy-done.3), channel_id=1, source_target_pairs={{0,4},{4,0},{8,12},{12,8},{1,5},{5,1},{9,13},{13,9},{2,6},{6,2},{1... | collective-permute-start | bytes 1376264 | tf_op jit(solution)/shard_map/ppermute | solution.py:25
  41.8 17.2 %collective-permute-start.14 = (bf16[224,1024]{1,0:T(8,128)(2,1)}, bf16[224,1024]{1,0:T(8,128)(2,1)S(1)}, u32[]{:S(2)}, u32[]{:S(2)}) collective-permute-start(bf16[224,1024]{1,0:T(8,128)(2,1)} %get-tuple-element.31.refs_5_), channel_id=1, source_target_pairs={{0,8},{4,12},{8,0},{12,4},{1,9},{5,13},{9,1},{13,5},{2,10},{6,14},... | collective-permute-start | bytes 1376264 | tf_op jit(solution)/shard_map/ppermute | solution.py:25
  43.2 23.9 %collective-permute-start.15 = (bf16[224,1024]{1,0:T(8,128)(2,1)S(1)}, bf16[224,1024]{1,0:T(8,128)(2,1)S(1)}, u32[]{:S(2)}, u32[]{:S(2)}) collective-permute-start(bf16[224,1024]{1,0:T(8,128)(2,1)S(1)} %copy-done.1), channel_id=1, source_target_pairs={{0,12},{4,8},{8,4},{12,0},{1,13},{5,9},{9,5},{13,1},{2,14},{6,10},... | collective-permute-start | bytes 1376264 | tf_op jit(solution)/shard_map/ppermute | solution.py:25
  49.2 1.5 %collective-permute-start.10 = (bf16[224,512]{1,0:T(8,128)(2,1)S(1)}, bf16[224,512]{1,0:T(8,128)(2,1)S(1)}, u32[]{:S(2)}, u32[]{:S(2)}) collective-permute-start(bf16[224,512]{1,0:T(8,128)(2,1)S(1)} %collective-permute-done.6.refs_4_), channel_id=1, source_target_pairs={{0,4},{4,0},{8,12},{12,8},{1,5},{5,1},{9,13},{13,9},{2,6},{6,2},{1... | collective-permute-start | bytes 688136 | tf_op jit(solution)/shard_map/ppermute | solution.py:25
  50.7 33.4 %collective-permute-start.3 = (f32[4,64,256]{2,1,0:T(8,128)S(1)}, f32[4,64,256]{2,1,0:T(8,128)S(1)}, u32[]{:S(2)}, u32[]{:S(2)}) collective-permute-start(f32[4,64,256]{2,1,0:T(8,128)S(1)} %add.14.refs_1_), channel_id=1, source_target_pairs={{0,4},{4,0},{8,12},{12,8},{1,5},{5,1},{9,13},{13,9},{2,6},{6,2},{1... | collective-permute-start | bytes 786440 | tf_op jit(solution)/shard_map/ppermute | solution.py:25
  69.9 7.6 %collective-permute-start.16 = (bf16[224,256]{1,0:T(8,128)(2,1)S(1)}, bf16[224,256]{1,0:T(8,128)(2,1)S(1)}, u32[]{:S(2)}, u32[]{:S(2)}) collective-permute-start(bf16[224,256]{1,0:T(8,128)(2,1)S(1)} %get-tuple-element.37), channel_id=1, source_target_pairs={{0,4},{4,0},{8,12},{12,8},{1,5},{5,1},{9,13},{13,9},{2,6},{6,2},{1... | collective-permute-start | bytes 344072 | tf_op jit(solution)/shard_map/ppermute | solution.py:25
  70.6 8.5 %collective-permute-start.17 = (bf16[224,256]{1,0:T(8,128)(2,1)S(1)}, bf16[224,256]{1,0:T(8,128)(2,1)S(1)}, u32[]{:S(2)}, u32[]{:S(2)}) collective-permute-start(bf16[224,256]{1,0:T(8,128)(2,1)S(1)} %get-tuple-element.38), channel_id=1, source_target_pairs={{0,8},{4,12},{8,0},{12,4},{1,9},{5,13},{9,1},{13,5},{2,10},{6,14},... | collective-permute-start | bytes 344072 | tf_op jit(solution)/shard_map/ppermute | solution.py:25
  76.9 6.0 %collective-permute-start.22 = (bf16[224,512]{1,0:T(8,128)(2,1)S(1)}, bf16[224,512]{1,0:T(8,128)(2,1)S(1)}, u32[]{:S(2)}, u32[]{:S(2)}) collective-permute-start(bf16[224,512]{1,0:T(8,128)(2,1)S(1)} %get-tuple-element.47), channel_id=1, source_target_pairs={{0,4},{4,0},{8,12},{12,8},{1,5},{5,1},{9,13},{13,9},{2,6},{6,2},{1... | collective-permute-start | bytes 688136 | tf_op jit(solution)/shard_map/ppermute | solution.py:25
  77.0 4.9 %collective-permute-start.18 = (bf16[224,256]{1,0:T(8,128)(2,1)S(1)}, bf16[224,256]{1,0:T(8,128)(2,1)S(1)}, u32[]{:S(2)}, u32[]{:S(2)}) collective-permute-start(bf16[224,256]{1,0:T(8,128)(2,1)S(1)} %get-tuple-element.39), channel_id=1, source_target_pairs={{0,12},{4,8},{8,4},{12,0},{1,13},{5,9},{9,5},{13,1},{2,14},{6,10},... | collective-permute-start | bytes 344072 | tf_op jit(solution)/shard_map/ppermute | solution.py:25
  77.5 14.0 %collective-permute-start.23 = (bf16[224,512]{1,0:T(8,128)(2,1)S(1)}, bf16[224,512]{1,0:T(8,128)(2,1)S(1)}, u32[]{:S(2)}, u32[]{:S(2)}) collective-permute-start(bf16[224,512]{1,0:T(8,128)(2,1)S(1)} %get-tuple-element.48), channel_id=1, source_target_pairs={{0,8},{4,12},{8,0},{12,4},{1,9},{5,13},{9,1},{13,5},{2,10},{6,14},... | collective-permute-start | bytes 688136 | tf_op jit(solution)/shard_map/ppermute | solution.py:25
  79.1 12.6 %collective-permute-start.24 = (bf16[224,512]{1,0:T(8,128)(2,1)S(1)}, bf16[224,512]{1,0:T(8,128)(2,1)S(1)}, u32[]{:S(2)}, u32[]{:S(2)}) collective-permute-start(bf16[224,512]{1,0:T(8,128)(2,1)S(1)} %get-tuple-element.49), channel_id=1, source_target_pairs={{0,12},{4,8},{8,4},{12,0},{1,13},{5,9},{9,5},{13,1},{2,14},{6,10},... | collective-permute-start | bytes 688136 | tf_op jit(solution)/shard_map/ppermute | solution.py:25
  81.9 11.6 %collective-permute-start.19 = (bf16[224,256]{1,0:T(8,128)(2,1)S(1)}, bf16[224,256]{1,0:T(8,128)(2,1)S(1)}, u32[]{:S(2)}, u32[]{:S(2)}) collective-permute-start(bf16[224,256]{1,0:T(8,128)(2,1)S(1)} %get-tuple-element.42), channel_id=1, source_target_pairs={{0,4},{4,0},{8,12},{12,8},{1,5},{5,1},{9,13},{13,9},{2,6},{6,2},{1... | collective-permute-start | bytes 344072 | tf_op jit(solution)/shard_map/ppermute | solution.py:25
  82.9 12.5 %collective-permute-start.20 = (bf16[224,256]{1,0:T(8,128)(2,1)S(1)}, bf16[224,256]{1,0:T(8,128)(2,1)S(1)}, u32[]{:S(2)}, u32[]{:S(2)}) collective-permute-start(bf16[224,256]{1,0:T(8,128)(2,1)S(1)} %get-tuple-element.43), channel_id=1, source_target_pairs={{0,8},{4,12},{8,0},{12,4},{1,9},{5,13},{9,1},{13,5},{2,10},{6,14},... | collective-permute-start | bytes 344072 | tf_op jit(solution)/shard_map/ppermute | solution.py:25
  84.1 12.5 %collective-permute-start.21 = (bf16[224,256]{1,0:T(8,128)(2,1)S(1)}, bf16[224,256]{1,0:T(8,128)(2,1)S(1)}, u32[]{:S(2)}, u32[]{:S(2)}) collective-permute-start(bf16[224,256]{1,0:T(8,128)(2,1)S(1)} %get-tuple-element.44), channel_id=1, source_target_pairs={{0,12},{4,8},{8,4},{12,0},{1,13},{5,9},{9,5},{13,1},{2,14},{6,10},... | collective-permute-start | bytes 344072 | tf_op jit(solution)/shard_map/ppermute | solution.py:25

commit v3 on v2

--- a/solution.py
+++ b/solution.py
@@ -7,8 +7,8 @@
 
 
 LANES = 128
-QUARTERS = (1, 2, 1)
-GROUP = 16
+QUARTERS = (2, 2)
+GROUP = 32
 NT = (((1,), (1,)), ((), ()))
 NN = (((1,), (0,)), ((), ()))
 VMEM = pl.BlockSpec(memory_space=pltpu.VMEM)
@@ -75,6 +75,7 @@
     high_count = cols // LANES
     low_pos = lax.broadcasted_iota(jnp.int32, (LANES, samples), 0)
     high_pos = lax.broadcasted_iota(jnp.int32, (high_count, samples), 0)
+    blank = jnp.zeros((high_count, samples), jnp.bfloat16)
 
     def build(step, carry):
         first = pl.multiple_of(step * GROUP, GROUP)
@@ -82,10 +83,16 @@
         wgt = wgt_ref[pl.ds(first, GROUP), :].astype(jnp.float32) * (1.0 / 256.0)
         low = vox & (LANES - 1)
         high = lax.shift_right_logical(vox, LANES.bit_length() - 1)
+        hots = []
         for i in range(GROUP):
             low_hot = (low_pos == low[i:i + 1]).astype(jnp.float32).astype(jnp.bfloat16)
             high_hot = jnp.where(high_pos == high[i:i + 1], wgt[i:i + 1], 0.0).astype(jnp.bfloat16)
-            tile_ref[i * high_count:(i + 1) * high_count, :] = dot(high_hot, low_hot, NT)
+            hots.append((low_hot, high_hot))
+        for i in range(0, GROUP, 2):
+            (low_a, high_a), (low_b, high_b) = hots[i:i + 2]
+            left = jnp.concatenate([jnp.concatenate([high_a, blank], 1), jnp.concatenate([blank, high_b], 1)], 0)
+            right = jnp.concatenate([low_a, low_b], 1)
+            tile_ref[i * high_count:(i + 2) * high_count, :] = dot(left, right, NT)
         for h in range(high_count):
             part = tile_ref[pl.ds(h, GROUP, stride=high_count), :]
             matrix_ref[pl.ds(first, GROUP), h * LANES:(h + 1) * LANES] = part.astype(jnp.bfloat16)

time: 98.4 us -> 96.8 us (0.984)
  waiting for transfers between devices: 33.5 us -> 40.6 us
  Pallas kernels: 38.1 us -> 32.5 us
  starting transfers between devices: 21.1 us -> 17.9 us
    ppermute x22 -> x19, waiting for transfers between devices: 25 us -> 32.5 us  [swap(): return lax.ppermute(value, axis, [(i, i ^ mask) for i in range(count)])]
    ppermute x22 -> x19, starting transfers between devices: 15.2 us -> 13.1 us  [swap(): return lax.ppermute(value, axis, [(i, i ^ mask) for i in range(count)])]
    pallas_call x1, Pallas kernels: 7.07 us -> 5.17 us  [step_of(): kernel(build_kernel, [VMEM, VMEM], VMEM, shape((rows // 2, cols), bf16),...]
    pallas_call x2 -> x1, Pallas kernels: 3.35 us -> 1.84 us  [step_of(): kernel(lambda *refs: finish_kernel(count, cut, *refs), [SMEM] + [VMEM] *...]
    pallas_call x1, Pallas kernels: 7.22 us -> 6.1 us  [step_of(): kernel(lambda *refs: data_kernel(count, cuts, *refs), [SMEM] + [VMEM] * 5...]
    ppermute x3, starting transfers between devices: 5.86 us -> 4.83 us  [step_of(): fetched[m].append(lax.ppermute(fetched[m][0], ('groups', 'slab'), pairs))]
    pallas_call x3 -> x2, Pallas kernels: 10.2 us -> 9.22 us  [step_of(): kernel(lambda *refs: penalty_kernel(count, pieces, cut, *refs), [VMEM] *...]
    unnamed x10 -> x8, local copies, waits for them, and re-layouts: 3.58 us -> 3.58 us
  transfers between devices with their start and end apart: 25 -> 22, of which waited for: 11 -> 8; matrix products, arithmetic and copies ran while one was open for 1% -> 1% of each run, Pallas kernels for 26% -> 22%
where the time goes in v3:
time: 96.8 us; the launch traced here: 96.5 us
  waiting for transfers between devices  40.6 us (42%)
  Pallas kernels  32.5 us (34%)
  starting transfers between devices  17.9 us (18%)
  local copies, waits for them, and re-layouts  4.53 us (5%)
    ppermute x19, waiting for transfers between devices, swap(): return lax.ppermute(value, axis, [(i, i ^ mask) for i in range(count)])  32.5 us
    ppermute x19, starting transfers between devices, swap(): return lax.ppermute(value, axis, [(i, i ^ mask) for i in range(count)])  13.1 us
    pallas_call x2, Pallas kernels, step_of(): kernel(lambda *refs: penalty_kernel(count, pieces, cut, *refs), [VMEM] *...  9.22 us
    ppermute x3, waiting for transfers between devices, step_of(): fetched[m].append(lax.ppermute(fetched[m][0], ('groups', 'slab'), pairs))  8.17 us
    pallas_call x1, Pallas kernels, step_of(): kernel(lambda *refs: data_kernel(count, cuts, *refs), [SMEM] + [VMEM] * 5...  6.1 us
    pallas_call x1, Pallas kernels, step_of(): kernel(build_kernel, [VMEM, VMEM], VMEM, shape((rows // 2, cols), bf16),...  5.17 us
    ppermute x3, starting transfers between devices, step_of(): fetched[m].append(lax.ppermute(fetched[m][0], ('groups', 'slab'), pairs))  4.83 us
    pallas_call x1, Pallas kernels, step_of(): kernel(lambda *refs: sums_kernel(count, *refs), [SMEM] + [VMEM] * (count...  4.4 us
  transfers between devices with their start and end apart: 22, of which 8 were waited for; matrix products, arithmetic and copies ran while one was open for 1% of the time, Pallas kernels for 22%

profile of v3, /device:TPU:0, one launch (start us, length us, event | category | flops | bytes accessed | tf_op | source)
XLA Modules:
  0.0 96.5 jit_solution(14208185968108780856)
XLA Ops:
  0.6 0.1 pad_add_fusion.refs_0_
  0.7 3.9 %shard_map.86 = (bf16[224,1024]{1,0:T(8,128)(2,1)S(1)}, bf16[224,1024]{1,0:T(8,128)(2,1)S(1)}, bf16[224,1024]{1,0:T(8,128)(2,1)}, bf16[224,1024]{1,0:T(8,128)(2,...) custom-call(s32[3]{0:T(128)S(1)} %pad_add_fusion.refs_0_, s32[8]{0:T(128)} %refs_1_.2, ...), custom_call_target="tpu_custom_call" | custom-call | tf_op jit(solution)/shard_map/pallas_call | solution.py:268
  4.6 0.8 copy-done
  5.4 0.8 copy-done.2
  6.2 5.2 %shard_map.87.refs_1_.refs_4_ = bf16[256,4096]{1,0:T(8,128)(2,1)S(1)} custom-call(s32[256,128]{1,0:T(8,128)S(1)} %get-tuple-element.22.vox_ref, s32[256,128]{1,0:T(8,128)S(1)} %get-tuple-element.23.wgt_ref), custom_call_target="tpu_custom_call" | custom-call | tf_op jit(solution)/shard_map/pallas_call | solution.py:292
  11.3 0.6 collective-permute-start
  11.9 1.0 constant_dynamic-slice_fusion
  12.9 2.6 %collective-permute-start.5 = (bf16[224,512]{1,0:T(8,128)(2,1)S(1)}, bf16[224,512]{1,0:T(8,128)(2,1)S(1)}, u32[]{:S(2)}, u32[]{:S(2)}) collective-permute-start(bf16[224,512]{1,0:T(8,128)(2,1)S(1)} %constant_dynamic-slice_fusion), channel_id=1, source_target_pairs={{0,8},{4,12},{8,0},{12,4},{1,9},{5,13},{9,1},{13,5},{2,10},{6,14},... | collective-permute-start | bytes 688136 | tf_op jit(solution)/shard_map/ppermute | solution.py:25
  15.4 6.3 %collective-permute-done.5.refs_3_ = bf16[224,512]{1,0:T(8,128)(2,1)S(1)} collective-permute-done((bf16[224,512]{1,0:T(8,128)(2,1)S(1)}, bf16[224,512]{1,0:T(8,128)(2,1)S(1)}, u32[]{:S(2)}, u32[]{:S(2)}) %collective-permute-start.5) | collective-permute-done | bytes 229408 | tf_op jit(solution)/shard_map/ppermute | solution.py:25
  21.7 2.8 %collective-permute-start.8 = (bf16[224,512]{1,0:T(8,128)(2,1)S(1)}, bf16[224,512]{1,0:T(8,128)(2,1)S(1)}, u32[]{:S(2)}, u32[]{:S(2)}) collective-permute-start(bf16[224,512]{1,0:T(8,128)(2,1)S(1)} %collective-permute-done.5.refs_3_), channel_id=1, source_target_pairs={{0,17},{1,16},{2,19},{3,18},{16,1},{17,0},{18,3},{19,2},{4,21},{5,... | collective-permute-start | bytes 688136 | tf_op jit(solution)/shard_map/ppermute | solution.py:290
  24.5 0.5 collective-permute-start.7
  25.0 0.2 collective-permute-start.9
  25.2 4.9 %collective-permute-done.8.refs_6_ = bf16[224,512]{1,0:T(8,128)(2,1)S(1)} collective-permute-done((bf16[224,512]{1,0:T(8,128)(2,1)S(1)}, bf16[224,512]{1,0:T(8,128)(2,1)S(1)}, u32[]{:S(2)}, u32[]{:S(2)}) %collective-permute-start.8) | collective-permute-done | bytes 229408 | tf_op jit(solution)/shard_map/ppermute | solution.py:290
  30.1 1.5 %collective-permute-start.6 = (bf16[224,512]{1,0:T(8,128)(2,1)S(1)}, bf16[224,512]{1,0:T(8,128)(2,1)S(1)}, u32[]{:S(2)}, u32[]{:S(2)}) collective-permute-start(bf16[224,512]{1,0:T(8,128)(2,1)S(1)} %collective-permute-done.5.refs_3_), channel_id=1, source_target_pairs={{0,1},{1,0},{2,3},{3,2},{16,17},{17,16},{18,19},{19,18},{4,5},{5,4... | collective-permute-start | bytes 688136 | tf_op jit(solution)/shard_map/ppermute | solution.py:290
  31.6 3.3 %collective-permute-done.7.refs_5_ = bf16[224,512]{1,0:T(8,128)(2,1)S(1)} collective-permute-done((bf16[224,512]{1,0:T(8,128)(2,1)S(1)}, bf16[224,512]{1,0:T(8,128)(2,1)S(1)}, u32[]{:S(2)}, u32[]{:S(2)}) %collective-permute-start.7) | collective-permute-done | bytes 229408 | tf_op jit(solution)/shard_map/ppermute | solution.py:290
  34.9 0.1 collective-permute-start.12
  35.0 0.4 collective-permute-start.11
  35.4 1.0 %copy-done.1 = bf16[224,1024]{1,0:T(8,128)(2,1)S(1)} copy-done((bf16[224,1024]{1,0:T(8,128)(2,1)S(1)}, bf16[224,1024]{1,0:T(8,128)(2,1)}, u32[]{:S(2)}) %copy-start.1) | copy-done | bytes 458776
  36.4 1.0 %copy-done.3 = bf16[224,1024]{1,0:T(8,128)(2,1)S(1)} copy-done((bf16[224,1024]{1,0:T(8,128)(2,1)S(1)}, bf16[224,1024]{1,0:T(8,128)(2,1)}, u32[]{:S(2)}) %copy-start.3) | copy-done | bytes 458776
  37.5 4.4 %shard_map.88 = (f32[4,64,256]{2,1,0:T(8,128)S(1)}, f32[4,64,256]{2,1,0:T(8,128)S(1)}) custom-call(s32[3]{0:T(128)S(1)} %pad_add_fusion.refs_0_, bf16[256,4096]{1,0:T(8,128)(2,1)S(1)} %shard_map.87.refs_1_.refs_4_, bf16[256,4096]{1,0:T(8,128)(2,1)} %collective-permute-done.refs_2_.refs_5_, bf16[224,1024]{1,0:T(8,128)(2,1)S(1)} %get-tuple-element.24.refs_3_.refs_1_, ...), custom_call_target="tpu_custom_call" | custom-call | tf_op jit(solution)/shard_map/pallas_call | solution.py:304
  41.9 0.0 collective-permute-done.9.refs_7_
  41.9 0.1 collective-permute-start.1
  42.0 0.0 collective-permute-done.6.refs_4_
  42.0 0.4 collective-permute-start.13
  42.5 1.5 %collective-permute-start.14 = (bf16[224,1024]{1,0:T(8,128)(2,1)}, bf16[224,1024]{1,0:T(8,128)(2,1)S(1)}, u32[]{:S(2)}, u32[]{:S(2)}) collective-permute-start(bf16[224,1024]{1,0:T(8,128)(2,1)} %get-tuple-element.26.refs_5_), channel_id=1, source_target_pairs={{0,8},{4,12},{8,0},{12,4},{1,9},{5,13},{9,1},{13,5},{2,10},{6,14},... | collective-permute-start | bytes 1376264 | tf_op jit(solution)/shard_map/ppermute | solution.py:25
  43.9 0.0 collective-permute-done.1
  43.9 0.7 collective-permute-start.10
  44.6 1.1 %collective-permute-done.10.refs_8_ = bf16[224,512]{1,0:T(8,128)(2,1)S(1)} collective-permute-done((bf16[224,512]{1,0:T(8,128)(2,1)S(1)}, bf16[224,512]{1,0:T(8,128)(2,1)S(1)}, u32[]{:S(2)}, u32[]{:S(2)}) %collective-permute-start.10) | collective-permute-done | bytes 229408 | tf_op jit(solution)/shard_map/ppermute | solution.py:25
  45.7 1.5 %collective-permute-start.2 = (f32[4,64,256]{2,1,0:T(8,128)S(1)}, f32[4,64,256]{2,1,0:T(8,128)S(1)}, u32[]{:S(2)}, u32[]{:S(2)}) collective-permute-start(f32[4,64,256]{2,1,0:T(8,128)S(1)} %add.13), channel_id=1, source_target_pairs={{0,8},{4,12},{8,0},{12,4},{1,9},{5,13},{9,1},{13,5},{2,10},{6,14},... | collective-permute-start | bytes 786440 | tf_op jit(solution)/shard_map/ppermute | solution.py:25
  47.2 0.0 collective-permute-done.4.refs_2_
  47.2 1.9 %shard_map.89.refs_0_ = bf16[896,2048]{1,0:T(8,128)(2,1)S(1)} custom-call(s32[3]{0:T(128)S(1)} %pad_add_fusion.refs_0_, bf16[224,2048]{1,0:T(8,128)(2,1)} %refs_1_.3, bf16[224,2048]{1,0:T(8,128)(2,1)S(1)} %collective-permute-done.4.refs_2_, bf16[224,512]{1,0:T(8,128)(2,1)S(1)} %collective-permute-done.5.refs_3_, ...), custom_call_target="tpu_custom_call" | custom-call | tf_op jit(solution)/shard_map/pallas_call | solution.py:316
  49.1 0.0 collective-permute-done.13.refs_2_
  49.1 7.0 %collective-permute-done.14.refs_3_ = bf16[224,1024]{1,0:T(8,128)(2,1)S(1)} collective-permute-done((bf16[224,1024]{1,0:T(8,128)(2,1)}, bf16[224,1024]{1,0:T(8,128)(2,1)S(1)}, u32[]{:S(2)}, u32[]{:S(2)}) %collective-permute-start.14) | collective-permute-done | bytes 458784 | tf_op jit(solution)/shard_map/ppermute | solution.py:25
  56.1 8.8 %collective-permute-done.15.refs_4_ = bf16[224,1024]{1,0:T(8,128)(2,1)S(1)} collective-permute-done((bf16[224,1024]{1,0:T(8,128)(2,1)S(1)}, bf16[224,1024]{1,0:T(8,128)(2,1)S(1)}, u32[]{:S(2)}, u32[]{:S(2)}) %collective-permute-start.15) | collective-permute-done | bytes 458784 | tf_op jit(solution)/shard_map/ppermute | solution.py:25
  64.9 4.6 %shard_map.90 = (bf16[224,512]{1,0:T(8,128)(2,1)S(1)}, bf16[224,512]{1,0:T(8,128)(2,1)S(1)}, bf16[224,512]{1,0:T(8,128)(2,1)S(1)}, bf16[224,512]{1,0:T(8,128)(2,1)S(1)}) custom-call(bf16[896,2048]{1,0:T(8,128)(2,1)S(1)} %shard_map.89.refs_0_, bf16[224,1024]{1,0:T(8,128)(2,1)S(1)} %get-tuple-element.24.refs_3_.refs_1_, ...), custom_call_target="tpu_custom_call" | custom-call | tf_op jit(solution)/shard_map/pallas_call | solution.py:327
  69.5 0.9 collective-permute-start.16
  70.4 1.5 %collective-permute-start.17 = (bf16[224,512]{1,0:T(8,128)(2,1)S(1)}, bf16[224,512]{1,0:T(8,128)(2,1)S(1)}, u32[]{:S(2)}, u32[]{:S(2)}) collective-permute-start(bf16[224,512]{1,0:T(8,128)(2,1)S(1)} %get-tuple-element.33), channel_id=1, source_target_pairs={{0,8},{4,12},{8,0},{12,4},{1,9},{5,13},{9,1},{13,5},{2,10},{6,14},... | collective-permute-start | bytes 688136 | tf_op jit(solution)/shard_map/ppermute | solution.py:25
  71.9 0.0 collective-permute-done.2
  71.9 0.1 collective-permute-start.3
  72.0 4.6 %shard_map.92 = (bf16[224,512]{1,0:T(8,128)(2,1)S(1)}, bf16[224,512]{1,0:T(8,128)(2,1)S(1)}, bf16[224,512]{1,0:T(8,128)(2,1)S(1)}, bf16[224,512]{1,0:T(8,128)(2,1)S(1)}) custom-call(bf16[896,2048]{1,0:T(8,128)(2,1)S(1)} %shard_map.89.refs_0_, bf16[224,1024]{1,0:T(8,128)(2,1)S(1)} %get-tuple-element.24.refs_3_.refs_1_, ...), custom_call_target="tpu_custom_call" | custom-call | tf_op jit(solution)/shard_map/pallas_call | solution.py:327
  76.6 0.6 collective-permute-start.19
  77.2 0.2 collective-permute-start.18
  77.4 1.5 %collective-permute-start.20 = (bf16[224,512]{1,0:T(8,128)(2,1)S(1)}, bf16[224,512]{1,0:T(8,128)(2,1)S(1)}, u32[]{:S(2)}, u32[]{:S(2)}) collective-permute-start(bf16[224,512]{1,0:T(8,128)(2,1)S(1)} %get-tuple-element.38), channel_id=1, source_target_pairs={{0,8},{4,12},{8,0},{12,4},{1,9},{5,13},{9,1},{13,5},{2,10},{6,14},... | collective-permute-start | bytes 688136 | tf_op jit(solution)/shard_map/ppermute | solution.py:25
  78.9 0.3 collective-permute-start.21
  79.2 5.6 %collective-permute-done.18.refs_10_ = bf16[224,512]{1,0:T(8,128)(2,1)S(1)} collective-permute-done((bf16[224,512]{1,0:T(8,128)(2,1)S(1)}, bf16[224,512]{1,0:T(8,128)(2,1)S(1)}, u32[]{:S(2)}, u32[]{:S(2)}) %collective-permute-start.18) | collective-permute-done | bytes 229408 | tf_op jit(solution)/shard_map/ppermute | solution.py:25
  84.8 6.1 %shard_map.91 = (f32[224,4096]{1,0:T(8,128)}, f32[8,64,64]{2,1,0:T(8,128)}, f32[4,224,512]{2,1,0:T(8,128)S(1)}) custom-call(s32[3]{0:T(128)S(1)} %pad_add_fusion.refs_0_, f32[4,64,256]{2,1,0:T(8,128)S(1)} %add.14.refs_1_, f32[4,64,256]{2,1,0:T(8,128)S(1)} %collective-permute-done.3.refs_2_, bf16[8,224,256]{2,1,0:T(8,128)(2,1)S(1)} %get-tuple-element.28.refs_7_.refs_3_, ...), custom_call_target="tpu_custom_call" | custom-call | tf_op jit(solution)/shard_map/pallas_call | solution.py:341
  90.9 3.7 %collective-permute-done.21.refs_5_ = bf16[224,512]{1,0:T(8,128)(2,1)S(1)} collective-permute-done((bf16[224,512]{1,0:T(8,128)(2,1)S(1)}, bf16[224,512]{1,0:T(8,128)(2,1)S(1)}, u32[]{:S(2)}, u32[]{:S(2)}) %collective-permute-start.21) | collective-permute-done | bytes 229408 | tf_op jit(solution)/shard_map/ppermute | solution.py:25
  94.6 1.8 %shard_map.93 = f32[224,4096]{1,0:T(8,128)} custom-call(s32[3]{0:T(128)S(1)} %pad_add_fusion.refs_0_, f32[4,224,512]{2,1,0:T(8,128)S(1)} %get-tuple-element.35.refs_1_, bf16[224,512]{1,0:T(8,128)(2,1)S(1)} %get-tuple-element.36.refs_2_, bf16[224,512]{1,0:T(8,128)(2,1)S(1)} %collective-permute-done.19.refs_3_, ...), custom_call_target="tpu_custom_call", output_to_operand_aliasing={{}: (6, {})} | custom-call | tf_op jit(solution)/shard_map/pallas_call | solution.py:356
  (16 shorter events, 0.1 us)
Async XLA Ops:
  4.6 0.8 copy-start
  5.4 0.8 copy-start.2
  11.3 23.6 %collective-permute-start = (bf16[256,4096]{1,0:T(8,128)(2,1)S(1)}, bf16[256,4096]{1,0:T(8,128)(2,1)}, u32[]{:S(2)}, u32[]{:S(2)}) collective-permute-start(bf16[256,4096]{1,0:T(8,128)(2,1)S(1)} %shard_map.87.refs_1_.refs_4_), channel_id=1, source_target_pairs={{0,4},{4,0},{8,12},{12,8},{1,5},{5,1},{9,13},{13,9},{2,6},{6,2},{1... | collective-permute-start | bytes 6291464 | tf_op jit(solution)/shard_map/ppermute | solution.py:25
  12.9 8.8 %collective-permute-start.5 = (bf16[224,512]{1,0:T(8,128)(2,1)S(1)}, bf16[224,512]{1,0:T(8,128)(2,1)S(1)}, u32[]{:S(2)}, u32[]{:S(2)}) collective-permute-start(bf16[224,512]{1,0:T(8,128)(2,1)S(1)} %constant_dynamic-slice_fusion), channel_id=1, source_target_pairs={{0,8},{4,12},{8,0},{12,4},{1,9},{5,13},{9,1},{13,5},{2,10},{6,14},... | collective-permute-start | bytes 688136 | tf_op jit(solution)/shard_map/ppermute | solution.py:25
  21.7 8.4 %collective-permute-start.8 = (bf16[224,512]{1,0:T(8,128)(2,1)S(1)}, bf16[224,512]{1,0:T(8,128)(2,1)S(1)}, u32[]{:S(2)}, u32[]{:S(2)}) collective-permute-start(bf16[224,512]{1,0:T(8,128)(2,1)S(1)} %collective-permute-done.5.refs_3_), channel_id=1, source_target_pairs={{0,17},{1,16},{2,19},{3,18},{16,1},{17,0},{18,3},{19,2},{4,21},{5,... | collective-permute-start | bytes 688136 | tf_op jit(solution)/shard_map/ppermute | solution.py:290
  24.5 22.7 %collective-permute-start.4 = (bf16[224,2048]{1,0:T(8,128)(2,1)}, bf16[224,2048]{1,0:T(8,128)(2,1)S(1)}, u32[]{:S(2)}, u32[]{:S(2)}) collective-permute-start(bf16[224,2048]{1,0:T(8,128)(2,1)} %refs_1_.3), channel_id=1, source_target_pairs={{0,4},{4,0},{8,12},{12,8},{1,5},{5,1},{9,13},{13,9},{2,6},{6,2},{1... | collective-permute-start | bytes 2752520 | tf_op jit(solution)/shard_map/ppermute | solution.py:25
  24.5 10.4 %collective-permute-start.7 = (bf16[224,512]{1,0:T(8,128)(2,1)S(1)}, bf16[224,512]{1,0:T(8,128)(2,1)S(1)}, u32[]{:S(2)}, u32[]{:S(2)}) collective-permute-start(bf16[224,512]{1,0:T(8,128)(2,1)S(1)} %collective-permute-done.5.refs_3_), channel_id=1, source_target_pairs={{0,16},{1,17},{2,18},{3,19},{16,0},{17,1},{18,2},{19,3},{4,20},{5,... | collective-permute-start | bytes 688136 | tf_op jit(solution)/shard_map/ppermute | solution.py:290
  25.0 16.9 %collective-permute-start.9 = (bf16[224,512]{1,0:T(8,128)(2,1)S(1)}, bf16[224,512]{1,0:T(8,128)(2,1)S(1)}, u32[]{:S(2)}, u32[]{:S(2)}) collective-permute-start(bf16[224,512]{1,0:T(8,128)(2,1)S(1)} %collective-permute-done.5.refs_3_), channel_id=1, source_target_pairs={{0,4},{4,0},{8,12},{12,8},{1,5},{5,1},{9,13},{13,9},{2,6},{6,2},{1... | collective-permute-start | bytes 688136 | tf_op jit(solution)/shard_map/ppermute | solution.py:25
  30.1 11.9 %collective-permute-start.6 = (bf16[224,512]{1,0:T(8,128)(2,1)S(1)}, bf16[224,512]{1,0:T(8,128)(2,1)S(1)}, u32[]{:S(2)}, u32[]{:S(2)}) collective-permute-start(bf16[224,512]{1,0:T(8,128)(2,1)S(1)} %collective-permute-done.5.refs_3_), channel_id=1, source_target_pairs={{0,1},{1,0},{2,3},{3,2},{16,17},{17,16},{18,19},{19,18},{4,5},{5,4... | collective-permute-start | bytes 688136 | tf_op jit(solution)/shard_map/ppermute | solution.py:290
  34.9 7.6 %collective-permute-start.12 = (bf16[224,512]{1,0:T(8,128)(2,1)S(1)}, bf16[224,512]{1,0:T(8,128)(2,1)S(1)}, u32[]{:S(2)}, u32[]{:S(2)}) collective-permute-start(bf16[224,512]{1,0:T(8,128)(2,1)S(1)} %collective-permute-done.8.refs_6_), channel_id=1, source_target_pairs={{0,4},{4,0},{8,12},{12,8},{1,5},{5,1},{9,13},{13,9},{2,6},{6,2},{1... | collective-permute-start | bytes 688136 | tf_op jit(solution)/shard_map/ppermute | solution.py:25
  35.0 9.0 %collective-permute-start.11 = (bf16[224,512]{1,0:T(8,128)(2,1)S(1)}, bf16[224,512]{1,0:T(8,128)(2,1)S(1)}, u32[]{:S(2)}, u32[]{:S(2)}) collective-permute-start(bf16[224,512]{1,0:T(8,128)(2,1)S(1)} %collective-permute-done.7.refs_5_), channel_id=1, source_target_pairs={{0,4},{4,0},{8,12},{12,8},{1,5},{5,1},{9,13},{13,9},{2,6},{6,2},{1... | collective-permute-start | bytes 688136 | tf_op jit(solution)/shard_map/ppermute | solution.py:25
  35.4 1.0 %copy-start.1 = (bf16[224,1024]{1,0:T(8,128)(2,1)S(1)}, bf16[224,1024]{1,0:T(8,128)(2,1)}, u32[]{:S(2)}) copy-start(bf16[224,1024]{1,0:T(8,128)(2,1)} %copy-done) | copy-start | bytes 1376260
  36.4 1.0 %copy-start.3 = (bf16[224,1024]{1,0:T(8,128)(2,1)S(1)}, bf16[224,1024]{1,0:T(8,128)(2,1)}, u32[]{:S(2)}) copy-start(bf16[224,1024]{1,0:T(8,128)(2,1)} %copy-done.2) | copy-start | bytes 1376260
  41.9 2.1 %collective-permute-start.1 = (f32[4,64,256]{2,1,0:T(8,128)S(1)}, f32[4,64,256]{2,1,0:T(8,128)S(1)}, u32[]{:S(2)}, u32[]{:S(2)}) collective-permute-start(f32[4,64,256]{2,1,0:T(8,128)S(1)} %get-tuple-element.30), channel_id=1, source_target_pairs={{0,4},{4,0},{8,12},{12,8},{1,5},{5,1},{9,13},{13,9},{2,6},{6,2},{1... | collective-permute-start | bytes 786440 | tf_op jit(solution)/shard_map/ppermute | solution.py:25
  42.0 7.1 %collective-permute-start.13 = (bf16[224,1024]{1,0:T(8,128)(2,1)S(1)}, bf16[224,1024]{1,0:T(8,128)(2,1)S(1)}, u32[]{:S(2)}, u32[]{:S(2)}) collective-permute-start(bf16[224,1024]{1,0:T(8,128)(2,1)S(1)} %copy-done.3), channel_id=1, source_target_pairs={{0,4},{4,0},{8,12},{12,8},{1,5},{5,1},{9,13},{13,9},{2,6},{6,2},{1... | collective-permute-start | bytes 1376264 | tf_op jit(solution)/shard_map/ppermute | solution.py:25
  42.5 13.6 %collective-permute-start.14 = (bf16[224,1024]{1,0:T(8,128)(2,1)}, bf16[224,1024]{1,0:T(8,128)(2,1)S(1)}, u32[]{:S(2)}, u32[]{:S(2)}) collective-permute-start(bf16[224,1024]{1,0:T(8,128)(2,1)} %get-tuple-element.26.refs_5_), channel_id=1, source_target_pairs={{0,8},{4,12},{8,0},{12,4},{1,9},{5,13},{9,1},{13,5},{2,10},{6,14},... | collective-permute-start | bytes 1376264 | tf_op jit(solution)/shard_map/ppermute | solution.py:25
  43.9 20.9 %collective-permute-start.15 = (bf16[224,1024]{1,0:T(8,128)(2,1)S(1)}, bf16[224,1024]{1,0:T(8,128)(2,1)S(1)}, u32[]{:S(2)}, u32[]{:S(2)}) collective-permute-start(bf16[224,1024]{1,0:T(8,128)(2,1)S(1)} %copy-done.1), channel_id=1, source_target_pairs={{0,12},{4,8},{8,4},{12,0},{1,13},{5,9},{9,5},{13,1},{2,14},{6,10},... | collective-permute-start | bytes 1376264 | tf_op jit(solution)/shard_map/ppermute | solution.py:25
  43.9 1.8 %collective-permute-start.10 = (bf16[224,512]{1,0:T(8,128)(2,1)S(1)}, bf16[224,512]{1,0:T(8,128)(2,1)S(1)}, u32[]{:S(2)}, u32[]{:S(2)}) collective-permute-start(bf16[224,512]{1,0:T(8,128)(2,1)S(1)} %collective-permute-done.6.refs_4_), channel_id=1, source_target_pairs={{0,4},{4,0},{8,12},{12,8},{1,5},{5,1},{9,13},{13,9},{2,6},{6,2},{1... | collective-permute-start | bytes 688136 | tf_op jit(solution)/shard_map/ppermute | solution.py:25
  45.7 26.1 %collective-permute-start.2 = (f32[4,64,256]{2,1,0:T(8,128)S(1)}, f32[4,64,256]{2,1,0:T(8,128)S(1)}, u32[]{:S(2)}, u32[]{:S(2)}) collective-permute-start(f32[4,64,256]{2,1,0:T(8,128)S(1)} %add.13), channel_id=1, source_target_pairs={{0,8},{4,12},{8,0},{12,4},{1,9},{5,13},{9,1},{13,5},{2,10},{6,14},... | collective-permute-start | bytes 786440 | tf_op jit(solution)/shard_map/ppermute | solution.py:25
  69.5 7.9 %collective-permute-start.16 = (bf16[224,512]{1,0:T(8,128)(2,1)S(1)}, bf16[224,512]{1,0:T(8,128)(2,1)S(1)}, u32[]{:S(2)}, u32[]{:S(2)}) collective-permute-start(bf16[224,512]{1,0:T(8,128)(2,1)S(1)} %get-tuple-element.32), channel_id=1, source_target_pairs={{0,4},{4,0},{8,12},{12,8},{1,5},{5,1},{9,13},{13,9},{2,6},{6,2},{1... | collective-permute-start | bytes 688136 | tf_op jit(solution)/shard_map/ppermute | solution.py:25
  70.4 8.5 %collective-permute-start.17 = (bf16[224,512]{1,0:T(8,128)(2,1)S(1)}, bf16[224,512]{1,0:T(8,128)(2,1)S(1)}, u32[]{:S(2)}, u32[]{:S(2)}) collective-permute-start(bf16[224,512]{1,0:T(8,128)(2,1)S(1)} %get-tuple-element.33), channel_id=1, source_target_pairs={{0,8},{4,12},{8,0},{12,4},{1,9},{5,13},{9,1},{13,5},{2,10},{6,14},... | collective-permute-start | bytes 688136 | tf_op jit(solution)/shard_map/ppermute | solution.py:25
  71.9 12.9 %collective-permute-start.3 = (f32[4,64,256]{2,1,0:T(8,128)S(1)}, f32[4,64,256]{2,1,0:T(8,128)S(1)}, u32[]{:S(2)}, u32[]{:S(2)}) collective-permute-start(f32[4,64,256]{2,1,0:T(8,128)S(1)} %add.14.refs_1_), channel_id=1, source_target_pairs={{0,4},{4,0},{8,12},{12,8},{1,5},{5,1},{9,13},{13,9},{2,6},{6,2},{1... | collective-permute-start | bytes 786440 | tf_op jit(solution)/shard_map/ppermute | solution.py:25
  76.6 14.3 %collective-permute-start.19 = (bf16[224,512]{1,0:T(8,128)(2,1)S(1)}, bf16[224,512]{1,0:T(8,128)(2,1)S(1)}, u32[]{:S(2)}, u32[]{:S(2)}) collective-permute-start(bf16[224,512]{1,0:T(8,128)(2,1)S(1)} %get-tuple-element.37), channel_id=1, source_target_pairs={{0,4},{4,0},{8,12},{12,8},{1,5},{5,1},{9,13},{13,9},{2,6},{6,2},{1... | collective-permute-start | bytes 688136 | tf_op jit(solution)/shard_map/ppermute | solution.py:25
  77.2 7.6 %collective-permute-start.18 = (bf16[224,512]{1,0:T(8,128)(2,1)S(1)}, bf16[224,512]{1,0:T(8,128)(2,1)S(1)}, u32[]{:S(2)}, u32[]{:S(2)}) collective-permute-start(bf16[224,512]{1,0:T(8,128)(2,1)S(1)} %get-tuple-element.34), channel_id=1, source_target_pairs={{0,12},{4,8},{8,4},{12,0},{1,13},{5,9},{9,5},{13,1},{2,14},{6,10},... | collective-permute-start | bytes 688136 | tf_op jit(solution)/shard_map/ppermute | solution.py:25
  77.4 13.5 %collective-permute-start.20 = (bf16[224,512]{1,0:T(8,128)(2,1)S(1)}, bf16[224,512]{1,0:T(8,128)(2,1)S(1)}, u32[]{:S(2)}, u32[]{:S(2)}) collective-permute-start(bf16[224,512]{1,0:T(8,128)(2,1)S(1)} %get-tuple-element.38), channel_id=1, source_target_pairs={{0,8},{4,12},{8,0},{12,4},{1,9},{5,13},{9,1},{13,5},{2,10},{6,14},... | collective-permute-start | bytes 688136 | tf_op jit(solution)/shard_map/ppermute | solution.py:25
  78.9 15.8 %collective-permute-start.21 = (bf16[224,512]{1,0:T(8,128)(2,1)S(1)}, bf16[224,512]{1,0:T(8,128)(2,1)S(1)}, u32[]{:S(2)}, u32[]{:S(2)}) collective-permute-start(bf16[224,512]{1,0:T(8,128)(2,1)S(1)} %get-tuple-element.39), channel_id=1, source_target_pairs={{0,12},{4,8},{8,4},{12,0},{1,13},{5,9},{9,5},{13,1},{2,14},{6,10},... | collective-permute-start | bytes 688136 | tf_op jit(solution)/shard_map/ppermute | solution.py:25

commit v4 on v3

--- a/solution.py
+++ b/solution.py
@@ -101,23 +101,24 @@
     lax.fori_loop(0, rows // GROUP, build, 0)
 
 
-def sums_kernel(count, info, top_ref, low_ref, *refs):
+def sums_kernel(count, own, info, matrix_ref, *refs):
     blocks = refs[:count]
-    chosen, measured, mine_ref, other_ref, target, sem = refs[count:]
-    half, rays = mine_ref.shape[:2]
+    chosen, measured, out_ref, target, sem = refs[count:]
+    half, rays = out_ref.shape[:2]
     block = blocks[0].shape[1]
     me, side = info[0], info[1]
-    fetch = pltpu.make_async_copy(measured.at[pl.ds(side * half, half)], target, sem)
-    fetch.start()
-    for out_ref, ref, start in ((other_ref, low_ref, half), (mine_ref, top_ref, 0)):
-        sums = jnp.zeros((ref.shape[0], blocks[0].shape[0]), jnp.float32)
-        for j in range(count):
-            sums += dot(ref[:, aligned(me ^ j, block)], blocks[j][...], NT)
-        sums = sums.astype(jnp.bfloat16)
-        for i in range(half):
-            out_ref[i] = dot(sums[i * rays:(i + 1) * rays], chosen[start + i], NN)
-    fetch.wait()
-    mine_ref[...] = mine_ref[...] - (2.0 / count) * target[...]
+    if own:
+        fetch = pltpu.make_async_copy(measured.at[pl.ds(side * half, half)], target, sem)
+        fetch.start()
+    sums = jnp.zeros((matrix_ref.shape[0], blocks[0].shape[0]), jnp.float32)
+    for j in range(count):
+        sums += dot(matrix_ref[:, aligned(me ^ j, block)], blocks[j][...], NT)
+    sums = sums.astype(jnp.bfloat16)
+    for i in range(half):
+        out_ref[i] = dot(sums[i * rays:(i + 1) * rays], chosen[i + (0 if own else half)], NN)
+    if own:
+        fetch.wait()
+        out_ref[...] = out_ref[...] - (2.0 / count) * target[...]
 
 
 def gather_kernel(count, pieces, info, own, near, *refs):
@@ -200,15 +201,15 @@
         w.wait()
 
 
-def finish_kernel(count, cut, info, later, *refs):
-    grads = refs[:count]
-    _, updated, buf, sems = refs[count:]
+def finish_kernel(count, cut, masks, info, later, *refs):
+    grads = refs[:len(masks)]
+    _, updated, buf, sems = refs[len(masks):]
     block = updated.shape[1] // count
     writes = []
-    for j in range(count):
-        buf[j] = later[j] - 0.5 * grads[j][...].astype(jnp.float32)
+    for n, j in enumerate(masks):
+        buf[n] = later[j] - 0.5 * grads[n][...].astype(jnp.float32)
         at = columns(info[0] ^ j, block, cut)
-        writes.append(pltpu.make_async_copy(buf.at[j], updated.at[:, at], sems.at[j]))
+        writes.append(pltpu.make_async_copy(buf.at[n], updated.at[:, at], sems.at[n]))
         writes[-1].start()
     for w in writes:
         w.wait()
@@ -301,13 +302,17 @@
         fetched[m ^ 1] = [swap(v, "coef", 1) for v in fetched[m]]
     far = [v for m in range(2, count) for v in fetched[m]]
 
-    mine, other = kernel(
-        lambda *refs: sums_kernel(count, *refs),
-        [SMEM] + [VMEM] * (count + 3) + [HBM],
-        [VMEM, VMEM],
-        [shape((half, rays, channels), f32)] * 2,
-        [pltpu.VMEM((half, rays, channels), f32), pltpu.SemaphoreType.DMA(())],
-    )(info, top, low, *blocks, chosen, measured_far)
+    def ray_sums(own, matrix):
+        return kernel(
+            lambda *refs: sums_kernel(count, own, *refs),
+            [SMEM] + [VMEM] * (count + 2) + [HBM],
+            VMEM,
+            shape((half, rays, channels), f32),
+            [pltpu.VMEM((half, rays, channels), f32), pltpu.SemaphoreType.DMA(())],
+        )(info, matrix, *blocks, chosen, measured_far)
+
+    mine = ray_sums(True, top)
+    other = ray_sums(False, low)
     total = mine + swap(other, "coef", 1)
     mask = 2
     while mask < count:
@@ -335,7 +340,10 @@
                 pltpu.VMEM((count * coef_local, chunk), f32),
             ],
         )(waves, *[received[m] for m in range(count)])
-        returned.append([outs[0]] + [swap(outs[m], "coef", m) for m in range(1, count)])
+        back = [outs[0]]
+        for m in range(1, count):
+            back.append(swap(outs[m], "coef", m))
+        returned.append(back)
 
     resid_other = swap(total, "coef", 1)
     updated, residual, *later = kernel(
@@ -352,15 +360,20 @@
             pltpu.SemaphoreType.DMA((count,)),
         ],
     )(info, total, resid_other, chosen, top, low, coef_far, *returned[0])
+    remote = list(range(2, count))
+    middle = len(remote) // 2
     for t, cut in list(enumerate(cuts))[1:]:
-        updated = kernel(
-            lambda *refs: finish_kernel(count, cut, *refs),
-            [SMEM] + [VMEM] * (count + 1) + [HBM],
-            HBM,
-            shape((coef_local, cols), f32),
-            [pltpu.VMEM((count, coef_local, cut[1]), f32), pltpu.SemaphoreType.DMA((count,))],
-            aliases={count + 2: 0},
-        )(info, later[t - 1], *returned[t], updated)
+        for masks in ([0, 1], remote[:middle], remote[middle:]):
+            if not masks:
+                continue
+            updated = kernel(
+                lambda *refs: finish_kernel(count, cut, masks, *refs),
+                [SMEM] + [VMEM] * (len(masks) + 1) + [HBM],
+                HBM,
+                shape((coef_local, cols), f32),
+                [pltpu.VMEM((len(masks), coef_local, cut[1]), f32), pltpu.SemaphoreType.DMA((len(masks),))],
+                aliases={len(masks) + 2: 0},
+            )(info, later[t - 1], *[returned[t][m] for m in masks], updated)
     return (updated, residual[:, None])
 
 

time: 96.8 us -> 89.2 us (0.921)
  waiting for transfers between devices: 40.6 us -> 32.7 us
  local copies, waits for them, and re-layouts: 4.53 us -> 0.95 us
  Pallas kernels: 32.5 us -> 36 us
    ppermute x19, waiting for transfers between devices: 32.5 us -> 24.5 us  [swap(): return lax.ppermute(value, axis, [(i, i ^ mask) for i in range(count)])]
    unnamed x8 -> x0, local copies, waits for them, and re-layouts: 3.58 us -> none
    pallas_call x2 -> x5, Pallas kernels: 6.24 us -> 9.47 us  [the longest x2 5.22 us: ray_sums(): kernel(lambda *refs: sums_kernel(count, own, *refs), [SMEM] + [VMEM] * (c...]
  transfers between devices with their start and end apart: 22 -> 22, of which waited for: 8 -> 6; matrix products, arithmetic and copies ran while one was open for 1% -> 1% of each run, Pallas kernels for 22% -> 29%
where the time goes in v4:
time: 89.2 us; the launch traced here: 88.4 us
  Pallas kernels  36 us (40%)
  waiting for transfers between devices  32.7 us (37%)
  starting transfers between devices  17.9 us (20%)
  local copies, waits for them, and re-layouts  0.95 us (1%)
    ppermute x19, waiting for transfers between devices, swap(): return lax.ppermute(value, axis, [(i, i ^ mask) for i in range(count)])  24.5 us
    ppermute x19, starting transfers between devices, swap(): return lax.ppermute(value, axis, [(i, i ^ mask) for i in range(count)])  13 us
    pallas_call x2, Pallas kernels, step_of(): kernel(lambda *refs: penalty_kernel(count, pieces, cut, *refs), [VMEM] *...  9.21 us
    ppermute x3, waiting for transfers between devices, step_of(): fetched[m].append(lax.ppermute(fetched[m][0], ('groups', 'slab'), pairs))  8.16 us
    pallas_call x1, Pallas kernels, step_of(): kernel(lambda *refs: data_kernel(count, cuts, *refs), [SMEM] + [VMEM] * 5...  6.09 us
    pallas_call x2, Pallas kernels, ray_sums(): kernel(lambda *refs: sums_kernel(count, own, *refs), [SMEM] + [VMEM] * (c...  5.22 us
    pallas_call x1, Pallas kernels, step_of(): kernel(build_kernel, [VMEM, VMEM], VMEM, shape((rows // 2, cols), bf16),...  5.17 us
    ppermute x3, starting transfers between devices, step_of(): fetched[m].append(lax.ppermute(fetched[m][0], ('groups', 'slab'), pairs))  4.84 us
  transfers between devices with their start and end apart: 22, of which 6 were waited for; matrix products, arithmetic and copies ran while one was open for 1% of the time, Pallas kernels for 29%

profile of v4, /device:TPU:0, one launch (start us, length us, event | category | flops | bytes accessed | tf_op | source)
XLA Modules:
  0.0 88.4 jit_solution(7793783791274942975)
XLA Ops:
  0.6 0.1 pad_add_fusion.refs_0_
  0.7 4.2 %shard_map.86 = (bf16[224,1024]{1,0:T(8,128)(2,1)S(1)}, bf16[224,1024]{1,0:T(8,128)(2,1)}, bf16[224,1024]{1,0:T(8,128)(2,1)}, bf16[224,1024]{1,0:T(8,128)(2,1)},...) custom-call(s32[3]{0:T(128)S(1)} %pad_add_fusion.refs_0_, s32[8]{0:T(128)} %refs_1_.2, ...), custom_call_target="tpu_custom_call" | custom-call | tf_op jit(solution)/shard_map/pallas_call | solution.py:269
  4.9 5.2 %shard_map.87.refs_1_.refs_4_ = bf16[256,4096]{1,0:T(8,128)(2,1)S(1)} custom-call(s32[256,128]{1,0:T(8,128)S(1)} %get-tuple-element.20.vox_ref, s32[256,128]{1,0:T(8,128)S(1)} %get-tuple-element.21.wgt_ref), custom_call_target="tpu_custom_call" | custom-call | tf_op jit(solution)/shard_map/pallas_call | solution.py:293
  10.1 0.6 collective-permute-start
  10.7 1.0 %constant_dynamic-slice_fusion = bf16[224,512]{1,0:T(8,128)(2,1)S(1)} fusion(bf16[224,2048]{1,0:T(8,128)(2,1)} %refs_1_.3, s32[]{:T(128)S(6)} %select_n.3), kind=kLoop, calls=%fused_computation.1 | loop fusion | bytes 458756 | tf_op jit(solution)/shard_map/dynamic_slice | solution.py:267
  11.6 2.6 %collective-permute-start.5 = (bf16[224,512]{1,0:T(8,128)(2,1)S(1)}, bf16[224,512]{1,0:T(8,128)(2,1)S(1)}, u32[]{:S(2)}, u32[]{:S(2)}) collective-permute-start(bf16[224,512]{1,0:T(8,128)(2,1)S(1)} %constant_dynamic-slice_fusion), channel_id=1, source_target_pairs={{0,8},{4,12},{8,0},{12,4},{1,9},{5,13},{9,1},{13,5},{2,10},{6,14},... | collective-permute-start | bytes 688136 | tf_op jit(solution)/shard_map/ppermute | solution.py:25
  14.2 6.3 %collective-permute-done.5.refs_3_ = bf16[224,512]{1,0:T(8,128)(2,1)S(1)} collective-permute-done((bf16[224,512]{1,0:T(8,128)(2,1)S(1)}, bf16[224,512]{1,0:T(8,128)(2,1)S(1)}, u32[]{:S(2)}, u32[]{:S(2)}) %collective-permute-start.5) | collective-permute-done | bytes 229408 | tf_op jit(solution)/shard_map/ppermute | solution.py:25
  20.4 2.8 %collective-permute-start.8 = (bf16[224,512]{1,0:T(8,128)(2,1)S(1)}, bf16[224,512]{1,0:T(8,128)(2,1)S(1)}, u32[]{:S(2)}, u32[]{:S(2)}) collective-permute-start(bf16[224,512]{1,0:T(8,128)(2,1)S(1)} %collective-permute-done.5.refs_3_), channel_id=1, source_target_pairs={{0,17},{1,16},{2,19},{3,18},{16,1},{17,0},{18,3},{19,2},{4,21},{5,... | collective-permute-start | bytes 688136 | tf_op jit(solution)/shard_map/ppermute | solution.py:291
  23.2 0.5 collective-permute-start.7
  23.7 0.2 collective-permute-start.9
  24.0 4.9 %collective-permute-done.8.refs_6_ = bf16[224,512]{1,0:T(8,128)(2,1)S(1)} collective-permute-done((bf16[224,512]{1,0:T(8,128)(2,1)S(1)}, bf16[224,512]{1,0:T(8,128)(2,1)S(1)}, u32[]{:S(2)}, u32[]{:S(2)}) %collective-permute-start.8) | collective-permute-done | bytes 229408 | tf_op jit(solution)/shard_map/ppermute | solution.py:291
  28.9 1.5 %collective-permute-start.6 = (bf16[224,512]{1,0:T(8,128)(2,1)S(1)}, bf16[224,512]{1,0:T(8,128)(2,1)S(1)}, u32[]{:S(2)}, u32[]{:S(2)}) collective-permute-start(bf16[224,512]{1,0:T(8,128)(2,1)S(1)} %collective-permute-done.5.refs_3_), channel_id=1, source_target_pairs={{0,1},{1,0},{2,3},{3,2},{16,17},{17,16},{18,19},{19,18},{4,5},{5,4... | collective-permute-start | bytes 688136 | tf_op jit(solution)/shard_map/ppermute | solution.py:291
  30.4 3.3 %collective-permute-done.7.refs_5_ = bf16[224,512]{1,0:T(8,128)(2,1)S(1)} collective-permute-done((bf16[224,512]{1,0:T(8,128)(2,1)S(1)}, bf16[224,512]{1,0:T(8,128)(2,1)S(1)}, u32[]{:S(2)}, u32[]{:S(2)}) %collective-permute-start.7) | collective-permute-done | bytes 229408 | tf_op jit(solution)/shard_map/ppermute | solution.py:291
  33.7 0.1 collective-permute-start.12
  33.7 0.0 collective-permute-done.refs_1_.refs_5_
  33.8 0.4 collective-permute-start.11
  34.2 2.9 %shard_map.89 = f32[4,64,256]{2,1,0:T(8,128)S(1)} custom-call(s32[3]{0:T(128)S(1)} %pad_add_fusion.refs_0_, bf16[256,4096]{1,0:T(8,128)(2,1)} %collective-permute-done.refs_1_.refs_5_, bf16[224,1024]{1,0:T(8,128)(2,1)S(1)} %get-tuple-element.22.refs_2_.refs_1_, bf16[224,1024]{1,0:T(8,128)(2,1)} %get-tuple-element.23.refs_3_, ...), custom_call_target="tpu_custom_call" | custom-call | tf_op jit(solution)/shard_map/pallas_call | solution.py:306
  37.1 0.0 collective-permute-done.9.refs_7_
  37.1 0.1 collective-permute-start.1
  37.3 0.0 collective-permute-done.6.refs_4_
  37.3 0.4 collective-permute-start.13
  37.7 1.5 %collective-permute-start.14 = (bf16[224,1024]{1,0:T(8,128)(2,1)}, bf16[224,1024]{1,0:T(8,128)(2,1)S(1)}, u32[]{:S(2)}, u32[]{:S(2)}) collective-permute-start(bf16[224,1024]{1,0:T(8,128)(2,1)} %get-tuple-element.24.refs_4_), channel_id=1, source_target_pairs={{0,8},{4,12},{8,0},{12,4},{1,9},{5,13},{9,1},{13,5},{2,10},{6,14},... | collective-permute-start | bytes 1376264 | tf_op jit(solution)/shard_map/ppermute | solution.py:25
  39.2 0.0 collective-permute-done.11.refs_9_
  39.2 0.0 collective-permute-start.15
  39.2 0.7 collective-permute-start.10
  39.8 2.3 %shard_map.88 = f32[4,64,256]{2,1,0:T(8,128)S(1)} custom-call(s32[3]{0:T(128)S(1)} %pad_add_fusion.refs_0_, bf16[256,4096]{1,0:T(8,128)(2,1)S(1)} %shard_map.87.refs_1_.refs_4_, bf16[224,1024]{1,0:T(8,128)(2,1)S(1)} %get-tuple-element.22.refs_2_.refs_1_, bf16[224,1024]{1,0:T(8,128)(2,1)} %get-tuple-element.23.refs_3_, ...), custom_call_target="tpu_custom_call" | custom-call | tf_op jit(solution)/shard_map/pallas_call | solution.py:306
  42.2 0.0 collective-permute-done.10.refs_8_
  42.2 1.5 %collective-permute-start.2 = (f32[4,64,256]{2,1,0:T(8,128)S(1)}, f32[4,64,256]{2,1,0:T(8,128)S(1)}, u32[]{:S(2)}, u32[]{:S(2)}) collective-permute-start(f32[4,64,256]{2,1,0:T(8,128)S(1)} %add.13), channel_id=1, source_target_pairs={{0,8},{4,12},{8,0},{12,4},{1,9},{5,13},{9,1},{13,5},{2,10},{6,14},... | collective-permute-start | bytes 786440 | tf_op jit(solution)/shard_map/ppermute | solution.py:25
  43.8 0.0 collective-permute-done.4.refs_2_
  43.8 1.9 %shard_map.90.refs_0_ = bf16[896,2048]{1,0:T(8,128)(2,1)S(1)} custom-call(s32[3]{0:T(128)S(1)} %pad_add_fusion.refs_0_, bf16[224,2048]{1,0:T(8,128)(2,1)} %refs_1_.3, bf16[224,2048]{1,0:T(8,128)(2,1)S(1)} %collective-permute-done.4.refs_2_, bf16[224,512]{1,0:T(8,128)(2,1)S(1)} %collective-permute-done.5.refs_3_, ...), custom_call_target="tpu_custom_call" | custom-call | tf_op jit(solution)/shard_map/pallas_call | solution.py:321
  45.6 0.0 collective-permute-done.13.refs_2_
  45.6 5.7 %collective-permute-done.14.refs_3_ = bf16[224,1024]{1,0:T(8,128)(2,1)S(1)} collective-permute-done((bf16[224,1024]{1,0:T(8,128)(2,1)}, bf16[224,1024]{1,0:T(8,128)(2,1)S(1)}, u32[]{:S(2)}, u32[]{:S(2)}) %collective-permute-start.14) | collective-permute-done | bytes 458784 | tf_op jit(solution)/shard_map/ppermute | solution.py:25
  51.3 8.9 %collective-permute-done.15.refs_4_ = bf16[224,1024]{1,0:T(8,128)(2,1)S(1)} collective-permute-done((bf16[224,1024]{1,0:T(8,128)(2,1)}, bf16[224,1024]{1,0:T(8,128)(2,1)S(1)}, u32[]{:S(2)}, u32[]{:S(2)}) %collective-permute-start.15) | collective-permute-done | bytes 458784 | tf_op jit(solution)/shard_map/ppermute | solution.py:25
  60.2 4.6 %shard_map.91 = (bf16[224,512]{1,0:T(8,128)(2,1)S(1)}, bf16[224,512]{1,0:T(8,128)(2,1)S(1)}, bf16[224,512]{1,0:T(8,128)(2,1)S(1)}, bf16[224,512]{1,0:T(8,128)(2,1)S(1)}) custom-call(bf16[896,2048]{1,0:T(8,128)(2,1)S(1)} %shard_map.90.refs_0_, bf16[224,1024]{1,0:T(8,128)(2,1)S(1)} %get-tuple-element.22.refs_2_.refs_1_, ...), custom_call_target="tpu_custom_call" | custom-call | tf_op jit(solution)/shard_map/pallas_call | solution.py:332
  64.8 0.8 collective-permute-start.16
  65.6 1.5 %collective-permute-start.17 = (bf16[224,512]{1,0:T(8,128)(2,1)S(1)}, bf16[224,512]{1,0:T(8,128)(2,1)S(1)}, u32[]{:S(2)}, u32[]{:S(2)}) collective-permute-start(bf16[224,512]{1,0:T(8,128)(2,1)S(1)} %get-tuple-element.29), channel_id=1, source_target_pairs={{0,8},{4,12},{8,0},{12,4},{1,9},{5,13},{9,1},{13,5},{2,10},{6,14},... | collective-permute-start | bytes 688136 | tf_op jit(solution)/shard_map/ppermute | solution.py:25
  67.1 0.1 collective-permute-start.3
  67.2 0.7 collective-permute-start.18
  67.9 4.6 %shard_map.93 = (bf16[224,512]{1,0:T(8,128)(2,1)S(1)}, bf16[224,512]{1,0:T(8,128)(2,1)S(1)}, bf16[224,512]{1,0:T(8,128)(2,1)S(1)}, bf16[224,512]{1,0:T(8,128)(2,1)S(1)}) custom-call(bf16[896,2048]{1,0:T(8,128)(2,1)S(1)} %shard_map.90.refs_0_, bf16[224,1024]{1,0:T(8,128)(2,1)S(1)} %get-tuple-element.22.refs_2_.refs_1_, ...), custom_call_target="tpu_custom_call" | custom-call | tf_op jit(solution)/shard_map/pallas_call | solution.py:332
  72.5 0.1 collective-permute-start.21
  72.6 1.5 %collective-permute-start.20 = (bf16[224,512]{1,0:T(8,128)(2,1)S(1)}, bf16[224,512]{1,0:T(8,128)(2,1)S(1)}, u32[]{:S(2)}, u32[]{:S(2)}) collective-permute-start(bf16[224,512]{1,0:T(8,128)(2,1)S(1)} %get-tuple-element.33), channel_id=1, source_target_pairs={{0,8},{4,12},{8,0},{12,4},{1,9},{5,13},{9,1},{13,5},{2,10},{6,14},... | collective-permute-start | bytes 688136 | tf_op jit(solution)/shard_map/ppermute | solution.py:25
  74.1 0.3 collective-permute-start.19
  74.4 3.6 %collective-permute-done.18.refs_10_ = bf16[224,512]{1,0:T(8,128)(2,1)S(1)} collective-permute-done((bf16[224,512]{1,0:T(8,128)(2,1)S(1)}, bf16[224,512]{1,0:T(8,128)(2,1)S(1)}, u32[]{:S(2)}, u32[]{:S(2)}) %collective-permute-start.18) | collective-permute-done | bytes 229408 | tf_op jit(solution)/shard_map/ppermute | solution.py:25
  78.0 6.1 %shard_map.92 = (f32[224,4096]{1,0:T(8,128)}, f32[8,64,64]{2,1,0:T(8,128)}, f32[4,224,512]{2,1,0:T(8,128)S(1)}) custom-call(s32[3]{0:T(128)S(1)} %pad_add_fusion.refs_0_, f32[4,64,256]{2,1,0:T(8,128)S(1)} %add.14.refs_1_, f32[4,64,256]{2,1,0:T(8,128)S(1)} %collective-permute-done.3.refs_2_, bf16[8,224,256]{2,1,0:T(8,128)(2,1)S(1)} %get-tuple-element.26.refs_6_.refs_3_, ...), custom_call_target="tpu_custom_call" | custom-call | tf_op jit(solution)/shard_map/pallas_call | solution.py:349
  84.1 1.5 %shard_map.94.refs_3_ = f32[224,4096]{1,0:T(8,128)} custom-call(s32[3]{0:T(128)S(1)} %pad_add_fusion.refs_0_, f32[4,224,512]{2,1,0:T(8,128)S(1)} %get-tuple-element.31.refs_1_, bf16[224,512]{1,0:T(8,128)(2,1)S(1)} %get-tuple-element.34.refs_2_, bf16[224,512]{1,0:T(8,128)(2,1)S(1)} %collective-permute-done.21.refs_3_, ...), custom_call_target="tpu_custom_call", output_to_operand_aliasing={{}: (4, {})} | custom-call | tf_op jit(solution)/shard_map/pallas_call | solution.py:369
  85.7 1.4 %shard_map.95.refs_3_ = f32[224,4096]{1,0:T(8,128)} custom-call(s32[3]{0:T(128)S(1)} %pad_add_fusion.refs_0_, f32[4,224,512]{2,1,0:T(8,128)S(1)} %get-tuple-element.31.refs_1_, bf16[224,512]{1,0:T(8,128)(2,1)S(1)} %collective-permute-done.20.refs_2_, f32[224,4096]{1,0:T(8,128)} %shard_map.94.refs_3_), custom_call_target="tpu_custom_call", output_to_operand_aliasing={{}: (3, {})} | custom-call | tf_op jit(solution)/shard_map/pallas_call | solution.py:369
  87.0 0.0 collective-permute-done.19.refs_2_
  87.1 1.4 %shard_map.96 = f32[224,4096]{1,0:T(8,128)} custom-call(s32[3]{0:T(128)S(1)} %pad_add_fusion.refs_0_, f32[4,224,512]{2,1,0:T(8,128)S(1)} %get-tuple-element.31.refs_1_, bf16[224,512]{1,0:T(8,128)(2,1)S(1)} %collective-permute-done.19.refs_2_, f32[224,4096]{1,0:T(8,128)} %shard_map.95.refs_3_), custom_call_target="tpu_custom_call", output_to_operand_aliasing={{}: (3, {})} | custom-call | tf_op jit(solution)/shard_map/pallas_call | solution.py:369
  (11 shorter events, 0.1 us)
Async XLA Ops:
  10.1 23.6 %collective-permute-start = (bf16[256,4096]{1,0:T(8,128)(2,1)S(1)}, bf16[256,4096]{1,0:T(8,128)(2,1)}, u32[]{:S(2)}, u32[]{:S(2)}) collective-permute-start(bf16[256,4096]{1,0:T(8,128)(2,1)S(1)} %shard_map.87.refs_1_.refs_4_), channel_id=1, source_target_pairs={{0,4},{4,0},{8,12},{12,8},{1,5},{5,1},{9,13},{13,9},{2,6},{6,2},{1... | collective-permute-start | bytes 6291464 | tf_op jit(solution)/shard_map/ppermute | solution.py:25
  11.6 8.8 %collective-permute-start.5 = (bf16[224,512]{1,0:T(8,128)(2,1)S(1)}, bf16[224,512]{1,0:T(8,128)(2,1)S(1)}, u32[]{:S(2)}, u32[]{:S(2)}) collective-permute-start(bf16[224,512]{1,0:T(8,128)(2,1)S(1)} %constant_dynamic-slice_fusion), channel_id=1, source_target_pairs={{0,8},{4,12},{8,0},{12,4},{1,9},{5,13},{9,1},{13,5},{2,10},{6,14},... | collective-permute-start | bytes 688136 | tf_op jit(solution)/shard_map/ppermute | solution.py:25
  20.4 8.4 %collective-permute-start.8 = (bf16[224,512]{1,0:T(8,128)(2,1)S(1)}, bf16[224,512]{1,0:T(8,128)(2,1)S(1)}, u32[]{:S(2)}, u32[]{:S(2)}) collective-permute-start(bf16[224,512]{1,0:T(8,128)(2,1)S(1)} %collective-permute-done.5.refs_3_), channel_id=1, source_target_pairs={{0,17},{1,16},{2,19},{3,18},{16,1},{17,0},{18,3},{19,2},{4,21},{5,... | collective-permute-start | bytes 688136 | tf_op jit(solution)/shard_map/ppermute | solution.py:291
  23.2 20.5 %collective-permute-start.4 = (bf16[224,2048]{1,0:T(8,128)(2,1)}, bf16[224,2048]{1,0:T(8,128)(2,1)S(1)}, u32[]{:S(2)}, u32[]{:S(2)}) collective-permute-start(bf16[224,2048]{1,0:T(8,128)(2,1)} %refs_1_.3), channel_id=1, source_target_pairs={{0,4},{4,0},{8,12},{12,8},{1,5},{5,1},{9,13},{13,9},{2,6},{6,2},{1... | collective-permute-start | bytes 2752520 | tf_op jit(solution)/shard_map/ppermute | solution.py:25
  23.2 10.4 %collective-permute-start.7 = (bf16[224,512]{1,0:T(8,128)(2,1)S(1)}, bf16[224,512]{1,0:T(8,128)(2,1)S(1)}, u32[]{:S(2)}, u32[]{:S(2)}) collective-permute-start(bf16[224,512]{1,0:T(8,128)(2,1)S(1)} %collective-permute-done.5.refs_3_), channel_id=1, source_target_pairs={{0,16},{1,17},{2,18},{3,19},{16,0},{17,1},{18,2},{19,3},{4,20},{5,... | collective-permute-start | bytes 688136 | tf_op jit(solution)/shard_map/ppermute | solution.py:291
  23.7 13.4 %collective-permute-start.9 = (bf16[224,512]{1,0:T(8,128)(2,1)S(1)}, bf16[224,512]{1,0:T(8,128)(2,1)S(1)}, u32[]{:S(2)}, u32[]{:S(2)}) collective-permute-start(bf16[224,512]{1,0:T(8,128)(2,1)S(1)} %collective-permute-done.5.refs_3_), channel_id=1, source_target_pairs={{0,4},{4,0},{8,12},{12,8},{1,5},{5,1},{9,13},{13,9},{2,6},{6,2},{1... | collective-permute-start | bytes 688136 | tf_op jit(solution)/shard_map/ppermute | solution.py:25
  28.9 8.4 %collective-permute-start.6 = (bf16[224,512]{1,0:T(8,128)(2,1)S(1)}, bf16[224,512]{1,0:T(8,128)(2,1)S(1)}, u32[]{:S(2)}, u32[]{:S(2)}) collective-permute-start(bf16[224,512]{1,0:T(8,128)(2,1)S(1)} %collective-permute-done.5.refs_3_), channel_id=1, source_target_pairs={{0,1},{1,0},{2,3},{3,2},{16,17},{17,16},{18,19},{19,18},{4,5},{5,4... | collective-permute-start | bytes 688136 | tf_op jit(solution)/shard_map/ppermute | solution.py:291
  33.7 4.0 %collective-permute-start.12 = (bf16[224,512]{1,0:T(8,128)(2,1)S(1)}, bf16[224,512]{1,0:T(8,128)(2,1)S(1)}, u32[]{:S(2)}, u32[]{:S(2)}) collective-permute-start(bf16[224,512]{1,0:T(8,128)(2,1)S(1)} %collective-permute-done.8.refs_6_), channel_id=1, source_target_pairs={{0,4},{4,0},{8,12},{12,8},{1,5},{5,1},{9,13},{13,9},{2,6},{6,2},{1... | collective-permute-start | bytes 688136 | tf_op jit(solution)/shard_map/ppermute | solution.py:25
  33.8 5.4 %collective-permute-start.11 = (bf16[224,512]{1,0:T(8,128)(2,1)S(1)}, bf16[224,512]{1,0:T(8,128)(2,1)S(1)}, u32[]{:S(2)}, u32[]{:S(2)}) collective-permute-start(bf16[224,512]{1,0:T(8,128)(2,1)S(1)} %collective-permute-done.7.refs_5_), channel_id=1, source_target_pairs={{0,4},{4,0},{8,12},{12,8},{1,5},{5,1},{9,13},{13,9},{2,6},{6,2},{1... | collective-permute-start | bytes 688136 | tf_op jit(solution)/shard_map/ppermute | solution.py:25
  37.1 2.1 %collective-permute-start.1 = (f32[4,64,256]{2,1,0:T(8,128)S(1)}, f32[4,64,256]{2,1,0:T(8,128)S(1)}, u32[]{:S(2)}, u32[]{:S(2)}) collective-permute-start(f32[4,64,256]{2,1,0:T(8,128)S(1)} %shard_map.89), channel_id=1, source_target_pairs={{0,4},{4,0},{8,12},{12,8},{1,5},{5,1},{9,13},{13,9},{2,6},{6,2},{1... | collective-permute-start | bytes 786440 | tf_op jit(solution)/shard_map/ppermute | solution.py:25
  37.3 8.4 %collective-permute-start.13 = (bf16[224,1024]{1,0:T(8,128)(2,1)}, bf16[224,1024]{1,0:T(8,128)(2,1)S(1)}, u32[]{:S(2)}, u32[]{:S(2)}) collective-permute-start(bf16[224,1024]{1,0:T(8,128)(2,1)} %get-tuple-element.23.refs_3_), channel_id=1, source_target_pairs={{0,4},{4,0},{8,12},{12,8},{1,5},{5,1},{9,13},{13,9},{2,6},{6,2},{1... | collective-permute-start | bytes 1376264 | tf_op jit(solution)/shard_map/ppermute | solution.py:25
  37.7 13.6 %collective-permute-start.14 = (bf16[224,1024]{1,0:T(8,128)(2,1)}, bf16[224,1024]{1,0:T(8,128)(2,1)S(1)}, u32[]{:S(2)}, u32[]{:S(2)}) collective-permute-start(bf16[224,1024]{1,0:T(8,128)(2,1)} %get-tuple-element.24.refs_4_), channel_id=1, source_target_pairs={{0,8},{4,12},{8,0},{12,4},{1,9},{5,13},{9,1},{13,5},{2,10},{6,14},... | collective-permute-start | bytes 1376264 | tf_op jit(solution)/shard_map/ppermute | solution.py:25
  39.2 21.1 %collective-permute-start.15 = (bf16[224,1024]{1,0:T(8,128)(2,1)}, bf16[224,1024]{1,0:T(8,128)(2,1)S(1)}, u32[]{:S(2)}, u32[]{:S(2)}) collective-permute-start(bf16[224,1024]{1,0:T(8,128)(2,1)} %get-tuple-element.25.refs_5_), channel_id=1, source_target_pairs={{0,12},{4,8},{8,4},{12,0},{1,13},{5,9},{9,5},{13,1},{2,14},{6,10},... | collective-permute-start | bytes 1376264 | tf_op jit(solution)/shard_map/ppermute | solution.py:25
  39.2 3.0 %collective-permute-start.10 = (bf16[224,512]{1,0:T(8,128)(2,1)S(1)}, bf16[224,512]{1,0:T(8,128)(2,1)S(1)}, u32[]{:S(2)}, u32[]{:S(2)}) collective-permute-start(bf16[224,512]{1,0:T(8,128)(2,1)S(1)} %collective-permute-done.6.refs_4_), channel_id=1, source_target_pairs={{0,4},{4,0},{8,12},{12,8},{1,5},{5,1},{9,13},{13,9},{2,6},{6,2},{1... | collective-permute-start | bytes 688136 | tf_op jit(solution)/shard_map/ppermute | solution.py:25
  42.2 24.9 %collective-permute-start.2 = (f32[4,64,256]{2,1,0:T(8,128)S(1)}, f32[4,64,256]{2,1,0:T(8,128)S(1)}, u32[]{:S(2)}, u32[]{:S(2)}) collective-permute-start(f32[4,64,256]{2,1,0:T(8,128)S(1)} %add.13), channel_id=1, source_target_pairs={{0,8},{4,12},{8,0},{12,4},{1,9},{5,13},{9,1},{13,5},{2,10},{6,14},... | collective-permute-start | bytes 786440 | tf_op jit(solution)/shard_map/ppermute | solution.py:25
  64.8 7.8 %collective-permute-start.16 = (bf16[224,512]{1,0:T(8,128)(2,1)S(1)}, bf16[224,512]{1,0:T(8,128)(2,1)S(1)}, u32[]{:S(2)}, u32[]{:S(2)}) collective-permute-start(bf16[224,512]{1,0:T(8,128)(2,1)S(1)} %get-tuple-element.28), channel_id=1, source_target_pairs={{0,4},{4,0},{8,12},{12,8},{1,5},{5,1},{9,13},{13,9},{2,6},{6,2},{1... | collective-permute-start | bytes 688136 | tf_op jit(solution)/shard_map/ppermute | solution.py:25
  65.6 8.5 %collective-permute-start.17 = (bf16[224,512]{1,0:T(8,128)(2,1)S(1)}, bf16[224,512]{1,0:T(8,128)(2,1)S(1)}, u32[]{:S(2)}, u32[]{:S(2)}) collective-permute-start(bf16[224,512]{1,0:T(8,128)(2,1)S(1)} %get-tuple-element.29), channel_id=1, source_target_pairs={{0,8},{4,12},{8,0},{12,4},{1,9},{5,13},{9,1},{13,5},{2,10},{6,14},... | collective-permute-start | bytes 688136 | tf_op jit(solution)/shard_map/ppermute | solution.py:25
  67.1 10.9 %collective-permute-start.3 = (f32[4,64,256]{2,1,0:T(8,128)S(1)}, f32[4,64,256]{2,1,0:T(8,128)S(1)}, u32[]{:S(2)}, u32[]{:S(2)}) collective-permute-start(f32[4,64,256]{2,1,0:T(8,128)S(1)} %add.14.refs_1_), channel_id=1, source_target_pairs={{0,4},{4,0},{8,12},{12,8},{1,5},{5,1},{9,13},{13,9},{2,6},{6,2},{1... | collective-permute-start | bytes 786440 | tf_op jit(solution)/shard_map/ppermute | solution.py:25
  67.2 10.8 %collective-permute-start.18 = (bf16[224,512]{1,0:T(8,128)(2,1)S(1)}, bf16[224,512]{1,0:T(8,128)(2,1)S(1)}, u32[]{:S(2)}, u32[]{:S(2)}) collective-permute-start(bf16[224,512]{1,0:T(8,128)(2,1)S(1)} %get-tuple-element.30), channel_id=1, source_target_pairs={{0,12},{4,8},{8,4},{12,0},{1,13},{5,9},{9,5},{13,1},{2,14},{6,10},... | collective-permute-start | bytes 688136 | tf_op jit(solution)/shard_map/ppermute | solution.py:25
  72.5 11.6 %collective-permute-start.21 = (bf16[224,512]{1,0:T(8,128)(2,1)S(1)}, bf16[224,512]{1,0:T(8,128)(2,1)S(1)}, u32[]{:S(2)}, u32[]{:S(2)}) collective-permute-start(bf16[224,512]{1,0:T(8,128)(2,1)S(1)} %get-tuple-element.35), channel_id=1, source_target_pairs={{0,4},{4,0},{8,12},{12,8},{1,5},{5,1},{9,13},{13,9},{2,6},{6,2},{1... | collective-permute-start | bytes 688136 | tf_op jit(solution)/shard_map/ppermute | solution.py:25
  72.6 13.0 %collective-permute-start.20 = (bf16[224,512]{1,0:T(8,128)(2,1)S(1)}, bf16[224,512]{1,0:T(8,128)(2,1)S(1)}, u32[]{:S(2)}, u32[]{:S(2)}) collective-permute-start(bf16[224,512]{1,0:T(8,128)(2,1)S(1)} %get-tuple-element.33), channel_id=1, source_target_pairs={{0,8},{4,12},{8,0},{12,4},{1,9},{5,13},{9,1},{13,5},{2,10},{6,14},... | collective-permute-start | bytes 688136 | tf_op jit(solution)/shard_map/ppermute | solution.py:25
  74.1 13.0 %collective-permute-start.19 = (bf16[224,512]{1,0:T(8,128)(2,1)S(1)}, bf16[224,512]{1,0:T(8,128)(2,1)S(1)}, u32[]{:S(2)}, u32[]{:S(2)}) collective-permute-start(bf16[224,512]{1,0:T(8,128)(2,1)S(1)} %get-tuple-element.32), channel_id=1, source_target_pairs={{0,12},{4,8},{8,4},{12,0},{1,13},{5,9},{9,5},{13,1},{2,14},{6,10},... | collective-permute-start | bytes 688136 | tf_op jit(solution)/shard_map/ppermute | solution.py:25

commit v5 on v4

v5 whole, which is shorter than its diff:
```python
import jax
import jax.numpy as jnp
from jax import lax
from jax.experimental import pallas as pl
from jax.experimental.pallas import tpu as pltpu
from jax.sharding import PartitionSpec as P


LANES = 128
QUARTERS = (2, 2)
GROUP = 32
NT = (((1,), (1,)), ((), ()))
NN = (((1,), (0,)), ((), ()))
VMEM = pl.BlockSpec(memory_space=pltpu.VMEM)
SMEM = pl.BlockSpec(memory_space=pltpu.SMEM)
HBM = pl.BlockSpec(memory_space=pltpu.HBM)


def dot(a, b, dims):
    return lax.dot_general(a, b, dims, preferred_element_type=jnp.float32)


def swap(value, axis, mask):
    count = lax.axis_size(axis)
    return lax.ppermute(value, axis, [(i, i ^ mask) for i in range(count)])


def aligned(index, width):
    return pl.ds(pl.multiple_of(index * width, width), width)


def cuts_of(block):
    if block % (4 * LANES):
        return [(0, block)]
    unit = block // 4
    starts = [unit * sum(QUARTERS[:t]) for t in range(len(QUARTERS))]
    return [(start, unit * size) for start, size in zip(starts, QUARTERS)]


def columns(index, block, cut):
    return pl.ds(pl.multiple_of(index * block + cut[0], LANES), cut[1])


def prepare_kernel(count, cuts, info, ids, coef, vox, wgt, table, *refs):
    parts = refs[:(count - 2) * len(cuts)]
    whole, vox_out, wgt_out, table_mine, table_other, stage, sems = refs[len(parts):]
    me, side = info[0], info[1]
    block = coef.shape[1] // count
    half_rows, half = vox_out.shape[0], table_mine.shape[0]
    order = list(range(2, count)) + [1, 0]
    copies = {}
    for m in order:
        copies[m] = pltpu.make_async_copy(coef.at[:, aligned(me ^ m, block)], stage.at[m], sems.at[m])
    rest = [
        pltpu.make_async_copy(vox.at[aligned(side, half_rows)], vox_out, sems.at[count]),
        pltpu.make_async_copy(wgt.at[aligned(side, half_rows)], wgt_out, sems.at[count + 1]),
    ]
    for n, (out, first) in enumerate(((table_other, (1 - side) * half), (table_mine, side * half))):
        for i in range(half):
            rest.append(pltpu.make_async_copy(table.at[ids[first + i]], out.at[i], sems.at[count + 2 + n * half + i]))
    for m in order:
        copies[m].start()
    for c in rest:
        c.start()
    for m in order:
        copies[m].wait()
        values = stage[m].astype(jnp.bfloat16)
        whole[:, aligned(me ^ m, block)] = values
        if m > 1:
            for t, cut in enumerate(cuts):
                parts[(m - 2) * len(cuts) + t][...] = values[:, cut[0]:cut[0] + cut[1]]
    for c in rest:
        c.wait()


def build_kernel(vox_ref, wgt_ref, matrix_ref, tile_ref):
    rows, samples = vox_ref.shape
    cols = matrix_ref.shape[1]
    high_count = cols // LANES
    low_pos = lax.broadcasted_iota(jnp.int32, (LANES, samples), 0)
    high_pos = lax.broadcasted_iota(jnp.int32, (high_count, samples), 0)
    blank = jnp.zeros((high_count, samples), jnp.bfloat16)

    def build(step, carry):
        first = pl.multiple_of(step * GROUP, GROUP)
        vox = vox_ref[pl.ds(first, GROUP), :]
        wgt = wgt_ref[pl.ds(first, GROUP), :].astype(jnp.float32) * (1.0 / 256.0)
        low = vox & (LANES - 1)
        high = lax.shift_right_logical(vox, LANES.bit_length() - 1)
        hots = []
        for i in range(GROUP):
            low_hot = (low_pos == low[i:i + 1]).astype(jnp.float32).astype(jnp.bfloat16)
            high_hot = jnp.where(high_pos == high[i:i + 1], wgt[i:i + 1], 0.0).astype(jnp.bfloat16)
            hots.append((low_hot, high_hot))
        for i in range(0, GROUP, 2):
            (low_a, high_a), (low_b, high_b) = hots[i:i + 2]
            left = jnp.concatenate([jnp.concatenate([high_a, blank], 1), jnp.concatenate([blank, high_b], 1)], 0)
            right = jnp.concatenate([low_a, low_b], 1)
            tile_ref[i * high_count:(i + 2) * high_count, :] = dot(left, right, NT)
        for h in range(high_count):
            part = tile_ref[pl.ds(h, GROUP, stride=high_count), :]
            matrix_ref[pl.ds(first, GROUP), h * LANES:(h + 1) * LANES] = part.astype(jnp.bfloat16)
        return carry

    lax.fori_loop(0, rows // GROUP, build, 0)


def sums_kernel(count, info, matrix_ref, own, partner, table_own, table_partner, measured, keep, send, target, sem):
    half, rays, width = keep.shape
    me, side = info[0], info[1]
    fetch = pltpu.make_async_copy(measured.at[pl.ds(side * half, half)], target, sem)
    fetch.start()
    sums_own = dot(matrix_ref[...], own[...], NT).astype(jnp.bfloat16)
    sums_partner = dot(matrix_ref[...], partner[...], NT).astype(jnp.bfloat16)
    fetch.wait()
    high = (me // (count // 2)) & 1
    for i in range(half):
        rows = slice(i * rays, (i + 1) * rays)
        for out, bit in ((send, 1 - high), (keep, high)):
            at = aligned(bit, width)
            total = dot(sums_own[rows], table_own[i, :, at], NN) + dot(sums_partner[rows], table_partner[i, :, at], NN)
            out[i] = total - (2.0 / count) * target[i, :, at]


def penalty_kernel(count, pieces, cut, first, info, own, partner, *refs):
    blocks, refs = refs[:count - 2], refs[count - 2:]
    if first:
        harm, near, far = refs[0], refs[1], refs[2:2 + (count - 2) * pieces]
        refs = refs[2 + len(far):]
        outs, waves, sems = refs[:count], refs[count], refs[-1]
        refs = refs[count + 1:-1]
    else:
        waves, outs, refs = refs[0], refs[1:count + 1], refs[count + 1:]
    stack, turned, acc = refs
    me, place = info[0], info[2]
    height = outs[0].shape[0]
    width = waves.shape[1] // pieces
    if first:
        copies = []
        for r in range(pieces):
            spot = waves.at[0:height, r * width:(r + 1) * width]
            copies.append(pltpu.make_async_copy(harm.at[:, aligned(place ^ r, width)], spot, sems.at[r]))
            copies[-1].start()
    at = columns(me, own.shape[1] // count, cut)
    stack[0:height, :] = own[:, at]
    stack[height:2 * height, :] = partner[:, at]
    for j in range(2, count):
        stack[j * height:(j + 1) * height, :] = blocks[j - 2][...]
    turned[...] = jnp.swapaxes(stack[...], 0, 1)
    for r in range(pieces):
        span = slice(r * width, (r + 1) * width)
        if first:
            waves[height:2 * height, span] = near[:, aligned(place ^ r, width)]
            for j in range(2, count):
                waves[j * height:(j + 1) * height, span] = far[(j - 2) * pieces + r][...]
            copies[r].wait()
        wave = waves[:, span]
        field = dot(turned[...], wave, NN)
        slope = (0.5 * jnp.tanh(0.5 * field) - 0.5).astype(jnp.bfloat16)
        part = dot(wave, slope, NT)
        if r > 0:
            part += acc[...]
        if r < pieces - 1:
            acc[...] = part
        else:
            for j in range(count):
                outs[j][...] = part[j * height:(j + 1) * height].astype(outs[j].dtype)


def data_kernel(count, cuts, split, info, *refs):
    halves, refs = (refs[:split], refs[split:2 * split]), refs[2 * split:]
    res_mine, res_other, table_mine, table_other, top_ref, low_ref, coef = refs[:7]
    refs = refs[7:]
    order = [(0, j) for j in range(count)] + [(t, j) for t in range(1, len(cuts)) for j in range(count)]
    ready = [key for key in order if key[0] == 0 or key[1] < 2]
    grads, refs = dict(zip(ready, refs)), refs[len(ready):]
    updated, residual_ref, later = refs[0], refs[1], refs[2:1 + len(cuts)]
    back_a, back_b, buf, sems, out_sems = refs[1 + len(cuts):]
    me, side = info[0], info[1]
    half, rays, width = halves[0][0].shape
    block = coef.shape[1] // count
    own_width = residual_ref.shape[2]
    spots, copies = {}, {}
    for n, (t, j) in enumerate(order):
        if (t, j) in grads:
            spots[t, j] = buf.at[ready.index((t, j)), :, 0:cuts[t][1]]
        else:
            spots[t, j] = later[t - 1].at[j - 2]
        copies[t, j] = pltpu.make_async_copy(coef.at[:, columns(me ^ j, block, cuts[t])], spots[t, j], sems.at[n])
        copies[t, j].start()
    for back, parts, table in ((back_a, halves[0], table_mine), (back_b, halves[1], table_other)):
        for i in range(half):
            total = dot(table[i, :, aligned(me // 2 if split > 1 else 0, width)], parts[0][i], NT)
            for p in range(1, split):
                total += dot(table[i, :, aligned((me // 2) ^ p, width)], parts[p][i], NT)
            back[:, i * rays:(i + 1) * rays] = total.astype(jnp.bfloat16)
    writes = []
    for t, j in order:
        at = columns(me ^ j, block, cuts[t])
        grad = dot(back_a[...], top_ref[:, at], NN) + dot(back_b[...], low_ref[:, at], NN)
        copies[t, j].wait()
        spot = spots[t, j]
        if (t, j) in grads:
            spot[...] = spot[...] - 0.5 * grad - 0.5 * grads[t, j][...].astype(jnp.float32)
            writes.append(pltpu.make_async_copy(spot, updated.at[:, at], out_sems.at[len(writes)]))
            writes[-1].start()
        else:
            spot[...] = spot[...] - 0.5 * grad
    for q in range(2):
        @pl.when(side == q)
        def _():
            for i in range(half):
                residual_ref[side * half + i] = res_mine[i, :, q * own_width:(q + 1) * own_width]
                residual_ref[(1 - side) * half + i] = res_other[i, :, q * own_width:(q + 1) * own_width]
    for w in writes:
        w.wait()


def finish_kernel(count, cut, masks, info, later, *refs):
    grads = refs[:len(masks)]
    _, updated, buf, sems = refs[len(masks):]
    block = updated.shape[1] // count
    writes = []
    for n, j in enumerate(masks):
        buf[n] = later[j - 2] - 0.5 * grads[n][...].astype(jnp.float32)
        at = columns(info[0] ^ j, block, cut)
        writes.append(pltpu.make_async_copy(buf.at[n], updated.at[:, at], sems.at[n]))
        writes[-1].start()
    for w in writes:
        w.wait()


def step_of(coefficients, measured, ray_voxels, ray_weights, angle_ids, angle_table, harmonics):
    coef_local, cols = coefficients.shape
    projections, _, rays, channels = measured.shape
    rows = projections * rays
    samples = ray_voxels.shape[2]
    count = lax.axis_size("coef")
    me = lax.axis_index("coef")
    half = projections // 2
    block = cols // count
    cuts = cuts_of(block)
    bf16, f32 = jnp.bfloat16, jnp.float32
    shape = jax.ShapeDtypeStruct

    def kernel(body_of, ins, outs, out_shape, scratch=(), grant=12, aliases={}):
        return pl.pallas_call(
            body_of,
            in_specs=ins,
            out_specs=outs,
            out_shape=out_shape,
            scratch_shapes=list(scratch),
            input_output_aliases=aliases,
            compiler_params=pltpu.CompilerParams(vmem_limit_bytes=grant << 20),
        )

    group_bits = 1 if lax.axis_size("groups") % 2 == 0 else 0
    slab_count = lax.axis_size("slab")
    slab_bits = 1 if slab_count % 2 == 0 else 0
    pieces = 1 << (group_bits + slab_bits)
    place = jnp.zeros((), jnp.int32)
    if slab_bits:
        place = place + (lax.axis_index("slab") & 1)
    if group_bits:
        place = place + ((lax.axis_index("groups") & 1) << slab_bits)
    width = harmonics.shape[1] // pieces
    info = jnp.stack([me, me & 1, place]).astype(jnp.int32)
    rows_shape = (rows, samples)
    coef_far, measured_far, vox_far, wgt_far, ids_far, table_far, harm_far = [
        pltpu.with_memory_space_constraint(v, pltpu.HBM)
        for v in (
            coefficients,
            measured.reshape(projections, rays, channels),
            ray_voxels.reshape(rows_shape),
            ray_weights.reshape(rows_shape),
            angle_ids,
            angle_table,
            harmonics,
        )
    ]

    piece = lax.dynamic_slice_in_dim(harmonics, place * width, width, 1)
    fetched = {m: [swap(piece, "coef", m)] for m in range(2, count, 2)}
    table_shape = shape((half,) + angle_table.shape[1:], bf16)
    *parts, own, vox, wgt, table_mine, table_other = kernel(
        lambda *refs: prepare_kernel(count, cuts, *refs),
        [SMEM, SMEM] + [HBM] * 4,
        [VMEM] * ((count - 2) * len(cuts) + 5),
        [shape((coef_local, cut[1]), bf16) for _ in range(2, count) for cut in cuts]
        + [shape((coef_local, cols), bf16)]
        + [shape((rows // 2, samples), jnp.int32)] * 2
        + [table_shape] * 2,
        [pltpu.VMEM((count, coef_local, block), f32), pltpu.SemaphoreType.DMA((count + 2 + projections,))],
    )(info, ids_far, coef_far, vox_far, wgt_far, table_far)
    received = []
    for t in range(len(cuts)):
        received.append([swap(parts[(m - 2) * len(cuts) + t], "coef", m) for m in range(2, count)])
    partner = swap(own, "coef", 1)
    table_partner = swap(table_other, "coef", 1)
    near = swap(harmonics, "coef", 1)
    moves = [(0, 1)] * slab_bits + [(1, 0)] * group_bits + [(1, 1)] * (slab_bits * group_bits)
    for m in fetched:
        for up, along in moves:
            total = lax.axis_size("groups") * slab_count
            pairs = [(i, (((i // slab_count) ^ up) * slab_count) + ((i % slab_count) ^ along)) for i in range(total)]
            fetched[m].append(lax.ppermute(fetched[m][0], ("groups", "slab"), pairs))

    top = kernel(
        build_kernel,
        [VMEM, VMEM],
        VMEM,
        shape((rows // 2, cols), bf16),
        [pltpu.VMEM((GROUP * cols // LANES, LANES), f32)],
    )(vox, wgt)
    low = swap(top, "coef", 1)
    for m in list(fetched):
        fetched[m ^ 1] = [swap(v, "coef", 1) for v in fetched[m]]
    far = [v for m in range(2, count) for v in fetched[m]]

    total, send = kernel(
        lambda *refs: sums_kernel(count, *refs),
        [SMEM] + [VMEM] * 5 + [HBM],
        [VMEM, VMEM],
        [shape((half, rays, channels // 2), f32)] * 2,
        [pltpu.VMEM((half, rays, channels), f32), pltpu.SemaphoreType.DMA(())],
    )(info, top, own, partner, table_mine, table_partner, measured_far)

    masks = [1 << n for n in range(1, count.bit_length() - 1)]
    for mask in masks[::-1]:
        if mask < count // 2:
            width = total.shape[2] // 2
            bit = jnp.where((me & mask) == 0, 0, 1)
            send = lax.dynamic_slice_in_dim(total, (1 - bit) * width, width, 2)
            total = lax.dynamic_slice_in_dim(total, bit * width, width, 2)
        total = total + swap(send, "coef", mask)

    returned = []
    waves = None
    for t, cut in enumerate(cuts):
        first = t == 0
        extra = [harm_far, near] + far if first else [waves]
        wide = [shape((count * coef_local, harmonics.shape[1]), bf16)] if first else []
        outs = kernel(
            lambda *refs: penalty_kernel(count, pieces, cut, first, *refs),
            [SMEM] + [VMEM] * count + ([HBM] + [VMEM] * (1 + len(far)) if first else [VMEM]),
            [VMEM] * (count + len(wide)),
            [shape((coef_local, cut[1]), bf16)] * count + wide,
            [
                pltpu.VMEM((count * coef_local, cut[1]), bf16),
                pltpu.VMEM((cut[1], count * coef_local), bf16),
                pltpu.VMEM((count * coef_local, cut[1]), f32),
            ]
            + ([pltpu.SemaphoreType.DMA((pieces,))] if first else []),
        )(info, own, partner, *received[t], *extra)
        if first:
            waves = outs[-1]
        back = [outs[0]]
        for m in range(1, count):
            back.append(swap(outs[m], "coef", m))
        returned.append(back)
        if first:
            half_mine = [total.astype(bf16)]
            for mask in masks:
                other = [swap(v, "coef", mask) for v in half_mine]
                if total.shape[2] % LANES == 0:
                    half_mine = half_mine + other
                    continue
                low_bit, pair = (me & mask) == 0, (half_mine[0], other[0])
                ordered = [jnp.where(low_bit, *pair), jnp.where(low_bit, *pair[::-1])]
                half_mine = [jnp.concatenate(ordered, 2)]
    res_other = swap(total, "coef", 1)
    half_other = [swap(v, "coef", 1) for v in half_mine]

    ready = [(t, j) for t in range(len(cuts)) for j in range(count) if t == 0 or j < 2]
    updated, residual, *later = kernel(
        lambda *refs: data_kernel(count, cuts, len(half_mine), *refs),
        [SMEM] + [VMEM] * (2 * len(half_mine) + 6) + [HBM] + [VMEM] * len(ready),
        [HBM] + [VMEM] * len(cuts),
        [shape((coef_local, cols), f32), shape((projections, rays, channels // count), f32)]
        + [shape((count - 2, coef_local, cut[1]), f32) for cut in cuts[1:]],
        [
            pltpu.VMEM((coef_local, rows // 2), bf16),
            pltpu.VMEM((coef_local, rows // 2), bf16),
            pltpu.VMEM((len(ready), coef_local, max(cut[1] for cut in cuts)), f32),
            pltpu.SemaphoreType.DMA((len(cuts) * count,)),
            pltpu.SemaphoreType.DMA((len(ready),)),
        ],
    )(
        info,
        *half_mine,
        *half_other,
        total,
        res_other,
        table_mine,
        table_other,
        top,
        low,
        coef_far,
        *[returned[t][j] for t, j in ready],
    )
    remote = list(range(2, count))
    middle = len(remote) // 2
    for t, cut in list(enumerate(cuts))[1:]:
        for masks in (remote[:middle], remote[middle:]):
            if not masks:
                continue
            updated = kernel(
                lambda *refs: finish_kernel(count, cut, masks, *refs),
                [SMEM] + [VMEM] * (len(masks) + 1) + [HBM],
                HBM,
                shape((coef_local, cols), f32),
                [pltpu.VMEM((len(masks), coef_local, cut[1]), f32), pltpu.SemaphoreType.DMA((len(masks),))],
                aliases={len(masks) + 2: 0},
            )(info, later[t - 1], *[returned[t][m] for m in masks], updated)
    return (updated, residual[:, None])


def solution(mesh):
    in_specs = (
        P("coef", ("groups", "slab")),
        P("groups", "slab", None, None),
        P(),
        P(),
        P(),
        P(None, "coef", None),
        P("coef", None),
    )
    out_specs = (P("coef", ("groups", "slab")), P("groups", "slab", None, "coef"))
    return jax.shard_map(step_of, mesh=mesh, in_specs=in_specs, out_specs=out_specs, check_vma=False)
```

time: 89.2 us -> 94.3 us (1.057)
  starting transfers between devices: 17.9 us -> 22.3 us
  Pallas kernels: 36 us -> 38.3 us
  waiting for transfers between devices: 32.7 us -> 30.9 us
    pallas_call x7 -> x5, Pallas kernels: 26.6 us -> 30.4 us  [the longest x2 15.4 us: step_of(): kernel(lambda *refs: penalty_kernel(count, pieces, cut, first, *refs), [S...]
    ppermute x19 -> x24, starting transfers between devices: 13 us -> 15.7 us  [swap(): return lax.ppermute(value, axis, [(i, i ^ mask) for i in range(count)])]
    ppermute x3, waiting for transfers between devices: 8.16 us -> 5.97 us  [step_of(): fetched[m].append(lax.ppermute(fetched[m][0], ('groups', 'slab'), pairs))]
    ppermute x3, starting transfers between devices: 4.84 us -> 6.69 us  [step_of(): fetched[m].append(lax.ppermute(fetched[m][0], ('groups', 'slab'), pairs))]
    pallas_call x3 -> x2, Pallas kernels: 4.25 us -> 2.73 us  [step_of(): kernel(lambda *refs: finish_kernel(count, cut, masks, *refs), [SMEM] + [V...]
    ppermute x19 -> x24, waiting for transfers between devices: 24.5 us -> 25 us  [swap(): return lax.ppermute(value, axis, [(i, i ^ mask) for i in range(count)])]
  transfers between devices with their start and end apart: 22 -> 27, of which waited for: 6 -> 11; matrix products, arithmetic and copies ran while one was open for 1% -> 1% of each run, Pallas kernels for 29% -> 35%
where the time goes in v5:
time: 94.3 us; the launch traced here: 94.1 us
  Pallas kernels  38.3 us (41%)
  waiting for transfers between devices  30.9 us (33%)
  starting transfers between devices  22.3 us (24%)
  local copies, waits for them, and re-layouts  1.65 us (2%)
    ppermute x24, waiting for transfers between devices, swap(): return lax.ppermute(value, axis, [(i, i ^ mask) for i in range(count)])  25 us
    ppermute x24, starting transfers between devices, swap(): return lax.ppermute(value, axis, [(i, i ^ mask) for i in range(count)])  15.7 us
    pallas_call x2, Pallas kernels, step_of(): kernel(lambda *refs: penalty_kernel(count, pieces, cut, first, *refs), [S...  15.4 us
    pallas_call x1, Pallas kernels, step_of(): kernel(lambda *refs: data_kernel(count, cuts, len(half_mine), *refs), [SM...  6.82 us
    ppermute x3, starting transfers between devices, step_of(): fetched[m].append(lax.ppermute(fetched[m][0], ('groups', 'slab'), pairs))  6.69 us
    ppermute x3, waiting for transfers between devices, step_of(): fetched[m].append(lax.ppermute(fetched[m][0], ('groups', 'slab'), pairs))  5.97 us
    pallas_call x1, Pallas kernels, step_of(): kernel(build_kernel, [VMEM, VMEM], VMEM, shape((rows // 2, cols), bf16),...  5.16 us
    pallas_call x1, Pallas kernels, step_of(): kernel(lambda *refs: prepare_kernel(count, cuts, *refs), [SMEM, SMEM] + [...  4.36 us
  transfers between devices with their start and end apart: 27, of which 11 were waited for; matrix products, arithmetic and copies ran while one was open for 1% of the time, Pallas kernels for 35%

profile of v5, /device:TPU:0, one launch (start us, length us, event | category | flops | bytes accessed | tf_op | source)
XLA Modules:
  0.0 94.1 jit_solution(16120525571030871879)
XLA Ops:
  0.6 0.1 pad_add_fusion.refs_0_
  0.7 4.4 %shard_map.86 = (bf16[224,512]{1,0:T(8,128)(2,1)S(1)}, bf16[224,512]{1,0:T(8,128)(2,1)S(1)}, bf16[224,512]{1,0:T(8,128)(2,1)S(1)}, bf16[224,512]{1,0:T(8,128)(2,...) custom-call(s32[3]{0:T(128)S(1)} %pad_add_fusion.refs_0_, ...), custom_call_target="tpu_custom_call" | custom-call | tf_op jit(solution)/shard_map/pallas_call | solution.py:285
  5.1 0.7 copy-done.1
  5.8 0.5 collective-permute-start
  6.3 5.2 %shard_map.87.refs_1_.refs_9_ = bf16[256,4096]{1,0:T(8,128)(2,1)S(1)} custom-call(s32[256,128]{1,0:T(8,128)S(1)} %get-tuple-element.25.vox_ref, s32[256,128]{1,0:T(8,128)S(1)} %get-tuple-element.26.wgt_ref), custom_call_target="tpu_custom_call" | custom-call | tf_op jit(solution)/shard_map/pallas_call | solution.py:308
  11.4 0.1 collective-permute-start.7
  11.5 1.0 %constant_dynamic-slice_fusion = bf16[224,512]{1,0:T(8,128)(2,1)S(1)} fusion(bf16[224,2048]{1,0:T(8,128)(2,1)} %refs_5_.3, s32[]{:T(128)S(6)} %select_n.3), kind=kLoop, calls=%fused_computation.1 | loop fusion | bytes 458756 | tf_op jit(solution)/shard_map/dynamic_slice | solution.py:282
  12.5 3.0 %collective-permute-start.11 = (bf16[224,512]{1,0:T(8,128)(2,1)S(1)}, bf16[224,512]{1,0:T(8,128)(2,1)S(1)}, u32[]{:S(2)}, u32[]{:S(2)}) collective-permute-start(bf16[224,512]{1,0:T(8,128)(2,1)S(1)} %constant_dynamic-slice_fusion), channel_id=1, source_target_pairs={{0,8},{4,12},{8,0},{12,4},{1,9},{5,13},{9,1},{13,5},{2,10},{6,14},... | collective-permute-start | bytes 688136 | tf_op jit(solution)/shard_map/ppermute | solution.py:25
  15.5 0.1 collective-permute-start.8
  15.6 1.0 %collective-permute-start.9 = (bf16[224,512]{1,0:T(8,128)(2,1)}, bf16[224,512]{1,0:T(8,128)(2,1)S(1)}, u32[]{:S(2)}, u32[]{:S(2)}) collective-permute-start(bf16[224,512]{1,0:T(8,128)(2,1)} %copy-done), channel_id=1, source_target_pairs={{0,12},{4,8},{8,4},{12,0},{1,13},{5,9},{9,5},{13,1},{2,14},{6,10},... | collective-permute-start | bytes 688136 | tf_op jit(solution)/shard_map/ppermute | solution.py:25
  16.6 5.4 %collective-permute-done.11.refs_7_ = bf16[224,512]{1,0:T(8,128)(2,1)S(1)} collective-permute-done((bf16[224,512]{1,0:T(8,128)(2,1)S(1)}, bf16[224,512]{1,0:T(8,128)(2,1)S(1)}, u32[]{:S(2)}, u32[]{:S(2)}) %collective-permute-start.11) | collective-permute-done | bytes 229408 | tf_op jit(solution)/shard_map/ppermute | solution.py:25
  22.0 2.1 %collective-permute-start.12 = (bf16[224,512]{1,0:T(8,128)(2,1)S(1)}, bf16[224,512]{1,0:T(8,128)(2,1)S(1)}, u32[]{:S(2)}, u32[]{:S(2)}) collective-permute-start(bf16[224,512]{1,0:T(8,128)(2,1)S(1)} %collective-permute-done.11.refs_7_), channel_id=1, source_target_pairs={{0,1},{1,0},{2,3},{3,2},{16,17},{17,16},{18,19},{19,18},{4,5},{5,4... | collective-permute-start | bytes 688136 | tf_op jit(solution)/shard_map/ppermute | solution.py:306
  24.1 2.8 %collective-permute-done.8.refs_3_ = bf16[224,512]{1,0:T(8,128)(2,1)S(1)} collective-permute-done((bf16[224,512]{1,0:T(8,128)(2,1)}, bf16[224,512]{1,0:T(8,128)(2,1)S(1)}, u32[]{:S(2)}, u32[]{:S(2)}) %collective-permute-start.8) | collective-permute-done | bytes 229408 | tf_op jit(solution)/shard_map/ppermute | solution.py:25
  26.9 2.0 %collective-permute-start.13 = (bf16[224,512]{1,0:T(8,128)(2,1)S(1)}, bf16[224,512]{1,0:T(8,128)(2,1)S(1)}, u32[]{:S(2)}, u32[]{:S(2)}) collective-permute-start(bf16[224,512]{1,0:T(8,128)(2,1)S(1)} %collective-permute-done.11.refs_7_), channel_id=1, source_target_pairs={{0,16},{1,17},{2,18},{3,19},{16,0},{17,1},{18,2},{19,3},{4,20},{5,... | collective-permute-start | bytes 688136 | tf_op jit(solution)/shard_map/ppermute | solution.py:306
  28.9 1.6 %collective-permute-done.9.refs_4_ = bf16[224,512]{1,0:T(8,128)(2,1)S(1)} collective-permute-done((bf16[224,512]{1,0:T(8,128)(2,1)}, bf16[224,512]{1,0:T(8,128)(2,1)S(1)}, u32[]{:S(2)}, u32[]{:S(2)}) %collective-permute-start.9) | collective-permute-done | bytes 229408 | tf_op jit(solution)/shard_map/ppermute | solution.py:25
  30.5 2.5 %collective-permute-start.14 = (bf16[224,512]{1,0:T(8,128)(2,1)S(1)}, bf16[224,512]{1,0:T(8,128)(2,1)S(1)}, u32[]{:S(2)}, u32[]{:S(2)}) collective-permute-start(bf16[224,512]{1,0:T(8,128)(2,1)S(1)} %collective-permute-done.11.refs_7_), channel_id=1, source_target_pairs={{0,17},{1,16},{2,19},{3,18},{16,1},{17,0},{18,3},{19,2},{4,21},{5,... | collective-permute-start | bytes 688136 | tf_op jit(solution)/shard_map/ppermute | solution.py:306
  33.0 0.7 collective-permute-start.1
  33.8 0.1 collective-permute-start.10
  33.8 6.0 %collective-permute-done.14.refs_10_ = bf16[224,512]{1,0:T(8,128)(2,1)S(1)} collective-permute-done((bf16[224,512]{1,0:T(8,128)(2,1)S(1)}, bf16[224,512]{1,0:T(8,128)(2,1)S(1)}, u32[]{:S(2)}, u32[]{:S(2)}) %collective-permute-start.14) | collective-permute-done | bytes 229408 | tf_op jit(solution)/shard_map/ppermute | solution.py:306
  39.8 0.0 collective-permute-start.15
  39.8 1.5 %collective-permute-done.15.refs_11_ = bf16[224,512]{1,0:T(8,128)(2,1)S(1)} collective-permute-done((bf16[224,512]{1,0:T(8,128)(2,1)S(1)}, bf16[224,512]{1,0:T(8,128)(2,1)S(1)}, u32[]{:S(2)}, u32[]{:S(2)}) %collective-permute-start.15) | collective-permute-done | bytes 229408 | tf_op jit(solution)/shard_map/ppermute | solution.py:25
  41.3 0.1 collective-permute-start.16
  41.4 0.4 collective-permute-start.17
  41.8 1.0 %collective-permute-done.16.refs_12_ = bf16[224,512]{1,0:T(8,128)(2,1)S(1)} collective-permute-done((bf16[224,512]{1,0:T(8,128)(2,1)S(1)}, bf16[224,512]{1,0:T(8,128)(2,1)S(1)}, u32[]{:S(2)}, u32[]{:S(2)}) %collective-permute-start.16) | collective-permute-done | bytes 229408 | tf_op jit(solution)/shard_map/ppermute | solution.py:25
  42.8 0.1 collective-permute-start.18
  42.9 0.2 collective-permute-done.17.refs_13_
  43.1 1.4 %collective-permute-start.22 = (bf16[224,512]{1,0:T(8,128)(2,1)S(1)}, bf16[224,512]{1,0:T(8,128)(2,1)S(1)}, u32[]{:S(2)}, u32[]{:S(2)}) collective-permute-start(bf16[224,512]{1,0:T(8,128)(2,1)S(1)} %get-tuple-element.38), channel_id=1, source_target_pairs={{0,8},{4,12},{8,0},{12,4},{1,9},{5,13},{9,1},{13,5},{2,10},{6,14},... | collective-permute-start | bytes 688136 | tf_op jit(solution)/shard_map/ppermute | solution.py:25
  44.5 0.1 collective-permute-start.23
  44.7 3.8 %shard_map.88 = (f32[4,64,128]{2,1,0:T(8,128)S(1)}, f32[4,64,128]{2,1,0:T(8,128)S(1)}) custom-call(s32[3]{0:T(128)S(1)} %pad_add_fusion.refs_0_, bf16[256,4096]{1,0:T(8,128)(2,1)S(1)} %shard_map.87.refs_1_.refs_9_, bf16[224,4096]{1,0:T(8,128)(2,1)} %get-tuple-element.27.refs_2_.refs_1_, bf16[224,4096]{1,0:T(8,128)(2,1)} %collective-permute-done.refs_3_.refs_2_, ...), custom_call_target="tpu_custom_call" | custom-call | tf_op jit(solution)/shard_map/pallas_call | solution.py:320
  48.5 1.5 %collective-permute-start.2 = (f32[4,64,128]{2,1,0:T(8,128)S(1)}, f32[4,64,128]{2,1,0:T(8,128)S(1)}, u32[]{:S(2)}, u32[]{:S(2)}) collective-permute-start(f32[4,64,128]{2,1,0:T(8,128)S(1)} %get-tuple-element.31), channel_id=1, source_target_pairs={{0,8},{4,12},{8,0},{12,4},{1,9},{5,13},{9,1},{13,5},{2,10},{6,14},... | collective-permute-start | bytes 393224 | tf_op jit(solution)/shard_map/ppermute | solution.py:25
  50.0 8.7 %shard_map.89 = (bf16[224,512]{1,0:T(8,128)(2,1)S(1)}, bf16[224,512]{1,0:T(8,128)(2,1)S(1)}, bf16[224,512]{1,0:T(8,128)(2,1)S(1)}, bf16[224,512]{1,0:T(8,128)(2,1)S(1)}, bf16[896,2048]{1,0:T(8,128)(2,1)S(1)}) custom-call(s32[3]{0:T(128)S(1)} %pad_add_fusion.refs_0_, bf16[224,4096]{1,0:T(8,128)(2,1)} %get-tuple-element.27.refs_2_.refs_1_, ...), custom_call_target="tpu_custom_call" | custom-call | tf_op jit(solution)/shard_map/pallas_call | solution.py:343
  58.7 6.7 %shard_map.90 = (bf16[224,512]{1,0:T(8,128)(2,1)S(1)}, bf16[224,512]{1,0:T(8,128)(2,1)S(1)}, bf16[224,512]{1,0:T(8,128)(2,1)S(1)}, bf16[224,512]{1,0:T(8,128)(2,1)S(1)}) custom-call(s32[3]{0:T(128)S(1)} %pad_add_fusion.refs_0_, bf16[224,4096]{1,0:T(8,128)(2,1)} %get-tuple-element.27.refs_2_.refs_1_, bf16[224,4096]{1,0:T(8,128)(2,1)} %collective-permute-done.refs_3_.refs_2_, ...), custom_call_target="tpu_custom_call" | custom-call | tf_op jit(solution)/shard_map/pallas_call | solution.py:343
  65.4 0.4 collective-permute-start.24
  65.8 0.2 collective-permute-start.19
  66.0 0.7 collective-permute-start.3
  66.7 0.0 collective-permute-start.4
  66.7 3.7 %collective-permute-done.3.refs_2_ = bf16[4,64,128]{2,1,0:T(8,128)(2,1)S(1)} collective-permute-done((bf16[4,64,128]{2,1,0:T(8,128)(2,1)S(1)}, bf16[4,64,128]{2,1,0:T(8,128)(2,1)S(1)}, u32[]{:S(2)}, u32[]{:S(2)}) %collective-permute-start.3) | collective-permute-done | bytes 65568 | tf_op jit(solution)/shard_map/ppermute | solution.py:25
  70.4 0.6 collective-permute-start.20
  71.0 0.2 collective-permute-start.21
  71.2 1.3 %collective-permute-start.26 = (bf16[224,512]{1,0:T(8,128)(2,1)S(1)}, bf16[224,512]{1,0:T(8,128)(2,1)S(1)}, u32[]{:S(2)}, u32[]{:S(2)}) collective-permute-start(bf16[224,512]{1,0:T(8,128)(2,1)S(1)} %get-tuple-element.45), channel_id=1, source_target_pairs={{0,8},{4,12},{8,0},{12,4},{1,9},{5,13},{9,1},{13,5},{2,10},{6,14},... | collective-permute-start | bytes 688136 | tf_op jit(solution)/shard_map/ppermute | solution.py:25
  72.5 1.4 %collective-permute-start.25 = (bf16[224,512]{1,0:T(8,128)(2,1)S(1)}, bf16[224,512]{1,0:T(8,128)(2,1)S(1)}, u32[]{:S(2)}, u32[]{:S(2)}) collective-permute-start(bf16[224,512]{1,0:T(8,128)(2,1)S(1)} %get-tuple-element.44), channel_id=1, source_target_pairs={{0,12},{4,8},{8,4},{12,0},{1,13},{5,9},{9,5},{13,1},{2,14},{6,10},... | collective-permute-start | bytes 688136 | tf_op jit(solution)/shard_map/ppermute | solution.py:25
  73.9 5.0 %collective-permute-done.20.refs_14_ = bf16[224,512]{1,0:T(8,128)(2,1)S(1)} collective-permute-done((bf16[224,512]{1,0:T(8,128)(2,1)S(1)}, bf16[224,512]{1,0:T(8,128)(2,1)S(1)}, u32[]{:S(2)}, u32[]{:S(2)}) %collective-permute-start.20) | collective-permute-done | bytes 229408 | tf_op jit(solution)/shard_map/ppermute | solution.py:25
  78.9 3.0 %collective-permute-done.21.refs_15_ = bf16[224,512]{1,0:T(8,128)(2,1)S(1)} collective-permute-done((bf16[224,512]{1,0:T(8,128)(2,1)S(1)}, bf16[224,512]{1,0:T(8,128)(2,1)S(1)}, u32[]{:S(2)}, u32[]{:S(2)}) %collective-permute-start.21) | collective-permute-done | bytes 229408 | tf_op jit(solution)/shard_map/ppermute | solution.py:25
  81.9 1.7 %collective-permute-start.5 = (bf16[4,64,128]{2,1,0:T(8,128)(2,1)S(1)}, bf16[4,64,128]{2,1,0:T(8,128)(2,1)S(1)}, u32[]{:S(2)}, u32[]{:S(2)}) collective-permute-start(bf16[4,64,128]{2,1,0:T(8,128)(2,1)S(1)} %collective-permute-done.3.refs_2_), channel_id=1, source_target_pairs={{0,4},{4,0},{8,12},{12,8},{1,5},{5,1},{9,13},{13,9},{2,6},{6,2},{1... | collective-permute-start | bytes 196616 | tf_op jit(solution)/shard_map/ppermute | solution.py:25
  83.6 0.9 collective-permute-done.5.refs_4_
  84.5 6.8 %shard_map.91 = (f32[224,4096]{1,0:T(8,128)}, f32[8,64,64]{2,1,0:T(8,128)}, f32[2,224,512]{2,1,0:T(8,128)S(1)}) custom-call(s32[3]{0:T(128)S(1)} %pad_add_fusion.refs_0_, bf16[4,64,128]{2,1,0:T(8,128)(2,1)S(1)} %get-tuple-element.50.refs_1_, bf16[4,64,128]{2,1,0:T(8,128)(2,1)S(1)} %collective-permute-done.3.refs_2_, ...), custom_call_target="tpu_custom_call" | custom-call | tf_op jit(solution)/shard_map/pallas_call | solution.py:375
  91.4 1.4 %shard_map.92.refs_3_ = f32[224,4096]{1,0:T(8,128)} custom-call(s32[3]{0:T(128)S(1)} %pad_add_fusion.refs_0_, f32[2,224,512]{2,1,0:T(8,128)S(1)} %get-tuple-element.43.refs_1_, bf16[224,512]{1,0:T(8,128)(2,1)S(1)} %collective-permute-done.26.refs_2_, f32[224,4096]{1,0:T(8,128)} %get-tuple-element.46.refs_3_), custom_call_target="tpu_custom_call", output_to_operand_aliasing={{}: (3, {})} | custom-call | tf_op jit(solution)/shard_map/pallas_call | solution.py:407
  92.7 1.4 %shard_map.93 = f32[224,4096]{1,0:T(8,128)} custom-call(s32[3]{0:T(128)S(1)} %pad_add_fusion.refs_0_, f32[2,224,512]{2,1,0:T(8,128)S(1)} %get-tuple-element.43.refs_1_, bf16[224,512]{1,0:T(8,128)(2,1)S(1)} %collective-permute-done.25.refs_2_, f32[224,4096]{1,0:T(8,128)} %shard_map.92.refs_3_), custom_call_target="tpu_custom_call", output_to_operand_aliasing={{}: (3, {})} | custom-call | tf_op jit(solution)/shard_map/pallas_call | solution.py:407
  (21 shorter events, 0.1 us)
Async XLA Ops:
  5.1 0.7 copy-start.1
  5.8 5.7 %copy-start = (bf16[224,512]{1,0:T(8,128)(2,1)}, bf16[224,512]{1,0:T(8,128)(2,1)S(1)}, u32[]{:S(2)}) copy-start(bf16[224,512]{1,0:T(8,128)(2,1)S(1)} %get-tuple-element.33) | copy-start | bytes 688132
  5.8 38.7 %collective-permute-start = (bf16[224,4096]{1,0:T(8,128)(2,1)}, bf16[224,4096]{1,0:T(8,128)(2,1)}, u32[]{:S(2)}, u32[]{:S(2)}) collective-permute-start(bf16[224,4096]{1,0:T(8,128)(2,1)} %get-tuple-element.27.refs_2_.refs_1_), channel_id=1, source_target_pairs={{0,4},{4,0},{8,12},{12,8},{1,5},{5,1},{9,13},{13,9},{2,6},{6,2},{1... | collective-permute-start | bytes 5505032 | tf_op jit(solution)/shard_map/ppermute | solution.py:25
  11.4 72.2 %collective-permute-start.7 = (bf16[256,4096]{1,0:T(8,128)(2,1)S(1)}, bf16[256,4096]{1,0:T(8,128)(2,1)}, u32[]{:S(2)}, u32[]{:S(2)}) collective-permute-start(bf16[256,4096]{1,0:T(8,128)(2,1)S(1)} %shard_map.87.refs_1_.refs_9_), channel_id=1, source_target_pairs={{0,4},{4,0},{8,12},{12,8},{1,5},{5,1},{9,13},{13,9},{2,6},{6,2},{1... | collective-permute-start | bytes 6291464 | tf_op jit(solution)/shard_map/ppermute | solution.py:25
  12.5 9.5 %collective-permute-start.11 = (bf16[224,512]{1,0:T(8,128)(2,1)S(1)}, bf16[224,512]{1,0:T(8,128)(2,1)S(1)}, u32[]{:S(2)}, u32[]{:S(2)}) collective-permute-start(bf16[224,512]{1,0:T(8,128)(2,1)S(1)} %constant_dynamic-slice_fusion), channel_id=1, source_target_pairs={{0,8},{4,12},{8,0},{12,4},{1,9},{5,13},{9,1},{13,5},{2,10},{6,14},... | collective-permute-start | bytes 688136 | tf_op jit(solution)/shard_map/ppermute | solution.py:25
  15.5 11.4 %collective-permute-start.8 = (bf16[224,512]{1,0:T(8,128)(2,1)}, bf16[224,512]{1,0:T(8,128)(2,1)S(1)}, u32[]{:S(2)}, u32[]{:S(2)}) collective-permute-start(bf16[224,512]{1,0:T(8,128)(2,1)} %copy-done.1), channel_id=1, source_target_pairs={{0,8},{4,12},{8,0},{12,4},{1,9},{5,13},{9,1},{13,5},{2,10},{6,14},... | collective-permute-start | bytes 688136 | tf_op jit(solution)/shard_map/ppermute | solution.py:25
  15.6 14.9 %collective-permute-start.9 = (bf16[224,512]{1,0:T(8,128)(2,1)}, bf16[224,512]{1,0:T(8,128)(2,1)S(1)}, u32[]{:S(2)}, u32[]{:S(2)}) collective-permute-start(bf16[224,512]{1,0:T(8,128)(2,1)} %copy-done), channel_id=1, source_target_pairs={{0,12},{4,8},{8,4},{12,0},{1,13},{5,9},{9,5},{13,1},{2,14},{6,10},... | collective-permute-start | bytes 688136 | tf_op jit(solution)/shard_map/ppermute | solution.py:25
  22.0 11.1 %collective-permute-start.12 = (bf16[224,512]{1,0:T(8,128)(2,1)S(1)}, bf16[224,512]{1,0:T(8,128)(2,1)S(1)}, u32[]{:S(2)}, u32[]{:S(2)}) collective-permute-start(bf16[224,512]{1,0:T(8,128)(2,1)S(1)} %collective-permute-done.11.refs_7_), channel_id=1, source_target_pairs={{0,1},{1,0},{2,3},{3,2},{16,17},{17,16},{18,19},{19,18},{4,5},{5,4... | collective-permute-start | bytes 688136 | tf_op jit(solution)/shard_map/ppermute | solution.py:306
  26.9 6.9 %collective-permute-start.13 = (bf16[224,512]{1,0:T(8,128)(2,1)S(1)}, bf16[224,512]{1,0:T(8,128)(2,1)S(1)}, u32[]{:S(2)}, u32[]{:S(2)}) collective-permute-start(bf16[224,512]{1,0:T(8,128)(2,1)S(1)} %collective-permute-done.11.refs_7_), channel_id=1, source_target_pairs={{0,16},{1,17},{2,18},{3,19},{16,0},{17,1},{18,2},{19,3},{4,20},{5,... | collective-permute-start | bytes 688136 | tf_op jit(solution)/shard_map/ppermute | solution.py:306
  30.5 9.3 %collective-permute-start.14 = (bf16[224,512]{1,0:T(8,128)(2,1)S(1)}, bf16[224,512]{1,0:T(8,128)(2,1)S(1)}, u32[]{:S(2)}, u32[]{:S(2)}) collective-permute-start(bf16[224,512]{1,0:T(8,128)(2,1)S(1)} %collective-permute-done.11.refs_7_), channel_id=1, source_target_pairs={{0,17},{1,16},{2,19},{3,18},{16,1},{17,0},{18,3},{19,2},{4,21},{5,... | collective-permute-start | bytes 688136 | tf_op jit(solution)/shard_map/ppermute | solution.py:306
  33.0 8.4 %collective-permute-start.1 = (bf16[4,224,256]{2,1,0:T(8,128)(2,1)S(1)}, bf16[4,224,256]{2,1,0:T(8,128)(2,1)S(1)}, u32[]{:S(2)}, u32[]{:S(2)}) collective-permute-start(bf16[4,224,256]{2,1,0:T(8,128)(2,1)S(1)} %get-tuple-element.29.refs_8_), channel_id=1, source_target_pairs={{0,4},{4,0},{8,12},{12,8},{1,5},{5,1},{9,13},{13,9},{2,6},{6,2},{1... | collective-permute-start | bytes 1376264 | tf_op jit(solution)/shard_map/ppermute | solution.py:25
  33.8 16.2 %collective-permute-start.10 = (bf16[224,2048]{1,0:T(8,128)(2,1)}, bf16[224,2048]{1,0:T(8,128)(2,1)S(1)}, u32[]{:S(2)}, u32[]{:S(2)}) collective-permute-start(bf16[224,2048]{1,0:T(8,128)(2,1)} %refs_5_.3), channel_id=1, source_target_pairs={{0,4},{4,0},{8,12},{12,8},{1,5},{5,1},{9,13},{13,9},{2,6},{6,2},{1... | collective-permute-start | bytes 2752520 | tf_op jit(solution)/shard_map/ppermute | solution.py:25
  39.8 1.5 %collective-permute-start.15 = (bf16[224,512]{1,0:T(8,128)(2,1)S(1)}, bf16[224,512]{1,0:T(8,128)(2,1)S(1)}, u32[]{:S(2)}, u32[]{:S(2)}) collective-permute-start(bf16[224,512]{1,0:T(8,128)(2,1)S(1)} %collective-permute-done.11.refs_7_), channel_id=1, source_target_pairs={{0,4},{4,0},{8,12},{12,8},{1,5},{5,1},{9,13},{13,9},{2,6},{6,2},{1... | collective-permute-start | bytes 688136 | tf_op jit(solution)/shard_map/ppermute | solution.py:25
  41.3 1.5 %collective-permute-start.16 = (bf16[224,512]{1,0:T(8,128)(2,1)S(1)}, bf16[224,512]{1,0:T(8,128)(2,1)S(1)}, u32[]{:S(2)}, u32[]{:S(2)}) collective-permute-start(bf16[224,512]{1,0:T(8,128)(2,1)S(1)} %collective-permute-done.12.refs_8_), channel_id=1, source_target_pairs={{0,4},{4,0},{8,12},{12,8},{1,5},{5,1},{9,13},{13,9},{2,6},{6,2},{1... | collective-permute-start | bytes 688136 | tf_op jit(solution)/shard_map/ppermute | solution.py:25
  41.4 1.7 %collective-permute-start.17 = (bf16[224,512]{1,0:T(8,128)(2,1)S(1)}, bf16[224,512]{1,0:T(8,128)(2,1)S(1)}, u32[]{:S(2)}, u32[]{:S(2)}) collective-permute-start(bf16[224,512]{1,0:T(8,128)(2,1)S(1)} %collective-permute-done.13.refs_9_), channel_id=1, source_target_pairs={{0,4},{4,0},{8,12},{12,8},{1,5},{5,1},{9,13},{13,9},{2,6},{6,2},{1... | collective-permute-start | bytes 688136 | tf_op jit(solution)/shard_map/ppermute | solution.py:25
  42.8 5.7 %collective-permute-start.18 = (bf16[224,512]{1,0:T(8,128)(2,1)S(1)}, bf16[224,512]{1,0:T(8,128)(2,1)S(1)}, u32[]{:S(2)}, u32[]{:S(2)}) collective-permute-start(bf16[224,512]{1,0:T(8,128)(2,1)S(1)} %collective-permute-done.14.refs_10_), channel_id=1, source_target_pairs={{0,4},{4,0},{8,12},{12,8},{1,5},{5,1},{9,13},{13,9},{2,6},{6,2},{1... | collective-permute-start | bytes 688136 | tf_op jit(solution)/shard_map/ppermute | solution.py:25
  43.1 15.6 %collective-permute-start.22 = (bf16[224,512]{1,0:T(8,128)(2,1)S(1)}, bf16[224,512]{1,0:T(8,128)(2,1)S(1)}, u32[]{:S(2)}, u32[]{:S(2)}) collective-permute-start(bf16[224,512]{1,0:T(8,128)(2,1)S(1)} %get-tuple-element.38), channel_id=1, source_target_pairs={{0,8},{4,12},{8,0},{12,4},{1,9},{5,13},{9,1},{13,5},{2,10},{6,14},... | collective-permute-start | bytes 688136 | tf_op jit(solution)/shard_map/ppermute | solution.py:25
  44.5 14.2 %collective-permute-start.23 = (bf16[224,512]{1,0:T(8,128)(2,1)S(1)}, bf16[224,512]{1,0:T(8,128)(2,1)S(1)}, u32[]{:S(2)}, u32[]{:S(2)}) collective-permute-start(bf16[224,512]{1,0:T(8,128)(2,1)S(1)} %get-tuple-element.39), channel_id=1, source_target_pairs={{0,12},{4,8},{8,4},{12,0},{1,13},{5,9},{9,5},{13,1},{2,14},{6,10},... | collective-permute-start | bytes 688136 | tf_op jit(solution)/shard_map/ppermute | solution.py:25
  48.5 17.5 %collective-permute-start.2 = (f32[4,64,128]{2,1,0:T(8,128)S(1)}, f32[4,64,128]{2,1,0:T(8,128)S(1)}, u32[]{:S(2)}, u32[]{:S(2)}) collective-permute-start(f32[4,64,128]{2,1,0:T(8,128)S(1)} %get-tuple-element.31), channel_id=1, source_target_pairs={{0,8},{4,12},{8,0},{12,4},{1,9},{5,13},{9,1},{13,5},{2,10},{6,14},... | collective-permute-start | bytes 393224 | tf_op jit(solution)/shard_map/ppermute | solution.py:25
  65.4 5.8 %collective-permute-start.24 = (bf16[224,512]{1,0:T(8,128)(2,1)S(1)}, bf16[224,512]{1,0:T(8,128)(2,1)S(1)}, u32[]{:S(2)}, u32[]{:S(2)}) collective-permute-start(bf16[224,512]{1,0:T(8,128)(2,1)S(1)} %get-tuple-element.42), channel_id=1, source_target_pairs={{0,4},{4,0},{8,12},{12,8},{1,5},{5,1},{9,13},{13,9},{2,6},{6,2},{1... | collective-permute-start | bytes 688136 | tf_op jit(solution)/shard_map/ppermute | solution.py:25
  65.8 6.7 %collective-permute-start.19 = (bf16[224,512]{1,0:T(8,128)(2,1)S(1)}, bf16[224,512]{1,0:T(8,128)(2,1)S(1)}, u32[]{:S(2)}, u32[]{:S(2)}) collective-permute-start(bf16[224,512]{1,0:T(8,128)(2,1)S(1)} %get-tuple-element.35), channel_id=1, source_target_pairs={{0,4},{4,0},{8,12},{12,8},{1,5},{5,1},{9,13},{13,9},{2,6},{6,2},{1... | collective-permute-start | bytes 688136 | tf_op jit(solution)/shard_map/ppermute | solution.py:25
  66.0 4.4 %collective-permute-start.3 = (bf16[4,64,128]{2,1,0:T(8,128)(2,1)S(1)}, bf16[4,64,128]{2,1,0:T(8,128)(2,1)S(1)}, u32[]{:S(2)}, u32[]{:S(2)}) collective-permute-start(bf16[4,64,128]{2,1,0:T(8,128)(2,1)S(1)} %get-tuple-element.50.refs_1_), channel_id=1, source_target_pairs={{0,8},{4,12},{8,0},{12,4},{1,9},{5,13},{9,1},{13,5},{2,10},{6,14},... | collective-permute-start | bytes 196616 | tf_op jit(solution)/shard_map/ppermute | solution.py:25
  66.7 4.3 %collective-permute-start.4 = (bf16[4,64,128]{2,1,0:T(8,128)(2,1)S(1)}, bf16[4,64,128]{2,1,0:T(8,128)(2,1)S(1)}, u32[]{:S(2)}, u32[]{:S(2)}) collective-permute-start(bf16[4,64,128]{2,1,0:T(8,128)(2,1)S(1)} %get-tuple-element.50.refs_1_), channel_id=1, source_target_pairs={{0,4},{4,0},{8,12},{12,8},{1,5},{5,1},{9,13},{13,9},{2,6},{6,2},{1... | collective-permute-start | bytes 196616 | tf_op jit(solution)/shard_map/ppermute | solution.py:25
  70.4 8.5 %collective-permute-start.20 = (bf16[224,512]{1,0:T(8,128)(2,1)S(1)}, bf16[224,512]{1,0:T(8,128)(2,1)S(1)}, u32[]{:S(2)}, u32[]{:S(2)}) collective-permute-start(bf16[224,512]{1,0:T(8,128)(2,1)S(1)} %get-tuple-element.36), channel_id=1, source_target_pairs={{0,8},{4,12},{8,0},{12,4},{1,9},{5,13},{9,1},{13,5},{2,10},{6,14},... | collective-permute-start | bytes 688136 | tf_op jit(solution)/shard_map/ppermute | solution.py:25
  71.0 10.9 %collective-permute-start.21 = (bf16[224,512]{1,0:T(8,128)(2,1)S(1)}, bf16[224,512]{1,0:T(8,128)(2,1)S(1)}, u32[]{:S(2)}, u32[]{:S(2)}) collective-permute-start(bf16[224,512]{1,0:T(8,128)(2,1)S(1)} %get-tuple-element.37), channel_id=1, source_target_pairs={{0,12},{4,8},{8,4},{12,0},{1,13},{5,9},{9,5},{13,1},{2,14},{6,10},... | collective-permute-start | bytes 688136 | tf_op jit(solution)/shard_map/ppermute | solution.py:25
  71.2 20.1 %collective-permute-start.26 = (bf16[224,512]{1,0:T(8,128)(2,1)S(1)}, bf16[224,512]{1,0:T(8,128)(2,1)S(1)}, u32[]{:S(2)}, u32[]{:S(2)}) collective-permute-start(bf16[224,512]{1,0:T(8,128)(2,1)S(1)} %get-tuple-element.45), channel_id=1, source_target_pairs={{0,8},{4,12},{8,0},{12,4},{1,9},{5,13},{9,1},{13,5},{2,10},{6,14},... | collective-permute-start | bytes 688136 | tf_op jit(solution)/shard_map/ppermute | solution.py:25
  72.5 20.2 %collective-permute-start.25 = (bf16[224,512]{1,0:T(8,128)(2,1)S(1)}, bf16[224,512]{1,0:T(8,128)(2,1)S(1)}, u32[]{:S(2)}, u32[]{:S(2)}) collective-permute-start(bf16[224,512]{1,0:T(8,128)(2,1)S(1)} %get-tuple-element.44), channel_id=1, source_target_pairs={{0,12},{4,8},{8,4},{12,0},{1,13},{5,9},{9,5},{13,1},{2,14},{6,10},... | collective-permute-start | bytes 688136 | tf_op jit(solution)/shard_map/ppermute | solution.py:25
  78.9 5.6 %collective-permute-start.6 = (f32[4,64,128]{2,1,0:T(8,128)S(1)}, f32[4,64,128]{2,1,0:T(8,128)S(1)}, u32[]{:S(2)}, u32[]{:S(2)}) collective-permute-start(f32[4,64,128]{2,1,0:T(8,128)S(1)} %get-tuple-element.51.refs_5_), channel_id=1, source_target_pairs={{0,4},{4,0},{8,12},{12,8},{1,5},{5,1},{9,13},{13,9},{2,6},{6,2},{1... | collective-permute-start | bytes 393224 | tf_op jit(solution)/shard_map/ppermute | solution.py:25
  81.9 2.6 %collective-permute-start.5 = (bf16[4,64,128]{2,1,0:T(8,128)(2,1)S(1)}, bf16[4,64,128]{2,1,0:T(8,128)(2,1)S(1)}, u32[]{:S(2)}, u32[]{:S(2)}) collective-permute-start(bf16[4,64,128]{2,1,0:T(8,128)(2,1)S(1)} %collective-permute-done.3.refs_2_), channel_id=1, source_target_pairs={{0,4},{4,0},{8,12},{12,8},{1,5},{5,1},{9,13},{13,9},{2,6},{6,2},{1... | collective-permute-start | bytes 196616 | tf_op jit(solution)/shard_map/ppermute | solution.py:25

commit v6 on v5

--- a/solution.py
+++ b/solution.py
@@ -122,39 +122,42 @@
             out[i] = total - (2.0 / count) * target[i, :, at]
 
 
-def penalty_kernel(count, pieces, cut, first, info, own, partner, *refs):
-    blocks, refs = refs[:count - 2], refs[count - 2:]
-    if first:
-        harm, near, far = refs[0], refs[1], refs[2:2 + (count - 2) * pieces]
-        refs = refs[2 + len(far):]
-        outs, waves, sems = refs[:count], refs[count], refs[-1]
-        refs = refs[count + 1:-1]
-    else:
-        waves, outs, refs = refs[0], refs[1:count + 1], refs[count + 1:]
-    stack, turned, acc = refs
-    me, place = info[0], info[2]
+def stack_near_kernel(pieces, info, harm, near, waves, sems):
+    place = info[2]
+    height = near.shape[0]
+    width = waves.shape[1] // pieces
+    copies = []
+    for r in range(pieces):
+        spot = waves.at[0:height, r * width:(r + 1) * width]
+        copies.append(pltpu.make_async_copy(harm.at[:, aligned(place ^ r, width)], spot, sems.at[r]))
+        copies[-1].start()
+    for r in range(pieces):
+        waves[height:2 * height, r * width:(r + 1) * width] = near[:, aligned(place ^ r, width)]
+    for c in copies:
+        c.wait()
+
+
+def stack_far_kernel(pieces, _, *refs):
+    far, waves = refs[:-1], refs[-1]
+    height, width = far[0].shape
+    for n, ref in enumerate(far):
+        j, r = divmod(n, pieces)
+        waves[(j + 2) * height:(j + 3) * height, r * width:(r + 1) * width] = ref[...]
+
+
+def penalty_kernel(count, pieces, cut, info, waves, own, partner, *refs):
+    blocks, outs = refs[:count - 2], refs[count - 2:2 * count - 2]
+    stack, turned, acc = refs[2 * count - 2:]
     height = outs[0].shape[0]
     width = waves.shape[1] // pieces
-    if first:
-        copies = []
-        for r in range(pieces):
-            spot = waves.at[0:height, r * width:(r + 1) * width]
-            copies.append(pltpu.make_async_copy(harm.at[:, aligned(place ^ r, width)], spot, sems.at[r]))
-            copies[-1].start()
-    at = columns(me, own.shape[1] // count, cut)
+    at = columns(info[0], own.shape[1] // count, cut)
     stack[0:height, :] = own[:, at]
     stack[height:2 * height, :] = partner[:, at]
     for j in range(2, count):
         stack[j * height:(j + 1) * height, :] = blocks[j - 2][...]
     turned[...] = jnp.swapaxes(stack[...], 0, 1)
     for r in range(pieces):
-        span = slice(r * width, (r + 1) * width)
-        if first:
-            waves[height:2 * height, span] = near[:, aligned(place ^ r, width)]
-            for j in range(2, count):
-                waves[j * height:(j + 1) * height, span] = far[(j - 2) * pieces + r][...]
-            copies[r].wait()
-        wave = waves[:, span]
+        wave = waves[:, r * width:(r + 1) * width]
         field = dot(turned[...], wave, NN)
         slope = (0.5 * jnp.tanh(0.5 * field) - 0.5).astype(jnp.bfloat16)
         part = dot(wave, slope, NT)
@@ -296,8 +299,8 @@
     for t in range(len(cuts)):
         received.append([swap(parts[(m - 2) * len(cuts) + t], "coef", m) for m in range(2, count)])
     partner = swap(own, "coef", 1)
+    near = swap(harmonics, "coef", 1)
     table_partner = swap(table_other, "coef", 1)
-    near = swap(harmonics, "coef", 1)
     moves = [(0, 1)] * slab_bits + [(1, 0)] * group_bits + [(1, 1)] * (slab_bits * group_bits)
     for m in fetched:
         for up, along in moves:
@@ -334,26 +337,32 @@
             total = lax.dynamic_slice_in_dim(total, bit * width, width, 2)
         total = total + swap(send, "coef", mask)
 
+    wide = shape((count * coef_local, harmonics.shape[1]), bf16)
+    waves = kernel(
+        lambda *refs: stack_near_kernel(pieces, *refs),
+        [SMEM, HBM, VMEM],
+        VMEM,
+        wide,
+        [pltpu.SemaphoreType.DMA((pieces,))],
+    )(info, harm_far, near)
+    waves = kernel(
+        lambda *refs: stack_far_kernel(pieces, *refs), [VMEM] * (1 + len(far)), VMEM, wide, aliases={0: 0}
+    )(waves, *far)
+
     returned = []
-    waves = None
     for t, cut in enumerate(cuts):
         first = t == 0
-        extra = [harm_far, near] + far if first else [waves]
-        wide = [shape((count * coef_local, harmonics.shape[1]), bf16)] if first else []
         outs = kernel(
-            lambda *refs: penalty_kernel(count, pieces, cut, first, *refs),
-            [SMEM] + [VMEM] * count + ([HBM] + [VMEM] * (1 + len(far)) if first else [VMEM]),
-            [VMEM] * (count + len(wide)),
-            [shape((coef_local, cut[1]), bf16)] * count + wide,
+            lambda *refs: penalty_kernel(count, pieces, cut, *refs),
+            [SMEM] + [VMEM] * (count + 1),
+            [VMEM] * count,
+            [shape((coef_local, cut[1]), bf16)] * count,
             [
                 pltpu.VMEM((count * coef_local, cut[1]), bf16),
                 pltpu.VMEM((cut[1], count * coef_local), bf16),
                 pltpu.VMEM((count * coef_local, cut[1]), f32),
-            ]
-            + ([pltpu.SemaphoreType.DMA((pieces,))] if first else []),
-        )(info, own, partner, *received[t], *extra)
-        if first:
-            waves = outs[-1]
+            ],
+        )(info, waves, own, partner, *received[t])
         back = [outs[0]]
         for m in range(1, count):
             back.append(swap(outs[m], "coef", m))

time: 94.3 us -> 85.2 us (0.903)
  Pallas kernels: 38.3 us -> 34.1 us
  waiting for transfers between devices: 30.9 us -> 27.4 us
  starting transfers between devices: 22.3 us -> 20.3 us
    ppermute x24, waiting for transfers between devices: 25 us -> 22.6 us  [swap(): return lax.ppermute(value, axis, [(i, i ^ mask) for i in range(count)])]
    pallas_call x1, Pallas kernels: 6.82 us -> 5.51 us  [step_of(): kernel(lambda *refs: data_kernel(count, cuts, len(half_mine), *refs), [SM...]
    ppermute x24, starting transfers between devices: 15.7 us -> 14.4 us  [swap(): return lax.ppermute(value, axis, [(i, i ^ mask) for i in range(count)])]
    pallas_call x1, Pallas kernels: 4.36 us -> 3.13 us  [step_of(): kernel(lambda *refs: prepare_kernel(count, cuts, *refs), [SMEM, SMEM] + [...]
    ppermute x3, waiting for transfers between devices: 5.97 us -> 4.79 us  [step_of(): fetched[m].append(lax.ppermute(fetched[m][0], ('groups', 'slab'), pairs))]
    pallas_call x2 -> x4, Pallas kernels: 15.4 us -> 14.3 us  [the longest x2 12.3 us: step_of(): kernel(lambda *refs: penalty_kernel(count, pieces, cut, *refs), [SMEM] +...]
  transfers between devices with their start and end apart: 27 -> 27, of which waited for: 11 -> 12; matrix products, arithmetic and copies ran while one was open for 1% -> 1% of each run, Pallas kernels for 35% -> 35%
where the time goes in v6:
time: 85.2 us; the launch traced here: 84.9 us
  Pallas kernels  34.1 us (40%)
  waiting for transfers between devices  27.4 us (32%)
  starting transfers between devices  20.3 us (24%)
  local copies, waits for them, and re-layouts  2.32 us (3%)
    ppermute x24, waiting for transfers between devices, swap(): return lax.ppermute(value, axis, [(i, i ^ mask) for i in range(count)])  22.6 us
    ppermute x24, starting transfers between devices, swap(): return lax.ppermute(value, axis, [(i, i ^ mask) for i in range(count)])  14.4 us
    pallas_call x2, Pallas kernels, step_of(): kernel(lambda *refs: penalty_kernel(count, pieces, cut, *refs), [SMEM] +...  12.3 us
    ppermute x3, starting transfers between devices, step_of(): fetched[m].append(lax.ppermute(fetched[m][0], ('groups', 'slab'), pairs))  5.88 us
    pallas_call x1, Pallas kernels, step_of(): kernel(lambda *refs: data_kernel(count, cuts, len(half_mine), *refs), [SM...  5.51 us
    pallas_call x1, Pallas kernels, step_of(): kernel(build_kernel, [VMEM, VMEM], VMEM, shape((rows // 2, cols), bf16),...  5.16 us
    ppermute x3, waiting for transfers between devices, step_of(): fetched[m].append(lax.ppermute(fetched[m][0], ('groups', 'slab'), pairs))  4.79 us
    pallas_call x1, Pallas kernels, step_of(): kernel(lambda *refs: sums_kernel(count, *refs), [SMEM] + [VMEM] * 5 + [HB...  3.24 us
  transfers between devices with their start and end apart: 27, of which 12 were waited for; matrix products, arithmetic and copies ran while one was open for 1% of the time, Pallas kernels for 35%

profile of v6, /device:TPU:0, one launch (start us, length us, event | category | flops | bytes accessed | tf_op | source)
XLA Modules:
  0.0 84.9 jit_solution(2555307291536272679)
XLA Ops:
  0.6 0.1 pad_add_fusion.refs_0_
  0.7 3.1 %shard_map.86 = (bf16[224,512]{1,0:T(8,128)(2,1)S(1)}, bf16[224,512]{1,0:T(8,128)(2,1)S(1)}, bf16[224,512]{1,0:T(8,128)(2,1)S(1)}, bf16[224,512]{1,0:T(8,128)(2,...) custom-call(s32[3]{0:T(128)S(1)} %pad_add_fusion.refs_0_, ...), custom_call_target="tpu_custom_call" | custom-call | tf_op jit(solution)/shard_map/pallas_call | solution.py:288
  3.9 0.7 copy-done
  4.5 0.7 copy-done.1
  5.2 0.5 collective-permute-start
  5.7 1.0 %constant_dynamic-slice_fusion = bf16[224,512]{1,0:T(8,128)(2,1)S(1)} fusion(bf16[224,2048]{1,0:T(8,128)(2,1)} %refs_1_.3, s32[]{:T(128)S(6)} %select_n.3), kind=kLoop, calls=%fused_computation.1 | loop fusion | bytes 458756 | tf_op jit(solution)/shard_map/dynamic_slice | solution.py:285
  6.7 2.5 %collective-permute-start.9 = (bf16[224,512]{1,0:T(8,128)(2,1)S(1)}, bf16[224,512]{1,0:T(8,128)(2,1)S(1)}, u32[]{:S(2)}, u32[]{:S(2)}) collective-permute-start(bf16[224,512]{1,0:T(8,128)(2,1)S(1)} %constant_dynamic-slice_fusion), channel_id=1, source_target_pairs={{0,8},{4,12},{8,0},{12,4},{1,9},{5,13},{9,1},{13,5},{2,10},{6,14},... | collective-permute-start | bytes 688136 | tf_op jit(solution)/shard_map/ppermute | solution.py:25
  9.2 5.2 %shard_map.87.refs_1_.refs_9_ = bf16[256,4096]{1,0:T(8,128)(2,1)S(1)} custom-call(s32[256,128]{1,0:T(8,128)S(1)} %get-tuple-element.24.vox_ref, s32[256,128]{1,0:T(8,128)S(1)} %get-tuple-element.25.wgt_ref), custom_call_target="tpu_custom_call" | custom-call | tf_op jit(solution)/shard_map/pallas_call | solution.py:311
  14.4 0.3 collective-permute-start.7
  14.7 0.3 collective-permute-start.22
  15.0 0.5 collective-permute-done.9.refs_1_
  15.5 1.8 %collective-permute-start.10 = (bf16[224,512]{1,0:T(8,128)(2,1)S(1)}, bf16[224,512]{1,0:T(8,128)(2,1)S(1)}, u32[]{:S(2)}, u32[]{:S(2)}) collective-permute-start(bf16[224,512]{1,0:T(8,128)(2,1)S(1)} %collective-permute-done.9.refs_1_), channel_id=1, source_target_pairs={{0,1},{1,0},{2,3},{3,2},{16,17},{17,16},{18,19},{19,18},{4,5},{5,4... | collective-permute-start | bytes 688136 | tf_op jit(solution)/shard_map/ppermute | solution.py:309
  17.3 1.5 %collective-permute-start.11 = (bf16[224,512]{1,0:T(8,128)(2,1)S(1)}, bf16[224,512]{1,0:T(8,128)(2,1)S(1)}, u32[]{:S(2)}, u32[]{:S(2)}) collective-permute-start(bf16[224,512]{1,0:T(8,128)(2,1)S(1)} %collective-permute-done.9.refs_1_), channel_id=1, source_target_pairs={{0,16},{1,17},{2,18},{3,19},{16,0},{17,1},{18,2},{19,3},{4,20},{5,... | collective-permute-start | bytes 688136 | tf_op jit(solution)/shard_map/ppermute | solution.py:309
  18.8 3.8 %collective-permute-done.22.refs_4_ = bf16[224,512]{1,0:T(8,128)(2,1)S(1)} collective-permute-done((bf16[224,512]{1,0:T(8,128)(2,1)}, bf16[224,512]{1,0:T(8,128)(2,1)S(1)}, u32[]{:S(2)}, u32[]{:S(2)}) %collective-permute-start.22) | collective-permute-done | bytes 229408 | tf_op jit(solution)/shard_map/ppermute | solution.py:25
  22.7 2.5 %collective-permute-start.12 = (bf16[224,512]{1,0:T(8,128)(2,1)S(1)}, bf16[224,512]{1,0:T(8,128)(2,1)S(1)}, u32[]{:S(2)}, u32[]{:S(2)}) collective-permute-start(bf16[224,512]{1,0:T(8,128)(2,1)S(1)} %collective-permute-done.9.refs_1_), channel_id=1, source_target_pairs={{0,17},{1,16},{2,19},{3,18},{16,1},{17,0},{18,3},{19,2},{4,21},{5,... | collective-permute-start | bytes 688136 | tf_op jit(solution)/shard_map/ppermute | solution.py:309
  25.2 0.5 collective-permute-start.1
  25.7 4.8 %collective-permute-done.12.refs_4_ = bf16[224,512]{1,0:T(8,128)(2,1)S(1)} collective-permute-done((bf16[224,512]{1,0:T(8,128)(2,1)S(1)}, bf16[224,512]{1,0:T(8,128)(2,1)S(1)}, u32[]{:S(2)}, u32[]{:S(2)}) %collective-permute-start.12) | collective-permute-done | bytes 229408 | tf_op jit(solution)/shard_map/ppermute | solution.py:309
  30.5 1.5 %collective-permute-done.13.refs_5_ = bf16[224,512]{1,0:T(8,128)(2,1)S(1)} collective-permute-done((bf16[224,512]{1,0:T(8,128)(2,1)S(1)}, bf16[224,512]{1,0:T(8,128)(2,1)S(1)}, u32[]{:S(2)}, u32[]{:S(2)}) %collective-permute-start.13) | collective-permute-done | bytes 229408 | tf_op jit(solution)/shard_map/ppermute | solution.py:25
  32.0 0.1 collective-permute-start.14
  32.1 0.4 collective-permute-start.15
  32.5 1.0 %collective-permute-done.14.refs_6_ = bf16[224,512]{1,0:T(8,128)(2,1)S(1)} collective-permute-done((bf16[224,512]{1,0:T(8,128)(2,1)S(1)}, bf16[224,512]{1,0:T(8,128)(2,1)S(1)}, u32[]{:S(2)}, u32[]{:S(2)}) %collective-permute-start.14) | collective-permute-done | bytes 229408 | tf_op jit(solution)/shard_map/ppermute | solution.py:25
  33.5 0.1 collective-permute-start.16
  33.6 0.2 collective-permute-done.15.refs_7_
  33.8 0.2 collective-permute-start.23
  34.0 0.9 %collective-permute-done.16.refs_8_ = bf16[224,512]{1,0:T(8,128)(2,1)S(1)} collective-permute-done((bf16[224,512]{1,0:T(8,128)(2,1)S(1)}, bf16[224,512]{1,0:T(8,128)(2,1)S(1)}, u32[]{:S(2)}, u32[]{:S(2)}) %collective-permute-start.16) | collective-permute-done | bytes 229408 | tf_op jit(solution)/shard_map/ppermute | solution.py:25
  35.0 0.7 collective-permute-start.17
  35.7 0.8 collective-permute-start.18
  36.5 3.2 %shard_map.88 = (f32[4,64,128]{2,1,0:T(8,128)S(1)}, f32[4,64,128]{2,1,0:T(8,128)S(1)}) custom-call(s32[3]{0:T(128)S(1)} %pad_add_fusion.refs_0_, bf16[256,4096]{1,0:T(8,128)(2,1)S(1)} %shard_map.87.refs_1_.refs_9_, bf16[224,4096]{1,0:T(8,128)(2,1)S(1)} %get-tuple-element.26.refs_2_, bf16[224,4096]{1,0:T(8,128)(2,1)} %collective-permute-done.refs_3_, ...), custom_call_target="tpu_custom_call" | custom-call | tf_op jit(solution)/shard_map/pallas_call | solution.py:323
  39.7 0.9 %collective-permute-start.2 = (f32[4,64,128]{2,1,0:T(8,128)S(1)}, f32[4,64,128]{2,1,0:T(8,128)S(1)}, u32[]{:S(2)}, u32[]{:S(2)}) collective-permute-start(f32[4,64,128]{2,1,0:T(8,128)S(1)} %get-tuple-element.30), channel_id=1, source_target_pairs={{0,8},{4,12},{8,0},{12,4},{1,9},{5,13},{9,1},{13,5},{2,10},{6,14},... | collective-permute-start | bytes 393224 | tf_op jit(solution)/shard_map/ppermute | solution.py:25
  40.7 1.9 %shard_map.89.refs_0_ = bf16[896,2048]{1,0:T(8,128)(2,1)S(1)} custom-call(s32[3]{0:T(128)S(1)} %pad_add_fusion.refs_0_, bf16[224,2048]{1,0:T(8,128)(2,1)} %refs_1_.3, bf16[224,2048]{1,0:T(8,128)(2,1)S(1)} %collective-permute-done.8.refs_2_), custom_call_target="tpu_custom_call" | custom-call | tf_op jit(solution)/shard_map/pallas_call | solution.py:341
  42.5 0.1 shard_map.90.refs_1_
  42.7 6.2 %shard_map.92 = (bf16[224,512]{1,0:T(8,128)(2,1)S(1)}, bf16[224,512]{1,0:T(8,128)(2,1)S(1)}, bf16[224,512]{1,0:T(8,128)(2,1)S(1)}, bf16[224,512]{1,0:T(8,128)(2,1)S(1)}) custom-call(s32[3]{0:T(128)S(1)} %pad_add_fusion.refs_0_, bf16[896,2048]{1,0:T(8,128)(2,1)S(1)} %shard_map.90.refs_1_, bf16[224,4096]{1,0:T(8,128)(2,1)S(1)} %get-tuple-element.26.refs_2_, ...), custom_call_target="tpu_custom_call" | custom-call | tf_op jit(solution)/shard_map/pallas_call | solution.py:355
  48.8 0.3 collective-permute-start.24
  49.1 2.3 %collective-permute-done.18.refs_5_ = bf16[224,512]{1,0:T(8,128)(2,1)S(1)} collective-permute-done((bf16[224,512]{1,0:T(8,128)(2,1)S(1)}, bf16[224,512]{1,0:T(8,128)(2,1)S(1)}, u32[]{:S(2)}, u32[]{:S(2)}) %collective-permute-start.18) | collective-permute-done | bytes 229408 | tf_op jit(solution)/shard_map/ppermute | solution.py:25
  51.4 6.1 %shard_map.91 = (bf16[224,512]{1,0:T(8,128)(2,1)S(1)}, bf16[224,512]{1,0:T(8,128)(2,1)S(1)}, bf16[224,512]{1,0:T(8,128)(2,1)S(1)}, bf16[224,512]{1,0:T(8,128)(2,1)S(1)}) custom-call(s32[3]{0:T(128)S(1)} %pad_add_fusion.refs_0_, bf16[896,2048]{1,0:T(8,128)(2,1)S(1)} %shard_map.90.refs_1_, bf16[224,4096]{1,0:T(8,128)(2,1)S(1)} %get-tuple-element.26.refs_2_, ...), custom_call_target="tpu_custom_call" | custom-call | tf_op jit(solution)/shard_map/pallas_call | solution.py:355
  57.6 0.6 collective-permute-start.19
  58.2 0.5 collective-permute-start.3
  58.7 3.8 %collective-permute-done.3.refs_2_ = bf16[4,64,128]{2,1,0:T(8,128)(2,1)S(1)} collective-permute-done((bf16[4,64,128]{2,1,0:T(8,128)(2,1)S(1)}, bf16[4,64,128]{2,1,0:T(8,128)(2,1)S(1)}, u32[]{:S(2)}, u32[]{:S(2)}) %collective-permute-start.3) | collective-permute-done | bytes 65568 | tf_op jit(solution)/shard_map/ppermute | solution.py:25
  62.5 0.4 collective-permute-start.20
  63.0 1.7 %collective-permute-start.26 = (bf16[224,512]{1,0:T(8,128)(2,1)S(1)}, bf16[224,512]{1,0:T(8,128)(2,1)S(1)}, u32[]{:S(2)}, u32[]{:S(2)}) collective-permute-start(bf16[224,512]{1,0:T(8,128)(2,1)S(1)} %get-tuple-element.43), channel_id=1, source_target_pairs={{0,8},{4,12},{8,0},{12,4},{1,9},{5,13},{9,1},{13,5},{2,10},{6,14},... | collective-permute-start | bytes 688136 | tf_op jit(solution)/shard_map/ppermute | solution.py:25
  64.6 1.4 %collective-permute-start.25 = (bf16[224,512]{1,0:T(8,128)(2,1)S(1)}, bf16[224,512]{1,0:T(8,128)(2,1)S(1)}, u32[]{:S(2)}, u32[]{:S(2)}) collective-permute-start(bf16[224,512]{1,0:T(8,128)(2,1)S(1)} %get-tuple-element.42), channel_id=1, source_target_pairs={{0,12},{4,8},{8,4},{12,0},{1,13},{5,9},{9,5},{13,1},{2,14},{6,10},... | collective-permute-start | bytes 688136 | tf_op jit(solution)/shard_map/ppermute | solution.py:25
  66.0 5.0 %collective-permute-done.20.refs_14_ = bf16[224,512]{1,0:T(8,128)(2,1)S(1)} collective-permute-done((bf16[224,512]{1,0:T(8,128)(2,1)S(1)}, bf16[224,512]{1,0:T(8,128)(2,1)S(1)}, u32[]{:S(2)}, u32[]{:S(2)}) %collective-permute-start.20) | collective-permute-done | bytes 229408 | tf_op jit(solution)/shard_map/ppermute | solution.py:25
  71.0 2.6 %collective-permute-done.21.refs_15_ = bf16[224,512]{1,0:T(8,128)(2,1)S(1)} collective-permute-done((bf16[224,512]{1,0:T(8,128)(2,1)S(1)}, bf16[224,512]{1,0:T(8,128)(2,1)S(1)}, u32[]{:S(2)}, u32[]{:S(2)}) %collective-permute-start.21) | collective-permute-done | bytes 229408 | tf_op jit(solution)/shard_map/ppermute | solution.py:25
  73.6 2.2 %collective-permute-start.5 = (bf16[4,64,128]{2,1,0:T(8,128)(2,1)S(1)}, bf16[4,64,128]{2,1,0:T(8,128)(2,1)S(1)}, u32[]{:S(2)}, u32[]{:S(2)}) collective-permute-start(bf16[4,64,128]{2,1,0:T(8,128)(2,1)S(1)} %collective-permute-done.3.refs_2_), channel_id=1, source_target_pairs={{0,4},{4,0},{8,12},{12,8},{1,5},{5,1},{9,13},{13,9},{2,6},{6,2},{1... | collective-permute-start | bytes 196616 | tf_op jit(solution)/shard_map/ppermute | solution.py:25
  75.7 0.9 %collective-permute-done.5.refs_4_ = bf16[4,64,128]{2,1,0:T(8,128)(2,1)S(1)} collective-permute-done((bf16[4,64,128]{2,1,0:T(8,128)(2,1)S(1)}, bf16[4,64,128]{2,1,0:T(8,128)(2,1)S(1)}, u32[]{:S(2)}, u32[]{:S(2)}) %collective-permute-start.5) | collective-permute-done | bytes 65568 | tf_op jit(solution)/shard_map/ppermute | solution.py:25
  76.6 5.5 %shard_map.93 = (f32[224,4096]{1,0:T(8,128)}, f32[8,64,64]{2,1,0:T(8,128)}, f32[2,224,512]{2,1,0:T(8,128)S(1)}) custom-call(s32[3]{0:T(128)S(1)} %pad_add_fusion.refs_0_, bf16[4,64,128]{2,1,0:T(8,128)(2,1)S(1)} %get-tuple-element.48.refs_1_, bf16[4,64,128]{2,1,0:T(8,128)(2,1)S(1)} %collective-permute-done.3.refs_2_, ...), custom_call_target="tpu_custom_call" | custom-call | tf_op jit(solution)/shard_map/pallas_call | solution.py:384
  82.2 1.4 %shard_map.94.refs_3_ = f32[224,4096]{1,0:T(8,128)} custom-call(s32[3]{0:T(128)S(1)} %pad_add_fusion.refs_0_, f32[2,224,512]{2,1,0:T(8,128)S(1)} %get-tuple-element.41.refs_1_, bf16[224,512]{1,0:T(8,128)(2,1)S(1)} %collective-permute-done.26.refs_2_, f32[224,4096]{1,0:T(8,128)} %get-tuple-element.44.refs_3_), custom_call_target="tpu_custom_call", output_to_operand_aliasing={{}: (3, {})} | custom-call | tf_op jit(solution)/shard_map/pallas_call | solution.py:416
  83.6 1.4 %shard_map.95 = f32[224,4096]{1,0:T(8,128)} custom-call(s32[3]{0:T(128)S(1)} %pad_add_fusion.refs_0_, f32[2,224,512]{2,1,0:T(8,128)S(1)} %get-tuple-element.41.refs_1_, bf16[224,512]{1,0:T(8,128)(2,1)S(1)} %collective-permute-done.25.refs_2_, f32[224,4096]{1,0:T(8,128)} %shard_map.94.refs_3_), custom_call_target="tpu_custom_call", output_to_operand_aliasing={{}: (3, {})} | custom-call | tf_op jit(solution)/shard_map/pallas_call | solution.py:416
  (23 shorter events, 0.1 us)
Async XLA Ops:
  3.9 0.7 copy-start
  4.5 0.7 copy-start.1
  5.2 30.4 %collective-permute-start = (bf16[224,4096]{1,0:T(8,128)(2,1)S(1)}, bf16[224,4096]{1,0:T(8,128)(2,1)}, u32[]{:S(2)}, u32[]{:S(2)}) collective-permute-start(bf16[224,4096]{1,0:T(8,128)(2,1)S(1)} %get-tuple-element.26.refs_2_), channel_id=1, source_target_pairs={{0,4},{4,0},{8,12},{12,8},{1,5},{5,1},{9,13},{13,9},{2,6},{6,2},{1... | collective-permute-start | bytes 5505032 | tf_op jit(solution)/shard_map/ppermute | solution.py:25
  6.7 8.8 %collective-permute-start.9 = (bf16[224,512]{1,0:T(8,128)(2,1)S(1)}, bf16[224,512]{1,0:T(8,128)(2,1)S(1)}, u32[]{:S(2)}, u32[]{:S(2)}) collective-permute-start(bf16[224,512]{1,0:T(8,128)(2,1)S(1)} %constant_dynamic-slice_fusion), channel_id=1, source_target_pairs={{0,8},{4,12},{8,0},{12,4},{1,9},{5,13},{9,1},{13,5},{2,10},{6,14},... | collective-permute-start | bytes 688136 | tf_op jit(solution)/shard_map/ppermute | solution.py:25
  14.4 61.4 %collective-permute-start.7 = (bf16[256,4096]{1,0:T(8,128)(2,1)S(1)}, bf16[256,4096]{1,0:T(8,128)(2,1)S(1)}, u32[]{:S(2)}, u32[]{:S(2)}) collective-permute-start(bf16[256,4096]{1,0:T(8,128)(2,1)S(1)} %shard_map.87.refs_1_.refs_9_), channel_id=1, source_target_pairs={{0,4},{4,0},{8,12},{12,8},{1,5},{5,1},{9,13},{13,9},{2,6},{6,2},{1... | collective-permute-start | bytes 6291464 | tf_op jit(solution)/shard_map/ppermute | solution.py:25
  14.7 8.0 %collective-permute-start.22 = (bf16[224,512]{1,0:T(8,128)(2,1)}, bf16[224,512]{1,0:T(8,128)(2,1)S(1)}, u32[]{:S(2)}, u32[]{:S(2)}) collective-permute-start(bf16[224,512]{1,0:T(8,128)(2,1)} %copy-done.1), channel_id=1, source_target_pairs={{0,8},{4,12},{8,0},{12,4},{1,9},{5,13},{9,1},{13,5},{2,10},{6,14},... | collective-permute-start | bytes 688136 | tf_op jit(solution)/shard_map/ppermute | solution.py:25
  15.5 9.7 %collective-permute-start.10 = (bf16[224,512]{1,0:T(8,128)(2,1)S(1)}, bf16[224,512]{1,0:T(8,128)(2,1)S(1)}, u32[]{:S(2)}, u32[]{:S(2)}) collective-permute-start(bf16[224,512]{1,0:T(8,128)(2,1)S(1)} %collective-permute-done.9.refs_1_), channel_id=1, source_target_pairs={{0,1},{1,0},{2,3},{3,2},{16,17},{17,16},{18,19},{19,18},{4,5},{5,4... | collective-permute-start | bytes 688136 | tf_op jit(solution)/shard_map/ppermute | solution.py:309
  17.3 7.9 %collective-permute-start.11 = (bf16[224,512]{1,0:T(8,128)(2,1)S(1)}, bf16[224,512]{1,0:T(8,128)(2,1)S(1)}, u32[]{:S(2)}, u32[]{:S(2)}) collective-permute-start(bf16[224,512]{1,0:T(8,128)(2,1)S(1)} %collective-permute-done.9.refs_1_), channel_id=1, source_target_pairs={{0,16},{1,17},{2,18},{3,19},{16,0},{17,1},{18,2},{19,3},{4,20},{5,... | collective-permute-start | bytes 688136 | tf_op jit(solution)/shard_map/ppermute | solution.py:309
  22.7 7.8 %collective-permute-start.12 = (bf16[224,512]{1,0:T(8,128)(2,1)S(1)}, bf16[224,512]{1,0:T(8,128)(2,1)S(1)}, u32[]{:S(2)}, u32[]{:S(2)}) collective-permute-start(bf16[224,512]{1,0:T(8,128)(2,1)S(1)} %collective-permute-done.9.refs_1_), channel_id=1, source_target_pairs={{0,17},{1,16},{2,19},{3,18},{16,1},{17,0},{18,3},{19,2},{4,21},{5,... | collective-permute-start | bytes 688136 | tf_op jit(solution)/shard_map/ppermute | solution.py:309
  25.2 14.5 %collective-permute-start.8 = (bf16[224,2048]{1,0:T(8,128)(2,1)}, bf16[224,2048]{1,0:T(8,128)(2,1)S(1)}, u32[]{:S(2)}, u32[]{:S(2)}) collective-permute-start(bf16[224,2048]{1,0:T(8,128)(2,1)} %refs_1_.3), channel_id=1, source_target_pairs={{0,4},{4,0},{8,12},{12,8},{1,5},{5,1},{9,13},{13,9},{2,6},{6,2},{1... | collective-permute-start | bytes 2752520 | tf_op jit(solution)/shard_map/ppermute | solution.py:25
  25.2 6.9 %collective-permute-start.1 = (bf16[4,224,256]{2,1,0:T(8,128)(2,1)S(1)}, bf16[4,224,256]{2,1,0:T(8,128)(2,1)S(1)}, u32[]{:S(2)}, u32[]{:S(2)}) collective-permute-start(bf16[4,224,256]{2,1,0:T(8,128)(2,1)S(1)} %get-tuple-element.28.refs_8_), channel_id=1, source_target_pairs={{0,4},{4,0},{8,12},{12,8},{1,5},{5,1},{9,13},{13,9},{2,6},{6,2},{1... | collective-permute-start | bytes 1376264 | tf_op jit(solution)/shard_map/ppermute | solution.py:25
  30.5 1.5 %collective-permute-start.13 = (bf16[224,512]{1,0:T(8,128)(2,1)S(1)}, bf16[224,512]{1,0:T(8,128)(2,1)S(1)}, u32[]{:S(2)}, u32[]{:S(2)}) collective-permute-start(bf16[224,512]{1,0:T(8,128)(2,1)S(1)} %collective-permute-done.9.refs_1_), channel_id=1, source_target_pairs={{0,4},{4,0},{8,12},{12,8},{1,5},{5,1},{9,13},{13,9},{2,6},{6,2},{1... | collective-permute-start | bytes 688136 | tf_op jit(solution)/shard_map/ppermute | solution.py:25
  32.0 1.5 %collective-permute-start.14 = (bf16[224,512]{1,0:T(8,128)(2,1)S(1)}, bf16[224,512]{1,0:T(8,128)(2,1)S(1)}, u32[]{:S(2)}, u32[]{:S(2)}) collective-permute-start(bf16[224,512]{1,0:T(8,128)(2,1)S(1)} %collective-permute-done.10.refs_2_), channel_id=1, source_target_pairs={{0,4},{4,0},{8,12},{12,8},{1,5},{5,1},{9,13},{13,9},{2,6},{6,2},{1... | collective-permute-start | bytes 688136 | tf_op jit(solution)/shard_map/ppermute | solution.py:25
  32.1 1.7 %collective-permute-start.15 = (bf16[224,512]{1,0:T(8,128)(2,1)S(1)}, bf16[224,512]{1,0:T(8,128)(2,1)S(1)}, u32[]{:S(2)}, u32[]{:S(2)}) collective-permute-start(bf16[224,512]{1,0:T(8,128)(2,1)S(1)} %collective-permute-done.11.refs_3_), channel_id=1, source_target_pairs={{0,4},{4,0},{8,12},{12,8},{1,5},{5,1},{9,13},{13,9},{2,6},{6,2},{1... | collective-permute-start | bytes 688136 | tf_op jit(solution)/shard_map/ppermute | solution.py:25
  33.5 1.5 %collective-permute-start.16 = (bf16[224,512]{1,0:T(8,128)(2,1)S(1)}, bf16[224,512]{1,0:T(8,128)(2,1)S(1)}, u32[]{:S(2)}, u32[]{:S(2)}) collective-permute-start(bf16[224,512]{1,0:T(8,128)(2,1)S(1)} %collective-permute-done.12.refs_4_), channel_id=1, source_target_pairs={{0,4},{4,0},{8,12},{12,8},{1,5},{5,1},{9,13},{13,9},{2,6},{6,2},{1... | collective-permute-start | bytes 688136 | tf_op jit(solution)/shard_map/ppermute | solution.py:25
  33.8 8.8 %collective-permute-start.23 = (bf16[224,512]{1,0:T(8,128)(2,1)}, bf16[224,512]{1,0:T(8,128)(2,1)S(1)}, u32[]{:S(2)}, u32[]{:S(2)}) collective-permute-start(bf16[224,512]{1,0:T(8,128)(2,1)} %copy-done), channel_id=1, source_target_pairs={{0,12},{4,8},{8,4},{12,0},{1,13},{5,9},{9,5},{13,1},{2,14},{6,10},... | collective-permute-start | bytes 688136 | tf_op jit(solution)/shard_map/ppermute | solution.py:25
  35.0 14.1 %collective-permute-start.17 = (bf16[224,512]{1,0:T(8,128)(2,1)S(1)}, bf16[224,512]{1,0:T(8,128)(2,1)S(1)}, u32[]{:S(2)}, u32[]{:S(2)}) collective-permute-start(bf16[224,512]{1,0:T(8,128)(2,1)S(1)} %get-tuple-element.31), channel_id=1, source_target_pairs={{0,8},{4,12},{8,0},{12,4},{1,9},{5,13},{9,1},{13,5},{2,10},{6,14},... | collective-permute-start | bytes 688136 | tf_op jit(solution)/shard_map/ppermute | solution.py:25
  35.7 15.8 %collective-permute-start.18 = (bf16[224,512]{1,0:T(8,128)(2,1)S(1)}, bf16[224,512]{1,0:T(8,128)(2,1)S(1)}, u32[]{:S(2)}, u32[]{:S(2)}) collective-permute-start(bf16[224,512]{1,0:T(8,128)(2,1)S(1)} %get-tuple-element.32), channel_id=1, source_target_pairs={{0,12},{4,8},{8,4},{12,0},{1,13},{5,9},{9,5},{13,1},{2,14},{6,10},... | collective-permute-start | bytes 688136 | tf_op jit(solution)/shard_map/ppermute | solution.py:25
  39.7 18.4 %collective-permute-start.2 = (f32[4,64,128]{2,1,0:T(8,128)S(1)}, f32[4,64,128]{2,1,0:T(8,128)S(1)}, u32[]{:S(2)}, u32[]{:S(2)}) collective-permute-start(f32[4,64,128]{2,1,0:T(8,128)S(1)} %get-tuple-element.30), channel_id=1, source_target_pairs={{0,8},{4,12},{8,0},{12,4},{1,9},{5,13},{9,1},{13,5},{2,10},{6,14},... | collective-permute-start | bytes 393224 | tf_op jit(solution)/shard_map/ppermute | solution.py:25
  48.8 14.1 %collective-permute-start.24 = (bf16[224,512]{1,0:T(8,128)(2,1)S(1)}, bf16[224,512]{1,0:T(8,128)(2,1)S(1)}, u32[]{:S(2)}, u32[]{:S(2)}) collective-permute-start(bf16[224,512]{1,0:T(8,128)(2,1)S(1)} %get-tuple-element.40), channel_id=1, source_target_pairs={{0,4},{4,0},{8,12},{12,8},{1,5},{5,1},{9,13},{13,9},{2,6},{6,2},{1... | collective-permute-start | bytes 688136 | tf_op jit(solution)/shard_map/ppermute | solution.py:25
  57.6 7.1 %collective-permute-start.19 = (bf16[224,512]{1,0:T(8,128)(2,1)S(1)}, bf16[224,512]{1,0:T(8,128)(2,1)S(1)}, u32[]{:S(2)}, u32[]{:S(2)}) collective-permute-start(bf16[224,512]{1,0:T(8,128)(2,1)S(1)} %get-tuple-element.34), channel_id=1, source_target_pairs={{0,4},{4,0},{8,12},{12,8},{1,5},{5,1},{9,13},{13,9},{2,6},{6,2},{1... | collective-permute-start | bytes 688136 | tf_op jit(solution)/shard_map/ppermute | solution.py:25
  58.2 4.3 %collective-permute-start.3 = (bf16[4,64,128]{2,1,0:T(8,128)(2,1)S(1)}, bf16[4,64,128]{2,1,0:T(8,128)(2,1)S(1)}, u32[]{:S(2)}, u32[]{:S(2)}) collective-permute-start(bf16[4,64,128]{2,1,0:T(8,128)(2,1)S(1)} %get-tuple-element.48.refs_1_), channel_id=1, source_target_pairs={{0,8},{4,12},{8,0},{12,4},{1,9},{5,13},{9,1},{13,5},{2,10},{6,14},... | collective-permute-start | bytes 196616 | tf_op jit(solution)/shard_map/ppermute | solution.py:25
  58.7 4.3 %collective-permute-start.4 = (bf16[4,64,128]{2,1,0:T(8,128)(2,1)S(1)}, bf16[4,64,128]{2,1,0:T(8,128)(2,1)S(1)}, u32[]{:S(2)}, u32[]{:S(2)}) collective-permute-start(bf16[4,64,128]{2,1,0:T(8,128)(2,1)S(1)} %get-tuple-element.48.refs_1_), channel_id=1, source_target_pairs={{0,4},{4,0},{8,12},{12,8},{1,5},{5,1},{9,13},{13,9},{2,6},{6,2},{1... | collective-permute-start | bytes 196616 | tf_op jit(solution)/shard_map/ppermute | solution.py:25
  62.5 8.5 %collective-permute-start.20 = (bf16[224,512]{1,0:T(8,128)(2,1)S(1)}, bf16[224,512]{1,0:T(8,128)(2,1)S(1)}, u32[]{:S(2)}, u32[]{:S(2)}) collective-permute-start(bf16[224,512]{1,0:T(8,128)(2,1)S(1)} %get-tuple-element.35), channel_id=1, source_target_pairs={{0,8},{4,12},{8,0},{12,4},{1,9},{5,13},{9,1},{13,5},{2,10},{6,14},... | collective-permute-start | bytes 688136 | tf_op jit(solution)/shard_map/ppermute | solution.py:25
  63.0 10.6 %collective-permute-start.21 = (bf16[224,512]{1,0:T(8,128)(2,1)S(1)}, bf16[224,512]{1,0:T(8,128)(2,1)S(1)}, u32[]{:S(2)}, u32[]{:S(2)}) collective-permute-start(bf16[224,512]{1,0:T(8,128)(2,1)S(1)} %get-tuple-element.36), channel_id=1, source_target_pairs={{0,12},{4,8},{8,4},{12,0},{1,13},{5,9},{9,5},{13,1},{2,14},{6,10},... | collective-permute-start | bytes 688136 | tf_op jit(solution)/shard_map/ppermute | solution.py:25
  63.0 19.2 %collective-permute-start.26 = (bf16[224,512]{1,0:T(8,128)(2,1)S(1)}, bf16[224,512]{1,0:T(8,128)(2,1)S(1)}, u32[]{:S(2)}, u32[]{:S(2)}) collective-permute-start(bf16[224,512]{1,0:T(8,128)(2,1)S(1)} %get-tuple-element.43), channel_id=1, source_target_pairs={{0,8},{4,12},{8,0},{12,4},{1,9},{5,13},{9,1},{13,5},{2,10},{6,14},... | collective-permute-start | bytes 688136 | tf_op jit(solution)/shard_map/ppermute | solution.py:25
  64.6 18.9 %collective-permute-start.25 = (bf16[224,512]{1,0:T(8,128)(2,1)S(1)}, bf16[224,512]{1,0:T(8,128)(2,1)S(1)}, u32[]{:S(2)}, u32[]{:S(2)}) collective-permute-start(bf16[224,512]{1,0:T(8,128)(2,1)S(1)} %get-tuple-element.42), channel_id=1, source_target_pairs={{0,12},{4,8},{8,4},{12,0},{1,13},{5,9},{9,5},{13,1},{2,14},{6,10},... | collective-permute-start | bytes 688136 | tf_op jit(solution)/shard_map/ppermute | solution.py:25
  71.0 5.6 %collective-permute-start.6 = (f32[4,64,128]{2,1,0:T(8,128)S(1)}, f32[4,64,128]{2,1,0:T(8,128)S(1)}, u32[]{:S(2)}, u32[]{:S(2)}) collective-permute-start(f32[4,64,128]{2,1,0:T(8,128)S(1)} %get-tuple-element.49.refs_5_), channel_id=1, source_target_pairs={{0,4},{4,0},{8,12},{12,8},{1,5},{5,1},{9,13},{13,9},{2,6},{6,2},{1... | collective-permute-start | bytes 393224 | tf_op jit(solution)/shard_map/ppermute | solution.py:25
  73.6 3.1 %collective-permute-start.5 = (bf16[4,64,128]{2,1,0:T(8,128)(2,1)S(1)}, bf16[4,64,128]{2,1,0:T(8,128)(2,1)S(1)}, u32[]{:S(2)}, u32[]{:S(2)}) collective-permute-start(bf16[4,64,128]{2,1,0:T(8,128)(2,1)S(1)} %collective-permute-done.3.refs_2_), channel_id=1, source_target_pairs={{0,4},{4,0},{8,12},{12,8},{1,5},{5,1},{9,13},{13,9},{2,6},{6,2},{1... | collective-permute-start | bytes 196616 | tf_op jit(solution)/shard_map/ppermute | solution.py:25

commit v7 on v6

--- a/solution.py
+++ b/solution.py
@@ -12,7 +12,6 @@
 NT = (((1,), (1,)), ((), ()))
 NN = (((1,), (0,)), ((), ()))
 VMEM = pl.BlockSpec(memory_space=pltpu.VMEM)
-SMEM = pl.BlockSpec(memory_space=pltpu.SMEM)
 HBM = pl.BlockSpec(memory_space=pltpu.HBM)
 
 
@@ -37,14 +36,23 @@
     return [(start, unit * size) for start, size in zip(starts, QUARTERS)]
 
 
+def position():
+    me = lax.axis_index("coef")
+    place = jnp.zeros((), jnp.int32)
+    for axis in ("groups", "slab"):
+        if lax.axis_size(axis) % 2 == 0:
+            place = place * 2 + (lax.axis_index(axis) & 1)
+    return me, me & 1, place
+
+
 def columns(index, block, cut):
     return pl.ds(pl.multiple_of(index * block + cut[0], LANES), cut[1])
 
 
-def prepare_kernel(count, cuts, info, ids, coef, vox, wgt, table, *refs):
-    parts = refs[:(count - 2) * len(cuts)]
-    whole, vox_out, wgt_out, table_mine, table_other, stage, sems = refs[len(parts):]
-    me, side = info[0], info[1]
+def prepare_kernel(count, cuts, ids_far, coef, vox, wgt, table, *refs):
+    full, parts = refs[:count - 3], refs[count - 3:count - 3 + len(cuts)]
+    whole, vox_out, wgt_out, table_mine, table_other, stage, ids, sems = refs[count - 3 + len(cuts):]
+    me, side, _ = position()
     block = coef.shape[1] // count
     half_rows, half = vox_out.shape[0], table_mine.shape[0]
     order = list(range(2, count)) + [1, 0]
@@ -55,20 +63,25 @@
         pltpu.make_async_copy(vox.at[aligned(side, half_rows)], vox_out, sems.at[count]),
         pltpu.make_async_copy(wgt.at[aligned(side, half_rows)], wgt_out, sems.at[count + 1]),
     ]
+    numbers = pltpu.make_async_copy(ids_far, ids, sems.at[count + 2 + 2 * half])
+    numbers.start()
+    for m in order:
+        copies[m].start()
+    numbers.wait()
     for n, (out, first) in enumerate(((table_other, (1 - side) * half), (table_mine, side * half))):
         for i in range(half):
             rest.append(pltpu.make_async_copy(table.at[ids[first + i]], out.at[i], sems.at[count + 2 + n * half + i]))
-    for m in order:
-        copies[m].start()
     for c in rest:
         c.start()
     for m in order:
         copies[m].wait()
         values = stage[m].astype(jnp.bfloat16)
         whole[:, aligned(me ^ m, block)] = values
-        if m > 1:
+        if 1 < m < count - 1:
+            full[m - 2][...] = values
+        if m == count - 1:
             for t, cut in enumerate(cuts):
-                parts[(m - 2) * len(cuts) + t][...] = values[:, cut[0]:cut[0] + cut[1]]
+                parts[t][...] = values[:, cut[0]:cut[0] + cut[1]]
     for c in rest:
         c.wait()
 
@@ -105,9 +118,9 @@
     lax.fori_loop(0, rows // GROUP, build, 0)
 
 
-def sums_kernel(count, info, matrix_ref, own, partner, table_own, table_partner, measured, keep, send, target, sem):
+def sums_kernel(count, matrix_ref, own, partner, table_own, table_partner, measured, keep, send, target, sem):
     half, rays, width = keep.shape
-    me, side = info[0], info[1]
+    me, side, _ = position()
     fetch = pltpu.make_async_copy(measured.at[pl.ds(side * half, half)], target, sem)
     fetch.start()
     sums_own = dot(matrix_ref[...], own[...], NT).astype(jnp.bfloat16)
@@ -122,39 +135,30 @@
             out[i] = total - (2.0 / count) * target[i, :, at]
 
 
-def stack_near_kernel(pieces, info, harm, near, waves, sems):
-    place = info[2]
+def stack_kernel(pieces, own, near, *refs):
+    far, waves = refs[:-1], refs[-1]
+    place = position()[2]
     height = near.shape[0]
     width = waves.shape[1] // pieces
-    copies = []
     for r in range(pieces):
-        spot = waves.at[0:height, r * width:(r + 1) * width]
-        copies.append(pltpu.make_async_copy(harm.at[:, aligned(place ^ r, width)], spot, sems.at[r]))
-        copies[-1].start()
-    for r in range(pieces):
-        waves[height:2 * height, r * width:(r + 1) * width] = near[:, aligned(place ^ r, width)]
-    for c in copies:
-        c.wait()
-
-
-def stack_far_kernel(pieces, _, *refs):
-    far, waves = refs[:-1], refs[-1]
-    height, width = far[0].shape
-    for n, ref in enumerate(far):
-        j, r = divmod(n, pieces)
-        waves[(j + 2) * height:(j + 3) * height, r * width:(r + 1) * width] = ref[...]
-
-
-def penalty_kernel(count, pieces, cut, info, waves, own, partner, *refs):
+        span = slice(r * width, (r + 1) * width)
+        waves[0:height, span] = own[:, aligned(place ^ r, width)]
+        waves[height:2 * height, span] = near[:, aligned(place ^ r, width)]
+        for j in range(len(far) // pieces):
+            waves[(j + 2) * height:(j + 3) * height, span] = far[j * pieces + r][...]
+
+
+def penalty_kernel(count, pieces, cut, waves, own, partner, *refs):
     blocks, outs = refs[:count - 2], refs[count - 2:2 * count - 2]
     stack, turned, acc = refs[2 * count - 2:]
     height = outs[0].shape[0]
     width = waves.shape[1] // pieces
-    at = columns(info[0], own.shape[1] // count, cut)
+    at = columns(position()[0], own.shape[1] // count, cut)
     stack[0:height, :] = own[:, at]
     stack[height:2 * height, :] = partner[:, at]
     for j in range(2, count):
-        stack[j * height:(j + 1) * height, :] = blocks[j - 2][...]
+        start = 0 if j == count - 1 else cut[0]
+        stack[j * height:(j + 1) * height, :] = blocks[j - 2][:, start:start + cut[1]]
     turned[...] = jnp.swapaxes(stack[...], 0, 1)
     for r in range(pieces):
         wave = waves[:, r * width:(r + 1) * width]
@@ -170,7 +174,7 @@
                 outs[j][...] = part[j * height:(j + 1) * height].astype(outs[j].dtype)
 
 
-def data_kernel(count, cuts, split, info, *refs):
+def data_kernel(count, cuts, split, *refs):
     halves, refs = (refs[:split], refs[split:2 * split]), refs[2 * split:]
     res_mine, res_other, table_mine, table_other, top_ref, low_ref, coef = refs[:7]
     refs = refs[7:]
@@ -179,7 +183,7 @@
     grads, refs = dict(zip(ready, refs)), refs[len(ready):]
     updated, residual_ref, later = refs[0], refs[1], refs[2:1 + len(cuts)]
     back_a, back_b, buf, sems, out_sems = refs[1 + len(cuts):]
-    me, side = info[0], info[1]
+    me, side, _ = position()
     half, rays, width = halves[0][0].shape
     block = coef.shape[1] // count
     own_width = residual_ref.shape[2]
@@ -219,14 +223,14 @@
         w.wait()
 
 
-def finish_kernel(count, cut, masks, info, later, *refs):
+def finish_kernel(count, cut, masks, later, *refs):
     grads = refs[:len(masks)]
     _, updated, buf, sems = refs[len(masks):]
     block = updated.shape[1] // count
     writes = []
     for n, j in enumerate(masks):
         buf[n] = later[j - 2] - 0.5 * grads[n][...].astype(jnp.float32)
-        at = columns(info[0] ^ j, block, cut)
+        at = columns(position()[0] ^ j, block, cut)
         writes.append(pltpu.make_async_copy(buf.at[n], updated.at[:, at], sems.at[n]))
         writes[-1].start()
     for w in writes:
@@ -261,15 +265,10 @@
     slab_count = lax.axis_size("slab")
     slab_bits = 1 if slab_count % 2 == 0 else 0
     pieces = 1 << (group_bits + slab_bits)
-    place = jnp.zeros((), jnp.int32)
-    if slab_bits:
-        place = place + (lax.axis_index("slab") & 1)
-    if group_bits:
-        place = place + ((lax.axis_index("groups") & 1) << slab_bits)
+    place = position()[2]
     width = harmonics.shape[1] // pieces
-    info = jnp.stack([me, me & 1, place]).astype(jnp.int32)
     rows_shape = (rows, samples)
-    coef_far, measured_far, vox_far, wgt_far, ids_far, table_far, harm_far = [
+    coef_far, measured_far, vox_far, wgt_far, ids_far, table_far = [
         pltpu.with_memory_space_constraint(v, pltpu.HBM)
         for v in (
             coefficients,
@@ -278,7 +277,6 @@
             ray_weights.reshape(rows_shape),
             angle_ids,
             angle_table,
-            harmonics,
         )
     ]
 
@@ -287,17 +285,24 @@
     table_shape = shape((half,) + angle_table.shape[1:], bf16)
     *parts, own, vox, wgt, table_mine, table_other = kernel(
         lambda *refs: prepare_kernel(count, cuts, *refs),
-        [SMEM, SMEM] + [HBM] * 4,
-        [VMEM] * ((count - 2) * len(cuts) + 5),
-        [shape((coef_local, cut[1]), bf16) for _ in range(2, count) for cut in cuts]
+        [HBM] * 5,
+        [VMEM] * (count + len(cuts) + 2),
+        [shape((coef_local, block), bf16)] * (count - 3)
+        + [shape((coef_local, cut[1]), bf16) for cut in cuts]
         + [shape((coef_local, cols), bf16)]
         + [shape((rows // 2, samples), jnp.int32)] * 2
         + [table_shape] * 2,
-        [pltpu.VMEM((count, coef_local, block), f32), pltpu.SemaphoreType.DMA((count + 2 + projections,))],
-    )(info, ids_far, coef_far, vox_far, wgt_far, table_far)
+        [
+            pltpu.VMEM((count, coef_local, block), f32),
+            pltpu.SMEM(angle_ids.shape, jnp.int32),
+            pltpu.SemaphoreType.DMA((count + 3 + projections,)),
+        ],
+    )(ids_far, coef_far, vox_far, wgt_far, table_far)
     received = []
     for t in range(len(cuts)):
-        received.append([swap(parts[(m - 2) * len(cuts) + t], "coef", m) for m in range(2, count)])
+        if t == 0:
+            early = [swap(parts[m - 2], "coef", m) for m in range(2, count - 1)]
+        received.append(early + [swap(parts[count - 3 + t], "coef", count - 1)])
     partner = swap(own, "coef", 1)
     near = swap(harmonics, "coef", 1)
     table_partner = swap(table_other, "coef", 1)
@@ -317,16 +322,18 @@
     )(vox, wgt)
     low = swap(top, "coef", 1)
     for m in list(fetched):
-        fetched[m ^ 1] = [swap(v, "coef", 1) for v in fetched[m]]
+        fetched[m ^ 1] = []
+        for value in fetched[m]:
+            fetched[m ^ 1].append(swap(value, "coef", 1))
     far = [v for m in range(2, count) for v in fetched[m]]
 
     total, send = kernel(
         lambda *refs: sums_kernel(count, *refs),
-        [SMEM] + [VMEM] * 5 + [HBM],
+        [VMEM] * 5 + [HBM],
         [VMEM, VMEM],
         [shape((half, rays, channels // 2), f32)] * 2,
         [pltpu.VMEM((half, rays, channels), f32), pltpu.SemaphoreType.DMA(())],
-    )(info, top, own, partner, table_mine, table_partner, measured_far)
+    )(top, own, partner, table_mine, table_partner, measured_far)
 
     masks = [1 << n for n in range(1, count.bit_length() - 1)]
     for mask in masks[::-1]:
@@ -339,22 +346,15 @@
 
     wide = shape((count * coef_local, harmonics.shape[1]), bf16)
     waves = kernel(
-        lambda *refs: stack_near_kernel(pieces, *refs),
-        [SMEM, HBM, VMEM],
-        VMEM,
-        wide,
-        [pltpu.SemaphoreType.DMA((pieces,))],
-    )(info, harm_far, near)
-    waves = kernel(
-        lambda *refs: stack_far_kernel(pieces, *refs), [VMEM] * (1 + len(far)), VMEM, wide, aliases={0: 0}
-    )(waves, *far)
+        lambda *refs: stack_kernel(pieces, *refs), [VMEM] * (2 + len(far)), VMEM, wide
+    )(harmonics, near, *far)
 
     returned = []
     for t, cut in enumerate(cuts):
         first = t == 0
         outs = kernel(
             lambda *refs: penalty_kernel(count, pieces, cut, *refs),
-            [SMEM] + [VMEM] * (count + 1),
+            [VMEM] * (count + 1),
             [VMEM] * count,
             [shape((coef_local, cut[1]), bf16)] * count,
             [
@@ -362,7 +362,7 @@
                 pltpu.VMEM((cut[1], count * coef_local), bf16),
                 pltpu.VMEM((count * coef_local, cut[1]), f32),
             ],
-        )(info, waves, own, partner, *received[t])
+        )(waves, own, partner, *received[t])
         back = [outs[0]]
         for m in range(1, count):
             back.append(swap(outs[m], "coef", m))
@@ -383,7 +383,7 @@
     ready = [(t, j) for t in range(len(cuts)) for j in range(count) if t == 0 or j < 2]
     updated, residual, *later = kernel(
         lambda *refs: data_kernel(count, cuts, len(half_mine), *refs),
-        [SMEM] + [VMEM] * (2 * len(half_mine) + 6) + [HBM] + [VMEM] * len(ready),
+        [VMEM] * (2 * len(half_mine) + 6) + [HBM] + [VMEM] * len(ready),
         [HBM] + [VMEM] * len(cuts),
         [shape((coef_local, cols), f32), shape((projections, rays, channels // count), f32)]
         + [shape((count - 2, coef_local, cut[1]), f32) for cut in cuts[1:]],
@@ -395,7 +395,6 @@
             pltpu.SemaphoreType.DMA((len(ready),)),
         ],
     )(
-        info,
         *half_mine,
         *half_other,
         total,
@@ -415,12 +414,12 @@
                 continue
             updated = kernel(
                 lambda *refs: finish_kernel(count, cut, masks, *refs),
-                [SMEM] + [VMEM] * (len(masks) + 1) + [HBM],
+                [VMEM] * (len(masks) + 1) + [HBM],
                 HBM,
                 shape((coef_local, cols), f32),
                 [pltpu.VMEM((len(masks), coef_local, cut[1]), f32), pltpu.SemaphoreType.DMA((len(masks),))],
-                aliases={len(masks) + 2: 0},
-            )(info, later[t - 1], *[returned[t][m] for m in masks], updated)
+                aliases={len(masks) + 1: 0},
+            )(later[t - 1], *[returned[t][m] for m in masks], updated)
     return (updated, residual[:, None])
 
 

time: 85.2 us -> 90.3 us (1.060)
  waiting for transfers between devices: 27.4 us -> 36.4 us
  Pallas kernels: 34.1 us -> 31.3 us
    ppermute x3, waiting for transfers between devices: 4.79 us -> 10 us  [step_of(): fetched[m].append(lax.ppermute(fetched[m][0], ('groups', 'slab'), pairs))]
    ppermute x24 -> x23, waiting for transfers between devices: 22.6 us -> 26.4 us  [swap(): return lax.ppermute(value, axis, [(i, i ^ mask) for i in range(count)])]
    pallas_call x9 -> x8, Pallas kernels: 28.9 us -> 26.1 us  [the longest x2 12.2 us: step_of(): kernel(lambda *refs: penalty_kernel(count, pieces, cut, *refs), [VMEM] *...]
    ppermute x3, starting transfers between devices: 5.88 us -> 3.49 us  [step_of(): fetched[m].append(lax.ppermute(fetched[m][0], ('groups', 'slab'), pairs))]
    ppermute x24 -> x23, starting transfers between devices: 14.4 us -> 16.2 us  [swap(): return lax.ppermute(value, axis, [(i, i ^ mask) for i in range(count)])]
    dynamic_slice x1, local copies, waits for them, and re-layouts: 0.95 us -> 0.02 us  [step_of(): piece = lax.dynamic_slice_in_dim(harmonics, place * width, width, 1)]
  transfers between devices with their start and end apart: 27 -> 26, of which waited for: 12 -> 12; matrix products, arithmetic and copies ran while one was open for 1% -> 0% of each run, Pallas kernels for 35% -> 31%
where the time goes in v7:
time: 90.3 us; the launch traced here: 89.7 us
  waiting for transfers between devices  36.4 us (40%)
  Pallas kernels  31.3 us (35%)
  starting transfers between devices  19.6 us (22%)
  local copies, waits for them, and re-layouts  1.58 us (2%)
    ppermute x23, waiting for transfers between devices, swap(): return lax.ppermute(value, axis, [(i, i ^ mask) for i in range(count)])  26.4 us
    ppermute x23, starting transfers between devices, swap(): return lax.ppermute(value, axis, [(i, i ^ mask) for i in range(count)])  16.2 us
    pallas_call x2, Pallas kernels, step_of(): kernel(lambda *refs: penalty_kernel(count, pieces, cut, *refs), [VMEM] *...  12.2 us
    ppermute x3, waiting for transfers between devices, step_of(): fetched[m].append(lax.ppermute(fetched[m][0], ('groups', 'slab'), pairs))  10 us
    pallas_call x1, Pallas kernels, step_of(): kernel(lambda *refs: data_kernel(count, cuts, len(half_mine), *refs), [VM...  5.2 us
    pallas_call x1, Pallas kernels, step_of(): kernel(build_kernel, [VMEM, VMEM], VMEM, shape((rows // 2, cols), bf16),...  5.16 us
    pallas_call x1, Pallas kernels, step_of(): kernel(lambda *refs: sums_kernel(count, *refs), [VMEM] * 5 + [HBM], [VMEM...  4 us
    ppermute x3, starting transfers between devices, step_of(): fetched[m].append(lax.ppermute(fetched[m][0], ('groups', 'slab'), pairs))  3.49 us
  transfers between devices with their start and end apart: 26, of which 12 were waited for; matrix products, arithmetic and copies ran while one was open for 0% of the time, Pallas kernels for 31%

profile of v7, /device:TPU:0, one launch (start us, length us, event | category | flops | bytes accessed | tf_op | source)
XLA Modules:
  0.0 89.7 jit_solution(14545739224825518603)
XLA Ops:
  0.6 2.7 %shard_map.86 = (bf16[224,1024]{1,0:T(8,128)(2,1)S(1)}, bf16[224,512]{1,0:T(8,128)(2,1)S(1)}, bf16[224,512]{1,0:T(8,128)(2,1)S(1)}, bf16[224,4096]{1,0:T(8,128)(...) custom-call(s32[8]{0:T(128)} %refs_0_.2, ...), custom_call_target="tpu_custom_call" | custom-call | tf_op jit(solution)/shard_map/pallas_call | solution.py:286
  3.4 0.0 copy-start.1
  3.4 0.8 copy-done.1
  4.1 0.8 copy-done.3
  4.9 0.5 collective-permute-start
  5.5 2.7 %collective-permute-start.9 = (bf16[224,512]{1,0:T(8,128)(2,1)S(1)}, bf16[224,512]{1,0:T(8,128)(2,1)S(1)}, u32[]{:S(2)}, u32[]{:S(2)}) collective-permute-start(bf16[224,512]{1,0:T(8,128)(2,1)S(1)} %constant_dynamic-slice_fusion), channel_id=1, source_target_pairs={{0,8},{4,12},{8,0},{12,4},{1,9},{5,13},{9,1},{13,5},{2,10},{6,14},... | collective-permute-start | bytes 688136 | tf_op jit(solution)/shard_map/ppermute | solution.py:24
  8.1 5.2 %shard_map.87.refs_0_.refs_8_ = bf16[256,4096]{1,0:T(8,128)(2,1)S(1)} custom-call(s32[256,128]{1,0:T(8,128)S(1)} %get-tuple-element.23.vox_ref, s32[256,128]{1,0:T(8,128)S(1)} %get-tuple-element.24.wgt_ref), custom_call_target="tpu_custom_call" | custom-call | tf_op jit(solution)/shard_map/pallas_call | solution.py:316
  13.3 0.2 collective-permute-start.7
  13.5 0.8 collective-permute-done.9.refs_2_
  14.3 1.8 %collective-permute-start.10 = (bf16[224,512]{1,0:T(8,128)(2,1)S(1)}, bf16[224,512]{1,0:T(8,128)(2,1)S(1)}, u32[]{:S(2)}, u32[]{:S(2)}) collective-permute-start(bf16[224,512]{1,0:T(8,128)(2,1)S(1)} %collective-permute-done.9.refs_2_), channel_id=1, source_target_pairs={{0,1},{1,0},{2,3},{3,2},{16,17},{17,16},{18,19},{19,18},{4,5},{5,4... | collective-permute-start | bytes 688136 | tf_op jit(solution)/shard_map/ppermute | solution.py:314
  16.1 1.5 %collective-permute-start.11 = (bf16[224,512]{1,0:T(8,128)(2,1)S(1)}, bf16[224,512]{1,0:T(8,128)(2,1)S(1)}, u32[]{:S(2)}, u32[]{:S(2)}) collective-permute-start(bf16[224,512]{1,0:T(8,128)(2,1)S(1)} %collective-permute-done.9.refs_2_), channel_id=1, source_target_pairs={{0,16},{1,17},{2,18},{3,19},{16,0},{17,1},{18,2},{19,3},{4,20},{5,... | collective-permute-start | bytes 688136 | tf_op jit(solution)/shard_map/ppermute | solution.py:314
  17.6 0.1 collective-permute-start.12
  17.8 5.0 %collective-permute-done.10.refs_3_ = bf16[224,512]{1,0:T(8,128)(2,1)S(1)} collective-permute-done((bf16[224,512]{1,0:T(8,128)(2,1)S(1)}, bf16[224,512]{1,0:T(8,128)(2,1)S(1)}, u32[]{:S(2)}, u32[]{:S(2)}) %collective-permute-start.10) | collective-permute-done | bytes 229408 | tf_op jit(solution)/shard_map/ppermute | solution.py:314
  22.7 0.0 collective-permute-start.1
  22.7 5.0 %collective-permute-done.11.refs_4_ = bf16[224,512]{1,0:T(8,128)(2,1)S(1)} collective-permute-done((bf16[224,512]{1,0:T(8,128)(2,1)S(1)}, bf16[224,512]{1,0:T(8,128)(2,1)S(1)}, u32[]{:S(2)}, u32[]{:S(2)}) %collective-permute-start.11) | collective-permute-done | bytes 229408 | tf_op jit(solution)/shard_map/ppermute | solution.py:314
  27.8 0.5 collective-permute-start.13
  28.3 2.3 %collective-permute-done.13.refs_6_ = bf16[224,512]{1,0:T(8,128)(2,1)S(1)} collective-permute-done((bf16[224,512]{1,0:T(8,128)(2,1)S(1)}, bf16[224,512]{1,0:T(8,128)(2,1)S(1)}, u32[]{:S(2)}, u32[]{:S(2)}) %collective-permute-start.13) | collective-permute-done | bytes 229408 | tf_op jit(solution)/shard_map/ppermute | solution.py:24
  30.6 0.1 collective-permute-start.14
  30.7 0.4 collective-permute-start.15
  31.1 1.0 %collective-permute-done.14.refs_7_ = bf16[224,512]{1,0:T(8,128)(2,1)S(1)} collective-permute-done((bf16[224,512]{1,0:T(8,128)(2,1)S(1)}, bf16[224,512]{1,0:T(8,128)(2,1)S(1)}, u32[]{:S(2)}, u32[]{:S(2)}) %collective-permute-start.14) | collective-permute-done | bytes 229408 | tf_op jit(solution)/shard_map/ppermute | solution.py:24
  32.0 0.1 collective-permute-start.16
  32.2 0.2 collective-permute-done.15.refs_8_
  32.4 1.5 %collective-permute-start.17 = (bf16[224,1024]{1,0:T(8,128)(2,1)}, bf16[224,1024]{1,0:T(8,128)(2,1)S(1)}, u32[]{:S(2)}, u32[]{:S(2)}) collective-permute-start(bf16[224,1024]{1,0:T(8,128)(2,1)} %copy-done.3), channel_id=1, source_target_pairs={{0,8},{4,12},{8,0},{12,4},{1,9},{5,13},{9,1},{13,5},{2,10},{6,14},... | collective-permute-start | bytes 1376264 | tf_op jit(solution)/shard_map/ppermute | solution.py:24
  33.9 0.9 %collective-permute-start.22 = (bf16[224,512]{1,0:T(8,128)(2,1)}, bf16[224,512]{1,0:T(8,128)(2,1)S(1)}, u32[]{:S(2)}, u32[]{:S(2)}) collective-permute-start(bf16[224,512]{1,0:T(8,128)(2,1)} %copy-done.5), channel_id=1, source_target_pairs={{0,12},{4,8},{8,4},{12,0},{1,13},{5,9},{9,5},{13,1},{2,14},{6,10},... | collective-permute-start | bytes 688136 | tf_op jit(solution)/shard_map/ppermute | solution.py:24
  34.8 0.8 collective-permute-start.18
  35.6 4.0 %shard_map.88 = (f32[4,64,128]{2,1,0:T(8,128)S(1)}, f32[4,64,128]{2,1,0:T(8,128)S(1)}) custom-call(bf16[256,4096]{1,0:T(8,128)(2,1)S(1)} %shard_map.87.refs_0_.refs_8_, bf16[224,4096]{1,0:T(8,128)(2,1)S(1)} %get-tuple-element.25.refs_1_, bf16[224,4096]{1,0:T(8,128)(2,1)} %collective-permute-done.refs_2_, ...), custom_call_target="tpu_custom_call" | custom-call | tf_op jit(solution)/shard_map/pallas_call | solution.py:330
  39.6 1.2 %collective-permute-start.2 = (f32[4,64,128]{2,1,0:T(8,128)S(1)}, f32[4,64,128]{2,1,0:T(8,128)S(1)}, u32[]{:S(2)}, u32[]{:S(2)}) collective-permute-start(f32[4,64,128]{2,1,0:T(8,128)S(1)} %get-tuple-element.29), channel_id=1, source_target_pairs={{0,8},{4,12},{8,0},{12,4},{1,9},{5,13},{9,1},{13,5},{2,10},{6,14},... | collective-permute-start | bytes 393224 | tf_op jit(solution)/shard_map/ppermute | solution.py:24
  40.8 0.3 shard_map.89.refs_0_
  41.2 8.8 %collective-permute-done.22.refs_4_ = bf16[224,512]{1,0:T(8,128)(2,1)S(1)} collective-permute-done((bf16[224,512]{1,0:T(8,128)(2,1)}, bf16[224,512]{1,0:T(8,128)(2,1)S(1)}, u32[]{:S(2)}, u32[]{:S(2)}) %collective-permute-start.22) | collective-permute-done | bytes 229408 | tf_op jit(solution)/shard_map/ppermute | solution.py:24
  50.0 6.1 %shard_map.91 = (bf16[224,512]{1,0:T(8,128)(2,1)S(1)}, bf16[224,512]{1,0:T(8,128)(2,1)S(1)}, bf16[224,512]{1,0:T(8,128)(2,1)S(1)}, bf16[224,512]{1,0:T(8,128)(2,1)S(1)}) custom-call(bf16[896,2048]{1,0:T(8,128)(2,1)S(1)} %shard_map.89.refs_0_, bf16[224,4096]{1,0:T(8,128)(2,1)S(1)} %get-tuple-element.25.refs_1_, ...), custom_call_target="tpu_custom_call" | custom-call | tf_op jit(solution)/shard_map/pallas_call | solution.py:355
  56.1 0.0 copy-start.2
  56.1 1.1 %collective-permute-start.23 = (bf16[224,512]{1,0:T(8,128)(2,1)S(1)}, bf16[224,512]{1,0:T(8,128)(2,1)S(1)}, u32[]{:S(2)}, u32[]{:S(2)}) collective-permute-start(bf16[224,512]{1,0:T(8,128)(2,1)S(1)} %get-tuple-element.38), channel_id=1, source_target_pairs={{0,4},{4,0},{8,12},{12,8},{1,5},{5,1},{9,13},{13,9},{2,6},{6,2},{1... | collective-permute-start | bytes 688136 | tf_op jit(solution)/shard_map/ppermute | solution.py:24
  57.2 6.1 %shard_map.90 = (bf16[224,512]{1,0:T(8,128)(2,1)S(1)}, bf16[224,512]{1,0:T(8,128)(2,1)S(1)}, bf16[224,512]{1,0:T(8,128)(2,1)S(1)}, bf16[224,512]{1,0:T(8,128)(2,1)S(1)}) custom-call(bf16[896,2048]{1,0:T(8,128)(2,1)S(1)} %shard_map.89.refs_0_, bf16[224,4096]{1,0:T(8,128)(2,1)S(1)} %get-tuple-element.25.refs_1_, ...), custom_call_target="tpu_custom_call" | custom-call | tf_op jit(solution)/shard_map/pallas_call | solution.py:355
  63.3 0.1 collective-permute-start.19
  63.5 1.6 %collective-permute-start.3 = (bf16[4,64,128]{2,1,0:T(8,128)(2,1)S(1)}, bf16[4,64,128]{2,1,0:T(8,128)(2,1)S(1)}, u32[]{:S(2)}, u32[]{:S(2)}) collective-permute-start(bf16[4,64,128]{2,1,0:T(8,128)(2,1)S(1)} %get-tuple-element.46.refs_0_), channel_id=1, source_target_pairs={{0,8},{4,12},{8,0},{12,4},{1,9},{5,13},{9,1},{13,5},{2,10},{6,14},... | collective-permute-start | bytes 196616 | tf_op jit(solution)/shard_map/ppermute | solution.py:24
  65.1 0.2 collective-permute-start.4
  65.2 2.8 %collective-permute-done.3.refs_1_ = bf16[4,64,128]{2,1,0:T(8,128)(2,1)S(1)} collective-permute-done((bf16[4,64,128]{2,1,0:T(8,128)(2,1)S(1)}, bf16[4,64,128]{2,1,0:T(8,128)(2,1)S(1)}, u32[]{:S(2)}, u32[]{:S(2)}) %collective-permute-start.3) | collective-permute-done | bytes 65568 | tf_op jit(solution)/shard_map/ppermute | solution.py:24
  68.0 1.5 %collective-permute-start.20 = (bf16[224,512]{1,0:T(8,128)(2,1)S(1)}, bf16[224,512]{1,0:T(8,128)(2,1)S(1)}, u32[]{:S(2)}, u32[]{:S(2)}) collective-permute-start(bf16[224,512]{1,0:T(8,128)(2,1)S(1)} %get-tuple-element.34), channel_id=1, source_target_pairs={{0,8},{4,12},{8,0},{12,4},{1,9},{5,13},{9,1},{13,5},{2,10},{6,14},... | collective-permute-start | bytes 688136 | tf_op jit(solution)/shard_map/ppermute | solution.py:24
  69.5 0.9 %collective-permute-start.25 = (bf16[224,512]{1,0:T(8,128)(2,1)S(1)}, bf16[224,512]{1,0:T(8,128)(2,1)S(1)}, u32[]{:S(2)}, u32[]{:S(2)}) collective-permute-start(bf16[224,512]{1,0:T(8,128)(2,1)S(1)} %get-tuple-element.41), channel_id=1, source_target_pairs={{0,8},{4,12},{8,0},{12,4},{1,9},{5,13},{9,1},{13,5},{2,10},{6,14},... | collective-permute-start | bytes 688136 | tf_op jit(solution)/shard_map/ppermute | solution.py:24
  70.5 1.1 %collective-permute-start.24 = (bf16[224,512]{1,0:T(8,128)(2,1)S(1)}, bf16[224,512]{1,0:T(8,128)(2,1)S(1)}, u32[]{:S(2)}, u32[]{:S(2)}) collective-permute-start(bf16[224,512]{1,0:T(8,128)(2,1)S(1)} %get-tuple-element.40), channel_id=1, source_target_pairs={{0,12},{4,8},{8,4},{12,0},{1,13},{5,9},{9,5},{13,1},{2,14},{6,10},... | collective-permute-start | bytes 688136 | tf_op jit(solution)/shard_map/ppermute | solution.py:24
  71.5 5.0 %collective-permute-done.20.refs_13_ = bf16[224,512]{1,0:T(8,128)(2,1)S(1)} collective-permute-done((bf16[224,512]{1,0:T(8,128)(2,1)S(1)}, bf16[224,512]{1,0:T(8,128)(2,1)S(1)}, u32[]{:S(2)}, u32[]{:S(2)}) %collective-permute-start.20) | collective-permute-done | bytes 229408 | tf_op jit(solution)/shard_map/ppermute | solution.py:24
  76.5 3.9 %collective-permute-done.21.refs_14_ = bf16[224,512]{1,0:T(8,128)(2,1)S(1)} collective-permute-done((bf16[224,512]{1,0:T(8,128)(2,1)S(1)}, bf16[224,512]{1,0:T(8,128)(2,1)S(1)}, u32[]{:S(2)}, u32[]{:S(2)}) %collective-permute-start.21) | collective-permute-done | bytes 229408 | tf_op jit(solution)/shard_map/ppermute | solution.py:24
  80.4 0.8 collective-permute-start.5
  81.2 0.9 %collective-permute-done.5.refs_3_ = bf16[4,64,128]{2,1,0:T(8,128)(2,1)S(1)} collective-permute-done((bf16[4,64,128]{2,1,0:T(8,128)(2,1)S(1)}, bf16[4,64,128]{2,1,0:T(8,128)(2,1)S(1)}, u32[]{:S(2)}, u32[]{:S(2)}) %collective-permute-start.5) | collective-permute-done | bytes 65568 | tf_op jit(solution)/shard_map/ppermute | solution.py:24
  82.1 5.2 %shard_map.92 = (f32[224,4096]{1,0:T(8,128)}, f32[8,64,64]{2,1,0:T(8,128)}, f32[2,224,512]{2,1,0:T(8,128)S(1)}) custom-call(bf16[4,64,128]{2,1,0:T(8,128)(2,1)S(1)} %get-tuple-element.46.refs_0_, bf16[4,64,128]{2,1,0:T(8,128)(2,1)S(1)} %collective-permute-done.3.refs_1_, bf16[4,64,128]{2,1,0:T(8,128)(2,1)S(1)} %collective-permute-done.4.refs_2_, ...), custom_call_target="tpu_custom_call" | custom-call | tf_op jit(solution)/shard_map/pallas_call | solution.py:384
  87.3 0.8 shard_map.93.refs_2_
  88.2 0.7 collective-permute-done.24.refs_1_
  88.9 0.8 shard_map.94
  (27 shorter events, 0.1 us)
Async XLA Ops:
  0.6 4.8 %copy-start = (bf16[224,2048]{1,0:T(8,128)(2,1)S(1)}, bf16[224,2048]{1,0:T(8,128)(2,1)}, u32[]{:S(2)}) copy-start(bf16[224,2048]{1,0:T(8,128)(2,1)} %refs_0_.3) | copy-start | bytes 2752516
  3.4 0.8 copy-start.1
  4.1 0.8 copy-start.3
  4.1 1.3 %copy-start.4 = (bf16[224,512]{1,0:T(8,128)(2,1)}, bf16[224,512]{1,0:T(8,128)(2,1)S(1)}, u32[]{:S(2)}) copy-start(bf16[224,512]{1,0:T(8,128)(2,1)S(1)} %get-tuple-element.31) | copy-start | bytes 688132
  4.1 1.3 %copy-start.5 = (bf16[224,512]{1,0:T(8,128)(2,1)}, bf16[224,512]{1,0:T(8,128)(2,1)S(1)}, u32[]{:S(2)}) copy-start(bf16[224,512]{1,0:T(8,128)(2,1)S(1)} %get-tuple-element.36) | copy-start | bytes 688132
  4.9 29.9 %collective-permute-start = (bf16[224,4096]{1,0:T(8,128)(2,1)S(1)}, bf16[224,4096]{1,0:T(8,128)(2,1)}, u32[]{:S(2)}, u32[]{:S(2)}) collective-permute-start(bf16[224,4096]{1,0:T(8,128)(2,1)S(1)} %get-tuple-element.25.refs_1_), channel_id=1, source_target_pairs={{0,4},{4,0},{8,12},{12,8},{1,5},{5,1},{9,13},{13,9},{2,6},{6,2},{1... | collective-permute-start | bytes 5505032 | tf_op jit(solution)/shard_map/ppermute | solution.py:24
  5.5 8.8 %collective-permute-start.9 = (bf16[224,512]{1,0:T(8,128)(2,1)S(1)}, bf16[224,512]{1,0:T(8,128)(2,1)S(1)}, u32[]{:S(2)}, u32[]{:S(2)}) collective-permute-start(bf16[224,512]{1,0:T(8,128)(2,1)S(1)} %constant_dynamic-slice_fusion), channel_id=1, source_target_pairs={{0,8},{4,12},{8,0},{12,4},{1,9},{5,13},{9,1},{13,5},{2,10},{6,14},... | collective-permute-start | bytes 688136 | tf_op jit(solution)/shard_map/ppermute | solution.py:24
  13.3 67.9 %collective-permute-start.7 = (bf16[256,4096]{1,0:T(8,128)(2,1)S(1)}, bf16[256,4096]{1,0:T(8,128)(2,1)S(1)}, u32[]{:S(2)}, u32[]{:S(2)}) collective-permute-start(bf16[256,4096]{1,0:T(8,128)(2,1)S(1)} %shard_map.87.refs_0_.refs_8_), channel_id=1, source_target_pairs={{0,4},{4,0},{8,12},{12,8},{1,5},{5,1},{9,13},{13,9},{2,6},{6,2},{1... | collective-permute-start | bytes 6291464 | tf_op jit(solution)/shard_map/ppermute | solution.py:24
  14.3 8.5 %collective-permute-start.10 = (bf16[224,512]{1,0:T(8,128)(2,1)S(1)}, bf16[224,512]{1,0:T(8,128)(2,1)S(1)}, u32[]{:S(2)}, u32[]{:S(2)}) collective-permute-start(bf16[224,512]{1,0:T(8,128)(2,1)S(1)} %collective-permute-done.9.refs_2_), channel_id=1, source_target_pairs={{0,1},{1,0},{2,3},{3,2},{16,17},{17,16},{18,19},{19,18},{4,5},{5,4... | collective-permute-start | bytes 688136 | tf_op jit(solution)/shard_map/ppermute | solution.py:314
  16.1 11.7 %collective-permute-start.11 = (bf16[224,512]{1,0:T(8,128)(2,1)S(1)}, bf16[224,512]{1,0:T(8,128)(2,1)S(1)}, u32[]{:S(2)}, u32[]{:S(2)}) collective-permute-start(bf16[224,512]{1,0:T(8,128)(2,1)S(1)} %collective-permute-done.9.refs_2_), channel_id=1, source_target_pairs={{0,16},{1,17},{2,18},{3,19},{16,0},{17,1},{18,2},{19,3},{4,20},{5,... | collective-permute-start | bytes 688136 | tf_op jit(solution)/shard_map/ppermute | solution.py:314
  17.6 10.1 %collective-permute-start.12 = (bf16[224,512]{1,0:T(8,128)(2,1)S(1)}, bf16[224,512]{1,0:T(8,128)(2,1)S(1)}, u32[]{:S(2)}, u32[]{:S(2)}) collective-permute-start(bf16[224,512]{1,0:T(8,128)(2,1)S(1)} %collective-permute-done.9.refs_2_), channel_id=1, source_target_pairs={{0,17},{1,16},{2,19},{3,18},{16,1},{17,0},{18,3},{19,2},{4,21},{5,... | collective-permute-start | bytes 688136 | tf_op jit(solution)/shard_map/ppermute | solution.py:314
  22.7 8.0 %collective-permute-start.1 = (bf16[4,224,256]{2,1,0:T(8,128)(2,1)}, bf16[4,224,256]{2,1,0:T(8,128)(2,1)S(1)}, u32[]{:S(2)}, u32[]{:S(2)}) collective-permute-start(bf16[4,224,256]{2,1,0:T(8,128)(2,1)} %copy-done.1), channel_id=1, source_target_pairs={{0,4},{4,0},{8,12},{12,8},{1,5},{5,1},{9,13},{13,9},{2,6},{6,2},{1... | collective-permute-start | bytes 1376264 | tf_op jit(solution)/shard_map/ppermute | solution.py:24
  27.8 11.9 %collective-permute-start.8 = (bf16[224,2048]{1,0:T(8,128)(2,1)S(1)}, bf16[224,2048]{1,0:T(8,128)(2,1)S(1)}, u32[]{:S(2)}, u32[]{:S(2)}) collective-permute-start(bf16[224,2048]{1,0:T(8,128)(2,1)S(1)} %copy-done), channel_id=1, source_target_pairs={{0,4},{4,0},{8,12},{12,8},{1,5},{5,1},{9,13},{13,9},{2,6},{6,2},{1... | collective-permute-start | bytes 2752520 | tf_op jit(solution)/shard_map/ppermute | solution.py:24
  27.8 2.8 %collective-permute-start.13 = (bf16[224,512]{1,0:T(8,128)(2,1)S(1)}, bf16[224,512]{1,0:T(8,128)(2,1)S(1)}, u32[]{:S(2)}, u32[]{:S(2)}) collective-permute-start(bf16[224,512]{1,0:T(8,128)(2,1)S(1)} %collective-permute-done.9.refs_2_), channel_id=1, source_target_pairs={{0,4},{4,0},{8,12},{12,8},{1,5},{5,1},{9,13},{13,9},{2,6},{6,2},{1... | collective-permute-start | bytes 688136 | tf_op jit(solution)/shard_map/ppermute | solution.py:24
  30.6 1.5 %collective-permute-start.14 = (bf16[224,512]{1,0:T(8,128)(2,1)S(1)}, bf16[224,512]{1,0:T(8,128)(2,1)S(1)}, u32[]{:S(2)}, u32[]{:S(2)}) collective-permute-start(bf16[224,512]{1,0:T(8,128)(2,1)S(1)} %collective-permute-done.10.refs_3_), channel_id=1, source_target_pairs={{0,4},{4,0},{8,12},{12,8},{1,5},{5,1},{9,13},{13,9},{2,6},{6,2},{1... | collective-permute-start | bytes 688136 | tf_op jit(solution)/shard_map/ppermute | solution.py:24
  30.7 1.7 %collective-permute-start.15 = (bf16[224,512]{1,0:T(8,128)(2,1)S(1)}, bf16[224,512]{1,0:T(8,128)(2,1)S(1)}, u32[]{:S(2)}, u32[]{:S(2)}) collective-permute-start(bf16[224,512]{1,0:T(8,128)(2,1)S(1)} %collective-permute-done.11.refs_4_), channel_id=1, source_target_pairs={{0,4},{4,0},{8,12},{12,8},{1,5},{5,1},{9,13},{13,9},{2,6},{6,2},{1... | collective-permute-start | bytes 688136 | tf_op jit(solution)/shard_map/ppermute | solution.py:24
  32.0 1.8 %collective-permute-start.16 = (bf16[224,512]{1,0:T(8,128)(2,1)S(1)}, bf16[224,512]{1,0:T(8,128)(2,1)S(1)}, u32[]{:S(2)}, u32[]{:S(2)}) collective-permute-start(bf16[224,512]{1,0:T(8,128)(2,1)S(1)} %collective-permute-done.12.refs_5_), channel_id=1, source_target_pairs={{0,4},{4,0},{8,12},{12,8},{1,5},{5,1},{9,13},{13,9},{2,6},{6,2},{1... | collective-permute-start | bytes 688136 | tf_op jit(solution)/shard_map/ppermute | solution.py:24
  32.4 17.6 %collective-permute-start.17 = (bf16[224,1024]{1,0:T(8,128)(2,1)}, bf16[224,1024]{1,0:T(8,128)(2,1)S(1)}, u32[]{:S(2)}, u32[]{:S(2)}) collective-permute-start(bf16[224,1024]{1,0:T(8,128)(2,1)} %copy-done.3), channel_id=1, source_target_pairs={{0,8},{4,12},{8,0},{12,4},{1,9},{5,13},{9,1},{13,5},{2,10},{6,14},... | collective-permute-start | bytes 1376264 | tf_op jit(solution)/shard_map/ppermute | solution.py:24
  33.9 16.1 %collective-permute-start.22 = (bf16[224,512]{1,0:T(8,128)(2,1)}, bf16[224,512]{1,0:T(8,128)(2,1)S(1)}, u32[]{:S(2)}, u32[]{:S(2)}) collective-permute-start(bf16[224,512]{1,0:T(8,128)(2,1)} %copy-done.5), channel_id=1, source_target_pairs={{0,12},{4,8},{8,4},{12,0},{1,13},{5,9},{9,5},{13,1},{2,14},{6,10},... | collective-permute-start | bytes 688136 | tf_op jit(solution)/shard_map/ppermute | solution.py:24
  34.8 22.4 %collective-permute-start.18 = (bf16[224,512]{1,0:T(8,128)(2,1)}, bf16[224,512]{1,0:T(8,128)(2,1)S(1)}, u32[]{:S(2)}, u32[]{:S(2)}) collective-permute-start(bf16[224,512]{1,0:T(8,128)(2,1)} %copy-done.4), channel_id=1, source_target_pairs={{0,12},{4,8},{8,4},{12,0},{1,13},{5,9},{9,5},{13,1},{2,14},{6,10},... | collective-permute-start | bytes 688136 | tf_op jit(solution)/shard_map/ppermute | solution.py:24
  39.6 23.8 %collective-permute-start.2 = (f32[4,64,128]{2,1,0:T(8,128)S(1)}, f32[4,64,128]{2,1,0:T(8,128)S(1)}, u32[]{:S(2)}, u32[]{:S(2)}) collective-permute-start(f32[4,64,128]{2,1,0:T(8,128)S(1)} %get-tuple-element.29), channel_id=1, source_target_pairs={{0,8},{4,12},{8,0},{12,4},{1,9},{5,13},{9,1},{13,5},{2,10},{6,14},... | collective-permute-start | bytes 393224 | tf_op jit(solution)/shard_map/ppermute | solution.py:24
  56.1 26.0 %copy-start.2 = (bf16[4,224,256]{2,1,0:T(8,128)(2,1)S(1)}, bf16[4,224,256]{2,1,0:T(8,128)(2,1)}, u32[]{:S(2)}) copy-start(bf16[4,224,256]{2,1,0:T(8,128)(2,1)} %copy-done.1) | copy-start | bytes 1376260
  56.1 13.4 %collective-permute-start.23 = (bf16[224,512]{1,0:T(8,128)(2,1)S(1)}, bf16[224,512]{1,0:T(8,128)(2,1)S(1)}, u32[]{:S(2)}, u32[]{:S(2)}) collective-permute-start(bf16[224,512]{1,0:T(8,128)(2,1)S(1)} %get-tuple-element.38), channel_id=1, source_target_pairs={{0,4},{4,0},{8,12},{12,8},{1,5},{5,1},{9,13},{13,9},{2,6},{6,2},{1... | collective-permute-start | bytes 688136 | tf_op jit(solution)/shard_map/ppermute | solution.py:24
  63.3 7.1 %collective-permute-start.19 = (bf16[224,512]{1,0:T(8,128)(2,1)S(1)}, bf16[224,512]{1,0:T(8,128)(2,1)S(1)}, u32[]{:S(2)}, u32[]{:S(2)}) collective-permute-start(bf16[224,512]{1,0:T(8,128)(2,1)S(1)} %get-tuple-element.33), channel_id=1, source_target_pairs={{0,4},{4,0},{8,12},{12,8},{1,5},{5,1},{9,13},{13,9},{2,6},{6,2},{1... | collective-permute-start | bytes 688136 | tf_op jit(solution)/shard_map/ppermute | solution.py:24
  63.5 4.5 %collective-permute-start.3 = (bf16[4,64,128]{2,1,0:T(8,128)(2,1)S(1)}, bf16[4,64,128]{2,1,0:T(8,128)(2,1)S(1)}, u32[]{:S(2)}, u32[]{:S(2)}) collective-permute-start(bf16[4,64,128]{2,1,0:T(8,128)(2,1)S(1)} %get-tuple-element.46.refs_0_), channel_id=1, source_target_pairs={{0,8},{4,12},{8,0},{12,4},{1,9},{5,13},{9,1},{13,5},{2,10},{6,14},... | collective-permute-start | bytes 196616 | tf_op jit(solution)/shard_map/ppermute | solution.py:24
  65.1 4.5 %collective-permute-start.4 = (bf16[4,64,128]{2,1,0:T(8,128)(2,1)S(1)}, bf16[4,64,128]{2,1,0:T(8,128)(2,1)S(1)}, u32[]{:S(2)}, u32[]{:S(2)}) collective-permute-start(bf16[4,64,128]{2,1,0:T(8,128)(2,1)S(1)} %get-tuple-element.46.refs_0_), channel_id=1, source_target_pairs={{0,4},{4,0},{8,12},{12,8},{1,5},{5,1},{9,13},{13,9},{2,6},{6,2},{1... | collective-permute-start | bytes 196616 | tf_op jit(solution)/shard_map/ppermute | solution.py:24
  68.0 8.5 %collective-permute-start.20 = (bf16[224,512]{1,0:T(8,128)(2,1)S(1)}, bf16[224,512]{1,0:T(8,128)(2,1)S(1)}, u32[]{:S(2)}, u32[]{:S(2)}) collective-permute-start(bf16[224,512]{1,0:T(8,128)(2,1)S(1)} %get-tuple-element.34), channel_id=1, source_target_pairs={{0,8},{4,12},{8,0},{12,4},{1,9},{5,13},{9,1},{13,5},{2,10},{6,14},... | collective-permute-start | bytes 688136 | tf_op jit(solution)/shard_map/ppermute | solution.py:24
  69.5 10.9 %collective-permute-start.21 = (bf16[224,512]{1,0:T(8,128)(2,1)S(1)}, bf16[224,512]{1,0:T(8,128)(2,1)S(1)}, u32[]{:S(2)}, u32[]{:S(2)}) collective-permute-start(bf16[224,512]{1,0:T(8,128)(2,1)S(1)} %get-tuple-element.35), channel_id=1, source_target_pairs={{0,12},{4,8},{8,4},{12,0},{1,13},{5,9},{9,5},{13,1},{2,14},{6,10},... | collective-permute-start | bytes 688136 | tf_op jit(solution)/shard_map/ppermute | solution.py:24
  69.5 17.8 %collective-permute-start.25 = (bf16[224,512]{1,0:T(8,128)(2,1)S(1)}, bf16[224,512]{1,0:T(8,128)(2,1)S(1)}, u32[]{:S(2)}, u32[]{:S(2)}) collective-permute-start(bf16[224,512]{1,0:T(8,128)(2,1)S(1)} %get-tuple-element.41), channel_id=1, source_target_pairs={{0,8},{4,12},{8,0},{12,4},{1,9},{5,13},{9,1},{13,5},{2,10},{6,14},... | collective-permute-start | bytes 688136 | tf_op jit(solution)/shard_map/ppermute | solution.py:24
  70.5 18.4 %collective-permute-start.24 = (bf16[224,512]{1,0:T(8,128)(2,1)S(1)}, bf16[224,512]{1,0:T(8,128)(2,1)S(1)}, u32[]{:S(2)}, u32[]{:S(2)}) collective-permute-start(bf16[224,512]{1,0:T(8,128)(2,1)S(1)} %get-tuple-element.40), channel_id=1, source_target_pairs={{0,12},{4,8},{8,4},{12,0},{1,13},{5,9},{9,5},{13,1},{2,14},{6,10},... | collective-permute-start | bytes 688136 | tf_op jit(solution)/shard_map/ppermute | solution.py:24
  76.5 5.6 %collective-permute-start.6 = (f32[4,64,128]{2,1,0:T(8,128)S(1)}, f32[4,64,128]{2,1,0:T(8,128)S(1)}, u32[]{:S(2)}, u32[]{:S(2)}) collective-permute-start(f32[4,64,128]{2,1,0:T(8,128)S(1)} %get-tuple-element.47.refs_4_), channel_id=1, source_target_pairs={{0,4},{4,0},{8,12},{12,8},{1,5},{5,1},{9,13},{13,9},{2,6},{6,2},{1... | collective-permute-start | bytes 393224 | tf_op jit(solution)/shard_map/ppermute | solution.py:24
  80.4 1.7 %collective-permute-start.5 = (bf16[4,64,128]{2,1,0:T(8,128)(2,1)S(1)}, bf16[4,64,128]{2,1,0:T(8,128)(2,1)S(1)}, u32[]{:S(2)}, u32[]{:S(2)}) collective-permute-start(bf16[4,64,128]{2,1,0:T(8,128)(2,1)S(1)} %collective-permute-done.3.refs_1_), channel_id=1, source_target_pairs={{0,4},{4,0},{8,12},{12,8},{1,5},{5,1},{9,13},{13,9},{2,6},{6,2},{1... | collective-permute-start | bytes 196616 | tf_op jit(solution)/shard_map/ppermute | solution.py:24

commit v8 on v7

--- a/solution.py
+++ b/solution.py
@@ -7,7 +7,7 @@
 
 
 LANES = 128
-QUARTERS = (2, 2)
+EIGHTHS = (3, 3, 2)
 GROUP = 32
 NT = (((1,), (1,)), ((), ()))
 NN = (((1,), (0,)), ((), ()))
@@ -29,11 +29,16 @@
 
 
 def cuts_of(block):
-    if block % (4 * LANES):
+    if block % (8 * LANES):
         return [(0, block)]
-    unit = block // 4
-    starts = [unit * sum(QUARTERS[:t]) for t in range(len(QUARTERS))]
-    return [(start, unit * size) for start, size in zip(starts, QUARTERS)]
+    unit = block // 8
+    starts = [unit * sum(EIGHTHS[:t]) for t in range(len(EIGHTHS))]
+    return [(start, unit * size) for start, size in zip(starts, EIGHTHS)]
+
+
+def sides_of(cuts):
+    total = cuts[-1][0] + cuts[-1][1]
+    return [cuts[0]] + [(cuts[0][1], total - cuts[0][1])] * (len(cuts) > 1)
 
 
 def position():
@@ -148,7 +153,7 @@
             waves[(j + 2) * height:(j + 3) * height, span] = far[j * pieces + r][...]
 
 
-def penalty_kernel(count, pieces, cut, waves, own, partner, *refs):
+def penalty_kernel(count, pieces, cut, skip, waves, own, partner, *refs):
     blocks, outs = refs[:count - 2], refs[count - 2:2 * count - 2]
     stack, turned, acc = refs[2 * count - 2:]
     height = outs[0].shape[0]
@@ -157,7 +162,7 @@
     stack[0:height, :] = own[:, at]
     stack[height:2 * height, :] = partner[:, at]
     for j in range(2, count):
-        start = 0 if j == count - 1 else cut[0]
+        start = cut[0] - (skip if j == count - 1 else 0)
         stack[j * height:(j + 1) * height, :] = blocks[j - 2][:, start:start + cut[1]]
     turned[...] = jnp.swapaxes(stack[...], 0, 1)
     for r in range(pieces):
@@ -247,6 +252,7 @@
     half = projections // 2
     block = cols // count
     cuts = cuts_of(block)
+    sides = sides_of(cuts)
     bf16, f32 = jnp.bfloat16, jnp.float32
     shape = jax.ShapeDtypeStruct
 
@@ -284,11 +290,11 @@
     fetched = {m: [swap(piece, "coef", m)] for m in range(2, count, 2)}
     table_shape = shape((half,) + angle_table.shape[1:], bf16)
     *parts, own, vox, wgt, table_mine, table_other = kernel(
-        lambda *refs: prepare_kernel(count, cuts, *refs),
+        lambda *refs: prepare_kernel(count, sides, *refs),
         [HBM] * 5,
-        [VMEM] * (count + len(cuts) + 2),
+        [VMEM] * (count + len(sides) + 2),
         [shape((coef_local, block), bf16)] * (count - 3)
-        + [shape((coef_local, cut[1]), bf16) for cut in cuts]
+        + [shape((coef_local, cut[1]), bf16) for cut in sides]
         + [shape((coef_local, cols), bf16)]
         + [shape((rows // 2, samples), jnp.int32)] * 2
         + [table_shape] * 2,
@@ -299,7 +305,7 @@
         ],
     )(ids_far, coef_far, vox_far, wgt_far, table_far)
     received = []
-    for t in range(len(cuts)):
+    for t in range(len(sides)):
         if t == 0:
             early = [swap(parts[m - 2], "coef", m) for m in range(2, count - 1)]
         received.append(early + [swap(parts[count - 3 + t], "coef", count - 1)])
@@ -322,9 +328,7 @@
     )(vox, wgt)
     low = swap(top, "coef", 1)
     for m in list(fetched):
-        fetched[m ^ 1] = []
-        for value in fetched[m]:
-            fetched[m ^ 1].append(swap(value, "coef", 1))
+        fetched[m ^ 1] = [swap(v, "coef", 1) for v in fetched[m]]
     far = [v for m in range(2, count) for v in fetched[m]]
 
     total, send = kernel(
@@ -353,7 +357,7 @@
     for t, cut in enumerate(cuts):
         first = t == 0
         outs = kernel(
-            lambda *refs: penalty_kernel(count, pieces, cut, *refs),
+            lambda *refs: penalty_kernel(count, pieces, cut, sides[min(t, 1)][0], *refs),
             [VMEM] * (count + 1),
             [VMEM] * count,
             [shape((coef_local, cut[1]), bf16)] * count,
@@ -362,7 +366,7 @@
                 pltpu.VMEM((cut[1], count * coef_local), bf16),
                 pltpu.VMEM((count * coef_local, cut[1]), f32),
             ],
-        )(waves, own, partner, *received[t])
+        )(waves, own, partner, *received[min(t, 1)])
         back = [outs[0]]
         for m in range(1, count):
             back.append(swap(outs[m], "coef", m))

time: 90.3 us -> 102 us (1.13)
  Pallas kernels: 31.3 us -> 41.1 us
  starting transfers between devices: 19.6 us -> 21.6 us
    pallas_call x3 -> x4, Pallas kernels: 15 us -> 18.5 us  [the longest x3 15.8 us: step_of(): kernel(lambda *refs: penalty_kernel(count, pieces, cut, sides[min(t, 1)][...]
    pallas_call x1, Pallas kernels: 5.2 us -> 8.2 us  [step_of(): kernel(lambda *refs: data_kernel(count, cuts, len(half_mine), *refs), [VM...]
    ppermute x23 -> x26, starting transfers between devices: 16.2 us -> 18.1 us  [swap(): return lax.ppermute(value, axis, [(i, i ^ mask) for i in range(count)])]
    pallas_call x2 -> x4, Pallas kernels: 1.65 us -> 3.01 us  [step_of(): kernel(lambda *refs: finish_kernel(count, cut, masks, *refs), [VMEM] * (l...]
    pallas_call x1, Pallas kernels: 5.16 us -> 6.51 us  [step_of(): kernel(build_kernel, [VMEM, VMEM], VMEM, shape((rows // 2, cols), bf16),...]
    unnamed x12 -> x10, local copies, waits for them, and re-layouts: 1.56 us -> 2.21 us
    ppermute x23 -> x26, waiting for transfers between devices: 26.4 us -> 26 us  [swap(): return lax.ppermute(value, axis, [(i, i ^ mask) for i in range(count)])]
  transfers between devices with their start and end apart: 26 -> 29, of which waited for: 12 -> 9; matrix products, arithmetic and copies ran while one was open for 0% -> 0% of each run, Pallas kernels for 31% -> 37%
where the time goes in v8:
time: 102 us
  Pallas kernels  41.1 us (40%)
  waiting for transfers between devices  35.6 us (35%)
  starting transfers between devices  21.6 us (21%)
  local copies, waits for them, and re-layouts  2.22 us (2%)
    ppermute x26, waiting for transfers between devices, swap(): return lax.ppermute(value, axis, [(i, i ^ mask) for i in range(count)])  26 us
    ppermute x26, starting transfers between devices, swap(): return lax.ppermute(value, axis, [(i, i ^ mask) for i in range(count)])  18.1 us
    pallas_call x3, Pallas kernels, step_of(): kernel(lambda *refs: penalty_kernel(count, pieces, cut, sides[min(t, 1)][...  15.8 us
    ppermute x3, waiting for transfers between devices, step_of(): fetched[m].append(lax.ppermute(fetched[m][0], ('groups', 'slab'), pairs))  9.62 us
    pallas_call x1, Pallas kernels, step_of(): kernel(lambda *refs: data_kernel(count, cuts, len(half_mine), *refs), [VM...  8.2 us
    pallas_call x1, Pallas kernels, step_of(): kernel(build_kernel, [VMEM, VMEM], VMEM, shape((rows // 2, cols), bf16),...  6.51 us
    pallas_call x1, Pallas kernels, step_of(): kernel(lambda *refs: sums_kernel(count, *refs), [VMEM] * 5 + [HBM], [VMEM...  4.6 us
    ppermute x3, starting transfers between devices, step_of(): fetched[m].append(lax.ppermute(fetched[m][0], ('groups', 'slab'), pairs))  3.49 us
  transfers between devices with their start and end apart: 29, of which 9 were waited for; matrix products, arithmetic and copies ran while one was open for 0% of the time, Pallas kernels for 37%

profile of v8, /device:TPU:0, one launch (start us, length us, event | category | flops | bytes accessed | tf_op | source)
XLA Modules:
  0.0 101.6 jit_solution(17760164021782461164)
XLA Ops:
  0.6 2.7 %shard_map.86 = (bf16[224,1024]{1,0:T(8,128)(2,1)S(1)}, bf16[224,384]{1,0:T(8,128)(2,1)S(1)}, bf16[224,640]{1,0:T(8,128)(2,1)S(1)}, bf16[224,4096]{1,0:T(8,128)(...) custom-call(s32[8]{0:T(128)} %refs_0_.2, ...), custom_call_target="tpu_custom_call" | custom-call | tf_op jit(solution)/shard_map/pallas_call | solution.py:292
  3.4 0.8 copy-done.1
  4.1 0.8 copy-done.3
  4.9 0.7 copy-done.4
  5.6 0.5 collective-permute-start
  6.1 6.5 %shard_map.87.refs_0_.refs_8_ = bf16[256,4096]{1,0:T(8,128)(2,1)} custom-call(s32[256,128]{1,0:T(8,128)S(1)} %get-tuple-element.28.vox_ref, s32[256,128]{1,0:T(8,128)S(1)} %get-tuple-element.29.wgt_ref), custom_call_target="tpu_custom_call" | custom-call | tf_op jit(solution)/shard_map/pallas_call | solution.py:322
  12.6 3.0 %collective-permute-start.9 = (bf16[224,512]{1,0:T(8,128)(2,1)S(1)}, bf16[224,512]{1,0:T(8,128)(2,1)S(1)}, u32[]{:S(2)}, u32[]{:S(2)}) collective-permute-start(bf16[224,512]{1,0:T(8,128)(2,1)S(1)} %constant_dynamic-slice_fusion), channel_id=1, source_target_pairs={{0,8},{4,12},{8,0},{12,4},{1,9},{5,13},{9,1},{13,5},{2,10},{6,14},... | collective-permute-start | bytes 688136 | tf_op jit(solution)/shard_map/ppermute | solution.py:24
  15.7 5.8 %collective-permute-done.9.refs_2_ = bf16[224,512]{1,0:T(8,128)(2,1)S(1)} collective-permute-done((bf16[224,512]{1,0:T(8,128)(2,1)S(1)}, bf16[224,512]{1,0:T(8,128)(2,1)S(1)}, u32[]{:S(2)}, u32[]{:S(2)}) %collective-permute-start.9) | collective-permute-done | bytes 229408 | tf_op jit(solution)/shard_map/ppermute | solution.py:24
  21.4 1.8 %collective-permute-start.10 = (bf16[224,512]{1,0:T(8,128)(2,1)S(1)}, bf16[224,512]{1,0:T(8,128)(2,1)S(1)}, u32[]{:S(2)}, u32[]{:S(2)}) collective-permute-start(bf16[224,512]{1,0:T(8,128)(2,1)S(1)} %collective-permute-done.9.refs_2_), channel_id=1, source_target_pairs={{0,1},{1,0},{2,3},{3,2},{16,17},{17,16},{18,19},{19,18},{4,5},{5,4... | collective-permute-start | bytes 688136 | tf_op jit(solution)/shard_map/ppermute | solution.py:320
  23.3 1.5 %collective-permute-start.11 = (bf16[224,512]{1,0:T(8,128)(2,1)S(1)}, bf16[224,512]{1,0:T(8,128)(2,1)S(1)}, u32[]{:S(2)}, u32[]{:S(2)}) collective-permute-start(bf16[224,512]{1,0:T(8,128)(2,1)S(1)} %collective-permute-done.9.refs_2_), channel_id=1, source_target_pairs={{0,16},{1,17},{2,18},{3,19},{16,0},{17,1},{18,2},{19,3},{4,20},{5,... | collective-permute-start | bytes 688136 | tf_op jit(solution)/shard_map/ppermute | solution.py:320
  24.8 0.1 collective-permute-start.12
  24.9 5.0 %collective-permute-done.10.refs_3_ = bf16[224,512]{1,0:T(8,128)(2,1)S(1)} collective-permute-done((bf16[224,512]{1,0:T(8,128)(2,1)S(1)}, bf16[224,512]{1,0:T(8,128)(2,1)S(1)}, u32[]{:S(2)}, u32[]{:S(2)}) %collective-permute-start.10) | collective-permute-done | bytes 229408 | tf_op jit(solution)/shard_map/ppermute | solution.py:320
  29.9 4.6 %collective-permute-done.11.refs_4_ = bf16[224,512]{1,0:T(8,128)(2,1)S(1)} collective-permute-done((bf16[224,512]{1,0:T(8,128)(2,1)S(1)}, bf16[224,512]{1,0:T(8,128)(2,1)S(1)}, u32[]{:S(2)}, u32[]{:S(2)}) %collective-permute-start.11) | collective-permute-done | bytes 229408 | tf_op jit(solution)/shard_map/ppermute | solution.py:320
  34.6 0.5 collective-permute-start.8
  35.1 1.0 collective-permute-done.13.refs_6_
  36.0 0.1 collective-permute-start.14
  36.2 0.4 collective-permute-start.15
  36.6 1.1 %collective-permute-done.14.refs_7_ = bf16[224,512]{1,0:T(8,128)(2,1)S(1)} collective-permute-done((bf16[224,512]{1,0:T(8,128)(2,1)S(1)}, bf16[224,512]{1,0:T(8,128)(2,1)S(1)}, u32[]{:S(2)}, u32[]{:S(2)}) %collective-permute-start.14) | collective-permute-done | bytes 229408 | tf_op jit(solution)/shard_map/ppermute | solution.py:24
  37.7 0.2 collective-permute-start.16
  37.9 0.1 collective-permute-done.15.refs_8_
  38.0 1.5 %collective-permute-start.17 = (bf16[224,1024]{1,0:T(8,128)(2,1)}, bf16[224,1024]{1,0:T(8,128)(2,1)S(1)}, u32[]{:S(2)}, u32[]{:S(2)}) collective-permute-start(bf16[224,1024]{1,0:T(8,128)(2,1)} %copy-done.3), channel_id=1, source_target_pairs={{0,8},{4,12},{8,0},{12,4},{1,9},{5,13},{9,1},{13,5},{2,10},{6,14},... | collective-permute-start | bytes 1376264 | tf_op jit(solution)/shard_map/ppermute | solution.py:24
  39.5 0.9 collective-permute-start.22
  40.5 0.8 collective-permute-start.18
  41.3 4.6 %shard_map.88 = (f32[4,64,128]{2,1,0:T(8,128)S(1)}, f32[4,64,128]{2,1,0:T(8,128)S(1)}) custom-call(bf16[256,4096]{1,0:T(8,128)(2,1)} %shard_map.87.refs_0_.refs_8_, bf16[224,4096]{1,0:T(8,128)(2,1)S(1)} %get-tuple-element.30.refs_1_, bf16[224,4096]{1,0:T(8,128)(2,1)} %collective-permute-done.refs_2_, ...), custom_call_target="tpu_custom_call" | custom-call | tf_op jit(solution)/shard_map/pallas_call | solution.py:334
  45.9 1.2 %collective-permute-start.2 = (f32[4,64,128]{2,1,0:T(8,128)S(1)}, f32[4,64,128]{2,1,0:T(8,128)S(1)}, u32[]{:S(2)}, u32[]{:S(2)}) collective-permute-start(f32[4,64,128]{2,1,0:T(8,128)S(1)} %get-tuple-element.34), channel_id=1, source_target_pairs={{0,8},{4,12},{8,0},{12,4},{1,9},{5,13},{9,1},{13,5},{2,10},{6,14},... | collective-permute-start | bytes 393224 | tf_op jit(solution)/shard_map/ppermute | solution.py:24
  47.1 0.3 shard_map.89.refs_0_
  47.4 9.3 %collective-permute-done.22.refs_4_ = bf16[224,640]{1,0:T(8,128)(2,1)S(1)} collective-permute-done((bf16[224,640]{1,0:T(8,128)(2,1)S(1)}, bf16[224,640]{1,0:T(8,128)(2,1)S(1)}, u32[]{:S(2)}, u32[]{:S(2)}) %collective-permute-start.22) | collective-permute-done | bytes 286752 | tf_op jit(solution)/shard_map/ppermute | solution.py:24
  56.8 4.3 %shard_map.92 = (bf16[224,256]{1,0:T(8,128)(2,1)S(1)}, bf16[224,256]{1,0:T(8,128)(2,1)S(1)}, bf16[224,256]{1,0:T(8,128)(2,1)S(1)}, bf16[224,256]{1,0:T(8,128)(2,1)S(1)}) custom-call(bf16[896,2048]{1,0:T(8,128)(2,1)S(1)} %shard_map.89.refs_0_, bf16[224,4096]{1,0:T(8,128)(2,1)S(1)} %get-tuple-element.30.refs_1_, ...), custom_call_target="tpu_custom_call" | custom-call | tf_op jit(solution)/shard_map/pallas_call | solution.py:359
  61.1 1.2 %collective-permute-start.24 = (bf16[224,256]{1,0:T(8,128)(2,1)S(1)}, bf16[224,256]{1,0:T(8,128)(2,1)S(1)}, u32[]{:S(2)}, u32[]{:S(2)}) collective-permute-start(bf16[224,256]{1,0:T(8,128)(2,1)S(1)} %get-tuple-element.45), channel_id=1, source_target_pairs={{0,4},{4,0},{8,12},{12,8},{1,5},{5,1},{9,13},{13,9},{2,6},{6,2},{1... | collective-permute-start | bytes 344072 | tf_op jit(solution)/shard_map/ppermute | solution.py:24
  62.2 5.7 %shard_map.91 = (bf16[224,384]{1,0:T(8,128)(2,1)S(1)}, bf16[224,384]{1,0:T(8,128)(2,1)S(1)}, bf16[224,384]{1,0:T(8,128)(2,1)S(1)}, bf16[224,384]{1,0:T(8,128)(2,1)S(1)}) custom-call(bf16[896,2048]{1,0:T(8,128)(2,1)S(1)} %shard_map.89.refs_0_, bf16[224,4096]{1,0:T(8,128)(2,1)S(1)} %get-tuple-element.30.refs_1_, ...), custom_call_target="tpu_custom_call" | custom-call | tf_op jit(solution)/shard_map/pallas_call | solution.py:359
  68.0 0.1 collective-permute-start.23
  68.0 5.8 %shard_map.90 = (bf16[224,384]{1,0:T(8,128)(2,1)S(1)}, bf16[224,384]{1,0:T(8,128)(2,1)S(1)}, bf16[224,384]{1,0:T(8,128)(2,1)S(1)}, bf16[224,384]{1,0:T(8,128)(2,1)S(1)}) custom-call(bf16[896,2048]{1,0:T(8,128)(2,1)S(1)} %shard_map.89.refs_0_, bf16[224,4096]{1,0:T(8,128)(2,1)S(1)} %get-tuple-element.30.refs_1_, ...), custom_call_target="tpu_custom_call" | custom-call | tf_op jit(solution)/shard_map/pallas_call | solution.py:359
  73.8 0.5 collective-permute-start.19
  74.3 1.5 %collective-permute-start.20 = (bf16[224,384]{1,0:T(8,128)(2,1)S(1)}, bf16[224,384]{1,0:T(8,128)(2,1)S(1)}, u32[]{:S(2)}, u32[]{:S(2)}) collective-permute-start(bf16[224,384]{1,0:T(8,128)(2,1)S(1)} %get-tuple-element.39), channel_id=1, source_target_pairs={{0,8},{4,12},{8,0},{12,4},{1,9},{5,13},{9,1},{13,5},{2,10},{6,14},... | collective-permute-start | bytes 516104 | tf_op jit(solution)/shard_map/ppermute | solution.py:24
  75.9 1.5 %collective-permute-start.3 = (bf16[4,64,128]{2,1,0:T(8,128)(2,1)S(1)}, bf16[4,64,128]{2,1,0:T(8,128)(2,1)S(1)}, u32[]{:S(2)}, u32[]{:S(2)}) collective-permute-start(bf16[4,64,128]{2,1,0:T(8,128)(2,1)S(1)} %get-tuple-element.56.refs_0_), channel_id=1, source_target_pairs={{0,8},{4,12},{8,0},{12,4},{1,9},{5,13},{9,1},{13,5},{2,10},{6,14},... | collective-permute-start | bytes 196616 | tf_op jit(solution)/shard_map/ppermute | solution.py:24
  77.4 0.4 collective-permute-start.4
  77.8 8.0 %collective-permute-done.3.refs_1_ = bf16[4,64,128]{2,1,0:T(8,128)(2,1)S(1)} collective-permute-done((bf16[4,64,128]{2,1,0:T(8,128)(2,1)S(1)}, bf16[4,64,128]{2,1,0:T(8,128)(2,1)S(1)}, u32[]{:S(2)}, u32[]{:S(2)}) %collective-permute-start.3) | collective-permute-done | bytes 65568 | tf_op jit(solution)/shard_map/ppermute | solution.py:24
  85.8 1.5 %collective-permute-start.28 = (bf16[224,384]{1,0:T(8,128)(2,1)S(1)}, bf16[224,384]{1,0:T(8,128)(2,1)S(1)}, u32[]{:S(2)}, u32[]{:S(2)}) collective-permute-start(bf16[224,384]{1,0:T(8,128)(2,1)S(1)} %get-tuple-element.51), channel_id=1, source_target_pairs={{0,8},{4,12},{8,0},{12,4},{1,9},{5,13},{9,1},{13,5},{2,10},{6,14},... | collective-permute-start | bytes 516104 | tf_op jit(solution)/shard_map/ppermute | solution.py:24
  87.3 0.4 collective-permute-start.27
  87.7 0.3 collective-permute-start.6
  87.9 1.5 %collective-permute-start.26 = (bf16[224,256]{1,0:T(8,128)(2,1)S(1)}, bf16[224,256]{1,0:T(8,128)(2,1)S(1)}, u32[]{:S(2)}, u32[]{:S(2)}) collective-permute-start(bf16[224,256]{1,0:T(8,128)(2,1)S(1)} %get-tuple-element.48), channel_id=1, source_target_pairs={{0,8},{4,12},{8,0},{12,4},{1,9},{5,13},{9,1},{13,5},{2,10},{6,14},... | collective-permute-start | bytes 344072 | tf_op jit(solution)/shard_map/ppermute | solution.py:24
  89.4 0.1 collective-permute-start.25
  89.5 8.2 %shard_map.93 = (f32[224,4096]{1,0:T(8,128)}, f32[8,64,64]{2,1,0:T(8,128)}, f32[2,224,384]{2,1,0:T(8,128)S(1)}, f32[2,224,256]{2,1,0:T(8,128)S(1)}) custom-call(bf16[4,64,128]{2,1,0:T(8,128)(2,1)S(1)} %get-tuple-element.56.refs_0_, bf16[4,64,128]{2,1,0:T(8,128)(2,1)S(1)} %collective-permute-done.3.refs_1_, ...), custom_call_target="tpu_custom_call" | custom-call | tf_op jit(solution)/shard_map/pallas_call | solution.py:388
  97.7 0.8 shard_map.94.refs_2_
  98.5 0.8 shard_map.95.refs_2_
  99.3 0.7 shard_map.96.refs_2_
  100.1 0.6 collective-permute-done.25.refs_1_
  100.7 0.7 shard_map.97
  (34 shorter events, 0.1 us)
Async XLA Ops:
  0.6 12.0 %copy-start = (bf16[224,2048]{1,0:T(8,128)(2,1)S(1)}, bf16[224,2048]{1,0:T(8,128)(2,1)}, u32[]{:S(2)}) copy-start(bf16[224,2048]{1,0:T(8,128)(2,1)} %refs_0_.3) | copy-start | bytes 2752516
  3.4 0.8 copy-start.1
  4.1 0.8 copy-start.3
  4.9 0.7 copy-start.4
  5.6 34.9 %collective-permute-start = (bf16[224,4096]{1,0:T(8,128)(2,1)S(1)}, bf16[224,4096]{1,0:T(8,128)(2,1)}, u32[]{:S(2)}, u32[]{:S(2)}) collective-permute-start(bf16[224,4096]{1,0:T(8,128)(2,1)S(1)} %get-tuple-element.30.refs_1_), channel_id=1, source_target_pairs={{0,4},{4,0},{8,12},{12,8},{1,5},{5,1},{9,13},{13,9},{2,6},{6,2},{1... | collective-permute-start | bytes 5505032 | tf_op jit(solution)/shard_map/ppermute | solution.py:24
  12.6 75.3 %collective-permute-start.7 = (bf16[256,4096]{1,0:T(8,128)(2,1)}, bf16[256,4096]{1,0:T(8,128)(2,1)}, u32[]{:S(2)}, u32[]{:S(2)}) collective-permute-start(bf16[256,4096]{1,0:T(8,128)(2,1)} %shard_map.87.refs_0_.refs_8_), channel_id=1, source_target_pairs={{0,4},{4,0},{8,12},{12,8},{1,5},{5,1},{9,13},{13,9},{2,6},{6,2},{1... | collective-permute-start | bytes 6291464 | tf_op jit(solution)/shard_map/ppermute | solution.py:24
  12.6 8.8 %collective-permute-start.9 = (bf16[224,512]{1,0:T(8,128)(2,1)S(1)}, bf16[224,512]{1,0:T(8,128)(2,1)S(1)}, u32[]{:S(2)}, u32[]{:S(2)}) collective-permute-start(bf16[224,512]{1,0:T(8,128)(2,1)S(1)} %constant_dynamic-slice_fusion), channel_id=1, source_target_pairs={{0,8},{4,12},{8,0},{12,4},{1,9},{5,13},{9,1},{13,5},{2,10},{6,14},... | collective-permute-start | bytes 688136 | tf_op jit(solution)/shard_map/ppermute | solution.py:24
  21.4 8.5 %collective-permute-start.10 = (bf16[224,512]{1,0:T(8,128)(2,1)S(1)}, bf16[224,512]{1,0:T(8,128)(2,1)S(1)}, u32[]{:S(2)}, u32[]{:S(2)}) collective-permute-start(bf16[224,512]{1,0:T(8,128)(2,1)S(1)} %collective-permute-done.9.refs_2_), channel_id=1, source_target_pairs={{0,1},{1,0},{2,3},{3,2},{16,17},{17,16},{18,19},{19,18},{4,5},{5,4... | collective-permute-start | bytes 688136 | tf_op jit(solution)/shard_map/ppermute | solution.py:320
  23.3 11.3 %collective-permute-start.11 = (bf16[224,512]{1,0:T(8,128)(2,1)S(1)}, bf16[224,512]{1,0:T(8,128)(2,1)S(1)}, u32[]{:S(2)}, u32[]{:S(2)}) collective-permute-start(bf16[224,512]{1,0:T(8,128)(2,1)S(1)} %collective-permute-done.9.refs_2_), channel_id=1, source_target_pairs={{0,16},{1,17},{2,18},{3,19},{16,0},{17,1},{18,2},{19,3},{4,20},{5,... | collective-permute-start | bytes 688136 | tf_op jit(solution)/shard_map/ppermute | solution.py:320
  24.8 9.8 %collective-permute-start.12 = (bf16[224,512]{1,0:T(8,128)(2,1)S(1)}, bf16[224,512]{1,0:T(8,128)(2,1)S(1)}, u32[]{:S(2)}, u32[]{:S(2)}) collective-permute-start(bf16[224,512]{1,0:T(8,128)(2,1)S(1)} %collective-permute-done.9.refs_2_), channel_id=1, source_target_pairs={{0,17},{1,16},{2,19},{3,18},{16,1},{17,0},{18,3},{19,2},{4,21},{5,... | collective-permute-start | bytes 688136 | tf_op jit(solution)/shard_map/ppermute | solution.py:320
  29.9 6.3 %collective-permute-start.1 = (bf16[4,224,256]{2,1,0:T(8,128)(2,1)}, bf16[4,224,256]{2,1,0:T(8,128)(2,1)S(1)}, u32[]{:S(2)}, u32[]{:S(2)}) collective-permute-start(bf16[4,224,256]{2,1,0:T(8,128)(2,1)} %copy-done.1), channel_id=1, source_target_pairs={{0,4},{4,0},{8,12},{12,8},{1,5},{5,1},{9,13},{13,9},{2,6},{6,2},{1... | collective-permute-start | bytes 1376264 | tf_op jit(solution)/shard_map/ppermute | solution.py:24
  34.5 1.5 %collective-permute-start.13 = (bf16[224,512]{1,0:T(8,128)(2,1)S(1)}, bf16[224,512]{1,0:T(8,128)(2,1)S(1)}, u32[]{:S(2)}, u32[]{:S(2)}) collective-permute-start(bf16[224,512]{1,0:T(8,128)(2,1)S(1)} %collective-permute-done.9.refs_2_), channel_id=1, source_target_pairs={{0,4},{4,0},{8,12},{12,8},{1,5},{5,1},{9,13},{13,9},{2,6},{6,2},{1... | collective-permute-start | bytes 688136 | tf_op jit(solution)/shard_map/ppermute | solution.py:24
  34.6 11.3 %collective-permute-start.8 = (bf16[224,2048]{1,0:T(8,128)(2,1)S(1)}, bf16[224,2048]{1,0:T(8,128)(2,1)S(1)}, u32[]{:S(2)}, u32[]{:S(2)}) collective-permute-start(bf16[224,2048]{1,0:T(8,128)(2,1)S(1)} %copy-done), channel_id=1, source_target_pairs={{0,4},{4,0},{8,12},{12,8},{1,5},{5,1},{9,13},{13,9},{2,6},{6,2},{1... | collective-permute-start | bytes 2752520 | tf_op jit(solution)/shard_map/ppermute | solution.py:24
  36.0 1.6 %collective-permute-start.14 = (bf16[224,512]{1,0:T(8,128)(2,1)S(1)}, bf16[224,512]{1,0:T(8,128)(2,1)S(1)}, u32[]{:S(2)}, u32[]{:S(2)}) collective-permute-start(bf16[224,512]{1,0:T(8,128)(2,1)S(1)} %collective-permute-done.10.refs_3_), channel_id=1, source_target_pairs={{0,4},{4,0},{8,12},{12,8},{1,5},{5,1},{9,13},{13,9},{2,6},{6,2},{1... | collective-permute-start | bytes 688136 | tf_op jit(solution)/shard_map/ppermute | solution.py:24
  36.2 1.8 %collective-permute-start.15 = (bf16[224,512]{1,0:T(8,128)(2,1)S(1)}, bf16[224,512]{1,0:T(8,128)(2,1)S(1)}, u32[]{:S(2)}, u32[]{:S(2)}) collective-permute-start(bf16[224,512]{1,0:T(8,128)(2,1)S(1)} %collective-permute-done.11.refs_4_), channel_id=1, source_target_pairs={{0,4},{4,0},{8,12},{12,8},{1,5},{5,1},{9,13},{13,9},{2,6},{6,2},{1... | collective-permute-start | bytes 688136 | tf_op jit(solution)/shard_map/ppermute | solution.py:24
  37.7 1.8 %collective-permute-start.16 = (bf16[224,512]{1,0:T(8,128)(2,1)S(1)}, bf16[224,512]{1,0:T(8,128)(2,1)S(1)}, u32[]{:S(2)}, u32[]{:S(2)}) collective-permute-start(bf16[224,512]{1,0:T(8,128)(2,1)S(1)} %collective-permute-done.12.refs_5_), channel_id=1, source_target_pairs={{0,4},{4,0},{8,12},{12,8},{1,5},{5,1},{9,13},{13,9},{2,6},{6,2},{1... | collective-permute-start | bytes 688136 | tf_op jit(solution)/shard_map/ppermute | solution.py:24
  38.0 18.8 %collective-permute-start.17 = (bf16[224,1024]{1,0:T(8,128)(2,1)}, bf16[224,1024]{1,0:T(8,128)(2,1)S(1)}, u32[]{:S(2)}, u32[]{:S(2)}) collective-permute-start(bf16[224,1024]{1,0:T(8,128)(2,1)} %copy-done.3), channel_id=1, source_target_pairs={{0,8},{4,12},{8,0},{12,4},{1,9},{5,13},{9,1},{13,5},{2,10},{6,14},... | collective-permute-start | bytes 1376264 | tf_op jit(solution)/shard_map/ppermute | solution.py:24
  39.5 17.3 %collective-permute-start.22 = (bf16[224,640]{1,0:T(8,128)(2,1)S(1)}, bf16[224,640]{1,0:T(8,128)(2,1)S(1)}, u32[]{:S(2)}, u32[]{:S(2)}) collective-permute-start(bf16[224,640]{1,0:T(8,128)(2,1)S(1)} %get-tuple-element.41), channel_id=1, source_target_pairs={{0,12},{4,8},{8,4},{12,0},{1,13},{5,9},{9,5},{13,1},{2,14},{6,10},... | collective-permute-start | bytes 860168 | tf_op jit(solution)/shard_map/ppermute | solution.py:24
  40.5 27.6 %collective-permute-start.18 = (bf16[224,384]{1,0:T(8,128)(2,1)}, bf16[224,384]{1,0:T(8,128)(2,1)S(1)}, u32[]{:S(2)}, u32[]{:S(2)}) collective-permute-start(bf16[224,384]{1,0:T(8,128)(2,1)} %copy-done.4), channel_id=1, source_target_pairs={{0,12},{4,8},{8,4},{12,0},{1,13},{5,9},{9,5},{13,1},{2,14},{6,10},... | collective-permute-start | bytes 516104 | tf_op jit(solution)/shard_map/ppermute | solution.py:24
  45.9 29.9 %collective-permute-start.2 = (f32[4,64,128]{2,1,0:T(8,128)S(1)}, f32[4,64,128]{2,1,0:T(8,128)S(1)}, u32[]{:S(2)}, u32[]{:S(2)}) collective-permute-start(f32[4,64,128]{2,1,0:T(8,128)S(1)} %get-tuple-element.34), channel_id=1, source_target_pairs={{0,8},{4,12},{8,0},{12,4},{1,9},{5,13},{9,1},{13,5},{2,10},{6,14},... | collective-permute-start | bytes 393224 | tf_op jit(solution)/shard_map/ppermute | solution.py:24
  61.1 13.3 %collective-permute-start.24 = (bf16[224,256]{1,0:T(8,128)(2,1)S(1)}, bf16[224,256]{1,0:T(8,128)(2,1)S(1)}, u32[]{:S(2)}, u32[]{:S(2)}) collective-permute-start(bf16[224,256]{1,0:T(8,128)(2,1)S(1)} %get-tuple-element.45), channel_id=1, source_target_pairs={{0,4},{4,0},{8,12},{12,8},{1,5},{5,1},{9,13},{13,9},{2,6},{6,2},{1... | collective-permute-start | bytes 344072 | tf_op jit(solution)/shard_map/ppermute | solution.py:24
  67.9 21.6 %copy-start.2 = (bf16[4,224,256]{2,1,0:T(8,128)(2,1)S(1)}, bf16[4,224,256]{2,1,0:T(8,128)(2,1)}, u32[]{:S(2)}) copy-start(bf16[4,224,256]{2,1,0:T(8,128)(2,1)} %copy-done.1) | copy-start | bytes 1376260
  68.0 7.9 %collective-permute-start.23 = (bf16[224,384]{1,0:T(8,128)(2,1)S(1)}, bf16[224,384]{1,0:T(8,128)(2,1)S(1)}, u32[]{:S(2)}, u32[]{:S(2)}) collective-permute-start(bf16[224,384]{1,0:T(8,128)(2,1)S(1)} %get-tuple-element.43), channel_id=1, source_target_pairs={{0,4},{4,0},{8,12},{12,8},{1,5},{5,1},{9,13},{13,9},{2,6},{6,2},{1... | collective-permute-start | bytes 516104 | tf_op jit(solution)/shard_map/ppermute | solution.py:24
  73.8 3.6 %collective-permute-start.19 = (bf16[224,384]{1,0:T(8,128)(2,1)S(1)}, bf16[224,384]{1,0:T(8,128)(2,1)S(1)}, u32[]{:S(2)}, u32[]{:S(2)}) collective-permute-start(bf16[224,384]{1,0:T(8,128)(2,1)S(1)} %get-tuple-element.38), channel_id=1, source_target_pairs={{0,4},{4,0},{8,12},{12,8},{1,5},{5,1},{9,13},{13,9},{2,6},{6,2},{1... | collective-permute-start | bytes 516104 | tf_op jit(solution)/shard_map/ppermute | solution.py:24
  74.3 11.5 %collective-permute-start.20 = (bf16[224,384]{1,0:T(8,128)(2,1)S(1)}, bf16[224,384]{1,0:T(8,128)(2,1)S(1)}, u32[]{:S(2)}, u32[]{:S(2)}) collective-permute-start(bf16[224,384]{1,0:T(8,128)(2,1)S(1)} %get-tuple-element.39), channel_id=1, source_target_pairs={{0,8},{4,12},{8,0},{12,4},{1,9},{5,13},{9,1},{13,5},{2,10},{6,14},... | collective-permute-start | bytes 516104 | tf_op jit(solution)/shard_map/ppermute | solution.py:24
  75.8 11.5 %collective-permute-start.21 = (bf16[224,384]{1,0:T(8,128)(2,1)S(1)}, bf16[224,384]{1,0:T(8,128)(2,1)S(1)}, u32[]{:S(2)}, u32[]{:S(2)}) collective-permute-start(bf16[224,384]{1,0:T(8,128)(2,1)S(1)} %get-tuple-element.40), channel_id=1, source_target_pairs={{0,12},{4,8},{8,4},{12,0},{1,13},{5,9},{9,5},{13,1},{2,14},{6,10},... | collective-permute-start | bytes 516104 | tf_op jit(solution)/shard_map/ppermute | solution.py:24
  75.9 9.9 %collective-permute-start.3 = (bf16[4,64,128]{2,1,0:T(8,128)(2,1)S(1)}, bf16[4,64,128]{2,1,0:T(8,128)(2,1)S(1)}, u32[]{:S(2)}, u32[]{:S(2)}) collective-permute-start(bf16[4,64,128]{2,1,0:T(8,128)(2,1)S(1)} %get-tuple-element.56.refs_0_), channel_id=1, source_target_pairs={{0,8},{4,12},{8,0},{12,4},{1,9},{5,13},{9,1},{13,5},{2,10},{6,14},... | collective-permute-start | bytes 196616 | tf_op jit(solution)/shard_map/ppermute | solution.py:24
  77.4 10.3 %collective-permute-start.4 = (bf16[4,64,128]{2,1,0:T(8,128)(2,1)S(1)}, bf16[4,64,128]{2,1,0:T(8,128)(2,1)S(1)}, u32[]{:S(2)}, u32[]{:S(2)}) collective-permute-start(bf16[4,64,128]{2,1,0:T(8,128)(2,1)S(1)} %get-tuple-element.56.refs_0_), channel_id=1, source_target_pairs={{0,4},{4,0},{8,12},{12,8},{1,5},{5,1},{9,13},{13,9},{2,6},{6,2},{1... | collective-permute-start | bytes 196616 | tf_op jit(solution)/shard_map/ppermute | solution.py:24
  85.8 3.7 %collective-permute-start.5 = (bf16[4,64,128]{2,1,0:T(8,128)(2,1)S(1)}, bf16[4,64,128]{2,1,0:T(8,128)(2,1)S(1)}, u32[]{:S(2)}, u32[]{:S(2)}) collective-permute-start(bf16[4,64,128]{2,1,0:T(8,128)(2,1)S(1)} %collective-permute-done.3.refs_1_), channel_id=1, source_target_pairs={{0,4},{4,0},{8,12},{12,8},{1,5},{5,1},{9,13},{13,9},{2,6},{6,2},{1... | collective-permute-start | bytes 196616 | tf_op jit(solution)/shard_map/ppermute | solution.py:24
  85.8 12.0 %collective-permute-start.28 = (bf16[224,384]{1,0:T(8,128)(2,1)S(1)}, bf16[224,384]{1,0:T(8,128)(2,1)S(1)}, u32[]{:S(2)}, u32[]{:S(2)}) collective-permute-start(bf16[224,384]{1,0:T(8,128)(2,1)S(1)} %get-tuple-element.51), channel_id=1, source_target_pairs={{0,8},{4,12},{8,0},{12,4},{1,9},{5,13},{9,1},{13,5},{2,10},{6,14},... | collective-permute-start | bytes 516104 | tf_op jit(solution)/shard_map/ppermute | solution.py:24
  87.3 11.3 %collective-permute-start.27 = (bf16[224,384]{1,0:T(8,128)(2,1)S(1)}, bf16[224,384]{1,0:T(8,128)(2,1)S(1)}, u32[]{:S(2)}, u32[]{:S(2)}) collective-permute-start(bf16[224,384]{1,0:T(8,128)(2,1)S(1)} %get-tuple-element.50), channel_id=1, source_target_pairs={{0,12},{4,8},{8,4},{12,0},{1,13},{5,9},{9,5},{13,1},{2,14},{6,10},... | collective-permute-start | bytes 516104 | tf_op jit(solution)/shard_map/ppermute | solution.py:24
  87.7 1.9 %collective-permute-start.6 = (f32[4,64,128]{2,1,0:T(8,128)S(1)}, f32[4,64,128]{2,1,0:T(8,128)S(1)}, u32[]{:S(2)}, u32[]{:S(2)}) collective-permute-start(f32[4,64,128]{2,1,0:T(8,128)S(1)} %get-tuple-element.57.refs_4_), channel_id=1, source_target_pairs={{0,4},{4,0},{8,12},{12,8},{1,5},{5,1},{9,13},{13,9},{2,6},{6,2},{1... | collective-permute-start | bytes 393224 | tf_op jit(solution)/shard_map/ppermute | solution.py:24
  87.9 11.4 %collective-permute-start.26 = (bf16[224,256]{1,0:T(8,128)(2,1)S(1)}, bf16[224,256]{1,0:T(8,128)(2,1)S(1)}, u32[]{:S(2)}, u32[]{:S(2)}) collective-permute-start(bf16[224,256]{1,0:T(8,128)(2,1)S(1)} %get-tuple-element.48), channel_id=1, source_target_pairs={{0,8},{4,12},{8,0},{12,4},{1,9},{5,13},{9,1},{13,5},{2,10},{6,14},... | collective-permute-start | bytes 344072 | tf_op jit(solution)/shard_map/ppermute | solution.py:24
  89.4 11.3 %collective-permute-start.25 = (bf16[224,256]{1,0:T(8,128)(2,1)S(1)}, bf16[224,256]{1,0:T(8,128)(2,1)S(1)}, u32[]{:S(2)}, u32[]{:S(2)}) collective-permute-start(bf16[224,256]{1,0:T(8,128)(2,1)S(1)} %get-tuple-element.47), channel_id=1, source_target_pairs={{0,12},{4,8},{8,4},{12,0},{1,13},{5,9},{9,5},{13,1},{2,14},{6,10},... | collective-permute-start | bytes 344072 | tf_op jit(solution)/shard_map/ppermute | solution.py:24

commit v9 on v7

--- a/solution.py
+++ b/solution.py
@@ -8,7 +8,7 @@
 
 LANES = 128
 QUARTERS = (2, 2)
-GROUP = 32
+GROUP = 64
 NT = (((1,), (1,)), ((), ()))
 NN = (((1,), (0,)), ((), ()))
 VMEM = pl.BlockSpec(memory_space=pltpu.VMEM)
@@ -135,25 +135,18 @@
             out[i] = total - (2.0 / count) * target[i, :, at]
 
 
-def stack_kernel(pieces, own, near, *refs):
-    far, waves = refs[:-1], refs[-1]
-    place = position()[2]
-    height = near.shape[0]
-    width = waves.shape[1] // pieces
-    for r in range(pieces):
-        span = slice(r * width, (r + 1) * width)
-        waves[0:height, span] = own[:, aligned(place ^ r, width)]
-        waves[height:2 * height, span] = near[:, aligned(place ^ r, width)]
-        for j in range(len(far) // pieces):
-            waves[(j + 2) * height:(j + 3) * height, span] = far[j * pieces + r][...]
-
-
-def penalty_kernel(count, pieces, cut, waves, own, partner, *refs):
-    blocks, outs = refs[:count - 2], refs[count - 2:2 * count - 2]
-    stack, turned, acc = refs[2 * count - 2:]
+def penalty_kernel(count, pieces, cut, first, own, partner, *refs):
+    blocks, refs = refs[:count - 2], refs[count - 2:]
+    if first:
+        harm, near, far = refs[0], refs[1], refs[2:2 + (count - 2) * pieces]
+        outs, waves, refs = refs[2 + len(far):][:count], refs[2 + len(far) + count], refs[3 + len(far) + count:]
+    else:
+        waves, outs, refs = refs[0], refs[1:count + 1], refs[count + 1:]
+    stack, turned, acc = refs
+    me, _, place = position()
     height = outs[0].shape[0]
     width = waves.shape[1] // pieces
-    at = columns(position()[0], own.shape[1] // count, cut)
+    at = columns(me, own.shape[1] // count, cut)
     stack[0:height, :] = own[:, at]
     stack[height:2 * height, :] = partner[:, at]
     for j in range(2, count):
@@ -161,7 +154,13 @@
         stack[j * height:(j + 1) * height, :] = blocks[j - 2][:, start:start + cut[1]]
     turned[...] = jnp.swapaxes(stack[...], 0, 1)
     for r in range(pieces):
-        wave = waves[:, r * width:(r + 1) * width]
+        span = slice(r * width, (r + 1) * width)
+        if first:
+            waves[0:height, span] = harm[:, aligned(place ^ r, width)]
+            waves[height:2 * height, span] = near[:, aligned(place ^ r, width)]
+            for j in range(2, count):
+                waves[j * height:(j + 1) * height, span] = far[(j - 2) * pieces + r][...]
+        wave = waves[:, span]
         field = dot(turned[...], wave, NN)
         slope = (0.5 * jnp.tanh(0.5 * field) - 0.5).astype(jnp.bfloat16)
         part = dot(wave, slope, NT)
@@ -322,9 +321,7 @@
     )(vox, wgt)
     low = swap(top, "coef", 1)
     for m in list(fetched):
-        fetched[m ^ 1] = []
-        for value in fetched[m]:
-            fetched[m ^ 1].append(swap(value, "coef", 1))
+        fetched[m ^ 1] = [swap(v, "coef", 1) for v in fetched[m]]
     far = [v for m in range(2, count) for v in fetched[m]]
 
     total, send = kernel(
@@ -345,24 +342,23 @@
         total = total + swap(send, "coef", mask)
 
     wide = shape((count * coef_local, harmonics.shape[1]), bf16)
-    waves = kernel(
-        lambda *refs: stack_kernel(pieces, *refs), [VMEM] * (2 + len(far)), VMEM, wide
-    )(harmonics, near, *far)
-
     returned = []
     for t, cut in enumerate(cuts):
         first = t == 0
+        extra = [harmonics, near, *far] if first else [waves]
         outs = kernel(
-            lambda *refs: penalty_kernel(count, pieces, cut, *refs),
-            [VMEM] * (count + 1),
-            [VMEM] * count,
-            [shape((coef_local, cut[1]), bf16)] * count,
+            lambda *refs: penalty_kernel(count, pieces, cut, first, *refs),
+            [VMEM] * (count + len(extra)),
+            [VMEM] * (count + first),
+            [shape((coef_local, cut[1]), bf16)] * count + [wide] * first,
             [
                 pltpu.VMEM((count * coef_local, cut[1]), bf16),
                 pltpu.VMEM((cut[1], count * coef_local), bf16),
                 pltpu.VMEM((count * coef_local, cut[1]), f32),
             ],
-        )(waves, own, partner, *received[t])
+        )(own, partner, *received[t], *extra)
+        if first:
+            waves = outs[-1]
         back = [outs[0]]
         for m in range(1, count):
             back.append(swap(outs[m], "coef", m))

time: 90.3 us -> 82.5 us (0.914)
  waiting for transfers between devices: 36.4 us -> 28.7 us
  Pallas kernels: 31.3 us -> 30.2 us
  starting transfers between devices: 19.6 us -> 20.6 us
    ppermute x3, waiting for transfers between devices: 10 us -> 4.93 us  [step_of(): fetched[m].append(lax.ppermute(fetched[m][0], ('groups', 'slab'), pairs))]
    ppermute x23, waiting for transfers between devices: 26.4 us -> 23.7 us  [swap(): return lax.ppermute(value, axis, [(i, i ^ mask) for i in range(count)])]
    ppermute x3, starting transfers between devices: 3.49 us -> 5.88 us  [step_of(): fetched[m].append(lax.ppermute(fetched[m][0], ('groups', 'slab'), pairs))]
    ppermute x23, starting transfers between devices: 16.2 us -> 14.7 us  [swap(): return lax.ppermute(value, axis, [(i, i ^ mask) for i in range(count)])]
    pallas_call x3 -> x2, Pallas kernels: 12.5 us -> 12.3 us  [step_of(): kernel(lambda *refs: penalty_kernel(count, pieces, cut, first, *refs), [V...]
  transfers between devices with their start and end apart: 26 -> 26, of which waited for: 12 -> 9; matrix products, arithmetic and copies ran while one was open for 0% -> 0% of each run, Pallas kernels for 31% -> 33%
where the time goes in v9:
time: 82.5 us; the launch traced here: 81.9 us
  Pallas kernels  30.2 us (37%)
  waiting for transfers between devices  28.7 us (35%)
  starting transfers between devices  20.6 us (25%)
  local copies, waits for them, and re-layouts  1.58 us (2%)
    ppermute x23, waiting for transfers between devices, swap(): return lax.ppermute(value, axis, [(i, i ^ mask) for i in range(count)])  23.7 us
    ppermute x23, starting transfers between devices, swap(): return lax.ppermute(value, axis, [(i, i ^ mask) for i in range(count)])  14.7 us
    pallas_call x2, Pallas kernels, step_of(): kernel(lambda *refs: penalty_kernel(count, pieces, cut, first, *refs), [V...  12.3 us
    ppermute x3, starting transfers between devices, step_of(): fetched[m].append(lax.ppermute(fetched[m][0], ('groups', 'slab'), pairs))  5.88 us
    pallas_call x1, Pallas kernels, step_of(): kernel(lambda *refs: data_kernel(count, cuts, len(half_mine), *refs), [VM...  5.2 us
    ppermute x3, waiting for transfers between devices, step_of(): fetched[m].append(lax.ppermute(fetched[m][0], ('groups', 'slab'), pairs))  4.93 us
    pallas_call x1, Pallas kernels, step_of(): kernel(build_kernel, [VMEM, VMEM], VMEM, shape((rows // 2, cols), bf16),...  4.34 us
    pallas_call x1, Pallas kernels, step_of(): kernel(lambda *refs: sums_kernel(count, *refs), [VMEM] * 5 + [HBM], [VMEM...  3.99 us
  transfers between devices with their start and end apart: 26, of which 9 were waited for; matrix products, arithmetic and copies ran while one was open for 0% of the time, Pallas kernels for 33%

profile of v9, /device:TPU:0, one launch (start us, length us, event | category | flops | bytes accessed | tf_op | source)
XLA Modules:
  0.0 81.9 jit_solution(6577275249958577052)
XLA Ops:
  0.6 2.7 %shard_map.86 = (bf16[224,1024]{1,0:T(8,128)(2,1)S(1)}, bf16[224,512]{1,0:T(8,128)(2,1)S(1)}, bf16[224,512]{1,0:T(8,128)(2,1)S(1)}, bf16[224,4096]{1,0:T(8,128)(...) custom-call(s32[8]{0:T(128)} %refs_0_.1, ...), custom_call_target="tpu_custom_call" | custom-call | tf_op jit(solution)/shard_map/pallas_call | solution.py:285
  3.4 0.0 copy-start.1
  3.4 0.8 copy-done.1
  4.1 0.8 copy-done.3
  4.9 0.5 collective-permute-start
  5.5 2.7 %collective-permute-start.11 = (bf16[224,512]{1,0:T(8,128)(2,1)S(1)}, bf16[224,512]{1,0:T(8,128)(2,1)S(1)}, u32[]{:S(2)}, u32[]{:S(2)}) collective-permute-start(bf16[224,512]{1,0:T(8,128)(2,1)S(1)} %constant_dynamic-slice_fusion), channel_id=1, source_target_pairs={{0,8},{4,12},{8,0},{12,4},{1,9},{5,13},{9,1},{13,5},{2,10},{6,14},... | collective-permute-start | bytes 688136 | tf_op jit(solution)/shard_map/ppermute | solution.py:24
  8.1 4.3 %shard_map.87.refs_0_.refs_8_ = bf16[256,4096]{1,0:T(8,128)(2,1)S(1)} custom-call(s32[256,128]{1,0:T(8,128)S(1)} %get-tuple-element.24.vox_ref, s32[256,128]{1,0:T(8,128)S(1)} %get-tuple-element.25.wgt_ref), custom_call_target="tpu_custom_call" | custom-call | tf_op jit(solution)/shard_map/pallas_call | solution.py:315
  12.5 0.2 collective-permute-start.7
  12.6 0.0 collective-permute-start.9
  12.7 1.6 %collective-permute-done.11.refs_6_ = bf16[224,512]{1,0:T(8,128)(2,1)S(1)} collective-permute-done((bf16[224,512]{1,0:T(8,128)(2,1)S(1)}, bf16[224,512]{1,0:T(8,128)(2,1)S(1)}, u32[]{:S(2)}, u32[]{:S(2)}) %collective-permute-start.11) | collective-permute-done | bytes 229408 | tf_op jit(solution)/shard_map/ppermute | solution.py:24
  14.3 1.8 %collective-permute-start.12 = (bf16[224,512]{1,0:T(8,128)(2,1)S(1)}, bf16[224,512]{1,0:T(8,128)(2,1)S(1)}, u32[]{:S(2)}, u32[]{:S(2)}) collective-permute-start(bf16[224,512]{1,0:T(8,128)(2,1)S(1)} %collective-permute-done.11.refs_6_), channel_id=1, source_target_pairs={{0,1},{1,0},{2,3},{3,2},{16,17},{17,16},{18,19},{19,18},{4,5},{5,4... | collective-permute-start | bytes 688136 | tf_op jit(solution)/shard_map/ppermute | solution.py:313
  16.1 1.5 %collective-permute-start.13 = (bf16[224,512]{1,0:T(8,128)(2,1)S(1)}, bf16[224,512]{1,0:T(8,128)(2,1)S(1)}, u32[]{:S(2)}, u32[]{:S(2)}) collective-permute-start(bf16[224,512]{1,0:T(8,128)(2,1)S(1)} %collective-permute-done.11.refs_6_), channel_id=1, source_target_pairs={{0,16},{1,17},{2,18},{3,19},{16,0},{17,1},{18,2},{19,3},{4,20},{5,... | collective-permute-start | bytes 688136 | tf_op jit(solution)/shard_map/ppermute | solution.py:313
  17.6 2.6 %collective-permute-done.9.refs_3_ = bf16[224,512]{1,0:T(8,128)(2,1)S(1)} collective-permute-done((bf16[224,512]{1,0:T(8,128)(2,1)}, bf16[224,512]{1,0:T(8,128)(2,1)S(1)}, u32[]{:S(2)}, u32[]{:S(2)}) %collective-permute-start.9) | collective-permute-done | bytes 229408 | tf_op jit(solution)/shard_map/ppermute | solution.py:24
  20.2 2.5 %collective-permute-start.14 = (bf16[224,512]{1,0:T(8,128)(2,1)S(1)}, bf16[224,512]{1,0:T(8,128)(2,1)S(1)}, u32[]{:S(2)}, u32[]{:S(2)}) collective-permute-start(bf16[224,512]{1,0:T(8,128)(2,1)S(1)} %collective-permute-done.11.refs_6_), channel_id=1, source_target_pairs={{0,17},{1,16},{2,19},{3,18},{16,1},{17,0},{18,3},{19,2},{4,21},{5,... | collective-permute-start | bytes 688136 | tf_op jit(solution)/shard_map/ppermute | solution.py:313
  22.7 0.4 collective-permute-start.15
  23.1 0.0 collective-permute-done.13.refs_8_
  23.1 1.2 %collective-permute-start.8 = (bf16[224,1024]{1,0:T(8,128)(2,1)}, bf16[224,1024]{1,0:T(8,128)(2,1)S(1)}, u32[]{:S(2)}, u32[]{:S(2)}) collective-permute-start(bf16[224,1024]{1,0:T(8,128)(2,1)} %copy-done.3), channel_id=1, source_target_pairs={{0,8},{4,12},{8,0},{12,4},{1,9},{5,13},{9,1},{13,5},{2,10},{6,14},... | collective-permute-start | bytes 1376264 | tf_op jit(solution)/shard_map/ppermute | solution.py:24
  24.4 4.9 %collective-permute-done.14.refs_9_ = bf16[224,512]{1,0:T(8,128)(2,1)S(1)} collective-permute-done((bf16[224,512]{1,0:T(8,128)(2,1)S(1)}, bf16[224,512]{1,0:T(8,128)(2,1)S(1)}, u32[]{:S(2)}, u32[]{:S(2)}) %collective-permute-start.14) | collective-permute-done | bytes 229408 | tf_op jit(solution)/shard_map/ppermute | solution.py:313
  29.3 0.0 collective-permute-start.10
  29.3 0.0 collective-permute-done.15.refs_10_
  29.3 0.5 collective-permute-start.1
  29.8 6.1 %collective-permute-done.8.refs_2_ = bf16[224,1024]{1,0:T(8,128)(2,1)S(1)} collective-permute-done((bf16[224,1024]{1,0:T(8,128)(2,1)}, bf16[224,1024]{1,0:T(8,128)(2,1)S(1)}, u32[]{:S(2)}, u32[]{:S(2)}) %collective-permute-start.8) | collective-permute-done | bytes 458784 | tf_op jit(solution)/shard_map/ppermute | solution.py:24
  35.9 0.5 collective-permute-start.17
  36.4 1.0 %collective-permute-done.16.refs_11_ = bf16[224,512]{1,0:T(8,128)(2,1)S(1)} collective-permute-done((bf16[224,512]{1,0:T(8,128)(2,1)S(1)}, bf16[224,512]{1,0:T(8,128)(2,1)S(1)}, u32[]{:S(2)}, u32[]{:S(2)}) %collective-permute-start.16) | collective-permute-done | bytes 229408 | tf_op jit(solution)/shard_map/ppermute | solution.py:24
  37.3 0.1 collective-permute-start.18
  37.5 0.5 collective-permute-start.22
  38.0 4.0 %shard_map.88 = (f32[4,64,128]{2,1,0:T(8,128)S(1)}, f32[4,64,128]{2,1,0:T(8,128)S(1)}) custom-call(bf16[256,4096]{1,0:T(8,128)(2,1)S(1)} %shard_map.87.refs_0_.refs_8_, bf16[224,4096]{1,0:T(8,128)(2,1)S(1)} %get-tuple-element.26.refs_1_.refs_0_, bf16[224,4096]{1,0:T(8,128)(2,1)} %collective-permute-done.refs_2_.refs_1_, ...), custom_call_target="tpu_custom_call" | custom-call | tf_op jit(solution)/shard_map/pallas_call | solution.py:327
  42.0 1.6 %collective-permute-start.2 = (f32[4,64,128]{2,1,0:T(8,128)S(1)}, f32[4,64,128]{2,1,0:T(8,128)S(1)}, u32[]{:S(2)}, u32[]{:S(2)}) collective-permute-start(f32[4,64,128]{2,1,0:T(8,128)S(1)} %get-tuple-element.30), channel_id=1, source_target_pairs={{0,8},{4,12},{8,0},{12,4},{1,9},{5,13},{9,1},{13,5},{2,10},{6,14},... | collective-permute-start | bytes 393224 | tf_op jit(solution)/shard_map/ppermute | solution.py:24
  43.6 0.0 collective-permute-done.18.refs_13_
  43.6 0.0 collective-permute-done.10.refs_5_
  43.6 6.2 %shard_map.89 = (bf16[224,512]{1,0:T(8,128)(2,1)S(1)}, bf16[224,512]{1,0:T(8,128)(2,1)S(1)}, bf16[224,512]{1,0:T(8,128)(2,1)S(1)}, bf16[224,512]{1,0:T(8,128)(2,1)S(1)}, bf16[896,2048]{1,0:T(8,128)(2,1)S(1)}) custom-call(bf16[224,4096]{1,0:T(8,128)(2,1)S(1)} %get-tuple-element.26.refs_1_.refs_0_, bf16[224,4096]{1,0:T(8,128)(2,1)} %collective-permute-done.refs_2_.refs_1_, ...), custom_call_target="tpu_custom_call" | custom-call | tf_op jit(solution)/shard_map/pallas_call | solution.py:349
  49.7 0.0 collective-permute-done.22.refs_3_
  49.7 0.0 copy-start.2
  49.8 6.2 %shard_map.90 = (bf16[224,512]{1,0:T(8,128)(2,1)S(1)}, bf16[224,512]{1,0:T(8,128)(2,1)S(1)}, bf16[224,512]{1,0:T(8,128)(2,1)S(1)}, bf16[224,512]{1,0:T(8,128)(2,1)S(1)}) custom-call(bf16[224,4096]{1,0:T(8,128)(2,1)S(1)} %get-tuple-element.26.refs_1_.refs_0_, bf16[224,4096]{1,0:T(8,128)(2,1)} %collective-permute-done.refs_2_.refs_1_, ...), custom_call_target="tpu_custom_call" | custom-call | tf_op jit(solution)/shard_map/pallas_call | solution.py:349
  55.9 0.1 collective-permute-start.23
  56.0 0.5 collective-permute-start.19
  56.5 0.6 collective-permute-start.3
  57.1 3.7 %collective-permute-done.3.refs_1_ = bf16[4,64,128]{2,1,0:T(8,128)(2,1)S(1)} collective-permute-done((bf16[4,64,128]{2,1,0:T(8,128)(2,1)S(1)}, bf16[4,64,128]{2,1,0:T(8,128)(2,1)S(1)}, u32[]{:S(2)}, u32[]{:S(2)}) %collective-permute-start.3) | collective-permute-done | bytes 65568 | tf_op jit(solution)/shard_map/ppermute | solution.py:24
  60.9 0.5 collective-permute-start.20
  61.4 1.6 %collective-permute-start.25 = (bf16[224,512]{1,0:T(8,128)(2,1)S(1)}, bf16[224,512]{1,0:T(8,128)(2,1)S(1)}, u32[]{:S(2)}, u32[]{:S(2)}) collective-permute-start(bf16[224,512]{1,0:T(8,128)(2,1)S(1)} %get-tuple-element.43), channel_id=1, source_target_pairs={{0,8},{4,12},{8,0},{12,4},{1,9},{5,13},{9,1},{13,5},{2,10},{6,14},... | collective-permute-start | bytes 688136 | tf_op jit(solution)/shard_map/ppermute | solution.py:24
  63.0 1.4 %collective-permute-start.24 = (bf16[224,512]{1,0:T(8,128)(2,1)S(1)}, bf16[224,512]{1,0:T(8,128)(2,1)S(1)}, u32[]{:S(2)}, u32[]{:S(2)}) collective-permute-start(bf16[224,512]{1,0:T(8,128)(2,1)S(1)} %get-tuple-element.42), channel_id=1, source_target_pairs={{0,12},{4,8},{8,4},{12,0},{1,13},{5,9},{9,5},{13,1},{2,14},{6,10},... | collective-permute-start | bytes 688136 | tf_op jit(solution)/shard_map/ppermute | solution.py:24
  64.4 5.0 %collective-permute-done.20.refs_13_ = bf16[224,512]{1,0:T(8,128)(2,1)S(1)} collective-permute-done((bf16[224,512]{1,0:T(8,128)(2,1)S(1)}, bf16[224,512]{1,0:T(8,128)(2,1)S(1)}, u32[]{:S(2)}, u32[]{:S(2)}) %collective-permute-start.20) | collective-permute-done | bytes 229408 | tf_op jit(solution)/shard_map/ppermute | solution.py:24
  69.4 2.9 %collective-permute-done.21.refs_14_ = bf16[224,512]{1,0:T(8,128)(2,1)S(1)} collective-permute-done((bf16[224,512]{1,0:T(8,128)(2,1)S(1)}, bf16[224,512]{1,0:T(8,128)(2,1)S(1)}, u32[]{:S(2)}, u32[]{:S(2)}) %collective-permute-start.21) | collective-permute-done | bytes 229408 | tf_op jit(solution)/shard_map/ppermute | solution.py:24
  72.2 1.9 %collective-permute-start.5 = (bf16[4,64,128]{2,1,0:T(8,128)(2,1)S(1)}, bf16[4,64,128]{2,1,0:T(8,128)(2,1)S(1)}, u32[]{:S(2)}, u32[]{:S(2)}) collective-permute-start(bf16[4,64,128]{2,1,0:T(8,128)(2,1)S(1)} %collective-permute-done.3.refs_1_), channel_id=1, source_target_pairs={{0,4},{4,0},{8,12},{12,8},{1,5},{5,1},{9,13},{13,9},{2,6},{6,2},{1... | collective-permute-start | bytes 196616 | tf_op jit(solution)/shard_map/ppermute | solution.py:24
  74.1 0.9 %collective-permute-done.5.refs_3_ = bf16[4,64,128]{2,1,0:T(8,128)(2,1)S(1)} collective-permute-done((bf16[4,64,128]{2,1,0:T(8,128)(2,1)S(1)}, bf16[4,64,128]{2,1,0:T(8,128)(2,1)S(1)}, u32[]{:S(2)}, u32[]{:S(2)}) %collective-permute-start.5) | collective-permute-done | bytes 65568 | tf_op jit(solution)/shard_map/ppermute | solution.py:24
  75.0 5.2 %shard_map.91 = (f32[224,4096]{1,0:T(8,128)}, f32[8,64,64]{2,1,0:T(8,128)}, f32[2,224,512]{2,1,0:T(8,128)S(1)}) custom-call(bf16[4,64,128]{2,1,0:T(8,128)(2,1)S(1)} %get-tuple-element.48.refs_0_, bf16[4,64,128]{2,1,0:T(8,128)(2,1)S(1)} %collective-permute-done.3.refs_1_, bf16[4,64,128]{2,1,0:T(8,128)(2,1)S(1)} %collective-permute-done.4.refs_2_, ...), custom_call_target="tpu_custom_call" | custom-call | tf_op jit(solution)/shard_map/pallas_call | solution.py:380
  80.2 0.8 %shard_map.92.refs_2_ = f32[224,4096]{1,0:T(8,128)} custom-call(f32[2,224,512]{2,1,0:T(8,128)S(1)} %get-tuple-element.41.refs_0_, bf16[224,512]{1,0:T(8,128)(2,1)S(1)} %collective-permute-done.25.refs_1_, f32[224,4096]{1,0:T(8,128)} %get-tuple-element.44.refs_2_), custom_call_target="tpu_custom_call", output_to_operand_aliasing={{}: (2, {})} | custom-call | tf_op jit(solution)/shard_map/pallas_call | solution.py:411
  81.1 0.8 %shard_map.93 = f32[224,4096]{1,0:T(8,128)} custom-call(f32[2,224,512]{2,1,0:T(8,128)S(1)} %get-tuple-element.41.refs_0_, bf16[224,512]{1,0:T(8,128)(2,1)S(1)} %collective-permute-done.24.refs_1_, f32[224,4096]{1,0:T(8,128)} %shard_map.92.refs_2_), custom_call_target="tpu_custom_call", output_to_operand_aliasing={{}: (2, {})} | custom-call | tf_op jit(solution)/shard_map/pallas_call | solution.py:411
  (26 shorter events, 0.1 us)
Async XLA Ops:
  0.6 4.8 %copy-start = (bf16[224,2048]{1,0:T(8,128)(2,1)S(1)}, bf16[224,2048]{1,0:T(8,128)(2,1)}, u32[]{:S(2)}) copy-start(bf16[224,2048]{1,0:T(8,128)(2,1)} %refs_4_.3) | copy-start | bytes 2752516
  3.4 0.8 copy-start.1
  4.1 0.8 copy-start.3
  4.1 1.3 %copy-start.4 = (bf16[224,512]{1,0:T(8,128)(2,1)}, bf16[224,512]{1,0:T(8,128)(2,1)S(1)}, u32[]{:S(2)}) copy-start(bf16[224,512]{1,0:T(8,128)(2,1)S(1)} %get-tuple-element.37) | copy-start | bytes 688132
  4.1 1.3 %copy-start.5 = (bf16[224,512]{1,0:T(8,128)(2,1)}, bf16[224,512]{1,0:T(8,128)(2,1)S(1)}, u32[]{:S(2)}) copy-start(bf16[224,512]{1,0:T(8,128)(2,1)S(1)} %get-tuple-element.32) | copy-start | bytes 688132
  4.9 32.6 %collective-permute-start = (bf16[224,4096]{1,0:T(8,128)(2,1)S(1)}, bf16[224,4096]{1,0:T(8,128)(2,1)}, u32[]{:S(2)}, u32[]{:S(2)}) collective-permute-start(bf16[224,4096]{1,0:T(8,128)(2,1)S(1)} %get-tuple-element.26.refs_1_.refs_0_), channel_id=1, source_target_pairs={{0,4},{4,0},{8,12},{12,8},{1,5},{5,1},{9,13},{13,9},{2,6},{6,2},{1... | collective-permute-start | bytes 5505032 | tf_op jit(solution)/shard_map/ppermute | solution.py:24
  5.5 8.8 %collective-permute-start.11 = (bf16[224,512]{1,0:T(8,128)(2,1)S(1)}, bf16[224,512]{1,0:T(8,128)(2,1)S(1)}, u32[]{:S(2)}, u32[]{:S(2)}) collective-permute-start(bf16[224,512]{1,0:T(8,128)(2,1)S(1)} %constant_dynamic-slice_fusion), channel_id=1, source_target_pairs={{0,8},{4,12},{8,0},{12,4},{1,9},{5,13},{9,1},{13,5},{2,10},{6,14},... | collective-permute-start | bytes 688136 | tf_op jit(solution)/shard_map/ppermute | solution.py:24
  12.5 61.6 %collective-permute-start.7 = (bf16[256,4096]{1,0:T(8,128)(2,1)S(1)}, bf16[256,4096]{1,0:T(8,128)(2,1)S(1)}, u32[]{:S(2)}, u32[]{:S(2)}) collective-permute-start(bf16[256,4096]{1,0:T(8,128)(2,1)S(1)} %shard_map.87.refs_0_.refs_8_), channel_id=1, source_target_pairs={{0,4},{4,0},{8,12},{12,8},{1,5},{5,1},{9,13},{13,9},{2,6},{6,2},{1... | collective-permute-start | bytes 6291464 | tf_op jit(solution)/shard_map/ppermute | solution.py:24
  12.6 7.5 %collective-permute-start.9 = (bf16[224,512]{1,0:T(8,128)(2,1)}, bf16[224,512]{1,0:T(8,128)(2,1)S(1)}, u32[]{:S(2)}, u32[]{:S(2)}) collective-permute-start(bf16[224,512]{1,0:T(8,128)(2,1)} %copy-done.5), channel_id=1, source_target_pairs={{0,12},{4,8},{8,4},{12,0},{1,13},{5,9},{9,5},{13,1},{2,14},{6,10},... | collective-permute-start | bytes 688136 | tf_op jit(solution)/shard_map/ppermute | solution.py:24
  14.3 8.4 %collective-permute-start.12 = (bf16[224,512]{1,0:T(8,128)(2,1)S(1)}, bf16[224,512]{1,0:T(8,128)(2,1)S(1)}, u32[]{:S(2)}, u32[]{:S(2)}) collective-permute-start(bf16[224,512]{1,0:T(8,128)(2,1)S(1)} %collective-permute-done.11.refs_6_), channel_id=1, source_target_pairs={{0,1},{1,0},{2,3},{3,2},{16,17},{17,16},{18,19},{19,18},{4,5},{5,4... | collective-permute-start | bytes 688136 | tf_op jit(solution)/shard_map/ppermute | solution.py:313
  16.1 7.0 %collective-permute-start.13 = (bf16[224,512]{1,0:T(8,128)(2,1)S(1)}, bf16[224,512]{1,0:T(8,128)(2,1)S(1)}, u32[]{:S(2)}, u32[]{:S(2)}) collective-permute-start(bf16[224,512]{1,0:T(8,128)(2,1)S(1)} %collective-permute-done.11.refs_6_), channel_id=1, source_target_pairs={{0,16},{1,17},{2,18},{3,19},{16,0},{17,1},{18,2},{19,3},{4,20},{5,... | collective-permute-start | bytes 688136 | tf_op jit(solution)/shard_map/ppermute | solution.py:313
  20.2 9.1 %collective-permute-start.14 = (bf16[224,512]{1,0:T(8,128)(2,1)S(1)}, bf16[224,512]{1,0:T(8,128)(2,1)S(1)}, u32[]{:S(2)}, u32[]{:S(2)}) collective-permute-start(bf16[224,512]{1,0:T(8,128)(2,1)S(1)} %collective-permute-done.11.refs_6_), channel_id=1, source_target_pairs={{0,17},{1,16},{2,19},{3,18},{16,1},{17,0},{18,3},{19,2},{4,21},{5,... | collective-permute-start | bytes 688136 | tf_op jit(solution)/shard_map/ppermute | solution.py:313
  22.7 6.6 %collective-permute-start.15 = (bf16[224,512]{1,0:T(8,128)(2,1)S(1)}, bf16[224,512]{1,0:T(8,128)(2,1)S(1)}, u32[]{:S(2)}, u32[]{:S(2)}) collective-permute-start(bf16[224,512]{1,0:T(8,128)(2,1)S(1)} %collective-permute-done.11.refs_6_), channel_id=1, source_target_pairs={{0,4},{4,0},{8,12},{12,8},{1,5},{5,1},{9,13},{13,9},{2,6},{6,2},{1... | collective-permute-start | bytes 688136 | tf_op jit(solution)/shard_map/ppermute | solution.py:24
  23.1 12.7 %collective-permute-start.8 = (bf16[224,1024]{1,0:T(8,128)(2,1)}, bf16[224,1024]{1,0:T(8,128)(2,1)S(1)}, u32[]{:S(2)}, u32[]{:S(2)}) collective-permute-start(bf16[224,1024]{1,0:T(8,128)(2,1)} %copy-done.3), channel_id=1, source_target_pairs={{0,8},{4,12},{8,0},{12,4},{1,9},{5,13},{9,1},{13,5},{2,10},{6,14},... | collective-permute-start | bytes 1376264 | tf_op jit(solution)/shard_map/ppermute | solution.py:24
  29.3 14.3 %collective-permute-start.10 = (bf16[224,2048]{1,0:T(8,128)(2,1)S(1)}, bf16[224,2048]{1,0:T(8,128)(2,1)S(1)}, u32[]{:S(2)}, u32[]{:S(2)}) collective-permute-start(bf16[224,2048]{1,0:T(8,128)(2,1)S(1)} %copy-done), channel_id=1, source_target_pairs={{0,4},{4,0},{8,12},{12,8},{1,5},{5,1},{9,13},{13,9},{2,6},{6,2},{1... | collective-permute-start | bytes 2752520 | tf_op jit(solution)/shard_map/ppermute | solution.py:24
  29.3 6.6 %collective-permute-start.1 = (bf16[4,224,256]{2,1,0:T(8,128)(2,1)}, bf16[4,224,256]{2,1,0:T(8,128)(2,1)S(1)}, u32[]{:S(2)}, u32[]{:S(2)}) collective-permute-start(bf16[4,224,256]{2,1,0:T(8,128)(2,1)} %copy-done.1), channel_id=1, source_target_pairs={{0,4},{4,0},{8,12},{12,8},{1,5},{5,1},{9,13},{13,9},{2,6},{6,2},{1... | collective-permute-start | bytes 1376264 | tf_op jit(solution)/shard_map/ppermute | solution.py:24
  35.9 1.5 %collective-permute-start.16 = (bf16[224,512]{1,0:T(8,128)(2,1)S(1)}, bf16[224,512]{1,0:T(8,128)(2,1)S(1)}, u32[]{:S(2)}, u32[]{:S(2)}) collective-permute-start(bf16[224,512]{1,0:T(8,128)(2,1)S(1)} %collective-permute-done.12.refs_7_), channel_id=1, source_target_pairs={{0,4},{4,0},{8,12},{12,8},{1,5},{5,1},{9,13},{13,9},{2,6},{6,2},{1... | collective-permute-start | bytes 688136 | tf_op jit(solution)/shard_map/ppermute | solution.py:24
  35.9 6.1 %collective-permute-start.17 = (bf16[224,512]{1,0:T(8,128)(2,1)S(1)}, bf16[224,512]{1,0:T(8,128)(2,1)S(1)}, u32[]{:S(2)}, u32[]{:S(2)}) collective-permute-start(bf16[224,512]{1,0:T(8,128)(2,1)S(1)} %collective-permute-done.13.refs_8_), channel_id=1, source_target_pairs={{0,4},{4,0},{8,12},{12,8},{1,5},{5,1},{9,13},{13,9},{2,6},{6,2},{1... | collective-permute-start | bytes 688136 | tf_op jit(solution)/shard_map/ppermute | solution.py:24
  37.3 6.2 %collective-permute-start.18 = (bf16[224,512]{1,0:T(8,128)(2,1)S(1)}, bf16[224,512]{1,0:T(8,128)(2,1)S(1)}, u32[]{:S(2)}, u32[]{:S(2)}) collective-permute-start(bf16[224,512]{1,0:T(8,128)(2,1)S(1)} %collective-permute-done.14.refs_9_), channel_id=1, source_target_pairs={{0,4},{4,0},{8,12},{12,8},{1,5},{5,1},{9,13},{13,9},{2,6},{6,2},{1... | collective-permute-start | bytes 688136 | tf_op jit(solution)/shard_map/ppermute | solution.py:24
  37.5 12.3 %collective-permute-start.22 = (bf16[224,512]{1,0:T(8,128)(2,1)}, bf16[224,512]{1,0:T(8,128)(2,1)S(1)}, u32[]{:S(2)}, u32[]{:S(2)}) collective-permute-start(bf16[224,512]{1,0:T(8,128)(2,1)} %copy-done.4), channel_id=1, source_target_pairs={{0,12},{4,8},{8,4},{12,0},{1,13},{5,9},{9,5},{13,1},{2,14},{6,10},... | collective-permute-start | bytes 688136 | tf_op jit(solution)/shard_map/ppermute | solution.py:24
  42.0 14.5 %collective-permute-start.2 = (f32[4,64,128]{2,1,0:T(8,128)S(1)}, f32[4,64,128]{2,1,0:T(8,128)S(1)}, u32[]{:S(2)}, u32[]{:S(2)}) collective-permute-start(f32[4,64,128]{2,1,0:T(8,128)S(1)} %get-tuple-element.30), channel_id=1, source_target_pairs={{0,8},{4,12},{8,0},{12,4},{1,9},{5,13},{9,1},{13,5},{2,10},{6,14},... | collective-permute-start | bytes 393224 | tf_op jit(solution)/shard_map/ppermute | solution.py:24
  49.7 25.2 %copy-start.2 = (bf16[4,224,256]{2,1,0:T(8,128)(2,1)S(1)}, bf16[4,224,256]{2,1,0:T(8,128)(2,1)}, u32[]{:S(2)}) copy-start(bf16[4,224,256]{2,1,0:T(8,128)(2,1)} %copy-done.1) | copy-start | bytes 1376260
  55.9 5.5 %collective-permute-start.23 = (bf16[224,512]{1,0:T(8,128)(2,1)S(1)}, bf16[224,512]{1,0:T(8,128)(2,1)S(1)}, u32[]{:S(2)}, u32[]{:S(2)}) collective-permute-start(bf16[224,512]{1,0:T(8,128)(2,1)S(1)} %get-tuple-element.40), channel_id=1, source_target_pairs={{0,4},{4,0},{8,12},{12,8},{1,5},{5,1},{9,13},{13,9},{2,6},{6,2},{1... | collective-permute-start | bytes 688136 | tf_op jit(solution)/shard_map/ppermute | solution.py:24
  56.0 7.0 %collective-permute-start.19 = (bf16[224,512]{1,0:T(8,128)(2,1)S(1)}, bf16[224,512]{1,0:T(8,128)(2,1)S(1)}, u32[]{:S(2)}, u32[]{:S(2)}) collective-permute-start(bf16[224,512]{1,0:T(8,128)(2,1)S(1)} %get-tuple-element.34), channel_id=1, source_target_pairs={{0,4},{4,0},{8,12},{12,8},{1,5},{5,1},{9,13},{13,9},{2,6},{6,2},{1... | collective-permute-start | bytes 688136 | tf_op jit(solution)/shard_map/ppermute | solution.py:24
  56.5 4.3 %collective-permute-start.3 = (bf16[4,64,128]{2,1,0:T(8,128)(2,1)S(1)}, bf16[4,64,128]{2,1,0:T(8,128)(2,1)S(1)}, u32[]{:S(2)}, u32[]{:S(2)}) collective-permute-start(bf16[4,64,128]{2,1,0:T(8,128)(2,1)S(1)} %get-tuple-element.48.refs_0_), channel_id=1, source_target_pairs={{0,8},{4,12},{8,0},{12,4},{1,9},{5,13},{9,1},{13,5},{2,10},{6,14},... | collective-permute-start | bytes 196616 | tf_op jit(solution)/shard_map/ppermute | solution.py:24
  57.1 4.3 %collective-permute-start.4 = (bf16[4,64,128]{2,1,0:T(8,128)(2,1)S(1)}, bf16[4,64,128]{2,1,0:T(8,128)(2,1)S(1)}, u32[]{:S(2)}, u32[]{:S(2)}) collective-permute-start(bf16[4,64,128]{2,1,0:T(8,128)(2,1)S(1)} %get-tuple-element.48.refs_0_), channel_id=1, source_target_pairs={{0,4},{4,0},{8,12},{12,8},{1,5},{5,1},{9,13},{13,9},{2,6},{6,2},{1... | collective-permute-start | bytes 196616 | tf_op jit(solution)/shard_map/ppermute | solution.py:24
  60.9 8.5 %collective-permute-start.20 = (bf16[224,512]{1,0:T(8,128)(2,1)S(1)}, bf16[224,512]{1,0:T(8,128)(2,1)S(1)}, u32[]{:S(2)}, u32[]{:S(2)}) collective-permute-start(bf16[224,512]{1,0:T(8,128)(2,1)S(1)} %get-tuple-element.35), channel_id=1, source_target_pairs={{0,8},{4,12},{8,0},{12,4},{1,9},{5,13},{9,1},{13,5},{2,10},{6,14},... | collective-permute-start | bytes 688136 | tf_op jit(solution)/shard_map/ppermute | solution.py:24
  61.4 10.8 %collective-permute-start.21 = (bf16[224,512]{1,0:T(8,128)(2,1)S(1)}, bf16[224,512]{1,0:T(8,128)(2,1)S(1)}, u32[]{:S(2)}, u32[]{:S(2)}) collective-permute-start(bf16[224,512]{1,0:T(8,128)(2,1)S(1)} %get-tuple-element.36), channel_id=1, source_target_pairs={{0,12},{4,8},{8,4},{12,0},{1,13},{5,9},{9,5},{13,1},{2,14},{6,10},... | collective-permute-start | bytes 688136 | tf_op jit(solution)/shard_map/ppermute | solution.py:24
  61.4 18.8 %collective-permute-start.25 = (bf16[224,512]{1,0:T(8,128)(2,1)S(1)}, bf16[224,512]{1,0:T(8,128)(2,1)S(1)}, u32[]{:S(2)}, u32[]{:S(2)}) collective-permute-start(bf16[224,512]{1,0:T(8,128)(2,1)S(1)} %get-tuple-element.43), channel_id=1, source_target_pairs={{0,8},{4,12},{8,0},{12,4},{1,9},{5,13},{9,1},{13,5},{2,10},{6,14},... | collective-permute-start | bytes 688136 | tf_op jit(solution)/shard_map/ppermute | solution.py:24
  63.0 18.1 %collective-permute-start.24 = (bf16[224,512]{1,0:T(8,128)(2,1)S(1)}, bf16[224,512]{1,0:T(8,128)(2,1)S(1)}, u32[]{:S(2)}, u32[]{:S(2)}) collective-permute-start(bf16[224,512]{1,0:T(8,128)(2,1)S(1)} %get-tuple-element.42), channel_id=1, source_target_pairs={{0,12},{4,8},{8,4},{12,0},{1,13},{5,9},{9,5},{13,1},{2,14},{6,10},... | collective-permute-start | bytes 688136 | tf_op jit(solution)/shard_map/ppermute | solution.py:24
  69.4 5.6 %collective-permute-start.6 = (f32[4,64,128]{2,1,0:T(8,128)S(1)}, f32[4,64,128]{2,1,0:T(8,128)S(1)}, u32[]{:S(2)}, u32[]{:S(2)}) collective-permute-start(f32[4,64,128]{2,1,0:T(8,128)S(1)} %get-tuple-element.49.refs_4_), channel_id=1, source_target_pairs={{0,4},{4,0},{8,12},{12,8},{1,5},{5,1},{9,13},{13,9},{2,6},{6,2},{1... | collective-permute-start | bytes 393224 | tf_op jit(solution)/shard_map/ppermute | solution.py:24
  72.2 2.8 %collective-permute-start.5 = (bf16[4,64,128]{2,1,0:T(8,128)(2,1)S(1)}, bf16[4,64,128]{2,1,0:T(8,128)(2,1)S(1)}, u32[]{:S(2)}, u32[]{:S(2)}) collective-permute-start(bf16[4,64,128]{2,1,0:T(8,128)(2,1)S(1)} %collective-permute-done.3.refs_1_), channel_id=1, source_target_pairs={{0,4},{4,0},{8,12},{12,8},{1,5},{5,1},{9,13},{13,9},{2,6},{6,2},{1... | collective-permute-start | bytes 196616 | tf_op jit(solution)/shard_map/ppermute | solution.py:24

commit v10 on v9

--- a/solution.py
+++ b/solution.py
@@ -84,6 +84,12 @@
                 parts[t][...] = values[:, cut[0]:cut[0] + cut[1]]
     for c in rest:
         c.wait()
+
+
+def piece_kernel(harm, out, sem):
+    copy = pltpu.make_async_copy(harm.at[:, aligned(position()[2], out.shape[1])], out, sem)
+    copy.start()
+    copy.wait()
 
 
 def build_kernel(vox_ref, wgt_ref, matrix_ref, tile_ref):
@@ -264,10 +270,9 @@
     slab_count = lax.axis_size("slab")
     slab_bits = 1 if slab_count % 2 == 0 else 0
     pieces = 1 << (group_bits + slab_bits)
-    place = position()[2]
     width = harmonics.shape[1] // pieces
     rows_shape = (rows, samples)
-    coef_far, measured_far, vox_far, wgt_far, ids_far, table_far = [
+    coef_far, measured_far, vox_far, wgt_far, ids_far, table_far, harm_far = [
         pltpu.with_memory_space_constraint(v, pltpu.HBM)
         for v in (
             coefficients,
@@ -276,10 +281,13 @@
             ray_weights.reshape(rows_shape),
             angle_ids,
             angle_table,
+            harmonics,
         )
     ]
 
-    piece = lax.dynamic_slice_in_dim(harmonics, place * width, width, 1)
+    piece = kernel(
+        piece_kernel, [HBM], VMEM, shape((coef_local, width), bf16), [pltpu.SemaphoreType.DMA(())], grant=4
+    )(harm_far)
     fetched = {m: [swap(piece, "coef", m)] for m in range(2, count, 2)}
     table_shape = shape((half,) + angle_table.shape[1:], bf16)
     *parts, own, vox, wgt, table_mine, table_other = kernel(

time: 82.5 us -> 88.6 us (1.074)
  waiting for transfers between devices: 28.7 us -> 41 us
  Pallas kernels: 30.2 us -> 26.7 us
  local copies, waits for them, and re-layouts: 1.58 us -> 0.01 us
    ppermute x23, waiting for transfers between devices: 23.7 us -> 31.3 us  [swap(): return lax.ppermute(value, axis, [(i, i ^ mask) for i in range(count)])]
    ppermute x3, waiting for transfers between devices: 4.93 us -> 9.71 us  [step_of(): fetched[m].append(lax.ppermute(fetched[m][0], ('groups', 'slab'), pairs))]
    pallas_call x2, Pallas kernels: 12.3 us -> 9.3 us  [step_of(): kernel(lambda *refs: penalty_kernel(count, pieces, cut, first, *refs), [V...]
    unnamed x12 -> x2, local copies, waits for them, and re-layouts: 1.56 us -> 0.01 us
    pallas_call x1, Pallas kernels: 3.99 us -> 2.5 us  [step_of(): kernel(lambda *refs: sums_kernel(count, *refs), [VMEM] * 5 + [HBM], [VMEM...]
    pallas_call x0 -> x1, Pallas kernels: none -> 0.95 us  [step_of(): kernel(piece_kernel, [HBM], VMEM, shape((coef_local, width), bf16), [pltp...]
  transfers between devices with their start and end apart: 26 -> 26, of which waited for: 9 -> 10; matrix products, arithmetic and copies ran while one was open for 0% -> 0% of each run, Pallas kernels for 33% -> 26%
where the time goes in v10:
time: 88.6 us; the launch traced here: 88.3 us
  waiting for transfers between devices  41 us (46%)
  Pallas kernels  26.7 us (30%)
  starting transfers between devices  19.8 us (22%)
    ppermute x23, waiting for transfers between devices, swap(): return lax.ppermute(value, axis, [(i, i ^ mask) for i in range(count)])  31.3 us
    ppermute x23, starting transfers between devices, swap(): return lax.ppermute(value, axis, [(i, i ^ mask) for i in range(count)])  14.7 us
    ppermute x3, waiting for transfers between devices, step_of(): fetched[m].append(lax.ppermute(fetched[m][0], ('groups', 'slab'), pairs))  9.71 us
    pallas_call x2, Pallas kernels, step_of(): kernel(lambda *refs: penalty_kernel(count, pieces, cut, first, *refs), [V...  9.3 us
    pallas_call x1, Pallas kernels, step_of(): kernel(lambda *refs: data_kernel(count, cuts, len(half_mine), *refs), [VM...  5.2 us
    ppermute x3, starting transfers between devices, step_of(): fetched[m].append(lax.ppermute(fetched[m][0], ('groups', 'slab'), pairs))  5.12 us
    pallas_call x1, Pallas kernels, step_of(): kernel(build_kernel, [VMEM, VMEM], VMEM, shape((rows // 2, cols), bf16),...  4.34 us
    pallas_call x1, Pallas kernels, step_of(): kernel(lambda *refs: prepare_kernel(count, cuts, *refs), [HBM] * 5, [VMEM...  2.72 us
  transfers between devices with their start and end apart: 26, of which 10 were waited for; matrix products, arithmetic and copies ran while one was open for 0% of the time, Pallas kernels for 26%

profile of v10, /device:TPU:0, one launch (start us, length us, event | category | flops | bytes accessed | tf_op | source)
XLA Modules:
  0.0 88.3 jit_solution(922756538507009387)
XLA Ops:
  0.6 0.0 copy-start
  0.6 2.7 %shard_map.86 = (bf16[224,1024]{1,0:T(8,128)(2,1)S(1)}, bf16[224,512]{1,0:T(8,128)(2,1)S(1)}, bf16[224,512]{1,0:T(8,128)(2,1)S(1)}, bf16[224,4096]{1,0:T(8,128)(...) custom-call(s32[8]{0:T(128)} %refs_0_.1, ...), custom_call_target="tpu_custom_call" | custom-call | tf_op jit(solution)/shard_map/pallas_call | solution.py:293
  3.4 0.6 collective-permute-start
  3.9 4.3 %shard_map.87.refs_0_.refs_8_ = bf16[256,4096]{1,0:T(8,128)(2,1)S(1)} custom-call(s32[256,128]{1,0:T(8,128)S(1)} %get-tuple-element.24.vox_ref, s32[256,128]{1,0:T(8,128)S(1)} %get-tuple-element.25.wgt_ref), custom_call_target="tpu_custom_call" | custom-call | tf_op jit(solution)/shard_map/pallas_call | solution.py:323
  8.3 0.1 collective-permute-start.7
  8.4 3.0 %collective-permute-start.8 = (bf16[224,1024]{1,0:T(8,128)(2,1)S(1)}, bf16[224,1024]{1,0:T(8,128)(2,1)S(1)}, u32[]{:S(2)}, u32[]{:S(2)}) collective-permute-start(bf16[224,1024]{1,0:T(8,128)(2,1)S(1)} %get-tuple-element.31), channel_id=1, source_target_pairs={{0,8},{4,12},{8,0},{12,4},{1,9},{5,13},{9,1},{13,5},{2,10},{6,14},... | collective-permute-start | bytes 1376264 | tf_op jit(solution)/shard_map/ppermute | solution.py:24
  11.3 0.9 %shard_map.89 = bf16[224,512]{1,0:T(8,128)(2,1)S(1)} custom-call(bf16[224,2048]{1,0:T(8,128)(2,1)} %refs_4_.3), custom_call_target="tpu_custom_call" | custom-call | tf_op jit(solution)/shard_map/pallas_call | solution.py:288
  12.3 0.1 collective-permute-start.11
  12.4 1.1 %collective-permute-start.9 = (bf16[224,512]{1,0:T(8,128)(2,1)S(1)}, bf16[224,512]{1,0:T(8,128)(2,1)S(1)}, u32[]{:S(2)}, u32[]{:S(2)}) collective-permute-start(bf16[224,512]{1,0:T(8,128)(2,1)S(1)} %get-tuple-element.32), channel_id=1, source_target_pairs={{0,12},{4,8},{8,4},{12,0},{1,13},{5,9},{9,5},{13,1},{2,14},{6,10},... | collective-permute-start | bytes 688136 | tf_op jit(solution)/shard_map/ppermute | solution.py:24
  13.5 14.1 %collective-permute-done.11.refs_6_ = bf16[224,512]{1,0:T(8,128)(2,1)S(1)} collective-permute-done((bf16[224,512]{1,0:T(8,128)(2,1)S(1)}, bf16[224,512]{1,0:T(8,128)(2,1)S(1)}, u32[]{:S(2)}, u32[]{:S(2)}) %collective-permute-start.11) | collective-permute-done | bytes 229408 | tf_op jit(solution)/shard_map/ppermute | solution.py:24
  27.6 2.1 %collective-permute-start.12 = (bf16[224,512]{1,0:T(8,128)(2,1)S(1)}, bf16[224,512]{1,0:T(8,128)(2,1)S(1)}, u32[]{:S(2)}, u32[]{:S(2)}) collective-permute-start(bf16[224,512]{1,0:T(8,128)(2,1)S(1)} %collective-permute-done.11.refs_6_), channel_id=1, source_target_pairs={{0,1},{1,0},{2,3},{3,2},{16,17},{17,16},{18,19},{19,18},{4,5},{5,4... | collective-permute-start | bytes 688136 | tf_op jit(solution)/shard_map/ppermute | solution.py:321
  29.7 1.6 %collective-permute-done.9.refs_3_ = bf16[224,512]{1,0:T(8,128)(2,1)S(1)} collective-permute-done((bf16[224,512]{1,0:T(8,128)(2,1)S(1)}, bf16[224,512]{1,0:T(8,128)(2,1)S(1)}, u32[]{:S(2)}, u32[]{:S(2)}) %collective-permute-start.9) | collective-permute-done | bytes 229408 | tf_op jit(solution)/shard_map/ppermute | solution.py:24
  31.3 1.5 %collective-permute-start.13 = (bf16[224,512]{1,0:T(8,128)(2,1)S(1)}, bf16[224,512]{1,0:T(8,128)(2,1)S(1)}, u32[]{:S(2)}, u32[]{:S(2)}) collective-permute-start(bf16[224,512]{1,0:T(8,128)(2,1)S(1)} %collective-permute-done.11.refs_6_), channel_id=1, source_target_pairs={{0,16},{1,17},{2,18},{3,19},{16,0},{17,1},{18,2},{19,3},{4,20},{5,... | collective-permute-start | bytes 688136 | tf_op jit(solution)/shard_map/ppermute | solution.py:321
  32.8 1.5 %collective-permute-start.14 = (bf16[224,512]{1,0:T(8,128)(2,1)S(1)}, bf16[224,512]{1,0:T(8,128)(2,1)S(1)}, u32[]{:S(2)}, u32[]{:S(2)}) collective-permute-start(bf16[224,512]{1,0:T(8,128)(2,1)S(1)} %collective-permute-done.11.refs_6_), channel_id=1, source_target_pairs={{0,17},{1,16},{2,19},{3,18},{16,1},{17,0},{18,3},{19,2},{4,21},{5,... | collective-permute-start | bytes 688136 | tf_op jit(solution)/shard_map/ppermute | solution.py:321
  34.3 0.0 collective-permute-done.12.refs_7_
  34.3 0.5 collective-permute-start.10
  34.8 9.7 %collective-permute-done.13.refs_8_ = bf16[224,512]{1,0:T(8,128)(2,1)S(1)} collective-permute-done((bf16[224,512]{1,0:T(8,128)(2,1)S(1)}, bf16[224,512]{1,0:T(8,128)(2,1)S(1)}, u32[]{:S(2)}, u32[]{:S(2)}) %collective-permute-start.13) | collective-permute-done | bytes 229408 | tf_op jit(solution)/shard_map/ppermute | solution.py:321
  44.5 0.0 collective-permute-done.14.refs_9_
  44.5 0.5 collective-permute-start.15
  45.0 1.6 %collective-permute-done.15.refs_10_ = bf16[224,512]{1,0:T(8,128)(2,1)S(1)} collective-permute-done((bf16[224,512]{1,0:T(8,128)(2,1)S(1)}, bf16[224,512]{1,0:T(8,128)(2,1)S(1)}, u32[]{:S(2)}, u32[]{:S(2)}) %collective-permute-start.15) | collective-permute-done | bytes 229408 | tf_op jit(solution)/shard_map/ppermute | solution.py:24
  46.6 0.1 collective-permute-start.16
  46.8 0.0 collective-permute-done.1.refs_4_
  46.8 0.4 collective-permute-start.17
  47.1 1.0 %collective-permute-done.16.refs_11_ = bf16[224,512]{1,0:T(8,128)(2,1)S(1)} collective-permute-done((bf16[224,512]{1,0:T(8,128)(2,1)S(1)}, bf16[224,512]{1,0:T(8,128)(2,1)S(1)}, u32[]{:S(2)}, u32[]{:S(2)}) %collective-permute-start.16) | collective-permute-done | bytes 229408 | tf_op jit(solution)/shard_map/ppermute | solution.py:24
  48.1 0.1 collective-permute-start.18
  48.3 1.6 %collective-permute-start.22 = (bf16[224,512]{1,0:T(8,128)(2,1)S(1)}, bf16[224,512]{1,0:T(8,128)(2,1)S(1)}, u32[]{:S(2)}, u32[]{:S(2)}) collective-permute-start(bf16[224,512]{1,0:T(8,128)(2,1)S(1)} %get-tuple-element.37), channel_id=1, source_target_pairs={{0,12},{4,8},{8,4},{12,0},{1,13},{5,9},{9,5},{13,1},{2,14},{6,10},... | collective-permute-start | bytes 688136 | tf_op jit(solution)/shard_map/ppermute | solution.py:24
  49.9 2.5 %shard_map.88 = (f32[4,64,128]{2,1,0:T(8,128)S(1)}, f32[4,64,128]{2,1,0:T(8,128)S(1)}) custom-call(bf16[256,4096]{1,0:T(8,128)(2,1)S(1)} %shard_map.87.refs_0_.refs_8_, bf16[224,4096]{1,0:T(8,128)(2,1)S(1)} %get-tuple-element.26.refs_1_.refs_0_, bf16[224,4096]{1,0:T(8,128)(2,1)S(1)} %collective-permute-done.refs_2_.refs_1_, ...), custom_call_target="tpu_custom_call" | custom-call | tf_op jit(solution)/shard_map/pallas_call | solution.py:335
  52.4 0.0 collective-permute-done.17.refs_12_
  52.4 0.5 collective-permute-start.2
  52.8 4.7 %shard_map.90 = (bf16[224,512]{1,0:T(8,128)(2,1)S(1)}, bf16[224,512]{1,0:T(8,128)(2,1)S(1)}, bf16[224,512]{1,0:T(8,128)(2,1)S(1)}, bf16[224,512]{1,0:T(8,128)(2,1)S(1)}, bf16[896,2048]{1,0:T(8,128)(2,1)S(1)}) custom-call(bf16[224,4096]{1,0:T(8,128)(2,1)S(1)} %get-tuple-element.26.refs_1_.refs_0_, bf16[224,4096]{1,0:T(8,128)(2,1)S(1)} %collective-permute-done.refs_2_.refs_1_, ...), custom_call_target="tpu_custom_call" | custom-call | tf_op jit(solution)/shard_map/pallas_call | solution.py:357
  57.5 0.0 collective-permute-done.22.refs_3_
  57.5 4.6 %shard_map.91 = (bf16[224,512]{1,0:T(8,128)(2,1)S(1)}, bf16[224,512]{1,0:T(8,128)(2,1)S(1)}, bf16[224,512]{1,0:T(8,128)(2,1)S(1)}, bf16[224,512]{1,0:T(8,128)(2,1)S(1)}) custom-call(bf16[224,4096]{1,0:T(8,128)(2,1)S(1)} %get-tuple-element.26.refs_1_.refs_0_, bf16[224,4096]{1,0:T(8,128)(2,1)S(1)} %collective-permute-done.refs_2_.refs_1_, ...), custom_call_target="tpu_custom_call" | custom-call | tf_op jit(solution)/shard_map/pallas_call | solution.py:357
  62.2 0.1 collective-permute-start.23
  62.2 0.5 collective-permute-start.19
  62.8 1.7 %collective-permute-start.3 = (bf16[4,64,128]{2,1,0:T(8,128)(2,1)S(1)}, bf16[4,64,128]{2,1,0:T(8,128)(2,1)S(1)}, u32[]{:S(2)}, u32[]{:S(2)}) collective-permute-start(bf16[4,64,128]{2,1,0:T(8,128)(2,1)S(1)} %get-tuple-element.48.refs_0_), channel_id=1, source_target_pairs={{0,8},{4,12},{8,0},{12,4},{1,9},{5,13},{9,1},{13,5},{2,10},{6,14},... | collective-permute-start | bytes 196616 | tf_op jit(solution)/shard_map/ppermute | solution.py:24
  64.5 0.0 collective-permute-start.4
  64.5 2.6 %collective-permute-done.3.refs_1_ = bf16[4,64,128]{2,1,0:T(8,128)(2,1)S(1)} collective-permute-done((bf16[4,64,128]{2,1,0:T(8,128)(2,1)S(1)}, bf16[4,64,128]{2,1,0:T(8,128)(2,1)S(1)}, u32[]{:S(2)}, u32[]{:S(2)}) %collective-permute-start.3) | collective-permute-done | bytes 65568 | tf_op jit(solution)/shard_map/ppermute | solution.py:24
  67.1 1.6 %collective-permute-start.20 = (bf16[224,512]{1,0:T(8,128)(2,1)S(1)}, bf16[224,512]{1,0:T(8,128)(2,1)S(1)}, u32[]{:S(2)}, u32[]{:S(2)}) collective-permute-start(bf16[224,512]{1,0:T(8,128)(2,1)S(1)} %get-tuple-element.35), channel_id=1, source_target_pairs={{0,8},{4,12},{8,0},{12,4},{1,9},{5,13},{9,1},{13,5},{2,10},{6,14},... | collective-permute-start | bytes 688136 | tf_op jit(solution)/shard_map/ppermute | solution.py:24
  68.8 0.4 collective-permute-start.25
  69.2 1.4 %collective-permute-start.24 = (bf16[224,512]{1,0:T(8,128)(2,1)S(1)}, bf16[224,512]{1,0:T(8,128)(2,1)S(1)}, u32[]{:S(2)}, u32[]{:S(2)}) collective-permute-start(bf16[224,512]{1,0:T(8,128)(2,1)S(1)} %get-tuple-element.42), channel_id=1, source_target_pairs={{0,12},{4,8},{8,4},{12,0},{1,13},{5,9},{9,5},{13,1},{2,14},{6,10},... | collective-permute-start | bytes 688136 | tf_op jit(solution)/shard_map/ppermute | solution.py:24
  70.6 4.7 %collective-permute-done.20.refs_13_ = bf16[224,512]{1,0:T(8,128)(2,1)S(1)} collective-permute-done((bf16[224,512]{1,0:T(8,128)(2,1)S(1)}, bf16[224,512]{1,0:T(8,128)(2,1)S(1)}, u32[]{:S(2)}, u32[]{:S(2)}) %collective-permute-start.20) | collective-permute-done | bytes 229408 | tf_op jit(solution)/shard_map/ppermute | solution.py:24
  75.3 4.3 %collective-permute-done.21.refs_14_ = bf16[224,512]{1,0:T(8,128)(2,1)S(1)} collective-permute-done((bf16[224,512]{1,0:T(8,128)(2,1)S(1)}, bf16[224,512]{1,0:T(8,128)(2,1)S(1)}, u32[]{:S(2)}, u32[]{:S(2)}) %collective-permute-start.21) | collective-permute-done | bytes 229408 | tf_op jit(solution)/shard_map/ppermute | solution.py:24
  79.7 0.4 collective-permute-start.5
  80.1 0.9 %collective-permute-done.5.refs_3_ = bf16[4,64,128]{2,1,0:T(8,128)(2,1)S(1)} collective-permute-done((bf16[4,64,128]{2,1,0:T(8,128)(2,1)S(1)}, bf16[4,64,128]{2,1,0:T(8,128)(2,1)S(1)}, u32[]{:S(2)}, u32[]{:S(2)}) %collective-permute-start.5) | collective-permute-done | bytes 65568 | tf_op jit(solution)/shard_map/ppermute | solution.py:24
  81.0 5.2 %shard_map.92 = (f32[224,4096]{1,0:T(8,128)}, f32[8,64,64]{2,1,0:T(8,128)}, f32[2,224,512]{2,1,0:T(8,128)S(1)}) custom-call(bf16[4,64,128]{2,1,0:T(8,128)(2,1)S(1)} %get-tuple-element.48.refs_0_, bf16[4,64,128]{2,1,0:T(8,128)(2,1)S(1)} %collective-permute-done.3.refs_1_, bf16[4,64,128]{2,1,0:T(8,128)(2,1)S(1)} %collective-permute-done.4.refs_2_, ...), custom_call_target="tpu_custom_call" | custom-call | tf_op jit(solution)/shard_map/pallas_call | solution.py:388
  86.2 0.8 shard_map.93.refs_2_
  87.0 0.4 collective-permute-done.24.refs_1_
  87.4 0.8 shard_map.94
  (16 shorter events, 0.1 us)
Async XLA Ops:
  0.6 33.7 %copy-start = (bf16[224,2048]{1,0:T(8,128)(2,1)S(1)}, bf16[224,2048]{1,0:T(8,128)(2,1)}, u32[]{:S(2)}) copy-start(bf16[224,2048]{1,0:T(8,128)(2,1)} %refs_4_.3) | copy-start | bytes 2752516
  3.4 44.9 %collective-permute-start = (bf16[224,4096]{1,0:T(8,128)(2,1)S(1)}, bf16[224,4096]{1,0:T(8,128)(2,1)S(1)}, u32[]{:S(2)}, u32[]{:S(2)}) collective-permute-start(bf16[224,4096]{1,0:T(8,128)(2,1)S(1)} %get-tuple-element.26.refs_1_.refs_0_), channel_id=1, source_target_pairs={{0,4},{4,0},{8,12},{12,8},{1,5},{5,1},{9,13},{13,9},{2,6},{6,2},{1... | collective-permute-start | bytes 5505032 | tf_op jit(solution)/shard_map/ppermute | solution.py:24
  8.3 71.8 %collective-permute-start.7 = (bf16[256,4096]{1,0:T(8,128)(2,1)S(1)}, bf16[256,4096]{1,0:T(8,128)(2,1)S(1)}, u32[]{:S(2)}, u32[]{:S(2)}) collective-permute-start(bf16[256,4096]{1,0:T(8,128)(2,1)S(1)} %shard_map.87.refs_0_.refs_8_), channel_id=1, source_target_pairs={{0,4},{4,0},{8,12},{12,8},{1,5},{5,1},{9,13},{13,9},{2,6},{6,2},{1... | collective-permute-start | bytes 6291464 | tf_op jit(solution)/shard_map/ppermute | solution.py:24
  8.4 24.4 %collective-permute-start.8 = (bf16[224,1024]{1,0:T(8,128)(2,1)S(1)}, bf16[224,1024]{1,0:T(8,128)(2,1)S(1)}, u32[]{:S(2)}, u32[]{:S(2)}) collective-permute-start(bf16[224,1024]{1,0:T(8,128)(2,1)S(1)} %get-tuple-element.31), channel_id=1, source_target_pairs={{0,8},{4,12},{8,0},{12,4},{1,9},{5,13},{9,1},{13,5},{2,10},{6,14},... | collective-permute-start | bytes 1376264 | tf_op jit(solution)/shard_map/ppermute | solution.py:24
  12.3 15.3 %collective-permute-start.11 = (bf16[224,512]{1,0:T(8,128)(2,1)S(1)}, bf16[224,512]{1,0:T(8,128)(2,1)S(1)}, u32[]{:S(2)}, u32[]{:S(2)}) collective-permute-start(bf16[224,512]{1,0:T(8,128)(2,1)S(1)} %shard_map.89), channel_id=1, source_target_pairs={{0,8},{4,12},{8,0},{12,4},{1,9},{5,13},{9,1},{13,5},{2,10},{6,14},... | collective-permute-start | bytes 688136 | tf_op jit(solution)/shard_map/ppermute | solution.py:24
  12.4 19.0 %collective-permute-start.9 = (bf16[224,512]{1,0:T(8,128)(2,1)S(1)}, bf16[224,512]{1,0:T(8,128)(2,1)S(1)}, u32[]{:S(2)}, u32[]{:S(2)}) collective-permute-start(bf16[224,512]{1,0:T(8,128)(2,1)S(1)} %get-tuple-element.32), channel_id=1, source_target_pairs={{0,12},{4,8},{8,4},{12,0},{1,13},{5,9},{9,5},{13,1},{2,14},{6,10},... | collective-permute-start | bytes 688136 | tf_op jit(solution)/shard_map/ppermute | solution.py:24
  27.6 6.7 %collective-permute-start.12 = (bf16[224,512]{1,0:T(8,128)(2,1)S(1)}, bf16[224,512]{1,0:T(8,128)(2,1)S(1)}, u32[]{:S(2)}, u32[]{:S(2)}) collective-permute-start(bf16[224,512]{1,0:T(8,128)(2,1)S(1)} %collective-permute-done.11.refs_6_), channel_id=1, source_target_pairs={{0,1},{1,0},{2,3},{3,2},{16,17},{17,16},{18,19},{19,18},{4,5},{5,4... | collective-permute-start | bytes 688136 | tf_op jit(solution)/shard_map/ppermute | solution.py:321
  31.3 13.2 %collective-permute-start.13 = (bf16[224,512]{1,0:T(8,128)(2,1)S(1)}, bf16[224,512]{1,0:T(8,128)(2,1)S(1)}, u32[]{:S(2)}, u32[]{:S(2)}) collective-permute-start(bf16[224,512]{1,0:T(8,128)(2,1)S(1)} %collective-permute-done.11.refs_6_), channel_id=1, source_target_pairs={{0,16},{1,17},{2,18},{3,19},{16,0},{17,1},{18,2},{19,3},{4,20},{5,... | collective-permute-start | bytes 688136 | tf_op jit(solution)/shard_map/ppermute | solution.py:321
  32.8 11.7 %collective-permute-start.14 = (bf16[224,512]{1,0:T(8,128)(2,1)S(1)}, bf16[224,512]{1,0:T(8,128)(2,1)S(1)}, u32[]{:S(2)}, u32[]{:S(2)}) collective-permute-start(bf16[224,512]{1,0:T(8,128)(2,1)S(1)} %collective-permute-done.11.refs_6_), channel_id=1, source_target_pairs={{0,17},{1,16},{2,19},{3,18},{16,1},{17,0},{18,3},{19,2},{4,21},{5,... | collective-permute-start | bytes 688136 | tf_op jit(solution)/shard_map/ppermute | solution.py:321
  34.3 18.5 %collective-permute-start.10 = (bf16[224,2048]{1,0:T(8,128)(2,1)S(1)}, bf16[224,2048]{1,0:T(8,128)(2,1)S(1)}, u32[]{:S(2)}, u32[]{:S(2)}) collective-permute-start(bf16[224,2048]{1,0:T(8,128)(2,1)S(1)} %copy-done), channel_id=1, source_target_pairs={{0,4},{4,0},{8,12},{12,8},{1,5},{5,1},{9,13},{13,9},{2,6},{6,2},{1... | collective-permute-start | bytes 2752520 | tf_op jit(solution)/shard_map/ppermute | solution.py:24
  44.5 2.3 %collective-permute-start.1 = (bf16[4,224,256]{2,1,0:T(8,128)(2,1)S(1)}, bf16[4,224,256]{2,1,0:T(8,128)(2,1)S(1)}, u32[]{:S(2)}, u32[]{:S(2)}) collective-permute-start(bf16[4,224,256]{2,1,0:T(8,128)(2,1)S(1)} %get-tuple-element.28.refs_7_), channel_id=1, source_target_pairs={{0,4},{4,0},{8,12},{12,8},{1,5},{5,1},{9,13},{13,9},{2,6},{6,2},{1... | collective-permute-start | bytes 1376264 | tf_op jit(solution)/shard_map/ppermute | solution.py:24
  44.5 2.1 %collective-permute-start.15 = (bf16[224,512]{1,0:T(8,128)(2,1)S(1)}, bf16[224,512]{1,0:T(8,128)(2,1)S(1)}, u32[]{:S(2)}, u32[]{:S(2)}) collective-permute-start(bf16[224,512]{1,0:T(8,128)(2,1)S(1)} %collective-permute-done.11.refs_6_), channel_id=1, source_target_pairs={{0,4},{4,0},{8,12},{12,8},{1,5},{5,1},{9,13},{13,9},{2,6},{6,2},{1... | collective-permute-start | bytes 688136 | tf_op jit(solution)/shard_map/ppermute | solution.py:24
  46.6 1.5 %collective-permute-start.16 = (bf16[224,512]{1,0:T(8,128)(2,1)S(1)}, bf16[224,512]{1,0:T(8,128)(2,1)S(1)}, u32[]{:S(2)}, u32[]{:S(2)}) collective-permute-start(bf16[224,512]{1,0:T(8,128)(2,1)S(1)} %collective-permute-done.12.refs_7_), channel_id=1, source_target_pairs={{0,4},{4,0},{8,12},{12,8},{1,5},{5,1},{9,13},{13,9},{2,6},{6,2},{1... | collective-permute-start | bytes 688136 | tf_op jit(solution)/shard_map/ppermute | solution.py:24
  46.8 5.6 %collective-permute-start.17 = (bf16[224,512]{1,0:T(8,128)(2,1)S(1)}, bf16[224,512]{1,0:T(8,128)(2,1)S(1)}, u32[]{:S(2)}, u32[]{:S(2)}) collective-permute-start(bf16[224,512]{1,0:T(8,128)(2,1)S(1)} %collective-permute-done.13.refs_8_), channel_id=1, source_target_pairs={{0,4},{4,0},{8,12},{12,8},{1,5},{5,1},{9,13},{13,9},{2,6},{6,2},{1... | collective-permute-start | bytes 688136 | tf_op jit(solution)/shard_map/ppermute | solution.py:24
  48.1 4.7 %collective-permute-start.18 = (bf16[224,512]{1,0:T(8,128)(2,1)S(1)}, bf16[224,512]{1,0:T(8,128)(2,1)S(1)}, u32[]{:S(2)}, u32[]{:S(2)}) collective-permute-start(bf16[224,512]{1,0:T(8,128)(2,1)S(1)} %collective-permute-done.14.refs_9_), channel_id=1, source_target_pairs={{0,4},{4,0},{8,12},{12,8},{1,5},{5,1},{9,13},{13,9},{2,6},{6,2},{1... | collective-permute-start | bytes 688136 | tf_op jit(solution)/shard_map/ppermute | solution.py:24
  48.3 9.3 %collective-permute-start.22 = (bf16[224,512]{1,0:T(8,128)(2,1)S(1)}, bf16[224,512]{1,0:T(8,128)(2,1)S(1)}, u32[]{:S(2)}, u32[]{:S(2)}) collective-permute-start(bf16[224,512]{1,0:T(8,128)(2,1)S(1)} %get-tuple-element.37), channel_id=1, source_target_pairs={{0,12},{4,8},{8,4},{12,0},{1,13},{5,9},{9,5},{13,1},{2,14},{6,10},... | collective-permute-start | bytes 688136 | tf_op jit(solution)/shard_map/ppermute | solution.py:24
  52.4 10.4 %collective-permute-start.2 = (f32[4,64,128]{2,1,0:T(8,128)S(1)}, f32[4,64,128]{2,1,0:T(8,128)S(1)}, u32[]{:S(2)}, u32[]{:S(2)}) collective-permute-start(f32[4,64,128]{2,1,0:T(8,128)S(1)} %get-tuple-element.30), channel_id=1, source_target_pairs={{0,8},{4,12},{8,0},{12,4},{1,9},{5,13},{9,1},{13,5},{2,10},{6,14},... | collective-permute-start | bytes 393224 | tf_op jit(solution)/shard_map/ppermute | solution.py:24
  62.2 6.6 %collective-permute-start.23 = (bf16[224,512]{1,0:T(8,128)(2,1)S(1)}, bf16[224,512]{1,0:T(8,128)(2,1)S(1)}, u32[]{:S(2)}, u32[]{:S(2)}) collective-permute-start(bf16[224,512]{1,0:T(8,128)(2,1)S(1)} %get-tuple-element.40), channel_id=1, source_target_pairs={{0,4},{4,0},{8,12},{12,8},{1,5},{5,1},{9,13},{13,9},{2,6},{6,2},{1... | collective-permute-start | bytes 688136 | tf_op jit(solution)/shard_map/ppermute | solution.py:24
  62.2 7.0 %collective-permute-start.19 = (bf16[224,512]{1,0:T(8,128)(2,1)S(1)}, bf16[224,512]{1,0:T(8,128)(2,1)S(1)}, u32[]{:S(2)}, u32[]{:S(2)}) collective-permute-start(bf16[224,512]{1,0:T(8,128)(2,1)S(1)} %get-tuple-element.34), channel_id=1, source_target_pairs={{0,4},{4,0},{8,12},{12,8},{1,5},{5,1},{9,13},{13,9},{2,6},{6,2},{1... | collective-permute-start | bytes 688136 | tf_op jit(solution)/shard_map/ppermute | solution.py:24
  62.8 4.3 %collective-permute-start.3 = (bf16[4,64,128]{2,1,0:T(8,128)(2,1)S(1)}, bf16[4,64,128]{2,1,0:T(8,128)(2,1)S(1)}, u32[]{:S(2)}, u32[]{:S(2)}) collective-permute-start(bf16[4,64,128]{2,1,0:T(8,128)(2,1)S(1)} %get-tuple-element.48.refs_0_), channel_id=1, source_target_pairs={{0,8},{4,12},{8,0},{12,4},{1,9},{5,13},{9,1},{13,5},{2,10},{6,14},... | collective-permute-start | bytes 196616 | tf_op jit(solution)/shard_map/ppermute | solution.py:24
  64.5 4.3 %collective-permute-start.4 = (bf16[4,64,128]{2,1,0:T(8,128)(2,1)S(1)}, bf16[4,64,128]{2,1,0:T(8,128)(2,1)S(1)}, u32[]{:S(2)}, u32[]{:S(2)}) collective-permute-start(bf16[4,64,128]{2,1,0:T(8,128)(2,1)S(1)} %get-tuple-element.48.refs_0_), channel_id=1, source_target_pairs={{0,4},{4,0},{8,12},{12,8},{1,5},{5,1},{9,13},{13,9},{2,6},{6,2},{1... | collective-permute-start | bytes 196616 | tf_op jit(solution)/shard_map/ppermute | solution.py:24
  67.1 8.2 %collective-permute-start.20 = (bf16[224,512]{1,0:T(8,128)(2,1)S(1)}, bf16[224,512]{1,0:T(8,128)(2,1)S(1)}, u32[]{:S(2)}, u32[]{:S(2)}) collective-permute-start(bf16[224,512]{1,0:T(8,128)(2,1)S(1)} %get-tuple-element.35), channel_id=1, source_target_pairs={{0,8},{4,12},{8,0},{12,4},{1,9},{5,13},{9,1},{13,5},{2,10},{6,14},... | collective-permute-start | bytes 688136 | tf_op jit(solution)/shard_map/ppermute | solution.py:24
  68.7 10.9 %collective-permute-start.21 = (bf16[224,512]{1,0:T(8,128)(2,1)S(1)}, bf16[224,512]{1,0:T(8,128)(2,1)S(1)}, u32[]{:S(2)}, u32[]{:S(2)}) collective-permute-start(bf16[224,512]{1,0:T(8,128)(2,1)S(1)} %get-tuple-element.36), channel_id=1, source_target_pairs={{0,12},{4,8},{8,4},{12,0},{1,13},{5,9},{9,5},{13,1},{2,14},{6,10},... | collective-permute-start | bytes 688136 | tf_op jit(solution)/shard_map/ppermute | solution.py:24
  68.8 17.4 %collective-permute-start.25 = (bf16[224,512]{1,0:T(8,128)(2,1)S(1)}, bf16[224,512]{1,0:T(8,128)(2,1)S(1)}, u32[]{:S(2)}, u32[]{:S(2)}) collective-permute-start(bf16[224,512]{1,0:T(8,128)(2,1)S(1)} %get-tuple-element.43), channel_id=1, source_target_pairs={{0,8},{4,12},{8,0},{12,4},{1,9},{5,13},{9,1},{13,5},{2,10},{6,14},... | collective-permute-start | bytes 688136 | tf_op jit(solution)/shard_map/ppermute | solution.py:24
  69.2 18.2 %collective-permute-start.24 = (bf16[224,512]{1,0:T(8,128)(2,1)S(1)}, bf16[224,512]{1,0:T(8,128)(2,1)S(1)}, u32[]{:S(2)}, u32[]{:S(2)}) collective-permute-start(bf16[224,512]{1,0:T(8,128)(2,1)S(1)} %get-tuple-element.42), channel_id=1, source_target_pairs={{0,12},{4,8},{8,4},{12,0},{1,13},{5,9},{9,5},{13,1},{2,14},{6,10},... | collective-permute-start | bytes 688136 | tf_op jit(solution)/shard_map/ppermute | solution.py:24
  75.3 5.6 %collective-permute-start.6 = (f32[4,64,128]{2,1,0:T(8,128)S(1)}, f32[4,64,128]{2,1,0:T(8,128)S(1)}, u32[]{:S(2)}, u32[]{:S(2)}) collective-permute-start(f32[4,64,128]{2,1,0:T(8,128)S(1)} %get-tuple-element.49.refs_4_), channel_id=1, source_target_pairs={{0,4},{4,0},{8,12},{12,8},{1,5},{5,1},{9,13},{13,9},{2,6},{6,2},{1... | collective-permute-start | bytes 393224 | tf_op jit(solution)/shard_map/ppermute | solution.py:24
  79.7 1.3 %collective-permute-start.5 = (bf16[4,64,128]{2,1,0:T(8,128)(2,1)S(1)}, bf16[4,64,128]{2,1,0:T(8,128)(2,1)S(1)}, u32[]{:S(2)}, u32[]{:S(2)}) collective-permute-start(bf16[4,64,128]{2,1,0:T(8,128)(2,1)S(1)} %collective-permute-done.3.refs_1_), channel_id=1, source_target_pairs={{0,4},{4,0},{8,12},{12,8},{1,5},{5,1},{9,13},{13,9},{2,6},{6,2},{1... | collective-permute-start | bytes 196616 | tf_op jit(solution)/shard_map/ppermute | solution.py:24

commit v11 on v9

--- a/solution.py
+++ b/solution.py
@@ -49,9 +49,9 @@
     return pl.ds(pl.multiple_of(index * block + cut[0], LANES), cut[1])
 
 
-def prepare_kernel(count, cuts, ids_far, coef, vox, wgt, table, *refs):
+def prepare_kernel(count, cuts, ids_far, coef, vox, wgt, table, harm, *refs):
     full, parts = refs[:count - 3], refs[count - 3:count - 3 + len(cuts)]
-    whole, vox_out, wgt_out, table_mine, table_other, stage, ids, sems = refs[count - 3 + len(cuts):]
+    whole, vox_out, wgt_out, table_mine, table_other, harm_out, stage, ids, sems = refs[count - 3 + len(cuts):]
     me, side, _ = position()
     block = coef.shape[1] // count
     half_rows, half = vox_out.shape[0], table_mine.shape[0]
@@ -62,6 +62,7 @@
     rest = [
         pltpu.make_async_copy(vox.at[aligned(side, half_rows)], vox_out, sems.at[count]),
         pltpu.make_async_copy(wgt.at[aligned(side, half_rows)], wgt_out, sems.at[count + 1]),
+        pltpu.make_async_copy(harm, harm_out, sems.at[count + 3 + 2 * half]),
     ]
     numbers = pltpu.make_async_copy(ids_far, ids, sems.at[count + 2 + 2 * half])
     numbers.start()
@@ -267,7 +268,7 @@
     place = position()[2]
     width = harmonics.shape[1] // pieces
     rows_shape = (rows, samples)
-    coef_far, measured_far, vox_far, wgt_far, ids_far, table_far = [
+    coef_far, measured_far, vox_far, wgt_far, ids_far, table_far, harm_far = [
         pltpu.with_memory_space_constraint(v, pltpu.HBM)
         for v in (
             coefficients,
@@ -276,34 +277,36 @@
             ray_weights.reshape(rows_shape),
             angle_ids,
             angle_table,
+            harmonics,
         )
     ]
 
     piece = lax.dynamic_slice_in_dim(harmonics, place * width, width, 1)
     fetched = {m: [swap(piece, "coef", m)] for m in range(2, count, 2)}
     table_shape = shape((half,) + angle_table.shape[1:], bf16)
-    *parts, own, vox, wgt, table_mine, table_other = kernel(
+    *parts, own, vox, wgt, table_mine, table_other, harm_own = kernel(
         lambda *refs: prepare_kernel(count, cuts, *refs),
-        [HBM] * 5,
-        [VMEM] * (count + len(cuts) + 2),
+        [HBM] * 6,
+        [VMEM] * (count + len(cuts) + 3),
         [shape((coef_local, block), bf16)] * (count - 3)
         + [shape((coef_local, cut[1]), bf16) for cut in cuts]
         + [shape((coef_local, cols), bf16)]
         + [shape((rows // 2, samples), jnp.int32)] * 2
-        + [table_shape] * 2,
+        + [table_shape] * 2
+        + [shape(harmonics.shape, bf16)],
         [
             pltpu.VMEM((count, coef_local, block), f32),
             pltpu.SMEM(angle_ids.shape, jnp.int32),
-            pltpu.SemaphoreType.DMA((count + 3 + projections,)),
+            pltpu.SemaphoreType.DMA((count + 4 + projections,)),
         ],
-    )(ids_far, coef_far, vox_far, wgt_far, table_far)
+    )(ids_far, coef_far, vox_far, wgt_far, table_far, harm_far)
     received = []
     for t in range(len(cuts)):
         if t == 0:
             early = [swap(parts[m - 2], "coef", m) for m in range(2, count - 1)]
         received.append(early + [swap(parts[count - 3 + t], "coef", count - 1)])
     partner = swap(own, "coef", 1)
-    near = swap(harmonics, "coef", 1)
+    near = swap(harm_own, "coef", 1)
     table_partner = swap(table_other, "coef", 1)
     moves = [(0, 1)] * slab_bits + [(1, 0)] * group_bits + [(1, 1)] * (slab_bits * group_bits)
     for m in fetched:
@@ -345,7 +348,7 @@
     returned = []
     for t, cut in enumerate(cuts):
         first = t == 0
-        extra = [harmonics, near, *far] if first else [waves]
+        extra = [harm_own, near, *far] if first else [waves]
         outs = kernel(
             lambda *refs: penalty_kernel(count, pieces, cut, first, *refs),
             [VMEM] * (count + len(extra)),

time: 82.5 us -> 83.6 us (1.013)
  local copies, waits for them, and re-layouts: 1.58 us -> 2.52 us
    dynamic_slice x1, local copies, waits for them, and re-layouts: 0.02 us -> 0.95 us  [step_of(): piece = lax.dynamic_slice_in_dim(harmonics, place * width, width, 1)]
  transfers between devices with their start and end apart: 26 -> 26, of which waited for: 9 -> 9; matrix products, arithmetic and copies ran while one was open for 0% -> 1% of each run, Pallas kernels for 33% -> 32%
where the time goes in v11:
time: 83.6 us; the launch traced here: 83 us
  Pallas kernels  30.4 us (36%)
  waiting for transfers between devices  28.7 us (34%)
  starting transfers between devices  20.6 us (25%)
  local copies, waits for them, and re-layouts  2.52 us (3%)
    ppermute x23, waiting for transfers between devices, swap(): return lax.ppermute(value, axis, [(i, i ^ mask) for i in range(count)])  23.7 us
    ppermute x23, starting transfers between devices, swap(): return lax.ppermute(value, axis, [(i, i ^ mask) for i in range(count)])  14.7 us
    pallas_call x2, Pallas kernels, step_of(): kernel(lambda *refs: penalty_kernel(count, pieces, cut, first, *refs), [V...  12.3 us
    ppermute x3, starting transfers between devices, step_of(): fetched[m].append(lax.ppermute(fetched[m][0], ('groups', 'slab'), pairs))  5.88 us
    pallas_call x1, Pallas kernels, step_of(): kernel(lambda *refs: data_kernel(count, cuts, len(half_mine), *refs), [VM...  5.2 us
    ppermute x3, waiting for transfers between devices, step_of(): fetched[m].append(lax.ppermute(fetched[m][0], ('groups', 'slab'), pairs))  4.92 us
    pallas_call x1, Pallas kernels, step_of(): kernel(build_kernel, [VMEM, VMEM], VMEM, shape((rows // 2, cols), bf16),...  4.34 us
    pallas_call x1, Pallas kernels, step_of(): kernel(lambda *refs: sums_kernel(count, *refs), [VMEM] * 5 + [HBM], [VMEM...  3.99 us
  transfers between devices with their start and end apart: 26, of which 9 were waited for; matrix products, arithmetic and copies ran while one was open for 1% of the time, Pallas kernels for 32%

profile of v11, /device:TPU:0, one launch (start us, length us, event | category | flops | bytes accessed | tf_op | source)
XLA Modules:
  0.0 83.0 jit_solution(9549782487867480074)
XLA Ops:
  0.6 2.9 %shard_map.86 = (bf16[224,1024]{1,0:T(8,128)(2,1)S(1)}, bf16[224,512]{1,0:T(8,128)(2,1)S(1)}, bf16[224,512]{1,0:T(8,128)(2,1)S(1)}, bf16[224,4096]{1,0:T(8,128)(...) custom-call(s32[8]{0:T(128)} %refs_0_.1, ...), custom_call_target="tpu_custom_call" | custom-call | tf_op jit(solution)/shard_map/pallas_call | solution.py:287
  3.6 0.0 copy-start
  3.6 0.8 copy-done
  4.3 0.8 copy-done.2
  5.1 0.5 collective-permute-start
  5.6 1.0 %constant_dynamic-slice_fusion = bf16[224,512]{1,0:T(8,128)(2,1)S(1)} fusion(bf16[224,2048]{1,0:T(8,128)(2,1)} %refs_5_.1, s32[]{:T(128)S(6)} %select_n.3), kind=kLoop, calls=%fused_computation | loop fusion | bytes 458756 | tf_op jit(solution)/shard_map/dynamic_slice | solution.py:284
  6.6 2.7 %collective-permute-start.11 = (bf16[224,512]{1,0:T(8,128)(2,1)S(1)}, bf16[224,512]{1,0:T(8,128)(2,1)S(1)}, u32[]{:S(2)}, u32[]{:S(2)}) collective-permute-start(bf16[224,512]{1,0:T(8,128)(2,1)S(1)} %constant_dynamic-slice_fusion), channel_id=1, source_target_pairs={{0,8},{4,12},{8,0},{12,4},{1,9},{5,13},{9,1},{13,5},{2,10},{6,14},... | collective-permute-start | bytes 688136 | tf_op jit(solution)/shard_map/ppermute | solution.py:24
  9.2 4.3 %shard_map.87.refs_0_.refs_8_ = bf16[256,4096]{1,0:T(8,128)(2,1)S(1)} custom-call(s32[256,128]{1,0:T(8,128)S(1)} %get-tuple-element.25.vox_ref, s32[256,128]{1,0:T(8,128)S(1)} %get-tuple-element.26.wgt_ref), custom_call_target="tpu_custom_call" | custom-call | tf_op jit(solution)/shard_map/pallas_call | solution.py:318
  13.6 0.2 collective-permute-start.7
  13.8 0.0 collective-permute-start.9
  13.8 1.6 %collective-permute-done.11.refs_6_ = bf16[224,512]{1,0:T(8,128)(2,1)S(1)} collective-permute-done((bf16[224,512]{1,0:T(8,128)(2,1)S(1)}, bf16[224,512]{1,0:T(8,128)(2,1)S(1)}, u32[]{:S(2)}, u32[]{:S(2)}) %collective-permute-start.11) | collective-permute-done | bytes 229408 | tf_op jit(solution)/shard_map/ppermute | solution.py:24
  15.4 1.8 %collective-permute-start.12 = (bf16[224,512]{1,0:T(8,128)(2,1)S(1)}, bf16[224,512]{1,0:T(8,128)(2,1)S(1)}, u32[]{:S(2)}, u32[]{:S(2)}) collective-permute-start(bf16[224,512]{1,0:T(8,128)(2,1)S(1)} %collective-permute-done.11.refs_6_), channel_id=1, source_target_pairs={{0,1},{1,0},{2,3},{3,2},{16,17},{17,16},{18,19},{19,18},{4,5},{5,4... | collective-permute-start | bytes 688136 | tf_op jit(solution)/shard_map/ppermute | solution.py:316
  17.2 1.5 %collective-permute-start.13 = (bf16[224,512]{1,0:T(8,128)(2,1)S(1)}, bf16[224,512]{1,0:T(8,128)(2,1)S(1)}, u32[]{:S(2)}, u32[]{:S(2)}) collective-permute-start(bf16[224,512]{1,0:T(8,128)(2,1)S(1)} %collective-permute-done.11.refs_6_), channel_id=1, source_target_pairs={{0,16},{1,17},{2,18},{3,19},{16,0},{17,1},{18,2},{19,3},{4,20},{5,... | collective-permute-start | bytes 688136 | tf_op jit(solution)/shard_map/ppermute | solution.py:316
  18.7 2.6 %collective-permute-done.9.refs_3_ = bf16[224,512]{1,0:T(8,128)(2,1)S(1)} collective-permute-done((bf16[224,512]{1,0:T(8,128)(2,1)}, bf16[224,512]{1,0:T(8,128)(2,1)S(1)}, u32[]{:S(2)}, u32[]{:S(2)}) %collective-permute-start.9) | collective-permute-done | bytes 229408 | tf_op jit(solution)/shard_map/ppermute | solution.py:24
  21.3 2.5 %collective-permute-start.14 = (bf16[224,512]{1,0:T(8,128)(2,1)S(1)}, bf16[224,512]{1,0:T(8,128)(2,1)S(1)}, u32[]{:S(2)}, u32[]{:S(2)}) collective-permute-start(bf16[224,512]{1,0:T(8,128)(2,1)S(1)} %collective-permute-done.11.refs_6_), channel_id=1, source_target_pairs={{0,17},{1,16},{2,19},{3,18},{16,1},{17,0},{18,3},{19,2},{4,21},{5,... | collective-permute-start | bytes 688136 | tf_op jit(solution)/shard_map/ppermute | solution.py:316
  23.8 0.0 collective-permute-done.12.refs_7_
  23.8 0.4 collective-permute-start.15
  24.2 1.2 %collective-permute-start.8 = (bf16[224,1024]{1,0:T(8,128)(2,1)}, bf16[224,1024]{1,0:T(8,128)(2,1)S(1)}, u32[]{:S(2)}, u32[]{:S(2)}) collective-permute-start(bf16[224,1024]{1,0:T(8,128)(2,1)} %copy-done.2), channel_id=1, source_target_pairs={{0,8},{4,12},{8,0},{12,4},{1,9},{5,13},{9,1},{13,5},{2,10},{6,14},... | collective-permute-start | bytes 1376264 | tf_op jit(solution)/shard_map/ppermute | solution.py:24
  25.5 4.9 %collective-permute-done.14.refs_9_ = bf16[224,512]{1,0:T(8,128)(2,1)S(1)} collective-permute-done((bf16[224,512]{1,0:T(8,128)(2,1)S(1)}, bf16[224,512]{1,0:T(8,128)(2,1)S(1)}, u32[]{:S(2)}, u32[]{:S(2)}) %collective-permute-start.14) | collective-permute-done | bytes 229408 | tf_op jit(solution)/shard_map/ppermute | solution.py:316
  30.4 0.5 collective-permute-start.1
  30.9 6.1 %collective-permute-done.8.refs_2_ = bf16[224,1024]{1,0:T(8,128)(2,1)S(1)} collective-permute-done((bf16[224,1024]{1,0:T(8,128)(2,1)}, bf16[224,1024]{1,0:T(8,128)(2,1)S(1)}, u32[]{:S(2)}, u32[]{:S(2)}) %collective-permute-start.8) | collective-permute-done | bytes 458784 | tf_op jit(solution)/shard_map/ppermute | solution.py:24
  37.0 0.0 collective-permute-start.16
  37.0 0.0 collective-permute-done.1.refs_4_
  37.0 0.5 collective-permute-start.17
  37.5 1.0 %collective-permute-done.16.refs_11_ = bf16[224,512]{1,0:T(8,128)(2,1)S(1)} collective-permute-done((bf16[224,512]{1,0:T(8,128)(2,1)S(1)}, bf16[224,512]{1,0:T(8,128)(2,1)S(1)}, u32[]{:S(2)}, u32[]{:S(2)}) %collective-permute-start.16) | collective-permute-done | bytes 229408 | tf_op jit(solution)/shard_map/ppermute | solution.py:24
  38.5 0.1 collective-permute-start.18
  38.6 0.0 collective-permute-done.refs_2_.refs_1_
  38.6 0.5 collective-permute-start.22
  39.1 4.0 %shard_map.88 = (f32[4,64,128]{2,1,0:T(8,128)S(1)}, f32[4,64,128]{2,1,0:T(8,128)S(1)}) custom-call(bf16[256,4096]{1,0:T(8,128)(2,1)S(1)} %shard_map.87.refs_0_.refs_8_, bf16[224,4096]{1,0:T(8,128)(2,1)S(1)} %get-tuple-element.27.refs_1_.refs_0_, bf16[224,4096]{1,0:T(8,128)(2,1)} %collective-permute-done.refs_2_.refs_1_, ...), custom_call_target="tpu_custom_call" | custom-call | tf_op jit(solution)/shard_map/pallas_call | solution.py:330
  43.1 0.0 collective-permute-done.17.refs_12_
  43.1 1.6 %collective-permute-start.2 = (f32[4,64,128]{2,1,0:T(8,128)S(1)}, f32[4,64,128]{2,1,0:T(8,128)S(1)}, u32[]{:S(2)}, u32[]{:S(2)}) collective-permute-start(f32[4,64,128]{2,1,0:T(8,128)S(1)} %get-tuple-element.31), channel_id=1, source_target_pairs={{0,8},{4,12},{8,0},{12,4},{1,9},{5,13},{9,1},{13,5},{2,10},{6,14},... | collective-permute-start | bytes 393224 | tf_op jit(solution)/shard_map/ppermute | solution.py:24
  44.7 6.2 %shard_map.89 = (bf16[224,512]{1,0:T(8,128)(2,1)S(1)}, bf16[224,512]{1,0:T(8,128)(2,1)S(1)}, bf16[224,512]{1,0:T(8,128)(2,1)S(1)}, bf16[224,512]{1,0:T(8,128)(2,1)S(1)}, bf16[896,2048]{1,0:T(8,128)(2,1)S(1)}) custom-call(bf16[224,4096]{1,0:T(8,128)(2,1)S(1)} %get-tuple-element.27.refs_1_.refs_0_, bf16[224,4096]{1,0:T(8,128)(2,1)} %collective-permute-done.refs_2_.refs_1_, ...), custom_call_target="tpu_custom_call" | custom-call | tf_op jit(solution)/shard_map/pallas_call | solution.py:352
  50.9 0.0 copy-start.1
  50.9 6.2 %shard_map.90 = (bf16[224,512]{1,0:T(8,128)(2,1)S(1)}, bf16[224,512]{1,0:T(8,128)(2,1)S(1)}, bf16[224,512]{1,0:T(8,128)(2,1)S(1)}, bf16[224,512]{1,0:T(8,128)(2,1)S(1)}) custom-call(bf16[224,4096]{1,0:T(8,128)(2,1)S(1)} %get-tuple-element.27.refs_1_.refs_0_, bf16[224,4096]{1,0:T(8,128)(2,1)} %collective-permute-done.refs_2_.refs_1_, ...), custom_call_target="tpu_custom_call" | custom-call | tf_op jit(solution)/shard_map/pallas_call | solution.py:352
  57.1 0.1 collective-permute-start.23
  57.1 0.5 collective-permute-start.19
  57.7 0.6 collective-permute-start.3
  58.3 3.7 %collective-permute-done.3.refs_1_ = bf16[4,64,128]{2,1,0:T(8,128)(2,1)S(1)} collective-permute-done((bf16[4,64,128]{2,1,0:T(8,128)(2,1)S(1)}, bf16[4,64,128]{2,1,0:T(8,128)(2,1)S(1)}, u32[]{:S(2)}, u32[]{:S(2)}) %collective-permute-start.3) | collective-permute-done | bytes 65568 | tf_op jit(solution)/shard_map/ppermute | solution.py:24
  62.0 0.5 collective-permute-start.20
  62.5 1.6 %collective-permute-start.25 = (bf16[224,512]{1,0:T(8,128)(2,1)S(1)}, bf16[224,512]{1,0:T(8,128)(2,1)S(1)}, u32[]{:S(2)}, u32[]{:S(2)}) collective-permute-start(bf16[224,512]{1,0:T(8,128)(2,1)S(1)} %get-tuple-element.45), channel_id=1, source_target_pairs={{0,8},{4,12},{8,0},{12,4},{1,9},{5,13},{9,1},{13,5},{2,10},{6,14},... | collective-permute-start | bytes 688136 | tf_op jit(solution)/shard_map/ppermute | solution.py:24
  64.1 1.4 %collective-permute-start.24 = (bf16[224,512]{1,0:T(8,128)(2,1)S(1)}, bf16[224,512]{1,0:T(8,128)(2,1)S(1)}, u32[]{:S(2)}, u32[]{:S(2)}) collective-permute-start(bf16[224,512]{1,0:T(8,128)(2,1)S(1)} %get-tuple-element.44), channel_id=1, source_target_pairs={{0,12},{4,8},{8,4},{12,0},{1,13},{5,9},{9,5},{13,1},{2,14},{6,10},... | collective-permute-start | bytes 688136 | tf_op jit(solution)/shard_map/ppermute | solution.py:24
  65.5 5.0 %collective-permute-done.20.refs_13_ = bf16[224,512]{1,0:T(8,128)(2,1)S(1)} collective-permute-done((bf16[224,512]{1,0:T(8,128)(2,1)S(1)}, bf16[224,512]{1,0:T(8,128)(2,1)S(1)}, u32[]{:S(2)}, u32[]{:S(2)}) %collective-permute-start.20) | collective-permute-done | bytes 229408 | tf_op jit(solution)/shard_map/ppermute | solution.py:24
  70.5 2.9 %collective-permute-done.21.refs_14_ = bf16[224,512]{1,0:T(8,128)(2,1)S(1)} collective-permute-done((bf16[224,512]{1,0:T(8,128)(2,1)S(1)}, bf16[224,512]{1,0:T(8,128)(2,1)S(1)}, u32[]{:S(2)}, u32[]{:S(2)}) %collective-permute-start.21) | collective-permute-done | bytes 229408 | tf_op jit(solution)/shard_map/ppermute | solution.py:24
  73.4 1.9 %collective-permute-start.5 = (bf16[4,64,128]{2,1,0:T(8,128)(2,1)S(1)}, bf16[4,64,128]{2,1,0:T(8,128)(2,1)S(1)}, u32[]{:S(2)}, u32[]{:S(2)}) collective-permute-start(bf16[4,64,128]{2,1,0:T(8,128)(2,1)S(1)} %collective-permute-done.3.refs_1_), channel_id=1, source_target_pairs={{0,4},{4,0},{8,12},{12,8},{1,5},{5,1},{9,13},{13,9},{2,6},{6,2},{1... | collective-permute-start | bytes 196616 | tf_op jit(solution)/shard_map/ppermute | solution.py:24
  75.2 0.9 %collective-permute-done.5.refs_3_ = bf16[4,64,128]{2,1,0:T(8,128)(2,1)S(1)} collective-permute-done((bf16[4,64,128]{2,1,0:T(8,128)(2,1)S(1)}, bf16[4,64,128]{2,1,0:T(8,128)(2,1)S(1)}, u32[]{:S(2)}, u32[]{:S(2)}) %collective-permute-start.5) | collective-permute-done | bytes 65568 | tf_op jit(solution)/shard_map/ppermute | solution.py:24
  76.1 5.2 %shard_map.91 = (f32[224,4096]{1,0:T(8,128)}, f32[8,64,64]{2,1,0:T(8,128)}, f32[2,224,512]{2,1,0:T(8,128)S(1)}) custom-call(bf16[4,64,128]{2,1,0:T(8,128)(2,1)S(1)} %get-tuple-element.50.refs_0_, bf16[4,64,128]{2,1,0:T(8,128)(2,1)S(1)} %collective-permute-done.3.refs_1_, bf16[4,64,128]{2,1,0:T(8,128)(2,1)S(1)} %collective-permute-done.4.refs_2_, ...), custom_call_target="tpu_custom_call" | custom-call | tf_op jit(solution)/shard_map/pallas_call | solution.py:383
  81.3 0.8 shard_map.92.refs_2_
  82.2 0.8 shard_map.93
  (24 shorter events, 0.1 us)
Async XLA Ops:
  3.6 0.8 copy-start
  4.3 0.8 copy-start.2
  4.3 1.3 %copy-start.3 = (bf16[224,512]{1,0:T(8,128)(2,1)}, bf16[224,512]{1,0:T(8,128)(2,1)S(1)}, u32[]{:S(2)}) copy-start(bf16[224,512]{1,0:T(8,128)(2,1)S(1)} %get-tuple-element.39) | copy-start | bytes 688132
  4.3 1.3 %copy-start.4 = (bf16[224,512]{1,0:T(8,128)(2,1)}, bf16[224,512]{1,0:T(8,128)(2,1)S(1)}, u32[]{:S(2)}) copy-start(bf16[224,512]{1,0:T(8,128)(2,1)S(1)} %get-tuple-element.33) | copy-start | bytes 688132
  5.1 33.5 %collective-permute-start = (bf16[224,4096]{1,0:T(8,128)(2,1)S(1)}, bf16[224,4096]{1,0:T(8,128)(2,1)}, u32[]{:S(2)}, u32[]{:S(2)}) collective-permute-start(bf16[224,4096]{1,0:T(8,128)(2,1)S(1)} %get-tuple-element.27.refs_1_.refs_0_), channel_id=1, source_target_pairs={{0,4},{4,0},{8,12},{12,8},{1,5},{5,1},{9,13},{13,9},{2,6},{6,2},{1... | collective-permute-start | bytes 5505032 | tf_op jit(solution)/shard_map/ppermute | solution.py:24
  6.6 8.8 %collective-permute-start.11 = (bf16[224,512]{1,0:T(8,128)(2,1)S(1)}, bf16[224,512]{1,0:T(8,128)(2,1)S(1)}, u32[]{:S(2)}, u32[]{:S(2)}) collective-permute-start(bf16[224,512]{1,0:T(8,128)(2,1)S(1)} %constant_dynamic-slice_fusion), channel_id=1, source_target_pairs={{0,8},{4,12},{8,0},{12,4},{1,9},{5,13},{9,1},{13,5},{2,10},{6,14},... | collective-permute-start | bytes 688136 | tf_op jit(solution)/shard_map/ppermute | solution.py:24
  13.6 61.6 %collective-permute-start.7 = (bf16[256,4096]{1,0:T(8,128)(2,1)S(1)}, bf16[256,4096]{1,0:T(8,128)(2,1)S(1)}, u32[]{:S(2)}, u32[]{:S(2)}) collective-permute-start(bf16[256,4096]{1,0:T(8,128)(2,1)S(1)} %shard_map.87.refs_0_.refs_8_), channel_id=1, source_target_pairs={{0,4},{4,0},{8,12},{12,8},{1,5},{5,1},{9,13},{13,9},{2,6},{6,2},{1... | collective-permute-start | bytes 6291464 | tf_op jit(solution)/shard_map/ppermute | solution.py:24
  13.8 7.5 %collective-permute-start.9 = (bf16[224,512]{1,0:T(8,128)(2,1)}, bf16[224,512]{1,0:T(8,128)(2,1)S(1)}, u32[]{:S(2)}, u32[]{:S(2)}) collective-permute-start(bf16[224,512]{1,0:T(8,128)(2,1)} %copy-done.4), channel_id=1, source_target_pairs={{0,12},{4,8},{8,4},{12,0},{1,13},{5,9},{9,5},{13,1},{2,14},{6,10},... | collective-permute-start | bytes 688136 | tf_op jit(solution)/shard_map/ppermute | solution.py:24
  15.4 8.4 %collective-permute-start.12 = (bf16[224,512]{1,0:T(8,128)(2,1)S(1)}, bf16[224,512]{1,0:T(8,128)(2,1)S(1)}, u32[]{:S(2)}, u32[]{:S(2)}) collective-permute-start(bf16[224,512]{1,0:T(8,128)(2,1)S(1)} %collective-permute-done.11.refs_6_), channel_id=1, source_target_pairs={{0,1},{1,0},{2,3},{3,2},{16,17},{17,16},{18,19},{19,18},{4,5},{5,4... | collective-permute-start | bytes 688136 | tf_op jit(solution)/shard_map/ppermute | solution.py:316
  17.2 7.0 %collective-permute-start.13 = (bf16[224,512]{1,0:T(8,128)(2,1)S(1)}, bf16[224,512]{1,0:T(8,128)(2,1)S(1)}, u32[]{:S(2)}, u32[]{:S(2)}) collective-permute-start(bf16[224,512]{1,0:T(8,128)(2,1)S(1)} %collective-permute-done.11.refs_6_), channel_id=1, source_target_pairs={{0,16},{1,17},{2,18},{3,19},{16,0},{17,1},{18,2},{19,3},{4,20},{5,... | collective-permute-start | bytes 688136 | tf_op jit(solution)/shard_map/ppermute | solution.py:316
  21.3 9.1 %collective-permute-start.14 = (bf16[224,512]{1,0:T(8,128)(2,1)S(1)}, bf16[224,512]{1,0:T(8,128)(2,1)S(1)}, u32[]{:S(2)}, u32[]{:S(2)}) collective-permute-start(bf16[224,512]{1,0:T(8,128)(2,1)S(1)} %collective-permute-done.11.refs_6_), channel_id=1, source_target_pairs={{0,17},{1,16},{2,19},{3,18},{16,1},{17,0},{18,3},{19,2},{4,21},{5,... | collective-permute-start | bytes 688136 | tf_op jit(solution)/shard_map/ppermute | solution.py:316
  23.8 6.6 %collective-permute-start.15 = (bf16[224,512]{1,0:T(8,128)(2,1)S(1)}, bf16[224,512]{1,0:T(8,128)(2,1)S(1)}, u32[]{:S(2)}, u32[]{:S(2)}) collective-permute-start(bf16[224,512]{1,0:T(8,128)(2,1)S(1)} %collective-permute-done.11.refs_6_), channel_id=1, source_target_pairs={{0,4},{4,0},{8,12},{12,8},{1,5},{5,1},{9,13},{13,9},{2,6},{6,2},{1... | collective-permute-start | bytes 688136 | tf_op jit(solution)/shard_map/ppermute | solution.py:24
  24.2 12.7 %collective-permute-start.8 = (bf16[224,1024]{1,0:T(8,128)(2,1)}, bf16[224,1024]{1,0:T(8,128)(2,1)S(1)}, u32[]{:S(2)}, u32[]{:S(2)}) collective-permute-start(bf16[224,1024]{1,0:T(8,128)(2,1)} %copy-done.2), channel_id=1, source_target_pairs={{0,8},{4,12},{8,0},{12,4},{1,9},{5,13},{9,1},{13,5},{2,10},{6,14},... | collective-permute-start | bytes 1376264 | tf_op jit(solution)/shard_map/ppermute | solution.py:24
  30.4 14.3 %collective-permute-start.10 = (bf16[224,2048]{1,0:T(8,128)(2,1)S(1)}, bf16[224,2048]{1,0:T(8,128)(2,1)S(1)}, u32[]{:S(2)}, u32[]{:S(2)}) collective-permute-start(bf16[224,2048]{1,0:T(8,128)(2,1)S(1)} %get-tuple-element.34.refs_4_), channel_id=1, source_target_pairs={{0,4},{4,0},{8,12},{12,8},{1,5},{5,1},{9,13},{13,9},{2,6},{6,2},{1... | collective-permute-start | bytes 2752520 | tf_op jit(solution)/shard_map/ppermute | solution.py:24
  30.4 6.6 %collective-permute-start.1 = (bf16[4,224,256]{2,1,0:T(8,128)(2,1)}, bf16[4,224,256]{2,1,0:T(8,128)(2,1)S(1)}, u32[]{:S(2)}, u32[]{:S(2)}) collective-permute-start(bf16[4,224,256]{2,1,0:T(8,128)(2,1)} %copy-done), channel_id=1, source_target_pairs={{0,4},{4,0},{8,12},{12,8},{1,5},{5,1},{9,13},{13,9},{2,6},{6,2},{1... | collective-permute-start | bytes 1376264 | tf_op jit(solution)/shard_map/ppermute | solution.py:24
  37.0 1.5 %collective-permute-start.16 = (bf16[224,512]{1,0:T(8,128)(2,1)S(1)}, bf16[224,512]{1,0:T(8,128)(2,1)S(1)}, u32[]{:S(2)}, u32[]{:S(2)}) collective-permute-start(bf16[224,512]{1,0:T(8,128)(2,1)S(1)} %collective-permute-done.12.refs_7_), channel_id=1, source_target_pairs={{0,4},{4,0},{8,12},{12,8},{1,5},{5,1},{9,13},{13,9},{2,6},{6,2},{1... | collective-permute-start | bytes 688136 | tf_op jit(solution)/shard_map/ppermute | solution.py:24
  37.0 6.1 %collective-permute-start.17 = (bf16[224,512]{1,0:T(8,128)(2,1)S(1)}, bf16[224,512]{1,0:T(8,128)(2,1)S(1)}, u32[]{:S(2)}, u32[]{:S(2)}) collective-permute-start(bf16[224,512]{1,0:T(8,128)(2,1)S(1)} %collective-permute-done.13.refs_8_), channel_id=1, source_target_pairs={{0,4},{4,0},{8,12},{12,8},{1,5},{5,1},{9,13},{13,9},{2,6},{6,2},{1... | collective-permute-start | bytes 688136 | tf_op jit(solution)/shard_map/ppermute | solution.py:24
  38.5 6.2 %collective-permute-start.18 = (bf16[224,512]{1,0:T(8,128)(2,1)S(1)}, bf16[224,512]{1,0:T(8,128)(2,1)S(1)}, u32[]{:S(2)}, u32[]{:S(2)}) collective-permute-start(bf16[224,512]{1,0:T(8,128)(2,1)S(1)} %collective-permute-done.14.refs_9_), channel_id=1, source_target_pairs={{0,4},{4,0},{8,12},{12,8},{1,5},{5,1},{9,13},{13,9},{2,6},{6,2},{1... | collective-permute-start | bytes 688136 | tf_op jit(solution)/shard_map/ppermute | solution.py:24
  38.6 12.3 %collective-permute-start.22 = (bf16[224,512]{1,0:T(8,128)(2,1)}, bf16[224,512]{1,0:T(8,128)(2,1)S(1)}, u32[]{:S(2)}, u32[]{:S(2)}) collective-permute-start(bf16[224,512]{1,0:T(8,128)(2,1)} %copy-done.3), channel_id=1, source_target_pairs={{0,12},{4,8},{8,4},{12,0},{1,13},{5,9},{9,5},{13,1},{2,14},{6,10},... | collective-permute-start | bytes 688136 | tf_op jit(solution)/shard_map/ppermute | solution.py:24
  43.1 14.5 %collective-permute-start.2 = (f32[4,64,128]{2,1,0:T(8,128)S(1)}, f32[4,64,128]{2,1,0:T(8,128)S(1)}, u32[]{:S(2)}, u32[]{:S(2)}) collective-permute-start(f32[4,64,128]{2,1,0:T(8,128)S(1)} %get-tuple-element.31), channel_id=1, source_target_pairs={{0,8},{4,12},{8,0},{12,4},{1,9},{5,13},{9,1},{13,5},{2,10},{6,14},... | collective-permute-start | bytes 393224 | tf_op jit(solution)/shard_map/ppermute | solution.py:24
  50.9 25.2 %copy-start.1 = (bf16[4,224,256]{2,1,0:T(8,128)(2,1)S(1)}, bf16[4,224,256]{2,1,0:T(8,128)(2,1)}, u32[]{:S(2)}) copy-start(bf16[4,224,256]{2,1,0:T(8,128)(2,1)} %copy-done) | copy-start | bytes 1376260
  57.1 5.5 %collective-permute-start.23 = (bf16[224,512]{1,0:T(8,128)(2,1)S(1)}, bf16[224,512]{1,0:T(8,128)(2,1)S(1)}, u32[]{:S(2)}, u32[]{:S(2)}) collective-permute-start(bf16[224,512]{1,0:T(8,128)(2,1)S(1)} %get-tuple-element.42), channel_id=1, source_target_pairs={{0,4},{4,0},{8,12},{12,8},{1,5},{5,1},{9,13},{13,9},{2,6},{6,2},{1... | collective-permute-start | bytes 688136 | tf_op jit(solution)/shard_map/ppermute | solution.py:24
  57.1 7.0 %collective-permute-start.19 = (bf16[224,512]{1,0:T(8,128)(2,1)S(1)}, bf16[224,512]{1,0:T(8,128)(2,1)S(1)}, u32[]{:S(2)}, u32[]{:S(2)}) collective-permute-start(bf16[224,512]{1,0:T(8,128)(2,1)S(1)} %get-tuple-element.36), channel_id=1, source_target_pairs={{0,4},{4,0},{8,12},{12,8},{1,5},{5,1},{9,13},{13,9},{2,6},{6,2},{1... | collective-permute-start | bytes 688136 | tf_op jit(solution)/shard_map/ppermute | solution.py:24
  57.7 4.3 %collective-permute-start.3 = (bf16[4,64,128]{2,1,0:T(8,128)(2,1)S(1)}, bf16[4,64,128]{2,1,0:T(8,128)(2,1)S(1)}, u32[]{:S(2)}, u32[]{:S(2)}) collective-permute-start(bf16[4,64,128]{2,1,0:T(8,128)(2,1)S(1)} %get-tuple-element.50.refs_0_), channel_id=1, source_target_pairs={{0,8},{4,12},{8,0},{12,4},{1,9},{5,13},{9,1},{13,5},{2,10},{6,14},... | collective-permute-start | bytes 196616 | tf_op jit(solution)/shard_map/ppermute | solution.py:24
  58.3 4.3 %collective-permute-start.4 = (bf16[4,64,128]{2,1,0:T(8,128)(2,1)S(1)}, bf16[4,64,128]{2,1,0:T(8,128)(2,1)S(1)}, u32[]{:S(2)}, u32[]{:S(2)}) collective-permute-start(bf16[4,64,128]{2,1,0:T(8,128)(2,1)S(1)} %get-tuple-element.50.refs_0_), channel_id=1, source_target_pairs={{0,4},{4,0},{8,12},{12,8},{1,5},{5,1},{9,13},{13,9},{2,6},{6,2},{1... | collective-permute-start | bytes 196616 | tf_op jit(solution)/shard_map/ppermute | solution.py:24
  62.0 8.5 %collective-permute-start.20 = (bf16[224,512]{1,0:T(8,128)(2,1)S(1)}, bf16[224,512]{1,0:T(8,128)(2,1)S(1)}, u32[]{:S(2)}, u32[]{:S(2)}) collective-permute-start(bf16[224,512]{1,0:T(8,128)(2,1)S(1)} %get-tuple-element.37), channel_id=1, source_target_pairs={{0,8},{4,12},{8,0},{12,4},{1,9},{5,13},{9,1},{13,5},{2,10},{6,14},... | collective-permute-start | bytes 688136 | tf_op jit(solution)/shard_map/ppermute | solution.py:24
  62.5 10.8 %collective-permute-start.21 = (bf16[224,512]{1,0:T(8,128)(2,1)S(1)}, bf16[224,512]{1,0:T(8,128)(2,1)S(1)}, u32[]{:S(2)}, u32[]{:S(2)}) collective-permute-start(bf16[224,512]{1,0:T(8,128)(2,1)S(1)} %get-tuple-element.38), channel_id=1, source_target_pairs={{0,12},{4,8},{8,4},{12,0},{1,13},{5,9},{9,5},{13,1},{2,14},{6,10},... | collective-permute-start | bytes 688136 | tf_op jit(solution)/shard_map/ppermute | solution.py:24
  62.5 18.8 %collective-permute-start.25 = (bf16[224,512]{1,0:T(8,128)(2,1)S(1)}, bf16[224,512]{1,0:T(8,128)(2,1)S(1)}, u32[]{:S(2)}, u32[]{:S(2)}) collective-permute-start(bf16[224,512]{1,0:T(8,128)(2,1)S(1)} %get-tuple-element.45), channel_id=1, source_target_pairs={{0,8},{4,12},{8,0},{12,4},{1,9},{5,13},{9,1},{13,5},{2,10},{6,14},... | collective-permute-start | bytes 688136 | tf_op jit(solution)/shard_map/ppermute | solution.py:24
  64.1 18.1 %collective-permute-start.24 = (bf16[224,512]{1,0:T(8,128)(2,1)S(1)}, bf16[224,512]{1,0:T(8,128)(2,1)S(1)}, u32[]{:S(2)}, u32[]{:S(2)}) collective-permute-start(bf16[224,512]{1,0:T(8,128)(2,1)S(1)} %get-tuple-element.44), channel_id=1, source_target_pairs={{0,12},{4,8},{8,4},{12,0},{1,13},{5,9},{9,5},{13,1},{2,14},{6,10},... | collective-permute-start | bytes 688136 | tf_op jit(solution)/shard_map/ppermute | solution.py:24
  70.5 5.6 %collective-permute-start.6 = (f32[4,64,128]{2,1,0:T(8,128)S(1)}, f32[4,64,128]{2,1,0:T(8,128)S(1)}, u32[]{:S(2)}, u32[]{:S(2)}) collective-permute-start(f32[4,64,128]{2,1,0:T(8,128)S(1)} %get-tuple-element.51.refs_4_), channel_id=1, source_target_pairs={{0,4},{4,0},{8,12},{12,8},{1,5},{5,1},{9,13},{13,9},{2,6},{6,2},{1... | collective-permute-start | bytes 393224 | tf_op jit(solution)/shard_map/ppermute | solution.py:24
  73.4 2.8 %collective-permute-start.5 = (bf16[4,64,128]{2,1,0:T(8,128)(2,1)S(1)}, bf16[4,64,128]{2,1,0:T(8,128)(2,1)S(1)}, u32[]{:S(2)}, u32[]{:S(2)}) collective-permute-start(bf16[4,64,128]{2,1,0:T(8,128)(2,1)S(1)} %collective-permute-done.3.refs_1_), channel_id=1, source_target_pairs={{0,4},{4,0},{8,12},{12,8},{1,5},{5,1},{9,13},{13,9},{2,6},{6,2},{1... | collective-permute-start | bytes 196616 | tf_op jit(solution)/shard_map/ppermute | solution.py:24

commit v12 on v11

--- a/solution.py
+++ b/solution.py
@@ -8,7 +8,7 @@
 
 LANES = 128
 QUARTERS = (2, 2)
-GROUP = 64
+GROUP = 128
 NT = (((1,), (1,)), ((), ()))
 NN = (((1,), (0,)), ((), ()))
 VMEM = pl.BlockSpec(memory_space=pltpu.VMEM)
@@ -85,6 +85,12 @@
                 parts[t][...] = values[:, cut[0]:cut[0] + cut[1]]
     for c in rest:
         c.wait()
+
+
+def piece_kernel(harm, out, sem):
+    copy = pltpu.make_async_copy(harm.at[:, aligned(position()[2], out.shape[1])], out, sem)
+    copy.start()
+    copy.wait()
 
 
 def build_kernel(vox_ref, wgt_ref, matrix_ref, tile_ref):
@@ -228,11 +234,15 @@
     _, updated, buf, sems = refs[len(masks):]
     block = updated.shape[1] // count
     writes = []
+    height = updated.shape[0]
+    strip = height // 2 if height % 16 == 0 else height
     for n, j in enumerate(masks):
-        buf[n] = later[j - 2] - 0.5 * grads[n][...].astype(jnp.float32)
         at = columns(position()[0] ^ j, block, cut)
-        writes.append(pltpu.make_async_copy(buf.at[n], updated.at[:, at], sems.at[n]))
-        writes[-1].start()
+        for half, top in enumerate(range(0, height, strip)):
+            rows = slice(top, top + strip)
+            buf[n, rows] = later[j - 2, rows] - 0.5 * grads[n][rows].astype(jnp.float32)
+            writes.append(pltpu.make_async_copy(buf.at[n, rows], updated.at[rows, at], sems.at[n, half]))
+            writes[-1].start()
     for w in writes:
         w.wait()
 
@@ -265,7 +275,6 @@
     slab_count = lax.axis_size("slab")
     slab_bits = 1 if slab_count % 2 == 0 else 0
     pieces = 1 << (group_bits + slab_bits)
-    place = position()[2]
     width = harmonics.shape[1] // pieces
     rows_shape = (rows, samples)
     coef_far, measured_far, vox_far, wgt_far, ids_far, table_far, harm_far = [
@@ -281,7 +290,9 @@
         )
     ]
 
-    piece = lax.dynamic_slice_in_dim(harmonics, place * width, width, 1)
+    piece = kernel(
+        piece_kernel, [HBM], VMEM, shape((coef_local, width), bf16), [pltpu.SemaphoreType.DMA(())], grant=4
+    )(harm_far)
     fetched = {m: [swap(piece, "coef", m)] for m in range(2, count, 2)}
     table_shape = shape((half,) + angle_table.shape[1:], bf16)
     *parts, own, vox, wgt, table_mine, table_other, harm_own = kernel(
@@ -416,7 +427,7 @@
                 [VMEM] * (len(masks) + 1) + [HBM],
                 HBM,
                 shape((coef_local, cols), f32),
-                [pltpu.VMEM((len(masks), coef_local, cut[1]), f32), pltpu.SemaphoreType.DMA((len(masks),))],
+                [pltpu.VMEM((len(masks), coef_local, cut[1]), f32), pltpu.SemaphoreType.DMA((len(masks), 2))],
                 aliases={len(masks) + 1: 0},
             )(later[t - 1], *[returned[t][m] for m in masks], updated)
     return (updated, residual[:, None])

time: 83.6 us -> 88.7 us (1.061)
  waiting for transfers between devices: 28.7 us -> 41.1 us
  Pallas kernels: 30.4 us -> 26.6 us
  local copies, waits for them, and re-layouts: 2.52 us -> 0 us
    ppermute x23, waiting for transfers between devices: 23.7 us -> 31.3 us  [swap(): return lax.ppermute(value, axis, [(i, i ^ mask) for i in range(count)])]
    ppermute x3, waiting for transfers between devices: 4.92 us -> 9.72 us  [step_of(): fetched[m].append(lax.ppermute(fetched[m][0], ('groups', 'slab'), pairs))]
    pallas_call x2, Pallas kernels: 12.3 us -> 9.29 us  [step_of(): kernel(lambda *refs: penalty_kernel(count, pieces, cut, first, *refs), [V...]
    unnamed x10 -> x0, local copies, waits for them, and re-layouts: 1.57 us -> none
    pallas_call x1, Pallas kernels: 3.99 us -> 2.49 us  [step_of(): kernel(lambda *refs: sums_kernel(count, *refs), [VMEM] * 5 + [HBM], [VMEM...]
    dynamic_slice x1 -> x0, local copies, waits for them, and re-layouts: 0.95 us -> none  [step_of(): piece = lax.dynamic_slice_in_dim(harmonics, place * width, width, 1)]
    pallas_call x0 -> x1, Pallas kernels: none -> 0.95 us  [step_of(): kernel(piece_kernel, [HBM], VMEM, shape((coef_local, width), bf16), [pltp...]
  transfers between devices with their start and end apart: 26 -> 26, of which waited for: 9 -> 10; matrix products, arithmetic and copies ran while one was open for 1% -> 0% of each run, Pallas kernels for 32% -> 26%
where the time goes in v12:
time: 88.7 us; the launch traced here: 88.4 us
  waiting for transfers between devices  41.1 us (46%)
  Pallas kernels  26.6 us (30%)
  starting transfers between devices  19.8 us (22%)
  between operations  0.92 us (1%)
    ppermute x23, waiting for transfers between devices, swap(): return lax.ppermute(value, axis, [(i, i ^ mask) for i in range(count)])  31.3 us
    ppermute x23, starting transfers between devices, swap(): return lax.ppermute(value, axis, [(i, i ^ mask) for i in range(count)])  14.7 us
    ppermute x3, waiting for transfers between devices, step_of(): fetched[m].append(lax.ppermute(fetched[m][0], ('groups', 'slab'), pairs))  9.72 us
    pallas_call x2, Pallas kernels, step_of(): kernel(lambda *refs: penalty_kernel(count, pieces, cut, first, *refs), [V...  9.29 us
    pallas_call x1, Pallas kernels, step_of(): kernel(lambda *refs: data_kernel(count, cuts, len(half_mine), *refs), [VM...  5.2 us
    ppermute x3, starting transfers between devices, step_of(): fetched[m].append(lax.ppermute(fetched[m][0], ('groups', 'slab'), pairs))  5.12 us
    pallas_call x1, Pallas kernels, step_of(): kernel(build_kernel, [VMEM, VMEM], VMEM, shape((rows // 2, cols), bf16),...  4.14 us
    pallas_call x1, Pallas kernels, step_of(): kernel(lambda *refs: prepare_kernel(count, cuts, *refs), [HBM] * 6, [VMEM...  2.91 us
  transfers between devices with their start and end apart: 26, of which 10 were waited for; matrix products, arithmetic and copies ran while one was open for 0% of the time, Pallas kernels for 26%

profile of v12, /device:TPU:0, one launch (start us, length us, event | category | flops | bytes accessed | tf_op | source)
XLA Modules:
  0.0 88.4 jit_solution(4087842392107387348)
XLA Ops:
  0.6 2.9 %shard_map.86 = (bf16[224,1024]{1,0:T(8,128)(2,1)S(1)}, bf16[224,512]{1,0:T(8,128)(2,1)S(1)}, bf16[224,512]{1,0:T(8,128)(2,1)S(1)}, bf16[224,4096]{1,0:T(8,128)(...) custom-call(s32[8]{0:T(128)} %refs_0_.1, ...), custom_call_target="tpu_custom_call" | custom-call | tf_op jit(solution)/shard_map/pallas_call | solution.py:298
  3.6 0.6 collective-permute-start
  4.1 4.1 %shard_map.87.refs_0_.refs_8_ = bf16[256,4096]{1,0:T(8,128)(2,1)S(1)} custom-call(s32[256,128]{1,0:T(8,128)S(1)} %get-tuple-element.25.vox_ref, s32[256,128]{1,0:T(8,128)S(1)} %get-tuple-element.26.wgt_ref), custom_call_target="tpu_custom_call" | custom-call | tf_op jit(solution)/shard_map/pallas_call | solution.py:329
  8.3 0.1 collective-permute-start.7
  8.3 3.0 %collective-permute-start.8 = (bf16[224,1024]{1,0:T(8,128)(2,1)S(1)}, bf16[224,1024]{1,0:T(8,128)(2,1)S(1)}, u32[]{:S(2)}, u32[]{:S(2)}) collective-permute-start(bf16[224,1024]{1,0:T(8,128)(2,1)S(1)} %get-tuple-element.32), channel_id=1, source_target_pairs={{0,8},{4,12},{8,0},{12,4},{1,9},{5,13},{9,1},{13,5},{2,10},{6,14},... | collective-permute-start | bytes 1376264 | tf_op jit(solution)/shard_map/ppermute | solution.py:24
  11.3 0.9 %shard_map.89 = bf16[224,512]{1,0:T(8,128)(2,1)S(1)} custom-call(bf16[224,2048]{1,0:T(8,128)(2,1)} %harm.1), custom_call_target="tpu_custom_call" | custom-call | tf_op jit(solution)/shard_map/pallas_call | solution.py:293
  12.3 0.1 collective-permute-start.11
  12.3 1.1 %collective-permute-start.9 = (bf16[224,512]{1,0:T(8,128)(2,1)S(1)}, bf16[224,512]{1,0:T(8,128)(2,1)S(1)}, u32[]{:S(2)}, u32[]{:S(2)}) collective-permute-start(bf16[224,512]{1,0:T(8,128)(2,1)S(1)} %get-tuple-element.33), channel_id=1, source_target_pairs={{0,12},{4,8},{8,4},{12,0},{1,13},{5,9},{9,5},{13,1},{2,14},{6,10},... | collective-permute-start | bytes 688136 | tf_op jit(solution)/shard_map/ppermute | solution.py:24
  13.5 14.1 %collective-permute-done.11.refs_6_ = bf16[224,512]{1,0:T(8,128)(2,1)S(1)} collective-permute-done((bf16[224,512]{1,0:T(8,128)(2,1)S(1)}, bf16[224,512]{1,0:T(8,128)(2,1)S(1)}, u32[]{:S(2)}, u32[]{:S(2)}) %collective-permute-start.11) | collective-permute-done | bytes 229408 | tf_op jit(solution)/shard_map/ppermute | solution.py:24
  27.6 2.1 %collective-permute-start.12 = (bf16[224,512]{1,0:T(8,128)(2,1)S(1)}, bf16[224,512]{1,0:T(8,128)(2,1)S(1)}, u32[]{:S(2)}, u32[]{:S(2)}) collective-permute-start(bf16[224,512]{1,0:T(8,128)(2,1)S(1)} %collective-permute-done.11.refs_6_), channel_id=1, source_target_pairs={{0,1},{1,0},{2,3},{3,2},{16,17},{17,16},{18,19},{19,18},{4,5},{5,4... | collective-permute-start | bytes 688136 | tf_op jit(solution)/shard_map/ppermute | solution.py:327
  29.7 1.6 %collective-permute-done.9.refs_3_ = bf16[224,512]{1,0:T(8,128)(2,1)S(1)} collective-permute-done((bf16[224,512]{1,0:T(8,128)(2,1)S(1)}, bf16[224,512]{1,0:T(8,128)(2,1)S(1)}, u32[]{:S(2)}, u32[]{:S(2)}) %collective-permute-start.9) | collective-permute-done | bytes 229408 | tf_op jit(solution)/shard_map/ppermute | solution.py:24
  31.3 1.5 %collective-permute-start.13 = (bf16[224,512]{1,0:T(8,128)(2,1)S(1)}, bf16[224,512]{1,0:T(8,128)(2,1)S(1)}, u32[]{:S(2)}, u32[]{:S(2)}) collective-permute-start(bf16[224,512]{1,0:T(8,128)(2,1)S(1)} %collective-permute-done.11.refs_6_), channel_id=1, source_target_pairs={{0,16},{1,17},{2,18},{3,19},{16,0},{17,1},{18,2},{19,3},{4,20},{5,... | collective-permute-start | bytes 688136 | tf_op jit(solution)/shard_map/ppermute | solution.py:327
  32.8 0.0 collective-permute-done.8.refs_2_
  32.8 1.5 %collective-permute-start.14 = (bf16[224,512]{1,0:T(8,128)(2,1)S(1)}, bf16[224,512]{1,0:T(8,128)(2,1)S(1)}, u32[]{:S(2)}, u32[]{:S(2)}) collective-permute-start(bf16[224,512]{1,0:T(8,128)(2,1)S(1)} %collective-permute-done.11.refs_6_), channel_id=1, source_target_pairs={{0,17},{1,16},{2,19},{3,18},{16,1},{17,0},{18,3},{19,2},{4,21},{5,... | collective-permute-start | bytes 688136 | tf_op jit(solution)/shard_map/ppermute | solution.py:327
  34.3 0.0 collective-permute-done.12.refs_7_
  34.3 0.5 collective-permute-start.10
  34.8 9.7 %collective-permute-done.13.refs_8_ = bf16[224,512]{1,0:T(8,128)(2,1)S(1)} collective-permute-done((bf16[224,512]{1,0:T(8,128)(2,1)S(1)}, bf16[224,512]{1,0:T(8,128)(2,1)S(1)}, u32[]{:S(2)}, u32[]{:S(2)}) %collective-permute-start.13) | collective-permute-done | bytes 229408 | tf_op jit(solution)/shard_map/ppermute | solution.py:327
  44.5 0.0 collective-permute-start.1
  44.5 0.0 collective-permute-done.14.refs_9_
  44.5 0.5 collective-permute-start.15
  45.0 1.6 %collective-permute-done.15.refs_10_ = bf16[224,512]{1,0:T(8,128)(2,1)S(1)} collective-permute-done((bf16[224,512]{1,0:T(8,128)(2,1)S(1)}, bf16[224,512]{1,0:T(8,128)(2,1)S(1)}, u32[]{:S(2)}, u32[]{:S(2)}) %collective-permute-start.15) | collective-permute-done | bytes 229408 | tf_op jit(solution)/shard_map/ppermute | solution.py:24
  46.6 0.1 collective-permute-start.16
  46.8 0.4 collective-permute-start.17
  47.1 1.0 %collective-permute-done.16.refs_11_ = bf16[224,512]{1,0:T(8,128)(2,1)S(1)} collective-permute-done((bf16[224,512]{1,0:T(8,128)(2,1)S(1)}, bf16[224,512]{1,0:T(8,128)(2,1)S(1)}, u32[]{:S(2)}, u32[]{:S(2)}) %collective-permute-start.16) | collective-permute-done | bytes 229408 | tf_op jit(solution)/shard_map/ppermute | solution.py:24
  48.1 0.1 collective-permute-start.18
  48.2 0.0 collective-permute-done.refs_2_.refs_1_
  48.2 1.6 %collective-permute-start.22 = (bf16[224,512]{1,0:T(8,128)(2,1)S(1)}, bf16[224,512]{1,0:T(8,128)(2,1)S(1)}, u32[]{:S(2)}, u32[]{:S(2)}) collective-permute-start(bf16[224,512]{1,0:T(8,128)(2,1)S(1)} %get-tuple-element.39), channel_id=1, source_target_pairs={{0,12},{4,8},{8,4},{12,0},{1,13},{5,9},{9,5},{13,1},{2,14},{6,10},... | collective-permute-start | bytes 688136 | tf_op jit(solution)/shard_map/ppermute | solution.py:24
  49.9 2.5 %shard_map.88 = (f32[4,64,128]{2,1,0:T(8,128)S(1)}, f32[4,64,128]{2,1,0:T(8,128)S(1)}) custom-call(bf16[256,4096]{1,0:T(8,128)(2,1)S(1)} %shard_map.87.refs_0_.refs_8_, bf16[224,4096]{1,0:T(8,128)(2,1)S(1)} %get-tuple-element.27.refs_1_.refs_0_, bf16[224,4096]{1,0:T(8,128)(2,1)S(1)} %collective-permute-done.refs_2_.refs_1_, ...), custom_call_target="tpu_custom_call" | custom-call | tf_op jit(solution)/shard_map/pallas_call | solution.py:341
  52.4 0.5 collective-permute-start.2
  52.8 4.7 %shard_map.90 = (bf16[224,512]{1,0:T(8,128)(2,1)S(1)}, bf16[224,512]{1,0:T(8,128)(2,1)S(1)}, bf16[224,512]{1,0:T(8,128)(2,1)S(1)}, bf16[224,512]{1,0:T(8,128)(2,1)S(1)}, bf16[896,2048]{1,0:T(8,128)(2,1)S(1)}) custom-call(bf16[224,4096]{1,0:T(8,128)(2,1)S(1)} %get-tuple-element.27.refs_1_.refs_0_, bf16[224,4096]{1,0:T(8,128)(2,1)S(1)} %collective-permute-done.refs_2_.refs_1_, ...), custom_call_target="tpu_custom_call" | custom-call | tf_op jit(solution)/shard_map/pallas_call | solution.py:363
  57.5 4.6 %shard_map.91 = (bf16[224,512]{1,0:T(8,128)(2,1)S(1)}, bf16[224,512]{1,0:T(8,128)(2,1)S(1)}, bf16[224,512]{1,0:T(8,128)(2,1)S(1)}, bf16[224,512]{1,0:T(8,128)(2,1)S(1)}) custom-call(bf16[224,4096]{1,0:T(8,128)(2,1)S(1)} %get-tuple-element.27.refs_1_.refs_0_, bf16[224,4096]{1,0:T(8,128)(2,1)S(1)} %collective-permute-done.refs_2_.refs_1_, ...), custom_call_target="tpu_custom_call" | custom-call | tf_op jit(solution)/shard_map/pallas_call | solution.py:363
  62.1 0.1 collective-permute-start.23
  62.2 0.5 collective-permute-start.19
  62.7 1.7 %collective-permute-start.3 = (bf16[4,64,128]{2,1,0:T(8,128)(2,1)S(1)}, bf16[4,64,128]{2,1,0:T(8,128)(2,1)S(1)}, u32[]{:S(2)}, u32[]{:S(2)}) collective-permute-start(bf16[4,64,128]{2,1,0:T(8,128)(2,1)S(1)} %get-tuple-element.50.refs_0_), channel_id=1, source_target_pairs={{0,8},{4,12},{8,0},{12,4},{1,9},{5,13},{9,1},{13,5},{2,10},{6,14},... | collective-permute-start | bytes 196616 | tf_op jit(solution)/shard_map/ppermute | solution.py:24
  64.5 0.0 collective-permute-start.4
  64.5 2.6 %collective-permute-done.3.refs_1_ = bf16[4,64,128]{2,1,0:T(8,128)(2,1)S(1)} collective-permute-done((bf16[4,64,128]{2,1,0:T(8,128)(2,1)S(1)}, bf16[4,64,128]{2,1,0:T(8,128)(2,1)S(1)}, u32[]{:S(2)}, u32[]{:S(2)}) %collective-permute-start.3) | collective-permute-done | bytes 65568 | tf_op jit(solution)/shard_map/ppermute | solution.py:24
  67.1 1.6 %collective-permute-start.20 = (bf16[224,512]{1,0:T(8,128)(2,1)S(1)}, bf16[224,512]{1,0:T(8,128)(2,1)S(1)}, u32[]{:S(2)}, u32[]{:S(2)}) collective-permute-start(bf16[224,512]{1,0:T(8,128)(2,1)S(1)} %get-tuple-element.37), channel_id=1, source_target_pairs={{0,8},{4,12},{8,0},{12,4},{1,9},{5,13},{9,1},{13,5},{2,10},{6,14},... | collective-permute-start | bytes 688136 | tf_op jit(solution)/shard_map/ppermute | solution.py:24
  68.7 0.0 collective-permute-done.4.refs_2_
  68.7 0.5 collective-permute-start.25
  69.2 1.4 %collective-permute-start.24 = (bf16[224,512]{1,0:T(8,128)(2,1)S(1)}, bf16[224,512]{1,0:T(8,128)(2,1)S(1)}, u32[]{:S(2)}, u32[]{:S(2)}) collective-permute-start(bf16[224,512]{1,0:T(8,128)(2,1)S(1)} %get-tuple-element.44), channel_id=1, source_target_pairs={{0,12},{4,8},{8,4},{12,0},{1,13},{5,9},{9,5},{13,1},{2,14},{6,10},... | collective-permute-start | bytes 688136 | tf_op jit(solution)/shard_map/ppermute | solution.py:24
  70.6 4.7 %collective-permute-done.20.refs_13_ = bf16[224,512]{1,0:T(8,128)(2,1)S(1)} collective-permute-done((bf16[224,512]{1,0:T(8,128)(2,1)S(1)}, bf16[224,512]{1,0:T(8,128)(2,1)S(1)}, u32[]{:S(2)}, u32[]{:S(2)}) %collective-permute-start.20) | collective-permute-done | bytes 229408 | tf_op jit(solution)/shard_map/ppermute | solution.py:24
  75.3 4.3 %collective-permute-done.21.refs_14_ = bf16[224,512]{1,0:T(8,128)(2,1)S(1)} collective-permute-done((bf16[224,512]{1,0:T(8,128)(2,1)S(1)}, bf16[224,512]{1,0:T(8,128)(2,1)S(1)}, u32[]{:S(2)}, u32[]{:S(2)}) %collective-permute-start.21) | collective-permute-done | bytes 229408 | tf_op jit(solution)/shard_map/ppermute | solution.py:24
  79.6 0.4 collective-permute-start.5
  80.1 0.9 %collective-permute-done.5.refs_3_ = bf16[4,64,128]{2,1,0:T(8,128)(2,1)S(1)} collective-permute-done((bf16[4,64,128]{2,1,0:T(8,128)(2,1)S(1)}, bf16[4,64,128]{2,1,0:T(8,128)(2,1)S(1)}, u32[]{:S(2)}, u32[]{:S(2)}) %collective-permute-start.5) | collective-permute-done | bytes 65568 | tf_op jit(solution)/shard_map/ppermute | solution.py:24
  81.0 5.2 %shard_map.92 = (f32[224,4096]{1,0:T(8,128)}, f32[8,64,64]{2,1,0:T(8,128)}, f32[2,224,512]{2,1,0:T(8,128)S(1)}) custom-call(bf16[4,64,128]{2,1,0:T(8,128)(2,1)S(1)} %get-tuple-element.50.refs_0_, bf16[4,64,128]{2,1,0:T(8,128)(2,1)S(1)} %collective-permute-done.3.refs_1_, bf16[4,64,128]{2,1,0:T(8,128)(2,1)S(1)} %collective-permute-done.4.refs_2_, ...), custom_call_target="tpu_custom_call" | custom-call | tf_op jit(solution)/shard_map/pallas_call | solution.py:394
  86.2 0.8 shard_map.93.refs_2_
  87.0 0.4 collective-permute-done.24.refs_1_
  87.4 0.8 shard_map.94
  (14 shorter events, 0.1 us)
Async XLA Ops:
  3.6 44.7 %collective-permute-start = (bf16[224,4096]{1,0:T(8,128)(2,1)S(1)}, bf16[224,4096]{1,0:T(8,128)(2,1)S(1)}, u32[]{:S(2)}, u32[]{:S(2)}) collective-permute-start(bf16[224,4096]{1,0:T(8,128)(2,1)S(1)} %get-tuple-element.27.refs_1_.refs_0_), channel_id=1, source_target_pairs={{0,4},{4,0},{8,12},{12,8},{1,5},{5,1},{9,13},{13,9},{2,6},{6,2},{1... | collective-permute-start | bytes 5505032 | tf_op jit(solution)/shard_map/ppermute | solution.py:24
  8.3 71.8 %collective-permute-start.7 = (bf16[256,4096]{1,0:T(8,128)(2,1)S(1)}, bf16[256,4096]{1,0:T(8,128)(2,1)S(1)}, u32[]{:S(2)}, u32[]{:S(2)}) collective-permute-start(bf16[256,4096]{1,0:T(8,128)(2,1)S(1)} %shard_map.87.refs_0_.refs_8_), channel_id=1, source_target_pairs={{0,4},{4,0},{8,12},{12,8},{1,5},{5,1},{9,13},{13,9},{2,6},{6,2},{1... | collective-permute-start | bytes 6291464 | tf_op jit(solution)/shard_map/ppermute | solution.py:24
  8.3 24.4 %collective-permute-start.8 = (bf16[224,1024]{1,0:T(8,128)(2,1)S(1)}, bf16[224,1024]{1,0:T(8,128)(2,1)S(1)}, u32[]{:S(2)}, u32[]{:S(2)}) collective-permute-start(bf16[224,1024]{1,0:T(8,128)(2,1)S(1)} %get-tuple-element.32), channel_id=1, source_target_pairs={{0,8},{4,12},{8,0},{12,4},{1,9},{5,13},{9,1},{13,5},{2,10},{6,14},... | collective-permute-start | bytes 1376264 | tf_op jit(solution)/shard_map/ppermute | solution.py:24
  12.3 15.3 %collective-permute-start.11 = (bf16[224,512]{1,0:T(8,128)(2,1)S(1)}, bf16[224,512]{1,0:T(8,128)(2,1)S(1)}, u32[]{:S(2)}, u32[]{:S(2)}) collective-permute-start(bf16[224,512]{1,0:T(8,128)(2,1)S(1)} %shard_map.89), channel_id=1, source_target_pairs={{0,8},{4,12},{8,0},{12,4},{1,9},{5,13},{9,1},{13,5},{2,10},{6,14},... | collective-permute-start | bytes 688136 | tf_op jit(solution)/shard_map/ppermute | solution.py:24
  12.3 19.0 %collective-permute-start.9 = (bf16[224,512]{1,0:T(8,128)(2,1)S(1)}, bf16[224,512]{1,0:T(8,128)(2,1)S(1)}, u32[]{:S(2)}, u32[]{:S(2)}) collective-permute-start(bf16[224,512]{1,0:T(8,128)(2,1)S(1)} %get-tuple-element.33), channel_id=1, source_target_pairs={{0,12},{4,8},{8,4},{12,0},{1,13},{5,9},{9,5},{13,1},{2,14},{6,10},... | collective-permute-start | bytes 688136 | tf_op jit(solution)/shard_map/ppermute | solution.py:24
  27.6 6.7 %collective-permute-start.12 = (bf16[224,512]{1,0:T(8,128)(2,1)S(1)}, bf16[224,512]{1,0:T(8,128)(2,1)S(1)}, u32[]{:S(2)}, u32[]{:S(2)}) collective-permute-start(bf16[224,512]{1,0:T(8,128)(2,1)S(1)} %collective-permute-done.11.refs_6_), channel_id=1, source_target_pairs={{0,1},{1,0},{2,3},{3,2},{16,17},{17,16},{18,19},{19,18},{4,5},{5,4... | collective-permute-start | bytes 688136 | tf_op jit(solution)/shard_map/ppermute | solution.py:327
  31.3 13.2 %collective-permute-start.13 = (bf16[224,512]{1,0:T(8,128)(2,1)S(1)}, bf16[224,512]{1,0:T(8,128)(2,1)S(1)}, u32[]{:S(2)}, u32[]{:S(2)}) collective-permute-start(bf16[224,512]{1,0:T(8,128)(2,1)S(1)} %collective-permute-done.11.refs_6_), channel_id=1, source_target_pairs={{0,16},{1,17},{2,18},{3,19},{16,0},{17,1},{18,2},{19,3},{4,20},{5,... | collective-permute-start | bytes 688136 | tf_op jit(solution)/shard_map/ppermute | solution.py:327
  32.8 11.7 %collective-permute-start.14 = (bf16[224,512]{1,0:T(8,128)(2,1)S(1)}, bf16[224,512]{1,0:T(8,128)(2,1)S(1)}, u32[]{:S(2)}, u32[]{:S(2)}) collective-permute-start(bf16[224,512]{1,0:T(8,128)(2,1)S(1)} %collective-permute-done.11.refs_6_), channel_id=1, source_target_pairs={{0,17},{1,16},{2,19},{3,18},{16,1},{17,0},{18,3},{19,2},{4,21},{5,... | collective-permute-start | bytes 688136 | tf_op jit(solution)/shard_map/ppermute | solution.py:327
  34.3 18.5 %collective-permute-start.10 = (bf16[224,2048]{1,0:T(8,128)(2,1)S(1)}, bf16[224,2048]{1,0:T(8,128)(2,1)S(1)}, u32[]{:S(2)}, u32[]{:S(2)}) collective-permute-start(bf16[224,2048]{1,0:T(8,128)(2,1)S(1)} %get-tuple-element.34.refs_4_), channel_id=1, source_target_pairs={{0,4},{4,0},{8,12},{12,8},{1,5},{5,1},{9,13},{13,9},{2,6},{6,2},{1... | collective-permute-start | bytes 2752520 | tf_op jit(solution)/shard_map/ppermute | solution.py:24
  44.5 2.3 %collective-permute-start.1 = (bf16[4,224,256]{2,1,0:T(8,128)(2,1)S(1)}, bf16[4,224,256]{2,1,0:T(8,128)(2,1)S(1)}, u32[]{:S(2)}, u32[]{:S(2)}) collective-permute-start(bf16[4,224,256]{2,1,0:T(8,128)(2,1)S(1)} %get-tuple-element.29.refs_7_), channel_id=1, source_target_pairs={{0,4},{4,0},{8,12},{12,8},{1,5},{5,1},{9,13},{13,9},{2,6},{6,2},{1... | collective-permute-start | bytes 1376264 | tf_op jit(solution)/shard_map/ppermute | solution.py:24
  44.5 2.1 %collective-permute-start.15 = (bf16[224,512]{1,0:T(8,128)(2,1)S(1)}, bf16[224,512]{1,0:T(8,128)(2,1)S(1)}, u32[]{:S(2)}, u32[]{:S(2)}) collective-permute-start(bf16[224,512]{1,0:T(8,128)(2,1)S(1)} %collective-permute-done.11.refs_6_), channel_id=1, source_target_pairs={{0,4},{4,0},{8,12},{12,8},{1,5},{5,1},{9,13},{13,9},{2,6},{6,2},{1... | collective-permute-start | bytes 688136 | tf_op jit(solution)/shard_map/ppermute | solution.py:24
  46.6 1.5 %collective-permute-start.16 = (bf16[224,512]{1,0:T(8,128)(2,1)S(1)}, bf16[224,512]{1,0:T(8,128)(2,1)S(1)}, u32[]{:S(2)}, u32[]{:S(2)}) collective-permute-start(bf16[224,512]{1,0:T(8,128)(2,1)S(1)} %collective-permute-done.12.refs_7_), channel_id=1, source_target_pairs={{0,4},{4,0},{8,12},{12,8},{1,5},{5,1},{9,13},{13,9},{2,6},{6,2},{1... | collective-permute-start | bytes 688136 | tf_op jit(solution)/shard_map/ppermute | solution.py:24
  46.8 5.6 %collective-permute-start.17 = (bf16[224,512]{1,0:T(8,128)(2,1)S(1)}, bf16[224,512]{1,0:T(8,128)(2,1)S(1)}, u32[]{:S(2)}, u32[]{:S(2)}) collective-permute-start(bf16[224,512]{1,0:T(8,128)(2,1)S(1)} %collective-permute-done.13.refs_8_), channel_id=1, source_target_pairs={{0,4},{4,0},{8,12},{12,8},{1,5},{5,1},{9,13},{13,9},{2,6},{6,2},{1... | collective-permute-start | bytes 688136 | tf_op jit(solution)/shard_map/ppermute | solution.py:24
  48.1 4.7 %collective-permute-start.18 = (bf16[224,512]{1,0:T(8,128)(2,1)S(1)}, bf16[224,512]{1,0:T(8,128)(2,1)S(1)}, u32[]{:S(2)}, u32[]{:S(2)}) collective-permute-start(bf16[224,512]{1,0:T(8,128)(2,1)S(1)} %collective-permute-done.14.refs_9_), channel_id=1, source_target_pairs={{0,4},{4,0},{8,12},{12,8},{1,5},{5,1},{9,13},{13,9},{2,6},{6,2},{1... | collective-permute-start | bytes 688136 | tf_op jit(solution)/shard_map/ppermute | solution.py:24
  48.2 9.3 %collective-permute-start.22 = (bf16[224,512]{1,0:T(8,128)(2,1)S(1)}, bf16[224,512]{1,0:T(8,128)(2,1)S(1)}, u32[]{:S(2)}, u32[]{:S(2)}) collective-permute-start(bf16[224,512]{1,0:T(8,128)(2,1)S(1)} %get-tuple-element.39), channel_id=1, source_target_pairs={{0,12},{4,8},{8,4},{12,0},{1,13},{5,9},{9,5},{13,1},{2,14},{6,10},... | collective-permute-start | bytes 688136 | tf_op jit(solution)/shard_map/ppermute | solution.py:24
  52.4 10.4 %collective-permute-start.2 = (f32[4,64,128]{2,1,0:T(8,128)S(1)}, f32[4,64,128]{2,1,0:T(8,128)S(1)}, u32[]{:S(2)}, u32[]{:S(2)}) collective-permute-start(f32[4,64,128]{2,1,0:T(8,128)S(1)} %get-tuple-element.31), channel_id=1, source_target_pairs={{0,8},{4,12},{8,0},{12,4},{1,9},{5,13},{9,1},{13,5},{2,10},{6,14},... | collective-permute-start | bytes 393224 | tf_op jit(solution)/shard_map/ppermute | solution.py:24
  62.1 6.6 %collective-permute-start.23 = (bf16[224,512]{1,0:T(8,128)(2,1)S(1)}, bf16[224,512]{1,0:T(8,128)(2,1)S(1)}, u32[]{:S(2)}, u32[]{:S(2)}) collective-permute-start(bf16[224,512]{1,0:T(8,128)(2,1)S(1)} %get-tuple-element.42), channel_id=1, source_target_pairs={{0,4},{4,0},{8,12},{12,8},{1,5},{5,1},{9,13},{13,9},{2,6},{6,2},{1... | collective-permute-start | bytes 688136 | tf_op jit(solution)/shard_map/ppermute | solution.py:24
  62.2 7.0 %collective-permute-start.19 = (bf16[224,512]{1,0:T(8,128)(2,1)S(1)}, bf16[224,512]{1,0:T(8,128)(2,1)S(1)}, u32[]{:S(2)}, u32[]{:S(2)}) collective-permute-start(bf16[224,512]{1,0:T(8,128)(2,1)S(1)} %get-tuple-element.36), channel_id=1, source_target_pairs={{0,4},{4,0},{8,12},{12,8},{1,5},{5,1},{9,13},{13,9},{2,6},{6,2},{1... | collective-permute-start | bytes 688136 | tf_op jit(solution)/shard_map/ppermute | solution.py:24
  62.7 4.3 %collective-permute-start.3 = (bf16[4,64,128]{2,1,0:T(8,128)(2,1)S(1)}, bf16[4,64,128]{2,1,0:T(8,128)(2,1)S(1)}, u32[]{:S(2)}, u32[]{:S(2)}) collective-permute-start(bf16[4,64,128]{2,1,0:T(8,128)(2,1)S(1)} %get-tuple-element.50.refs_0_), channel_id=1, source_target_pairs={{0,8},{4,12},{8,0},{12,4},{1,9},{5,13},{9,1},{13,5},{2,10},{6,14},... | collective-permute-start | bytes 196616 | tf_op jit(solution)/shard_map/ppermute | solution.py:24
  64.5 4.3 %collective-permute-start.4 = (bf16[4,64,128]{2,1,0:T(8,128)(2,1)S(1)}, bf16[4,64,128]{2,1,0:T(8,128)(2,1)S(1)}, u32[]{:S(2)}, u32[]{:S(2)}) collective-permute-start(bf16[4,64,128]{2,1,0:T(8,128)(2,1)S(1)} %get-tuple-element.50.refs_0_), channel_id=1, source_target_pairs={{0,4},{4,0},{8,12},{12,8},{1,5},{5,1},{9,13},{13,9},{2,6},{6,2},{1... | collective-permute-start | bytes 196616 | tf_op jit(solution)/shard_map/ppermute | solution.py:24
  67.1 8.2 %collective-permute-start.20 = (bf16[224,512]{1,0:T(8,128)(2,1)S(1)}, bf16[224,512]{1,0:T(8,128)(2,1)S(1)}, u32[]{:S(2)}, u32[]{:S(2)}) collective-permute-start(bf16[224,512]{1,0:T(8,128)(2,1)S(1)} %get-tuple-element.37), channel_id=1, source_target_pairs={{0,8},{4,12},{8,0},{12,4},{1,9},{5,13},{9,1},{13,5},{2,10},{6,14},... | collective-permute-start | bytes 688136 | tf_op jit(solution)/shard_map/ppermute | solution.py:24
  68.7 10.9 %collective-permute-start.21 = (bf16[224,512]{1,0:T(8,128)(2,1)S(1)}, bf16[224,512]{1,0:T(8,128)(2,1)S(1)}, u32[]{:S(2)}, u32[]{:S(2)}) collective-permute-start(bf16[224,512]{1,0:T(8,128)(2,1)S(1)} %get-tuple-element.38), channel_id=1, source_target_pairs={{0,12},{4,8},{8,4},{12,0},{1,13},{5,9},{9,5},{13,1},{2,14},{6,10},... | collective-permute-start | bytes 688136 | tf_op jit(solution)/shard_map/ppermute | solution.py:24
  68.7 17.4 %collective-permute-start.25 = (bf16[224,512]{1,0:T(8,128)(2,1)S(1)}, bf16[224,512]{1,0:T(8,128)(2,1)S(1)}, u32[]{:S(2)}, u32[]{:S(2)}) collective-permute-start(bf16[224,512]{1,0:T(8,128)(2,1)S(1)} %get-tuple-element.45), channel_id=1, source_target_pairs={{0,8},{4,12},{8,0},{12,4},{1,9},{5,13},{9,1},{13,5},{2,10},{6,14},... | collective-permute-start | bytes 688136 | tf_op jit(solution)/shard_map/ppermute | solution.py:24
  69.2 18.2 %collective-permute-start.24 = (bf16[224,512]{1,0:T(8,128)(2,1)S(1)}, bf16[224,512]{1,0:T(8,128)(2,1)S(1)}, u32[]{:S(2)}, u32[]{:S(2)}) collective-permute-start(bf16[224,512]{1,0:T(8,128)(2,1)S(1)} %get-tuple-element.44), channel_id=1, source_target_pairs={{0,12},{4,8},{8,4},{12,0},{1,13},{5,9},{9,5},{13,1},{2,14},{6,10},... | collective-permute-start | bytes 688136 | tf_op jit(solution)/shard_map/ppermute | solution.py:24
  75.3 5.6 %collective-permute-start.6 = (f32[4,64,128]{2,1,0:T(8,128)S(1)}, f32[4,64,128]{2,1,0:T(8,128)S(1)}, u32[]{:S(2)}, u32[]{:S(2)}) collective-permute-start(f32[4,64,128]{2,1,0:T(8,128)S(1)} %get-tuple-element.51.refs_4_), channel_id=1, source_target_pairs={{0,4},{4,0},{8,12},{12,8},{1,5},{5,1},{9,13},{13,9},{2,6},{6,2},{1... | collective-permute-start | bytes 393224 | tf_op jit(solution)/shard_map/ppermute | solution.py:24
  79.6 1.3 %collective-permute-start.5 = (bf16[4,64,128]{2,1,0:T(8,128)(2,1)S(1)}, bf16[4,64,128]{2,1,0:T(8,128)(2,1)S(1)}, u32[]{:S(2)}, u32[]{:S(2)}) collective-permute-start(bf16[4,64,128]{2,1,0:T(8,128)(2,1)S(1)} %collective-permute-done.3.refs_1_), channel_id=1, source_target_pairs={{0,4},{4,0},{8,12},{12,8},{1,5},{5,1},{9,13},{13,9},{2,6},{6,2},{1... | collective-permute-start | bytes 196616 | tf_op jit(solution)/shard_map/ppermute | solution.py:24
